TPU v7x, 256 devices: a whole 4x4x8 slice. The times are simulated.
256 devices in a mesh: row: 32 (over y, z), col: 8 (over x, core).
Axes of the slice: x: 4, y: 4, z: 8, core: 2. Of those that a mesh axis runs over, the one named last changes fastest.
Arguments:
- tokens: bfloat16 [1536, 8192], P('row', 'col'), may hold values from -6 to 6
- weight: bfloat16 [8192, 32768], P('col', 'row'), may hold values from -0.109375 to 0.109375
- tile_rows: int32 [32, 8, 32], P('row', 'col'), may hold values from 0 to 63, as said below
- tile_cols: int32 [32, 8, 32], P('row', 'col'), may hold values from 0 to 255, as said below
- tile_count: int32 [32, 8], P('row', 'col'), may hold values from 8 to 32, as said below
- hidden_cotangent: bfloat16 [1536, 32768], P('col', 'row'), may hold values from -6 to 6
Outputs:
- hidden: bfloat16 [1536, 32768], P('col', 'row')
- input_grad: bfloat16 [1536, 8192], P('row', 'col')
- weight_grad: bfloat16 [8192, 32768], P('col', 'row')
Inputs may be any that keep to these rules, and one draw needn't show every extreme that they name: tile_rows[r, c, k] is a row block of the weight (tiles of 128 x 128) among the 8 blocks from c * 8 on, which index c of col holds. tile_cols[r, c, k] is a column block among the 8 blocks from r * 8 on, which index r of row holds; the 32 candidate tiles of one device are distinct. The first tile_count[r, c] candidates of device (r, c) are its nonzero tiles; some device holds 32.
All inputs are finite; a program needn't handle non-finite values.
Results may differ from a plain program's by a relative error of at most 0.0049.
Values may be sent and summed in bfloat16 or wider, within the bound.
No kernel may reach another device: no remote copies, remote signals or barrier semaphores. Data moves between devices by JAX's collectives and lax.ppermute only.
A program may use at most 128 MiB of HBM per device.

v0:
```python
import jax
import jax.numpy as jnp
from jax import lax
from jax.sharding import Mesh
from jax.sharding import PartitionSpec as P

TILE = 128
ROW = ("row_0", "row_1")


def laid_out(pieces, dim):
    pieces = jnp.moveaxis(pieces, 0, dim)
    dims = pieces.shape
    return pieces.reshape(*dims[:dim], dims[dim] * dims[dim + 1], *dims[dim + 2 :])


def all_blocks(shard, axes, turns):
    pieces = shard
    for k in turns:
        pieces = lax.all_gather(pieces, axes[k])
    done = turns[::-1]
    back = [done.index(k) for k in range(len(axes))]
    pieces = pieces.transpose(*back, *range(len(axes), pieces.ndim))
    return pieces.reshape(-1, *shard.shape)


def gathered_by_axis(shard, axes, turns, dim):
    return laid_out(all_blocks(shard, axes, turns), dim)


def own_rows(so_far, axes):
    for axis in axes:
        so_far = lax.psum_scatter(so_far, axis, scatter_dimension=0, tiled=True)
    return so_far


def sparse_apply(inputs, live_tiles, in_index, out_index, out_blocks, flipped):
    count_rows, in_width = inputs.shape
    in_blocks = in_width // TILE
    block_rows = 128
    picker = (in_index[:, None] == jnp.arange(in_blocks)[None, :]).astype(jnp.bfloat16)
    placer = (out_index[:, None] == jnp.arange(out_blocks)[None, :]).astype(jnp.float32)

    def per_block(rows_block):
        shaped_rows = rows_block.reshape(block_rows, in_blocks, TILE)
        pieces = jnp.einsum(
            "bjp,kj->bkp", shaped_rows, picker, preferred_element_type=jnp.float32
        ).astype(jnp.bfloat16)
        if flipped:
            product = jnp.einsum(
                "bkq,kpq->bkp", pieces, live_tiles, preferred_element_type=jnp.float32
            )
        else:
            product = jnp.einsum(
                "bkp,kpq->bkq", pieces, live_tiles, preferred_element_type=jnp.float32
            )
        placed = jnp.einsum("bkq,kc->bcq", product, placer, precision=lax.Precision.HIGHEST)
        return placed.reshape(block_rows, out_blocks * TILE)

    stacked = inputs.reshape(count_rows // block_rows, block_rows, in_width)
    return lax.map(per_block, stacked).reshape(count_rows, out_blocks * TILE)


def tile_grads(full_tokens, full_grads, local_rows, local_cols, is_live, row_blocks, col_blocks):
    count_rows = full_tokens.shape[0]
    block_rows = 128
    steps_count = count_rows // block_rows
    left_side = full_tokens.reshape(steps_count, block_rows, row_blocks, TILE)
    right_side = full_grads.reshape(steps_count, block_rows, col_blocks, TILE)

    def accumulate(running, block_pair):
        token_block, grad_block = block_pair
        product = jnp.einsum(
            "bkp,bkq->kpq",
            token_block[:, local_rows],
            grad_block[:, local_cols],
            preferred_element_type=jnp.float32,
        )
        return (running + product, None)

    start_sums = jnp.zeros((local_rows.shape[0], TILE, TILE), jnp.float32)
    tile_sums, leftover = lax.scan(accumulate, start_sums, (left_side, right_side))
    tile_sums = tile_sums * is_live[:, None, None].astype(jnp.float32)
    slot_ids = local_rows * col_blocks + local_cols
    placed = (
        jnp.zeros((row_blocks * col_blocks, TILE, TILE), jnp.float32).at[slot_ids].add(tile_sums)
    )
    placed = placed.reshape(row_blocks, col_blocks, TILE, TILE).transpose(0, 2, 1, 3)
    return placed.reshape(row_blocks * TILE, col_blocks * TILE).astype(jnp.bfloat16)


def on_device(tokens, weight, tile_rows, tile_cols, tile_count, hidden_cotangent):
    row_index = lax.axis_index(ROW)
    col_index = lax.axis_index("col")
    row_blocks = weight.shape[0] // TILE
    col_blocks = weight.shape[1] // TILE
    capacity = tile_rows.shape[2]
    local_rows = tile_rows.reshape(capacity) - col_index * row_blocks
    local_cols = tile_cols.reshape(capacity) - row_index * col_blocks
    is_live = jnp.arange(capacity) < tile_count.reshape(())
    shaped = weight.reshape(row_blocks, TILE, col_blocks, TILE)
    live_tiles = shaped[local_rows, :, local_cols, :] * is_live[:, None, None].astype(jnp.bfloat16)
    full_tokens = gathered_by_axis(tokens, ROW, (0, 1), 0)
    pre_act = lax.psum_scatter(
        sparse_apply(full_tokens, live_tiles, local_rows, local_cols, col_blocks, False),
        "col",
        scatter_dimension=0,
        tiled=True,
    )
    gate_value = jax.nn.sigmoid(pre_act)
    hidden = (pre_act * gate_value).astype(jnp.bfloat16)
    silu_slope = gate_value * (1.0 + pre_act * (1.0 - gate_value))
    grad_pre = (hidden_cotangent.astype(jnp.float32) * silu_slope).astype(jnp.bfloat16)
    full_grads = lax.all_gather(grad_pre, "col", axis=0, tiled=True)
    input_grad = own_rows(
        sparse_apply(full_grads, live_tiles, local_cols, local_rows, row_blocks, True), ROW
    ).astype(jnp.bfloat16)
    weight_grad = tile_grads(
        full_tokens, full_grads, local_rows, local_cols, is_live, row_blocks, col_blocks
    )
    return (hidden, input_grad, weight_grad)


def solution(mesh):
    split = Mesh(mesh.devices.reshape(4, 8, mesh.shape["col"]), ("row_0", "row_1", "col"))
    placed = (
        P(ROW, "col"),
        P("col", ROW),
        P(ROW, "col", None),
        P(ROW, "col", None),
        P(ROW, "col"),
        P("col", ROW),
    )
    return jax.shard_map(
        on_device,
        mesh=split,
        in_specs=placed,
        out_specs=(P("col", ROW), P(ROW, "col"), P("col", ROW)),
        check_vma=False,
    )
```

profile of v0, /device:TPU:6, one launch (start us, length us, event | category | flops | bytes accessed | tf_op | source)
XLA Modules:
  0.0 454.7 jit_solution(8898258210480005376)
XLA Ops:
  7.2 14.8 %all-gather = bf16[192,1024]{1,0:T(8,128)(2,1)} all-gather(bf16[48,1024]{1,0:T(8,128)(2,1)} %param.12), channel_id=2, replica_groups=mesh['row_0'=4,'row_1'=8,'col'=8] {'row_0'}, dimensions={0}, use_global_device_ids=true | all-gather | bytes 491520 | tf_op jit(solution)/shard_map/all_gather | solution.py:20
  26.5 42.0 %all-gather.7.cloned.1.call-done = bf16[32,48,1024]{2,1,0:T(8,128)(2,1)} async-done(((bf16[4,48,1024]{2,1,0:T(8,128)(2,1)}), bf16[32,48,1024]{2,1,0:T(8,128)(2,1)}) %all-gather.7.cloned.1.call-update) | async-done | bytes 3145744 | tf_op jit(solution)/shard_map/all_gather | solution.py:20
  68.6 4.1 copy.27
  72.7 3.5 broadcast.138.clone
  76.1 66.5 %while.33 = (s32[]{:T(128)}, f32[12,128,1024]{2,1,0:T(8,128)}, bf16[12,128,1024]{2,1,0:T(8,128)(2,1)}, bf16[32,128,128]{2,1,0:T(8,128)(2,1)S(1)}, s32[32]{0:T(128)S(1)}, /*index=5*/s32[32]{0:T(128)S(1)}, s32[]{:T(128)}) while((s32[]{:T(128)}, f32[12,128,1024]{2,1,0:T(8,128)}, bf16[12,128,1024]{2,1,0:T(8,128)(2,1)}, ...), condition=%wide.region_1.2_spmd.clone, body=%wide.region_0.1_spmd.clone.sunk | while | flops 193463296 | bytes 11273041 | solution.py:61
  78.3 2.4 fusion.79
  83.9 2.4 fusion.79
  95.0 2.4 fusion.79
  122.7 2.4 fusion.79
  142.7 41.9 %reduce-scatter.4.cloned.1.call-done = f32[192,1024]{1,0:T(8,128)} async-done(((f32[1536,1024]{1,0:T(8,128)}), f32[192,1024]{1,0:T(8,128)}) %reduce-scatter.4.cloned.1.call-update) | async-done | bytes 786448 | tf_op jit(solution)/shard_map/reduce_scatter | solution.py:104
  184.6 2.4 multiply_convert_fusion
  187.0 30.9 %all-gather.5.cloned.1.call-done = bf16[1536,1024]{1,0:T(8,128)(2,1)} async-done(((bf16[192,1024]{1,0:T(8,128)(2,1)}), bf16[1536,1024]{1,0:T(8,128)(2,1)}) %all-gather.5.cloned.1.call-update) | async-done | bytes 3145744 | tf_op jit(solution)/shard_map/all_gather | solution.py:114
  217.9 3.5 broadcast.138
  221.4 68.4 %while.34 = (s32[]{:T(128)}, f32[12,128,1024]{2,1,0:T(8,128)}, bf16[12,128,1024]{2,1,0:T(8,128)(2,1)}, bf16[32,128,128]{2,1,0:T(8,128)(2,1)S(1)}, s32[32]{0:T(128)S(1)}, /*index=5*/s32[32]{0:T(128)S(1)}, s32[]{:T(128)}) while((s32[]{:T(128)}, f32[12,128,1024]{2,1,0:T(8,128)}, bf16[12,128,1024]{2,1,0:T(8,128)(2,1)}, ...), condition=%wide.region_4.5_spmd.clone, body=%wide.region_3.4_spmd.clone.sunk | while | flops 193463296 | bytes 11273041 | solution.py:61
  291.7 2.6 copy.39
  294.2 2.5 copy.40
  296.7 61.0 %reduce-scatter.6.cloned.1.call-done = f32[384,1024]{1,0:T(8,128)} async-done(((f32[1536,1024]{1,0:T(8,128)}), f32[384,1024]{1,0:T(8,128)}) %reduce-scatter.6.cloned.1.call-update) | async-done | bytes 1572880 | tf_op jit(solution)/shard_map/reduce_scatter | solution.py:33
  357.7 72.4 %while.35 = (s32[]{:T(128)}, f32[32,128,128]{2,1,0:T(8,128)}, bf16[12,128,8,128]{3,2,1,0:T(8,128)(2,1)}, s32[32]{0:T(128)S(1)}, bf16[12,128,8,128]{3,2,1,0:T(8,1...) while((s32[]{:T(128)}, f32[32,128,128]{2,1,0:T(8,128)}, bf16[12,128,8,128]{3,2,1,0:T(8,128)(2,1)}, ...), condition=%wide.region_8.9_spmd.clone, body=%wide.region_7.8_spmd.clone.sunk | while | flops 135268544 | bytes 12592227 | solution.py:82
  365.0 3.4 select_add_fusion.2
  371.2 3.5 select_add_fusion.2
  377.3 3.5 select_add_fusion.2
  383.5 3.5 select_add_fusion.2
  389.7 3.4 select_add_fusion.2
  395.9 3.5 select_add_fusion.2
  402.1 3.4 select_add_fusion.2
  408.2 3.4 select_add_fusion.2
  414.4 3.4 select_add_fusion.2
  420.5 3.4 select_add_fusion.2
  426.7 3.4 select_add_fusion.2
  431.9 2.5 broadcast_in_dim.11
  434.4 6.3 %scatter_fusion = f32[64,128,128]{2,1,0:T(8,128)} fusion(f32[64,128,128]{2,1,0:T(8,128)} %broadcast_in_dim.11, s32[32]{0:T(128)S(1)} %get-tuple-element.217, f32[32,128,128]{2,1,0:T(8,128)S(1)} %broadcast_multiply_fusion), kind=kCustom, calls=%fused_computation.3 | custom fusion | flops 524288 | bytes 6291584 | tf_op jit(solution)/shard_map/scatter-add | solution.py:86
  440.7 2.6 convert_element_type.74
  (295 shorter events, 170.8 us)
Async XLA Ops:
  7.2 61.4 %all-gather.7.cloned.1.call-start = ((), (), s32[]{:S(2)}) async-start(), calls=%async_computation.7 | async-start | bytes 3538944 | tf_op jit(solution)/shard_map/all_gather | solution.py:20
  22.0 162.6 %reduce-scatter.4.cloned.1.call-start = ((), (), s32[]{:S(2)}) async-start(), calls=%async_computation.3 | async-start | bytes 7077888 | tf_op jit(solution)/shard_map/reduce_scatter | solution.py:104
  24.3 1.3 copy-start.3
  24.3 1.3 copy-start.4
  142.6 42.0 %copy-start.2 = (bf16[192,1024]{1,0:T(8,128)(2,1)S(1)}, bf16[192,1024]{1,0:T(8,128)(2,1)}, u32[]{:S(2)}) copy-start(bf16[192,1024]{1,0:T(8,128)(2,1)} %param.17) | copy-start | bytes 1179652
  142.7 75.3 %all-gather.5.cloned.1.call-start = ((), (), s32[]{:S(2)}) async-start(), calls=%async_computation.4 | async-start | bytes 3538944 | tf_op jit(solution)/shard_map/all_gather | solution.py:114
  187.0 170.7 %reduce-scatter.6.cloned.1.call-start = ((), (), s32[]{:S(2)}) async-start(), calls=%async_computation.5 | async-start | bytes 7864320 | tf_op jit(solution)/shard_map/reduce_scatter | solution.py:33
  289.8 1.9 copy-start
  289.8 156.8 %reduce-scatter.8.cloned.1.call-start = ((), (), s32[]{:S(2)}) async-start(), calls=%async_computation.6 | async-start | bytes 1769472 | tf_op jit(solution)/shard_map/reduce_scatter | solution.py:33
  291.7 2.6 copy-start.1
Sparse Core Ops, SparseCore 0:
  22.1 46.3 all-gather.6
  142.8 41.7 reduce-scatter.3
  187.1 30.7 all-gather.4
  289.9 67.6 reduce-scatter.5
  360.1 40.0 reduce-scatter.7
where the time goes:
time: 457 us; the launch traced here: 455 us
  waiting for transfers between devices  176 us (39%)
  matrix products  127 us (28%)
  local copies, waits for them, and re-layouts  105 us (23%)
  other arithmetic  14.9 us (3%)
  blocking collectives  14.8 us (3%)
  between operations  14.6 us (3%)
    reduce_scatter x2, waiting for transfers between devices, own_rows(): so_far = lax.psum_scatter(so_far, axis, scatter_dimension=0, tiled=True)  61 us
    dot_general x24, matrix products, per_block(): jnp.einsum('bkq,kc->bcq', product, placer, precision=lax.Precision.HIGHEST)  56.6 us
    all_gather x1, waiting for transfers between devices, all_blocks(): pieces = lax.all_gather(pieces, axes[k])  42 us
    reduce_scatter x1, waiting for transfers between devices, on_device(): lax.psum_scatter(sparse_apply(full_tokens, live_tiles, local_rows, local_...  41.9 us
    dot_general x12, matrix products, accumulate(): jnp.einsum('bkp,bkq->kpq', token_block[:, local_rows], grad_block[:, loca...  39.8 us
    all_gather x1, waiting for transfers between devices, on_device(): full_grads = lax.all_gather(grad_pre, 'col', axis=0, tiled=True)  30.9 us
    while x48, local copies, waits for them, and re-layouts  24.3 us
    dynamic_update_slice x24, local copies, waits for them, and re-layouts, sparse_apply(): return lax.map(per_block, stacked).reshape(count_rows, out_blocks * TILE)  20.5 us
  transfers between devices with their start and end apart: 5, of which 4 were waited for; matrix products, arithmetic and copies ran while one was open for 21% of the time, Pallas kernels for 0%

commit v1 on v0

v1 whole, which is shorter than its diff:
```python
import jax
import jax.numpy as jnp
from jax import lax
from jax.experimental import pallas as pl
from jax.experimental.pallas import tpu as pltpu
from jax.sharding import Mesh
from jax.sharding import PartitionSpec as P

TILE = 128
SIZES = {"y": 4, "z": 8, "x": 4, "core": 2}
ROW = ("y", "z")
COL = ("x", "core")
VM = pltpu.VMEM
F32 = jnp.float32
BF16 = jnp.bfloat16


def from_ahead(value, axis, k):
    n = SIZES[axis]
    return lax.ppermute(value, axis, [((i + k) % n, i) for i in range(n)])


def to_ahead(value, axis, k):
    n = SIZES[axis]
    return lax.ppermute(value, axis, [(i, (i + k) % n) for i in range(n)])


def call(body, outs, smem, vmem, flops=0, scratch=(), limit=40):
    outs = [jax.ShapeDtypeStruct(s, d) for s, d in outs]
    return pl.pallas_call(
        body,
        out_shape=outs,
        in_specs=[pl.BlockSpec(memory_space=pltpu.SMEM)] * len(smem)
        + [pl.BlockSpec(memory_space=VM)] * len(vmem),
        out_specs=[pl.BlockSpec(memory_space=VM)] * len(outs),
        scratch_shapes=list(scratch),
        compiler_params=pltpu.CompilerParams(vmem_limit_bytes=limit * 2**20),
        cost_estimate=pl.CostEstimate(
            flops=flops,
            transcendentals=0,
            bytes_accessed=sum(v.size * v.dtype.itemsize for v in vmem)
            + sum(o.size * o.dtype.itemsize for o in outs),
        ),
    )(*smem, *vmem)


def tile_ref(ref, r, c):
    return ref.at[
        pl.ds(pl.multiple_of(r * TILE, TILE), TILE), pl.ds(pl.multiple_of(c * TILE, TILE), TILE)
    ]


def mask_body(rows, cols, count, w, out, flipped):
    out[...] = jnp.zeros_like(out)
    flipped[...] = jnp.zeros_like(flipped)

    @pl.loop(0, count[0])
    def _(k):
        tile = tile_ref(w, rows[k], cols[k])[...]
        tile_ref(out, rows[k], cols[k])[...] = tile
        tile_ref(flipped, cols[k], rows[k])[...] = tile.T


def place_body(pos, *refs):
    pieces, out = refs[:-1], refs[-1]
    for i, piece in enumerate(pieces):
        out[(pos[1] + i) % SIZES["z"]] = piece[...]


def up_body(pos, tok, w, keep, send, acc):
    core = pos[3]
    rows = keep.shape[0]
    part = jnp.dot(tok[...].reshape(2 * rows, tok.shape[2]), w[...], preferred_element_type=F32)
    acc[...] = part.reshape(acc.shape)
    keep[...] = acc[core]
    send[...] = acc[1 - core].astype(BF16)


def add_body(pos, *refs):
    keep, recv, out = refs[:4], refs[4:8], refs[8:]
    shift = pos[2] - pos[0] + 4
    for d in range(4):
        for j in range(4):

            @pl.when((shift + d) % 4 == j)
            def _(d=d, j=j):
                @pl.loop(0, out[d].shape[0] // 16)
                def _(i):
                    at = pl.ds(pl.multiple_of(i * 16, 16), 16)
                    total = keep[j][at] + recv[j][at].astype(F32)
                    out[d][at] = total.astype(out[d].dtype)


def fetch(choice, pieces, slots, sems):
    def each(act):
        for i in range(4):
            for k in range(4):

                @pl.when(choice(i) == k)
                def _(i=i, k=k):
                    act(pltpu.make_async_copy(pieces[k], slots(i), sems.at[i]))

    each(lambda c: c.start())
    return lambda: each(lambda c: c.wait())


def back_body(pos, *refs):
    mine, other, w, out = refs[:4], refs[4:8], refs[8], refs[9:13]
    grads, sems = refs[13:]
    core = pos[3]
    shift = pos[0] - pos[2] + 4
    waits = [
        fetch(lambda j: (shift + j) % 4, g, lambda j, s=s: grads.at[j, s], sems.at[k])
        for k, (s, g) in enumerate(((core, mine), (1 - core, other)))
    ]
    for wait in waits:
        wait()

    for j in range(4):
        part = jnp.dot(
            grads[j].reshape(-1, w.shape[0]), w[...], preferred_element_type=F32
        )
        out[j][...] = part.astype(out[j].dtype).reshape(out[j].shape)


def sum_y_body(pos, own, r1, r2, r3, *out):
    n = SIZES["z"]
    for i in range(n):
        b = (pos[1] + i) % n
        total = own[b] + r1[b].astype(F32) + r2[b].astype(F32) + r3[b].astype(F32)
        out[i][...] = total.astype(out[i].dtype)


def wgrad_body(pos, rows, cols, count, *refs):
    out, toks, grads, acc, sems = refs[-5:]
    refs = refs[:-5]
    n = len(refs) // 12
    core = pos[3]
    shift = pos[2] - pos[0] + 4
    waits = []
    for k in range(n):
        tok, mine, other = (refs[12 * k + 4 * s : 12 * k + 4 * s + 4] for s in range(3))
        moves = (
            (tok, lambda d: (shift + d) % 4, lambda d, k=k: toks.at[k, d]),
            (mine, lambda d: d, lambda d, k=k: grads.at[k, d, core]),
            (other, lambda d: d, lambda d, k=k: grads.at[k, d, 1 - core]),
        )
        for m, (pieces, choice, slots) in enumerate(moves):
            waits.append(fetch(choice, pieces, slots, sems.at[k, m]))
    acc[...] = jnp.zeros_like(acc)
    for wait in waits:
        wait()
    for k in range(n):

        @pl.loop(0, 4)
        def _(d, k=k):
            t = toks[k, d].reshape(-1, toks.shape[-1])
            g = grads[k, d].reshape(-1, grads.shape[-1])
            acc[...] += lax.dot_general(
                t, g, (((0,), (0,)), ((), ())), preferred_element_type=F32
            )

    out[...] = jnp.zeros_like(out)

    @pl.loop(0, count[0])
    def _(k):
        tile_ref(out, rows[k], cols[k])[...] = tile_ref(acc, rows[k], cols[k])[...].astype(BF16)


def gather_tokens(part, pos):
    rows, width = part.shape
    zs = [part] + [from_ahead(part, "z", i) for i in range(1, 8)]
    (own,) = call(place_body, [((8, rows, width), BF16)], [pos], zs)
    return [own] + [from_ahead(own, "y", j) for j in range(1, 4)]


def forward(blocks, wm, pos, cot):
    rows = blocks[0].shape[1] * 4
    depth, width = wm.shape
    keeps, recvs = [], []
    for block in blocks:
        keep, send = call(
            up_body,
            [((rows, width), F32), ((rows, width), BF16)],
            [pos],
            [block, wm],
            4 * rows * depth * width,
            [VM((2, rows, width), F32)],
        )
        keeps.append(keep)
        recvs.append(to_ahead(send, "core", 1))
    shape = (rows, width)
    own, *sends = call(add_body, [(shape, F32)] + [(shape, BF16)] * 3, [pos], keeps + recvs)
    pre_act = own
    for d, send in enumerate(sends):
        pre_act = pre_act + to_ahead(send, "x", d + 1).astype(F32)
    gate = jax.nn.sigmoid(pre_act)
    hidden = (pre_act * gate).astype(BF16)
    slope = gate * (1.0 + pre_act * (1.0 - gate))
    grad_pre = (cot.astype(F32) * slope).astype(BF16)
    return hidden, grad_pre


def gather_grads(grad_pre):
    mine = [grad_pre] + [from_ahead(grad_pre, "x", d) for d in range(1, 4)]
    other = [to_ahead(g, "core", 1) for g in mine]
    return mine, other


def backward(mine, other, flipped, pos):
    rows = mine[0].shape[0] // 4
    width, depth = flipped.shape
    shape = (8, rows, depth)
    own, *sends = call(
        back_body,
        [(shape, F32)] + [(shape, BF16)] * 3,
        [pos],
        mine + other + [flipped],
        64 * rows * depth * width,
        [VM((4, 2, 4 * rows, width), BF16), pltpu.SemaphoreType.DMA((2, 4))],
    )
    recvs = [to_ahead(s, "y", j + 1) for j, s in enumerate(sends)]
    shape = (rows, depth)
    own, *sends = call(sum_y_body, [(shape, F32)] + [(shape, BF16)] * 7, [pos], [own] + recvs)
    total = own
    for i, s in enumerate(sends):
        total = total + to_ahead(s, "z", i + 1).astype(F32)
    return total.astype(BF16)


CUTS = ((0, 48),)


def on_device(tokens, weight, tile_rows, tile_cols, tile_count, hidden_cotangent):
    y, z, x, core = (lax.axis_index(a) for a in ("y", "z", "x", "core"))
    pos = jnp.stack([y, z, x, core]).astype(jnp.int32)
    row_blocks = weight.shape[0] // TILE
    col_blocks = weight.shape[1] // TILE
    rows = tile_rows.reshape(-1) - (x * 2 + core) * row_blocks
    cols = tile_cols.reshape(-1) - (y * 8 + z) * col_blocks
    count = tile_count.reshape(1)
    wm, flipped = call(mask_body, [(weight.shape, BF16), (weight.shape[::-1], BF16)], [rows, cols, count], [weight])
    cot4 = hidden_cotangent.reshape(4, 48, -1)
    hiddens, in_grads, saved = [], [], []
    for a, b in CUTS:
        blocks = gather_tokens(tokens[a:b], pos)
        cot = cot4[:, a:b].reshape((b - a) * 4, -1)
        hidden, grad_pre = forward(blocks, wm, pos, cot)
        mine, other = gather_grads(grad_pre)
        in_grads.append(backward(mine, other, flipped, pos))
        hiddens.append(hidden.reshape(4, b - a, -1))
        saved += blocks + mine + other
    n, per = len(CUTS), (CUTS[0][1] - CUTS[0][0]) * 4
    (weight_grad,) = call(
        wgrad_body,
        [(weight.shape, BF16)],
        [pos, rows, cols, count],
        saved,
        2 * 1536 * weight.size,
        [
            VM((n, 4, 8, per // 4, weight.shape[0]), BF16),
            VM((n, 4, 2, per, weight.shape[1]), BF16),
            VM(weight.shape, F32),
            pltpu.SemaphoreType.DMA((n, 3, 4)),
        ],
    )
    hidden = jnp.concatenate(hiddens, axis=1).reshape(192, -1)
    return hidden, jnp.concatenate(in_grads, axis=0), weight_grad


def solution(mesh):
    split = Mesh(mesh.devices.reshape(4, 8, 4, 2), ("y", "z", "x", "core"))
    return jax.shard_map(
        on_device,
        mesh=split,
        in_specs=(
            P(ROW, COL),
            P(COL, ROW),
            P(ROW, COL, None),
            P(ROW, COL, None),
            P(ROW, COL),
            P(COL, ROW),
        ),
        out_specs=(P(COL, ROW), P(ROW, COL), P(COL, ROW)),
        check_vma=False,
    )
```

time: 457 us -> 196 us (0.43)
  matrix products: 127 us -> 0 us
  local copies, waits for them, and re-layouts: 105 us -> 2.49 us
  waiting for transfers between devices: 176 us -> 109 us
  starting transfers between devices: 0.39 us -> 50.7 us
  Pallas kernels: 0 us -> 28 us
  blocking collectives: 14.8 us -> 0 us
  between operations: 14.6 us -> 1.46 us
  other arithmetic: 14.9 us -> 2.74 us
    dot_general x84 -> x0, matrix products: 127 us -> none  [the longest x24 56.6 us: per_block(): jnp.einsum('bkq,kc->bcq', product, placer, precision=lax.Precision.HIGHEST)]
    ppermute x0 -> x34, waiting for transfers between devices: none -> 109 us  [the longest x21 57.6 us: to_ahead(): return lax.ppermute(value, axis, [(i, (i + k) % n) for i in range(n)])]
    reduce_scatter x3 -> x0, waiting for transfers between devices: 103 us -> none  [the longest x2 61 us: own_rows(): so_far = lax.psum_scatter(so_far, axis, scatter_dimension=0, tiled=True)]
    all_gather x2 -> x0, waiting for transfers between devices: 72.9 us -> none  [the longest x1 42 us: all_blocks(): pieces = lax.all_gather(pieces, axes[k])]
    ppermute x0 -> x34, starting transfers between devices: none -> 50.7 us  [the longest x13 28.1 us: from_ahead(): return lax.ppermute(value, axis, [((i + k) % n, i) for i in range(n)])]
    pallas_call x0 -> x10, Pallas kernels: none -> 28 us  [call(): pl.pallas_call(body, out_shape=outs, in_specs=[pl.BlockSpec(memory_space=...]
    while x48 -> x0, local copies, waits for them, and re-layouts: 24.3 us -> none
    dynamic_update_slice x24 -> x0, local copies, waits for them, and re-layouts: 20.5 us -> none  [sparse_apply(): return lax.map(per_block, stacked).reshape(count_rows, out_blocks * TILE)]
  transfers between devices with their start and end apart: 5 -> 34, of which waited for: 4 -> 19; matrix products, arithmetic and copies ran while one was open for 21% -> 0% of each run, Pallas kernels for 0% -> 10%
where the time goes in v1:
time: 196 us; the launch traced here: 194 us
  waiting for transfers between devices  109 us (56%)
  starting transfers between devices  50.7 us (26%)
  Pallas kernels  28 us (14%)
  other arithmetic  2.74 us (1%)
  local copies, waits for them, and re-layouts  2.49 us (1%)
    ppermute x21, waiting for transfers between devices, to_ahead(): return lax.ppermute(value, axis, [(i, (i + k) % n) for i in range(n)])  57.6 us
    ppermute x13, waiting for transfers between devices, from_ahead(): return lax.ppermute(value, axis, [((i + k) % n, i) for i in range(n)])  51.3 us
    ppermute x13, starting transfers between devices, from_ahead(): return lax.ppermute(value, axis, [((i + k) % n, i) for i in range(n)])  28.1 us
    pallas_call x10, Pallas kernels, call(): pl.pallas_call(body, out_shape=outs, in_specs=[pl.BlockSpec(memory_space=...  28 us
    ppermute x21, starting transfers between devices, to_ahead(): return lax.ppermute(value, axis, [(i, (i + k) % n) for i in range(n)])  22.7 us
  transfers between devices with their start and end apart: 34, of which 19 were waited for; matrix products, arithmetic and copies ran while one was open for 0% of the time, Pallas kernels for 10%

profile of v1, /device:TPU:6, one launch (start us, length us, event | category | flops | bytes accessed | tf_op | source)
XLA Modules:
  0.0 194.3 jit_solution(7042574642615246737)
XLA Ops:
  0.6 3.3 %collective-permute-start.5 = (bf16[48,1024]{1,0:T(8,128)(2,1)}, bf16[48,1024]{1,0:T(8,128)(2,1)S(1)}, u32[]{:S(2)}, u32[]{:S(2)}) collective-permute-start(bf16[48,1024]{1,0:T(8,128)(2,1)} %refs_0_.1), channel_id=1, source_target_pairs={{48,0},{56,8},{0,16},{8,24},{16,32},{24,40},{32,48},{40,56},{49,1}... | collective-permute-start | bytes 294920 | tf_op jit(solution)/shard_map/ppermute | solution.py:20
  4.0 4.9 %collective-permute-start.4 = (bf16[48,1024]{1,0:T(8,128)(2,1)}, bf16[48,1024]{1,0:T(8,128)(2,1)S(1)}, u32[]{:S(2)}, u32[]{:S(2)}) collective-permute-start(bf16[48,1024]{1,0:T(8,128)(2,1)} %refs_0_.1), channel_id=1, source_target_pairs={{40,0},{48,8},{56,16},{0,24},{8,32},{16,40},{24,48},{32,56},{41,1}... | collective-permute-start | bytes 294920 | tf_op jit(solution)/shard_map/ppermute | solution.py:20
  9.9 4.5 %collective-permute-start.2 = (bf16[48,1024]{1,0:T(8,128)(2,1)}, bf16[48,1024]{1,0:T(8,128)(2,1)S(1)}, u32[]{:S(2)}, u32[]{:S(2)}) collective-permute-start(bf16[48,1024]{1,0:T(8,128)(2,1)} %refs_0_.1), channel_id=1, source_target_pairs={{24,0},{32,8},{40,16},{48,24},{56,32},{0,40},{8,48},{16,56},{25,1}... | collective-permute-start | bytes 294920 | tf_op jit(solution)/shard_map/ppermute | solution.py:20
  14.4 2.7 %collective-permute-start.1 = (bf16[48,1024]{1,0:T(8,128)(2,1)}, bf16[48,1024]{1,0:T(8,128)(2,1)S(1)}, u32[]{:S(2)}, u32[]{:S(2)}) collective-permute-start(bf16[48,1024]{1,0:T(8,128)(2,1)} %refs_0_.1), channel_id=1, source_target_pairs={{16,0},{24,8},{32,16},{40,24},{48,32},{56,40},{0,48},{8,56},{17,1}... | collective-permute-start | bytes 294920 | tf_op jit(solution)/shard_map/ppermute | solution.py:20
  17.1 2.6 %collective-permute-start = (bf16[48,1024]{1,0:T(8,128)(2,1)}, bf16[48,1024]{1,0:T(8,128)(2,1)S(1)}, u32[]{:S(2)}, u32[]{:S(2)}) collective-permute-start(bf16[48,1024]{1,0:T(8,128)(2,1)} %refs_0_.1), channel_id=1, source_target_pairs={{8,0},{16,8},{24,16},{32,24},{40,32},{48,40},{56,48},{0,56},{9,1},... | collective-permute-start | bytes 294920 | tf_op jit(solution)/shard_map/ppermute | solution.py:20
  20.9 2.2 %collective-permute-done.3.refs_4_ = bf16[48,1024]{1,0:T(8,128)(2,1)S(1)} collective-permute-done((bf16[48,1024]{1,0:T(8,128)(2,1)}, bf16[48,1024]{1,0:T(8,128)(2,1)S(1)}, u32[]{:S(2)}, u32[]{:S(2)}) %collective-permute-start.3) | collective-permute-done | bytes 98336 | tf_op jit(solution)/shard_map/ppermute | solution.py:20
  23.1 2.9 %collective-permute-done.2.refs_3_ = bf16[48,1024]{1,0:T(8,128)(2,1)S(1)} collective-permute-done((bf16[48,1024]{1,0:T(8,128)(2,1)}, bf16[48,1024]{1,0:T(8,128)(2,1)S(1)}, u32[]{:S(2)}, u32[]{:S(2)}) %collective-permute-start.2) | collective-permute-done | bytes 98336 | tf_op jit(solution)/shard_map/ppermute | solution.py:20
  26.0 2.7 %collective-permute-done.1.refs_2_ = bf16[48,1024]{1,0:T(8,128)(2,1)S(1)} collective-permute-done((bf16[48,1024]{1,0:T(8,128)(2,1)}, bf16[48,1024]{1,0:T(8,128)(2,1)S(1)}, u32[]{:S(2)}, u32[]{:S(2)}) %collective-permute-start.1) | collective-permute-done | bytes 98336 | tf_op jit(solution)/shard_map/ppermute | solution.py:20
  30.8 1.7 collective-permute-start.9
  32.4 2.9 %collective-permute-start.8 = (bf16[8,48,1024]{2,1,0:T(8,128)(2,1)S(1)}, bf16[8,48,1024]{2,1,0:T(8,128)(2,1)S(1)}, u32[]{:S(2)}, u32[]{:S(2)}) collective-permute-start(bf16[8,48,1024]{2,1,0:T(8,128)(2,1)S(1)} %shard_map.85.tok.refs_0_), channel_id=1, source_target_pairs={{128,0},{192,64},{0,128},{64,192},{129,1},{193,65},{1,129},{65,193... | collective-permute-start | bytes 2359304 | tf_op jit(solution)/shard_map/ppermute | solution.py:20
  39.6 2.3 %shard_map.86 = (bf16[1024,1024]{1,0:T(8,128)(2,1)S(1)}, bf16[1024,1024]{1,0:T(8,128)(2,1)S(1)}) custom-call(s32[32]{0:T(128)S(1)} %get-tuple-element.58.rows, s32[32]{0:T(128)S(1)} %get-tuple-element.57.cols, s32[1]{0:T(128)} %bitcast.9.count, bf16[1024,1024]{1,0:T(8,128)(2,1)S(1)} %copy-done), custom_call_target="tpu_custom_call" | custom-call | bytes 6291456 | tf_op jit(solution)/shard_map/pallas_call | solution.py:30
  41.9 1.6 shard_map.87
  43.6 7.8 %collective-permute-done.9.tok.refs_3_ = bf16[8,48,1024]{2,1,0:T(8,128)(2,1)S(1)} collective-permute-done((bf16[8,48,1024]{2,1,0:T(8,128)(2,1)S(1)}, bf16[8,48,1024]{2,1,0:T(8,128)(2,1)S(1)}, u32[]{:S(2)}, u32[]{:S(2)}) %collective-permute-start.9) | collective-permute-done | bytes 786464 | tf_op jit(solution)/shard_map/ppermute | solution.py:20
  53.2 15.8 %collective-permute-done.8.tok.refs_2_ = bf16[8,48,1024]{2,1,0:T(8,128)(2,1)S(1)} collective-permute-done((bf16[8,48,1024]{2,1,0:T(8,128)(2,1)S(1)}, bf16[8,48,1024]{2,1,0:T(8,128)(2,1)S(1)}, u32[]{:S(2)}, u32[]{:S(2)}) %collective-permute-start.8) | collective-permute-done | bytes 786464 | tf_op jit(solution)/shard_map/ppermute | solution.py:20
  70.7 2.2 %shard_map.88 = (f32[192,1024]{1,0:T(8,128)S(1)}, bf16[192,1024]{1,0:T(8,128)(2,1)S(1)}) custom-call(s32[4]{0:T(128)S(1)} %pad_add_fusion.pos, bf16[8,48,1024]{2,1,0:T(8,128)(2,1)} %collective-permute-done.7.tok.refs_1_, bf16[1024,1024]{1,0:T(8,128)(2,1)S(1)} %get-tuple-element.29.w), custom_call_target="tpu_custom_call" | custom-call | flops 805306368 | bytes 4063232 | tf_op jit(solution)/shard_map/pallas_call | solution.py:30
  76.8 2.4 %collective-permute-start.15 = (bf16[192,1024]{1,0:T(8,128)(2,1)S(1)}, bf16[192,1024]{1,0:T(8,128)(2,1)S(1)}, u32[]{:S(2)}, u32[]{:S(2)}) collective-permute-start(bf16[192,1024]{1,0:T(8,128)(2,1)S(1)} %get-tuple-element.40), channel_id=1, source_target_pairs={{0,4},{2,6},{4,0},{6,2},{1,5},{3,7},{5,1},{7,3},{8,12},{10,14},{12... | collective-permute-start | bytes 1179656 | tf_op jit(solution)/shard_map/ppermute | solution.py:25
  79.2 9.0 %collective-permute-done.14 = bf16[192,1024]{1,0:T(8,128)(2,1)S(1)} collective-permute-done((bf16[192,1024]{1,0:T(8,128)(2,1)S(1)}, bf16[192,1024]{1,0:T(8,128)(2,1)S(1)}, u32[]{:S(2)}, u32[]{:S(2)}) %collective-permute-start.14) | collective-permute-done | bytes 393248 | tf_op jit(solution)/shard_map/ppermute | solution.py:25
  88.2 2.1 %collective-permute-done.15 = bf16[192,1024]{1,0:T(8,128)(2,1)S(1)} collective-permute-done((bf16[192,1024]{1,0:T(8,128)(2,1)S(1)}, bf16[192,1024]{1,0:T(8,128)(2,1)S(1)}, u32[]{:S(2)}, u32[]{:S(2)}) %collective-permute-start.15) | collective-permute-done | bytes 393248 | tf_op jit(solution)/shard_map/ppermute | solution.py:25
  90.3 7.5 %collective-permute-done.16 = bf16[192,1024]{1,0:T(8,128)(2,1)S(1)} collective-permute-done((bf16[192,1024]{1,0:T(8,128)(2,1)S(1)}, bf16[192,1024]{1,0:T(8,128)(2,1)S(1)}, u32[]{:S(2)}, u32[]{:S(2)}) %collective-permute-start.16) | collective-permute-done | bytes 393248 | tf_op jit(solution)/shard_map/ppermute | solution.py:25
  100.0 2.1 %collective-permute-start.18 = (bf16[192,1024]{1,0:T(8,128)(2,1)S(1)}, bf16[192,1024]{1,0:T(8,128)(2,1)S(1)}, u32[]{:S(2)}, u32[]{:S(2)}) collective-permute-start(bf16[192,1024]{1,0:T(8,128)(2,1)S(1)} %get-tuple-element.55.refs_0_.refs_4_), channel_id=1, source_target_pairs={{4,0},{6,2},{0,4},{2,6},{5,1},{7,3},{1,5},{3,7},{12,8},{14,10},{8,... | collective-permute-start | bytes 1179656 | tf_op jit(solution)/shard_map/ppermute | solution.py:20
  102.2 8.8 %collective-permute-done.19.refs_3_.refs_7_ = bf16[192,1024]{1,0:T(8,128)(2,1)S(1)} collective-permute-done((bf16[192,1024]{1,0:T(8,128)(2,1)S(1)}, bf16[192,1024]{1,0:T(8,128)(2,1)S(1)}, u32[]{:S(2)}, u32[]{:S(2)}) %collective-permute-start.19) | collective-permute-done | bytes 393248 | tf_op jit(solution)/shard_map/ppermute | solution.py:20
  111.0 2.6 %collective-permute-done.18.refs_2_.refs_6_ = bf16[192,1024]{1,0:T(8,128)(2,1)S(1)} collective-permute-done((bf16[192,1024]{1,0:T(8,128)(2,1)S(1)}, bf16[192,1024]{1,0:T(8,128)(2,1)S(1)}, u32[]{:S(2)}, u32[]{:S(2)}) %collective-permute-start.18) | collective-permute-done | bytes 393248 | tf_op jit(solution)/shard_map/ppermute | solution.py:20
  113.6 6.6 %collective-permute-done.17.refs_1_.refs_5_ = bf16[192,1024]{1,0:T(8,128)(2,1)S(1)} collective-permute-done((bf16[192,1024]{1,0:T(8,128)(2,1)S(1)}, bf16[192,1024]{1,0:T(8,128)(2,1)S(1)}, u32[]{:S(2)}, u32[]{:S(2)}) %collective-permute-start.17) | collective-permute-done | bytes 393248 | tf_op jit(solution)/shard_map/ppermute | solution.py:20
  120.3 1.7 collective-permute-done.21.refs_5_.refs_9_
  122.0 5.8 %shard_map.92 = (f32[8,48,1024]{2,1,0:T(8,128)S(1)}, bf16[8,48,1024]{2,1,0:T(8,128)(2,1)S(1)}, bf16[8,48,1024]{2,1,0:T(8,128)(2,1)S(1)}, bf16[8,48,1024]{2,1,0:T(8,128)(2,1)S(1)}) custom-call(s32[4]{0:T(128)S(1)} %pad_add_fusion.pos, bf16[192,1024]{1,0:T(8,128)(2,1)S(1)} %get-tuple-element.55.refs_0_.refs_4_, ...), custom_call_target="tpu_custom_call" | custom-call | flops 3221225472 | bytes 9175040 | tf_op jit(solution)/shard_map/pallas_call | solution.py:30
  127.9 2.4 %collective-permute-start.25 = (bf16[8,48,1024]{2,1,0:T(8,128)(2,1)S(1)}, bf16[8,48,1024]{2,1,0:T(8,128)(2,1)S(1)}, u32[]{:S(2)}, u32[]{:S(2)}) collective-permute-start(bf16[8,48,1024]{2,1,0:T(8,128)(2,1)S(1)} %get-tuple-element.45), channel_id=1, source_target_pairs={{0,128},{64,192},{128,0},{192,64},{1,129},{65,193},{129,1},{193,65... | collective-permute-start | bytes 2359304 | tf_op jit(solution)/shard_map/ppermute | solution.py:25
  130.3 2.5 %collective-permute-start.26 = (bf16[8,48,1024]{2,1,0:T(8,128)(2,1)S(1)}, bf16[8,48,1024]{2,1,0:T(8,128)(2,1)S(1)}, u32[]{:S(2)}, u32[]{:S(2)}) collective-permute-start(bf16[8,48,1024]{2,1,0:T(8,128)(2,1)S(1)} %get-tuple-element.46), channel_id=1, source_target_pairs={{0,192},{64,0},{128,64},{192,128},{1,193},{65,1},{129,65},{193,129... | collective-permute-start | bytes 2359304 | tf_op jit(solution)/shard_map/ppermute | solution.py:25
  132.8 32.7 %collective-permute-done.24.r1 = bf16[8,48,1024]{2,1,0:T(8,128)(2,1)S(1)} collective-permute-done((bf16[8,48,1024]{2,1,0:T(8,128)(2,1)S(1)}, bf16[8,48,1024]{2,1,0:T(8,128)(2,1)S(1)}, u32[]{:S(2)}, u32[]{:S(2)}) %collective-permute-start.24) | collective-permute-done | bytes 786464 | tf_op jit(solution)/shard_map/ppermute | solution.py:25
  167.0 3.3 %collective-permute-start.27 = (bf16[48,1024]{1,0:T(8,128)(2,1)S(1)}, bf16[48,1024]{1,0:T(8,128)(2,1)S(1)}, u32[]{:S(2)}, u32[]{:S(2)}) collective-permute-start(bf16[48,1024]{1,0:T(8,128)(2,1)S(1)} %get-tuple-element.48), channel_id=1, source_target_pairs={{0,8},{8,16},{16,24},{24,32},{32,40},{40,48},{48,56},{56,0},{1,9},... | collective-permute-start | bytes 294920 | tf_op jit(solution)/shard_map/ppermute | solution.py:25
  172.0 4.3 %collective-permute-start.30 = (bf16[48,1024]{1,0:T(8,128)(2,1)S(1)}, bf16[48,1024]{1,0:T(8,128)(2,1)S(1)}, u32[]{:S(2)}, u32[]{:S(2)}) collective-permute-start(bf16[48,1024]{1,0:T(8,128)(2,1)S(1)} %get-tuple-element.51), channel_id=1, source_target_pairs={{0,32},{8,40},{16,48},{24,56},{32,0},{40,8},{48,16},{56,24},{1,33}... | collective-permute-start | bytes 294920 | tf_op jit(solution)/shard_map/ppermute | solution.py:25
  176.3 2.8 %collective-permute-start.31 = (bf16[48,1024]{1,0:T(8,128)(2,1)S(1)}, bf16[48,1024]{1,0:T(8,128)(2,1)S(1)}, u32[]{:S(2)}, u32[]{:S(2)}) collective-permute-start(bf16[48,1024]{1,0:T(8,128)(2,1)S(1)} %get-tuple-element.52), channel_id=1, source_target_pairs={{0,40},{8,48},{16,56},{24,0},{32,8},{40,16},{48,24},{56,32},{1,41}... | collective-permute-start | bytes 294920 | tf_op jit(solution)/shard_map/ppermute | solution.py:25
  181.7 10.3 %shard_map.94 = bf16[1024,1024]{1,0:T(8,128)(2,1)} custom-call(s32[4]{0:T(128)S(1)} %pad_add_fusion.pos, s32[32]{0:T(128)S(1)} %get-tuple-element.58.rows, s32[32]{0:T(128)S(1)} %get-tuple-element.57.cols, s32[1]{0:T(128)} %bitcast.10.count, bf16[8,48,1024]{2,1,0:T(8,128)(2,1)S(1)} %shard_map.85.tok.refs_0_, ...), custom_call_target="tpu_custom_call" | custom-call | flops 3221225472 | bytes 8388608 | tf_op jit(solution)/shard_map/pallas_call | solution.py:30
  (56 shorter events, 25.8 us)
Async XLA Ops:
  0.6 16.4 %collective-permute-start.5 = (bf16[48,1024]{1,0:T(8,128)(2,1)}, bf16[48,1024]{1,0:T(8,128)(2,1)S(1)}, u32[]{:S(2)}, u32[]{:S(2)}) collective-permute-start(bf16[48,1024]{1,0:T(8,128)(2,1)} %refs_0_.1), channel_id=1, source_target_pairs={{48,0},{56,8},{0,16},{8,24},{16,32},{24,40},{32,48},{40,56},{49,1}... | collective-permute-start | bytes 294920 | tf_op jit(solution)/shard_map/ppermute | solution.py:20
  4.0 16.8 %collective-permute-start.4 = (bf16[48,1024]{1,0:T(8,128)(2,1)}, bf16[48,1024]{1,0:T(8,128)(2,1)S(1)}, u32[]{:S(2)}, u32[]{:S(2)}) collective-permute-start(bf16[48,1024]{1,0:T(8,128)(2,1)} %refs_0_.1), channel_id=1, source_target_pairs={{40,0},{48,8},{56,16},{0,24},{8,32},{16,40},{24,48},{32,56},{41,1}... | collective-permute-start | bytes 294920 | tf_op jit(solution)/shard_map/ppermute | solution.py:20
  8.9 14.2 %collective-permute-start.3 = (bf16[48,1024]{1,0:T(8,128)(2,1)}, bf16[48,1024]{1,0:T(8,128)(2,1)S(1)}, u32[]{:S(2)}, u32[]{:S(2)}) collective-permute-start(bf16[48,1024]{1,0:T(8,128)(2,1)} %refs_0_.1), channel_id=1, source_target_pairs={{32,0},{40,8},{48,16},{56,24},{0,32},{8,40},{16,48},{24,56},{33,1}... | collective-permute-start | bytes 294920 | tf_op jit(solution)/shard_map/ppermute | solution.py:20
  9.9 16.1 %collective-permute-start.2 = (bf16[48,1024]{1,0:T(8,128)(2,1)}, bf16[48,1024]{1,0:T(8,128)(2,1)S(1)}, u32[]{:S(2)}, u32[]{:S(2)}) collective-permute-start(bf16[48,1024]{1,0:T(8,128)(2,1)} %refs_0_.1), channel_id=1, source_target_pairs={{24,0},{32,8},{40,16},{48,24},{56,32},{0,40},{8,48},{16,56},{25,1}... | collective-permute-start | bytes 294920 | tf_op jit(solution)/shard_map/ppermute | solution.py:20
  14.4 14.3 %collective-permute-start.1 = (bf16[48,1024]{1,0:T(8,128)(2,1)}, bf16[48,1024]{1,0:T(8,128)(2,1)S(1)}, u32[]{:S(2)}, u32[]{:S(2)}) collective-permute-start(bf16[48,1024]{1,0:T(8,128)(2,1)} %refs_0_.1), channel_id=1, source_target_pairs={{16,0},{24,8},{32,16},{40,24},{48,32},{56,40},{0,48},{8,56},{17,1}... | collective-permute-start | bytes 294920 | tf_op jit(solution)/shard_map/ppermute | solution.py:20
  17.1 12.2 %collective-permute-start = (bf16[48,1024]{1,0:T(8,128)(2,1)}, bf16[48,1024]{1,0:T(8,128)(2,1)S(1)}, u32[]{:S(2)}, u32[]{:S(2)}) collective-permute-start(bf16[48,1024]{1,0:T(8,128)(2,1)} %refs_0_.1), channel_id=1, source_target_pairs={{8,0},{16,8},{24,16},{32,24},{40,32},{48,40},{56,48},{0,56},{9,1},... | collective-permute-start | bytes 294920 | tf_op jit(solution)/shard_map/ppermute | solution.py:20
  20.8 8.5 %collective-permute-start.6 = (bf16[48,1024]{1,0:T(8,128)(2,1)}, bf16[48,1024]{1,0:T(8,128)(2,1)S(1)}, u32[]{:S(2)}, u32[]{:S(2)}) collective-permute-start(bf16[48,1024]{1,0:T(8,128)(2,1)} %refs_0_.1), channel_id=1, source_target_pairs={{56,0},{0,8},{8,16},{16,24},{24,32},{32,40},{40,48},{48,56},{57,1}... | collective-permute-start | bytes 294920 | tf_op jit(solution)/shard_map/ppermute | solution.py:20
  30.8 20.7 %collective-permute-start.9 = (bf16[8,48,1024]{2,1,0:T(8,128)(2,1)S(1)}, bf16[8,48,1024]{2,1,0:T(8,128)(2,1)S(1)}, u32[]{:S(2)}, u32[]{:S(2)}) collective-permute-start(bf16[8,48,1024]{2,1,0:T(8,128)(2,1)S(1)} %shard_map.85.tok.refs_0_), channel_id=1, source_target_pairs={{192,0},{0,64},{64,128},{128,192},{193,1},{1,65},{65,129},{129,193... | collective-permute-start | bytes 2359304 | tf_op jit(solution)/shard_map/ppermute | solution.py:20
  32.4 36.5 %collective-permute-start.8 = (bf16[8,48,1024]{2,1,0:T(8,128)(2,1)S(1)}, bf16[8,48,1024]{2,1,0:T(8,128)(2,1)S(1)}, u32[]{:S(2)}, u32[]{:S(2)}) collective-permute-start(bf16[8,48,1024]{2,1,0:T(8,128)(2,1)S(1)} %shard_map.85.tok.refs_0_), channel_id=1, source_target_pairs={{128,0},{192,64},{0,128},{64,192},{129,1},{193,65},{1,129},{65,193... | collective-permute-start | bytes 2359304 | tf_op jit(solution)/shard_map/ppermute | solution.py:20
  35.3 35.4 %collective-permute-start.7 = (bf16[8,48,1024]{2,1,0:T(8,128)(2,1)S(1)}, bf16[8,48,1024]{2,1,0:T(8,128)(2,1)}, u32[]{:S(2)}, u32[]{:S(2)}) collective-permute-start(bf16[8,48,1024]{2,1,0:T(8,128)(2,1)S(1)} %shard_map.85.tok.refs_0_), channel_id=1, source_target_pairs={{64,0},{128,64},{192,128},{0,192},{65,1},{129,65},{193,129},{1,193... | collective-permute-start | bytes 2359304 | tf_op jit(solution)/shard_map/ppermute | solution.py:20
  43.5 30.2 %collective-permute-start.10 = (bf16[192,1024]{1,0:T(8,128)(2,1)S(1)}, bf16[192,1024]{1,0:T(8,128)(2,1)S(1)}, u32[]{:S(2)}, u32[]{:S(2)}) collective-permute-start(bf16[192,1024]{1,0:T(8,128)(2,1)S(1)} %get-tuple-element.34), channel_id=1, source_target_pairs={{0,1},{1,0},{2,3},{3,2},{4,5},{5,4},{6,7},{7,6},{8,9},{9,8},{10,11... | collective-permute-start | bytes 1179656 | tf_op jit(solution)/shard_map/ppermute | solution.py:25
  53.1 20.6 %collective-permute-start.13 = (bf16[192,1024]{1,0:T(8,128)(2,1)S(1)}, bf16[192,1024]{1,0:T(8,128)(2,1)S(1)}, u32[]{:S(2)}, u32[]{:S(2)}) collective-permute-start(bf16[192,1024]{1,0:T(8,128)(2,1)S(1)} %get-tuple-element.37), channel_id=1, source_target_pairs={{0,1},{1,0},{2,3},{3,2},{4,5},{5,4},{6,7},{7,6},{8,9},{9,8},{10,11... | collective-permute-start | bytes 1179656 | tf_op jit(solution)/shard_map/ppermute | solution.py:25
  70.6 3.1 %collective-permute-start.12 = (bf16[192,1024]{1,0:T(8,128)(2,1)S(1)}, bf16[192,1024]{1,0:T(8,128)(2,1)S(1)}, u32[]{:S(2)}, u32[]{:S(2)}) collective-permute-start(bf16[192,1024]{1,0:T(8,128)(2,1)S(1)} %get-tuple-element.36), channel_id=1, source_target_pairs={{0,1},{1,0},{2,3},{3,2},{4,5},{5,4},{6,7},{7,6},{8,9},{9,8},{10,11... | collective-permute-start | bytes 1179656 | tf_op jit(solution)/shard_map/ppermute | solution.py:25
  76.2 12.0 %collective-permute-start.14 = (bf16[192,1024]{1,0:T(8,128)(2,1)S(1)}, bf16[192,1024]{1,0:T(8,128)(2,1)S(1)}, u32[]{:S(2)}, u32[]{:S(2)}) collective-permute-start(bf16[192,1024]{1,0:T(8,128)(2,1)S(1)} %get-tuple-element.39), channel_id=1, source_target_pairs={{0,2},{2,4},{4,6},{6,0},{1,3},{3,5},{5,7},{7,1},{8,10},{10,12},{12... | collective-permute-start | bytes 1179656 | tf_op jit(solution)/shard_map/ppermute | solution.py:25
  76.8 13.5 %collective-permute-start.15 = (bf16[192,1024]{1,0:T(8,128)(2,1)S(1)}, bf16[192,1024]{1,0:T(8,128)(2,1)S(1)}, u32[]{:S(2)}, u32[]{:S(2)}) collective-permute-start(bf16[192,1024]{1,0:T(8,128)(2,1)S(1)} %get-tuple-element.40), channel_id=1, source_target_pairs={{0,4},{2,6},{4,0},{6,2},{1,5},{3,7},{5,1},{7,3},{8,12},{10,14},{12... | collective-permute-start | bytes 1179656 | tf_op jit(solution)/shard_map/ppermute | solution.py:25
  79.2 18.6 %collective-permute-start.16 = (bf16[192,1024]{1,0:T(8,128)(2,1)S(1)}, bf16[192,1024]{1,0:T(8,128)(2,1)S(1)}, u32[]{:S(2)}, u32[]{:S(2)}) collective-permute-start(bf16[192,1024]{1,0:T(8,128)(2,1)S(1)} %get-tuple-element.41), channel_id=1, source_target_pairs={{0,6},{2,0},{4,2},{6,4},{1,7},{3,1},{5,3},{7,5},{8,14},{10,8},{12,... | collective-permute-start | bytes 1179656 | tf_op jit(solution)/shard_map/ppermute | solution.py:25
  99.1 12.0 %collective-permute-start.19 = (bf16[192,1024]{1,0:T(8,128)(2,1)S(1)}, bf16[192,1024]{1,0:T(8,128)(2,1)S(1)}, u32[]{:S(2)}, u32[]{:S(2)}) collective-permute-start(bf16[192,1024]{1,0:T(8,128)(2,1)S(1)} %get-tuple-element.55.refs_0_.refs_4_), channel_id=1, source_target_pairs={{6,0},{0,2},{2,4},{4,6},{7,1},{1,3},{3,5},{5,7},{14,8},{8,10},{10,... | collective-permute-start | bytes 1179656 | tf_op jit(solution)/shard_map/ppermute | solution.py:20
  100.0 13.6 %collective-permute-start.18 = (bf16[192,1024]{1,0:T(8,128)(2,1)S(1)}, bf16[192,1024]{1,0:T(8,128)(2,1)S(1)}, u32[]{:S(2)}, u32[]{:S(2)}) collective-permute-start(bf16[192,1024]{1,0:T(8,128)(2,1)S(1)} %get-tuple-element.55.refs_0_.refs_4_), channel_id=1, source_target_pairs={{4,0},{6,2},{0,4},{2,6},{5,1},{7,3},{1,5},{3,7},{12,8},{14,10},{8,... | collective-permute-start | bytes 1179656 | tf_op jit(solution)/shard_map/ppermute | solution.py:20
  102.1 18.2 %collective-permute-start.17 = (bf16[192,1024]{1,0:T(8,128)(2,1)S(1)}, bf16[192,1024]{1,0:T(8,128)(2,1)S(1)}, u32[]{:S(2)}, u32[]{:S(2)}) collective-permute-start(bf16[192,1024]{1,0:T(8,128)(2,1)S(1)} %get-tuple-element.55.refs_0_.refs_4_), channel_id=1, source_target_pairs={{2,0},{4,2},{6,4},{0,6},{3,1},{5,3},{7,5},{1,7},{10,8},{12,10},{14... | collective-permute-start | bytes 1179656 | tf_op jit(solution)/shard_map/ppermute | solution.py:20
  102.2 18.1 %collective-permute-start.20 = (bf16[192,1024]{1,0:T(8,128)(2,1)S(1)}, bf16[192,1024]{1,0:T(8,128)(2,1)S(1)}, u32[]{:S(2)}, u32[]{:S(2)}) collective-permute-start(bf16[192,1024]{1,0:T(8,128)(2,1)S(1)} %get-tuple-element.55.refs_0_.refs_4_), channel_id=1, source_target_pairs={{0,1},{1,0},{2,3},{3,2},{4,5},{5,4},{6,7},{7,6},{8,9},{9,8},{10,11... | collective-permute-start | bytes 1179656 | tf_op jit(solution)/shard_map/ppermute | solution.py:25
  111.0 9.2 %collective-permute-start.23 = (bf16[192,1024]{1,0:T(8,128)(2,1)S(1)}, bf16[192,1024]{1,0:T(8,128)(2,1)S(1)}, u32[]{:S(2)}, u32[]{:S(2)}) collective-permute-start(bf16[192,1024]{1,0:T(8,128)(2,1)S(1)} %collective-permute-done.19.refs_3_.refs_7_), channel_id=1, source_target_pairs={{0,1},{1,0},{2,3},{3,2},{4,5},{5,4},{6,7},{7,6},{8,9},{9,8},{10,11... | collective-permute-start | bytes 1179656 | tf_op jit(solution)/shard_map/ppermute | solution.py:25
  113.6 6.7 %collective-permute-start.22 = (bf16[192,1024]{1,0:T(8,128)(2,1)S(1)}, bf16[192,1024]{1,0:T(8,128)(2,1)S(1)}, u32[]{:S(2)}, u32[]{:S(2)}) collective-permute-start(bf16[192,1024]{1,0:T(8,128)(2,1)S(1)} %collective-permute-done.18.refs_2_.refs_6_), channel_id=1, source_target_pairs={{0,1},{1,0},{2,3},{3,2},{4,5},{5,4},{6,7},{7,6},{8,9},{9,8},{10,11... | collective-permute-start | bytes 1179656 | tf_op jit(solution)/shard_map/ppermute | solution.py:25
  127.8 37.7 %collective-permute-start.24 = (bf16[8,48,1024]{2,1,0:T(8,128)(2,1)S(1)}, bf16[8,48,1024]{2,1,0:T(8,128)(2,1)S(1)}, u32[]{:S(2)}, u32[]{:S(2)}) collective-permute-start(bf16[8,48,1024]{2,1,0:T(8,128)(2,1)S(1)} %get-tuple-element.44), channel_id=1, source_target_pairs={{0,64},{64,128},{128,192},{192,0},{1,65},{65,129},{129,193},{193,1... | collective-permute-start | bytes 2359304 | tf_op jit(solution)/shard_map/ppermute | solution.py:25
  127.9 37.6 %collective-permute-start.25 = (bf16[8,48,1024]{2,1,0:T(8,128)(2,1)S(1)}, bf16[8,48,1024]{2,1,0:T(8,128)(2,1)S(1)}, u32[]{:S(2)}, u32[]{:S(2)}) collective-permute-start(bf16[8,48,1024]{2,1,0:T(8,128)(2,1)S(1)} %get-tuple-element.45), channel_id=1, source_target_pairs={{0,128},{64,192},{128,0},{192,64},{1,129},{65,193},{129,1},{193,65... | collective-permute-start | bytes 2359304 | tf_op jit(solution)/shard_map/ppermute | solution.py:25
  130.3 35.8 %collective-permute-start.26 = (bf16[8,48,1024]{2,1,0:T(8,128)(2,1)S(1)}, bf16[8,48,1024]{2,1,0:T(8,128)(2,1)S(1)}, u32[]{:S(2)}, u32[]{:S(2)}) collective-permute-start(bf16[8,48,1024]{2,1,0:T(8,128)(2,1)S(1)} %get-tuple-element.46), channel_id=1, source_target_pairs={{0,192},{64,0},{128,64},{192,128},{1,193},{65,1},{129,65},{193,129... | collective-permute-start | bytes 2359304 | tf_op jit(solution)/shard_map/ppermute | solution.py:25
  167.0 12.2 %collective-permute-start.27 = (bf16[48,1024]{1,0:T(8,128)(2,1)S(1)}, bf16[48,1024]{1,0:T(8,128)(2,1)S(1)}, u32[]{:S(2)}, u32[]{:S(2)}) collective-permute-start(bf16[48,1024]{1,0:T(8,128)(2,1)S(1)} %get-tuple-element.48), channel_id=1, source_target_pairs={{0,8},{8,16},{16,24},{24,32},{32,40},{40,48},{48,56},{56,0},{1,9},... | collective-permute-start | bytes 294920 | tf_op jit(solution)/shard_map/ppermute | solution.py:25
  170.3 11.4 %collective-permute-start.28 = (bf16[48,1024]{1,0:T(8,128)(2,1)S(1)}, bf16[48,1024]{1,0:T(8,128)(2,1)S(1)}, u32[]{:S(2)}, u32[]{:S(2)}) collective-permute-start(bf16[48,1024]{1,0:T(8,128)(2,1)S(1)} %get-tuple-element.49), channel_id=1, source_target_pairs={{0,16},{8,24},{16,32},{24,40},{32,48},{40,56},{48,0},{56,8},{1,17}... | collective-permute-start | bytes 294920 | tf_op jit(solution)/shard_map/ppermute | solution.py:25
  171.1 20.9 %collective-permute-start.29 = (bf16[48,1024]{1,0:T(8,128)(2,1)S(1)}, bf16[48,1024]{1,0:T(8,128)(2,1)S(1)}, u32[]{:S(2)}, u32[]{:S(2)}) collective-permute-start(bf16[48,1024]{1,0:T(8,128)(2,1)S(1)} %get-tuple-element.50), channel_id=1, source_target_pairs={{0,24},{8,32},{16,40},{24,48},{32,56},{40,0},{48,8},{56,16},{1,25}... | collective-permute-start | bytes 294920 | tf_op jit(solution)/shard_map/ppermute | solution.py:25
  172.0 20.0 %collective-permute-start.30 = (bf16[48,1024]{1,0:T(8,128)(2,1)S(1)}, bf16[48,1024]{1,0:T(8,128)(2,1)S(1)}, u32[]{:S(2)}, u32[]{:S(2)}) collective-permute-start(bf16[48,1024]{1,0:T(8,128)(2,1)S(1)} %get-tuple-element.51), channel_id=1, source_target_pairs={{0,32},{8,40},{16,48},{24,56},{32,0},{40,8},{48,16},{56,24},{1,33}... | collective-permute-start | bytes 294920 | tf_op jit(solution)/shard_map/ppermute | solution.py:25
  176.3 15.7 %collective-permute-start.31 = (bf16[48,1024]{1,0:T(8,128)(2,1)S(1)}, bf16[48,1024]{1,0:T(8,128)(2,1)S(1)}, u32[]{:S(2)}, u32[]{:S(2)}) collective-permute-start(bf16[48,1024]{1,0:T(8,128)(2,1)S(1)} %get-tuple-element.52), channel_id=1, source_target_pairs={{0,40},{8,48},{16,56},{24,0},{32,8},{40,16},{48,24},{56,32},{1,41}... | collective-permute-start | bytes 294920 | tf_op jit(solution)/shard_map/ppermute | solution.py:25
  179.2 14.4 %collective-permute-start.32 = (bf16[48,1024]{1,0:T(8,128)(2,1)S(1)}, bf16[48,1024]{1,0:T(8,128)(2,1)S(1)}, u32[]{:S(2)}, u32[]{:S(2)}) collective-permute-start(bf16[48,1024]{1,0:T(8,128)(2,1)S(1)} %get-tuple-element.53), channel_id=1, source_target_pairs={{0,48},{8,56},{16,0},{24,8},{32,16},{40,24},{48,32},{56,40},{1,49}... | collective-permute-start | bytes 294920 | tf_op jit(solution)/shard_map/ppermute | solution.py:25
  181.7 11.8 %collective-permute-start.33 = (bf16[48,1024]{1,0:T(8,128)(2,1)S(1)}, bf16[48,1024]{1,0:T(8,128)(2,1)S(1)}, u32[]{:S(2)}, u32[]{:S(2)}) collective-permute-start(bf16[48,1024]{1,0:T(8,128)(2,1)S(1)} %get-tuple-element.54), channel_id=1, source_target_pairs={{0,56},{8,0},{16,8},{24,16},{32,24},{40,32},{48,40},{56,48},{1,57}... | collective-permute-start | bytes 294920 | tf_op jit(solution)/shard_map/ppermute | solution.py:25
  (5 other events, 29.1 us)

commit v2 on v1

v2 whole, which is shorter than its diff:
```python
import jax
import jax.numpy as jnp
from jax import lax
from jax.experimental import pallas as pl
from jax.experimental.pallas import tpu as pltpu
from jax.sharding import Mesh
from jax.sharding import PartitionSpec as P

TILE = 128
SIZES = {"y": 4, "z": 8, "x": 4, "core": 2}
ROW = ("y", "z")
COL = ("x", "core")
VM = pltpu.VMEM
F32 = jnp.float32
BF16 = jnp.bfloat16
STEPS = (0, 1, 2, -1)


def from_ahead(value, axis, k):
    n = SIZES[axis]
    return lax.ppermute(value, axis, [((i + k) % n, i) for i in range(n)])


def to_ahead(value, axis, k):
    n = SIZES[axis]
    return lax.ppermute(value, axis, [(i, (i + k) % n) for i in range(n)])


def call(body, outs, smem, vmem, flops=0, scratch=(), limit=40):
    outs = [jax.ShapeDtypeStruct(s, d) for s, d in outs]
    return pl.pallas_call(
        body,
        out_shape=outs,
        in_specs=[pl.BlockSpec(memory_space=pltpu.SMEM)] * len(smem)
        + [pl.BlockSpec(memory_space=VM)] * len(vmem),
        out_specs=[pl.BlockSpec(memory_space=VM)] * len(outs),
        scratch_shapes=list(scratch),
        compiler_params=pltpu.CompilerParams(vmem_limit_bytes=limit * 2**20),
        cost_estimate=pl.CostEstimate(
            flops=flops,
            transcendentals=0,
            bytes_accessed=sum(v.size * v.dtype.itemsize for v in vmem)
            + sum(o.size * o.dtype.itemsize for o in outs),
        ),
    )(*smem, *vmem)


def tile_ref(ref, r, c):
    return ref.at[
        pl.ds(pl.multiple_of(r * TILE, TILE), TILE), pl.ds(pl.multiple_of(c * TILE, TILE), TILE)
    ]


def mask_body(rows, cols, count, w, out, flipped):
    out[...] = jnp.zeros_like(out)
    flipped[...] = jnp.zeros_like(flipped)

    @pl.loop(0, count[0])
    def _(k):
        tile = tile_ref(w, rows[k], cols[k])[...]
        tile_ref(out, rows[k], cols[k])[...] = tile
        tile_ref(flipped, cols[k], rows[k])[...] = tile.T


def zpos(pos, i, hi):
    return (pos[1] + i + 4 * hi + 8) % 8


def up_body(pos, *refs):
    a3, b3, w = refs[:4], refs[4:8], refs[8]
    keep, send, toks, acc = refs[9:]
    core = pos[3]
    cut = a3[0].shape[-1]
    rows = keep.shape[1]
    back = pos[0] - pos[2] + 4
    for j in range(4):
        d = (j + back) % 4
        for i in range(4):
            for hi in range(2):
                at = zpos(pos, STEPS[i], hi)
                toks[d, at, :, :cut] = a3[i][j, hi]
                toks[d, at, :, cut:] = b3[j][i, hi]

    @pl.loop(0, 4)
    def _(d):
        part = jnp.dot(
            toks[d].reshape(2 * rows, toks.shape[-1]), w[...], preferred_element_type=F32
        )
        acc[...] = part.reshape(acc.shape)
        keep[d] = acc[core]
        send[d] = acc[1 - core].astype(BF16)


def back_body(pos, *refs):
    mine, other, w = refs[:4], refs[4:8], refs[8]
    a3, b3, grads = refs[9:13], refs[13:17], refs[17]
    acc, sems = refs[18:]
    core = pos[3]
    cut = a3[0].shape[-1]
    back = pos[0] - pos[2] + 4
    copies = [
        pltpu.make_async_copy(g[d], grads.at[d, side], sems.at[s, d])
        for s, (side, g) in enumerate(((core, mine), (1 - core, other)))
        for d in range(4)
    ]
    for c in copies:
        c.start()
    for c in copies:
        c.wait()
    for j in range(4):
        part = jnp.dot(
            grads[(j + back) % 4].reshape(-1, w.shape[0]), w[...], preferred_element_type=F32
        )
        acc[...] = part.reshape(acc.shape)
        for i in range(4):
            for hi in range(2):
                piece = acc[zpos(pos, STEPS[i], hi)]
                a3[i][j, hi] = piece[:, :cut].astype(a3[i].dtype)
                b3[j][i, hi] = piece[:, cut:].astype(b3[j].dtype)


def wgrad_body(rows, cols, count, toks, grads, out, acc):
    acc[...] = jnp.zeros_like(acc)

    @pl.loop(0, 4)
    def _(d):
        t = toks[d].reshape(-1, toks.shape[-1])
        g = grads[d].reshape(-1, grads.shape[-1])
        acc[...] += lax.dot_general(t, g, (((0,), (0,)), ((), ())), preferred_element_type=F32)

    out[...] = jnp.zeros_like(out)

    @pl.loop(0, count[0])
    def _(k):
        tile_ref(out, rows[k], cols[k])[...] = tile_ref(acc, rows[k], cols[k])[...].astype(BF16)


def gather_four(piece, axis):
    return [piece] + [from_ahead(piece, axis, k) for k in STEPS[1:]]


def gather_tokens(tokens):
    pair = jnp.stack([tokens, from_ahead(tokens, "z", 4)])
    cut = tokens.shape[1] // 2
    a2 = jnp.stack(gather_four(pair[:, :, :cut], "y"))
    b2 = jnp.stack(gather_four(pair[:, :, cut:], "z"))
    return gather_four(a2, "z"), gather_four(b2, "y")


def forward(a3, b3, wm, pos, cot):
    rows = a3[0].shape[2] * 4
    depth, width = wm.shape
    keep, send, toks = call(
        up_body,
        [
            ((4, rows, width), F32),
            ((4, rows, width), BF16),
            ((4, 8, rows // 4, depth), BF16),
        ],
        [pos],
        a3 + b3 + [wm],
        16 * rows * depth * width,
        [VM((2, rows, width), F32)],
    )
    total = keep + to_ahead(send, "core", 1).astype(F32)
    pre_act = total[0]
    for d in range(1, 4):
        pre_act = pre_act + to_ahead(total[d].astype(BF16), "x", d).astype(F32)
    gate = jax.nn.sigmoid(pre_act)
    hidden = (pre_act * gate).astype(BF16)
    slope = gate * (1.0 + pre_act * (1.0 - gate))
    grad_pre = (cot.astype(F32) * slope).astype(BF16)
    return hidden, grad_pre, toks


def gather_grads(grad_pre):
    mine = [grad_pre] + [from_ahead(grad_pre, "x", d) for d in range(1, 4)]
    other = [to_ahead(g, "core", 1) for g in mine]
    return mine, other


def reduce_four(own, sends, axis):
    total = own
    for k, s in zip(STEPS[1:], sends):
        total = total + to_ahead(s.astype(BF16), axis, k).astype(F32)
    return total


def backward(mine, other, flipped, pos, finish):
    rows = mine[0].shape[0]
    width, depth = flipped.shape
    shape = (4, 2, rows // 4, depth // 2)
    outs = [(shape, F32)] + [(shape, BF16)] * 3
    *parts, grads = call(
        back_body,
        outs + outs + [((4, 2, rows, width), BF16)],
        [pos],
        mine + other + [flipped],
        16 * rows * depth * width,
        [VM((8, rows // 4, depth), F32), pltpu.SemaphoreType.DMA((2, 4))],
    )
    weight_grad = finish(grads)
    a2 = reduce_four(parts[0], parts[1:4], "z")
    b2 = reduce_four(parts[4], parts[5:], "y")
    a2, b2, weight_grad = lax.optimization_barrier((a2, b2, weight_grad))
    a1 = reduce_four(a2[0], a2[1:], "y")
    b1 = reduce_four(b2[0], b2[1:], "z")
    both = jnp.concatenate([a1, b1], axis=-1)
    total = both[0] + to_ahead(both[1].astype(BF16), "z", 4).astype(F32)
    return total.astype(BF16), weight_grad


def on_device(tokens, weight, tile_rows, tile_cols, tile_count, hidden_cotangent):
    y, z, x, core = (lax.axis_index(a) for a in ("y", "z", "x", "core"))
    pos = jnp.stack([y, z, x, core]).astype(jnp.int32)
    row_blocks = weight.shape[0] // TILE
    col_blocks = weight.shape[1] // TILE
    rows = tile_rows.reshape(-1) - (x * 2 + core) * row_blocks
    cols = tile_cols.reshape(-1) - (y * 8 + z) * col_blocks
    count = tile_count.reshape(1)
    shapes = [(weight.shape, BF16), (weight.shape[::-1], BF16)]
    wm, flipped = call(mask_body, shapes, [rows, cols, count], [weight])
    a3, b3 = gather_tokens(tokens)
    hidden, grad_pre, toks = forward(a3, b3, wm, pos, hidden_cotangent)
    mine, other = gather_grads(grad_pre)

    def finish(grads):
        (weight_grad,) = call(
            wgrad_body,
            [(weight.shape, BF16)],
            [rows, cols, count],
            [toks, grads],
            2 * 1536 * weight.size,
            [VM(weight.shape, F32)],
        )
        return weight_grad

    input_grad, weight_grad = backward(mine, other, flipped, pos, finish)
    return hidden, input_grad, weight_grad


def solution(mesh):
    split = Mesh(mesh.devices.reshape(4, 8, 4, 2), ("y", "z", "x", "core"))
    return jax.shard_map(
        on_device,
        mesh=split,
        in_specs=(
            P(ROW, COL),
            P(COL, ROW),
            P(ROW, COL, None),
            P(ROW, COL, None),
            P(ROW, COL),
            P(COL, ROW),
        ),
        out_specs=(P(COL, ROW), P(ROW, COL), P(COL, ROW)),
        check_vma=False,
    )
```

time: 196 us -> 177 us (0.903)
  waiting for transfers between devices: 109 us -> 82.1 us
  starting transfers between devices: 50.7 us -> 64.6 us
  Pallas kernels: 28 us -> 21.9 us
  other arithmetic: 2.74 us -> 5.05 us
    ppermute x13 -> x16, waiting for transfers between devices: 51.3 us -> 35.9 us  [from_ahead(): return lax.ppermute(value, axis, [((i + k) % n, i) for i in range(n)])]
    ppermute x21, waiting for transfers between devices: 57.6 us -> 46.1 us  [to_ahead(): return lax.ppermute(value, axis, [(i, (i + k) % n) for i in range(n)])]
    ppermute x13 -> x16, starting transfers between devices: 28.1 us -> 35.2 us  [from_ahead(): return lax.ppermute(value, axis, [((i + k) % n, i) for i in range(n)])]
    ppermute x21, starting transfers between devices: 22.7 us -> 29.4 us  [to_ahead(): return lax.ppermute(value, axis, [(i, (i + k) % n) for i in range(n)])]
    pallas_call x10 -> x4, Pallas kernels: 28 us -> 21.9 us  [call(): pl.pallas_call(body, out_shape=outs, in_specs=[pl.BlockSpec(memory_space=...]
  transfers between devices with their start and end apart: 34 -> 37, of which waited for: 19 -> 19; matrix products, arithmetic and copies ran while one was open for 0% -> 1% of each run, Pallas kernels for 10% -> 6%
where the time goes in v2:
time: 177 us
  waiting for transfers between devices  82.1 us (46%)
  starting transfers between devices  64.6 us (36%)
  Pallas kernels  21.9 us (12%)
  other arithmetic  5.05 us (3%)
    ppermute x21, waiting for transfers between devices, to_ahead(): return lax.ppermute(value, axis, [(i, (i + k) % n) for i in range(n)])  46.1 us
    ppermute x16, waiting for transfers between devices, from_ahead(): return lax.ppermute(value, axis, [((i + k) % n, i) for i in range(n)])  35.9 us
    ppermute x16, starting transfers between devices, from_ahead(): return lax.ppermute(value, axis, [((i + k) % n, i) for i in range(n)])  35.2 us
    ppermute x21, starting transfers between devices, to_ahead(): return lax.ppermute(value, axis, [(i, (i + k) % n) for i in range(n)])  29.4 us
    pallas_call x4, Pallas kernels, call(): pl.pallas_call(body, out_shape=outs, in_specs=[pl.BlockSpec(memory_space=...  21.9 us
  transfers between devices with their start and end apart: 37, of which 19 were waited for; matrix products, arithmetic and copies ran while one was open for 1% of the time, Pallas kernels for 6%

profile of v2, /device:TPU:6, one launch (start us, length us, event | category | flops | bytes accessed | tf_op | source)
XLA Modules:
  0.0 176.9 jit_solution(17828247570744715344)
XLA Ops:
  0.6 7.3 %collective-permute-start = (bf16[48,1024]{1,0:T(8,128)(2,1)}, bf16[48,1024]{1,0:T(8,128)(2,1)S(1)}, u32[]{:S(2)}, u32[]{:S(2)}) collective-permute-start(bf16[48,1024]{1,0:T(8,128)(2,1)} %param.6), channel_id=1, source_target_pairs={{32,0},{40,8},{48,16},{56,24},{0,32},{8,40},{16,48},{24,56},{33,1}... | collective-permute-start | bytes 294920 | tf_op jit(solution)/shard_map/ppermute | solution.py:21
  7.9 3.1 %collective-permute-done = bf16[48,1024]{1,0:T(8,128)(2,1)S(1)} collective-permute-done((bf16[48,1024]{1,0:T(8,128)(2,1)}, bf16[48,1024]{1,0:T(8,128)(2,1)S(1)}, u32[]{:S(2)}, u32[]{:S(2)}) %collective-permute-start) | collective-permute-done | bytes 98336 | tf_op jit(solution)/shard_map/ppermute | solution.py:21
  11.9 1.7 collective-permute-start.3
  13.5 2.9 %collective-permute-start.2 = (bf16[2,48,512]{2,1,0:T(8,128)(2,1)S(1)}, bf16[2,48,512]{2,1,0:T(8,128)(2,1)S(1)}, u32[]{:S(2)}, u32[]{:S(2)}) collective-permute-start(bf16[2,48,512]{2,1,0:T(8,128)(2,1)S(1)} %get-tuple-element.51), channel_id=1, source_target_pairs={{128,0},{192,64},{0,128},{64,192},{129,1},{193,65},{1,129},{65,193... | collective-permute-start | bytes 294920 | tf_op jit(solution)/shard_map/ppermute | solution.py:21
  21.1 2.6 %collective-permute-start.6 = (bf16[4,2,48,512]{3,2,1,0:T(8,128)(2,1)S(1)}, bf16[4,2,48,512]{3,2,1,0:T(8,128)(2,1)S(1)}, u32[]{:S(2)}, u32[]{:S(2)}) collective-permute-start(bf16[4,2,48,512]{3,2,1,0:T(8,128)(2,1)S(1)} %pad_maximum_fusion.refs_0_), channel_id=1, source_target_pairs={{56,0},{0,8},{8,16},{16,24},{24,32},{32,40},{40,48},{48,56},{57,1}... | collective-permute-start | bytes 1179656 | tf_op jit(solution)/shard_map/ppermute | solution.py:21
  23.6 4.2 %collective-permute-start.8 = (bf16[2,48,512]{2,1,0:T(8,128)(2,1)S(1)}, bf16[2,48,512]{2,1,0:T(8,128)(2,1)S(1)}, u32[]{:S(2)}, u32[]{:S(2)}) collective-permute-start(bf16[2,48,512]{2,1,0:T(8,128)(2,1)S(1)} %get-tuple-element.50), channel_id=1, source_target_pairs={{16,0},{24,8},{32,16},{40,24},{48,32},{56,40},{0,48},{8,56},{17,1}... | collective-permute-start | bytes 294920 | tf_op jit(solution)/shard_map/ppermute | solution.py:21
  27.9 1.9 %collective-permute-start.7 = (bf16[2,48,512]{2,1,0:T(8,128)(2,1)S(1)}, bf16[2,48,512]{2,1,0:T(8,128)(2,1)S(1)}, u32[]{:S(2)}, u32[]{:S(2)}) collective-permute-start(bf16[2,48,512]{2,1,0:T(8,128)(2,1)S(1)} %get-tuple-element.50), channel_id=1, source_target_pairs={{8,0},{16,8},{24,16},{32,24},{40,32},{48,40},{56,48},{0,56},{9,1},... | collective-permute-start | bytes 294920 | tf_op jit(solution)/shard_map/ppermute | solution.py:21
  29.9 2.6 %collective-permute-start.5 = (bf16[4,2,48,512]{3,2,1,0:T(8,128)(2,1)S(1)}, bf16[4,2,48,512]{3,2,1,0:T(8,128)(2,1)S(1)}, u32[]{:S(2)}, u32[]{:S(2)}) collective-permute-start(bf16[4,2,48,512]{3,2,1,0:T(8,128)(2,1)S(1)} %pad_maximum_fusion.refs_0_), channel_id=1, source_target_pairs={{16,0},{24,8},{32,16},{40,24},{48,32},{56,40},{0,48},{8,56},{17,1}... | collective-permute-start | bytes 1179656 | tf_op jit(solution)/shard_map/ppermute | solution.py:21
  32.5 1.9 %collective-permute-start.4 = (bf16[4,2,48,512]{3,2,1,0:T(8,128)(2,1)S(1)}, bf16[4,2,48,512]{3,2,1,0:T(8,128)(2,1)S(1)}, u32[]{:S(2)}, u32[]{:S(2)}) collective-permute-start(bf16[4,2,48,512]{3,2,1,0:T(8,128)(2,1)S(1)} %pad_maximum_fusion.refs_0_), channel_id=1, source_target_pairs={{8,0},{16,8},{24,16},{32,24},{40,32},{48,40},{56,48},{0,56},{9,1},... | collective-permute-start | bytes 1179656 | tf_op jit(solution)/shard_map/ppermute | solution.py:21
  37.7 2.8 %collective-permute-start.11 = (bf16[4,2,48,512]{3,2,1,0:T(8,128)(2,1)S(1)}, bf16[4,2,48,512]{3,2,1,0:T(8,128)(2,1)S(1)}, u32[]{:S(2)}, u32[]{:S(2)}) collective-permute-start(bf16[4,2,48,512]{3,2,1,0:T(8,128)(2,1)S(1)} %pad_maximum_fusion.1.refs_4_), channel_id=1, source_target_pairs={{128,0},{192,64},{0,128},{64,192},{129,1},{193,65},{1,129},{65,193... | collective-permute-start | bytes 1179656 | tf_op jit(solution)/shard_map/ppermute | solution.py:21
  44.8 2.9 %shard_map.85 = (bf16[1024,1024]{1,0:T(8,128)(2,1)S(1)}, bf16[1024,1024]{1,0:T(8,128)(2,1)S(1)}) custom-call(s32[32]{0:T(128)S(1)} %get-tuple-element.53.rows, s32[32]{0:T(128)S(1)} %get-tuple-element.52.cols, s32[1]{0:T(128)} %bitcast.69.count, bf16[1024,1024]{1,0:T(8,128)(2,1)S(1)} %copy-done), custom_call_target="tpu_custom_call" | custom-call | bytes 6291456 | tf_op jit(solution)/shard_map/pallas_call | solution.py:31
  47.8 3.2 %collective-permute-done.5.refs_2_ = bf16[4,2,48,512]{3,2,1,0:T(8,128)(2,1)S(1)} collective-permute-done((bf16[4,2,48,512]{3,2,1,0:T(8,128)(2,1)S(1)}, bf16[4,2,48,512]{3,2,1,0:T(8,128)(2,1)S(1)}, u32[]{:S(2)}, u32[]{:S(2)}) %collective-permute-start.5) | collective-permute-done | bytes 393248 | tf_op jit(solution)/shard_map/ppermute | solution.py:21
  51.0 6.9 %collective-permute-done.4.refs_1_ = bf16[4,2,48,512]{3,2,1,0:T(8,128)(2,1)S(1)} collective-permute-done((bf16[4,2,48,512]{3,2,1,0:T(8,128)(2,1)S(1)}, bf16[4,2,48,512]{3,2,1,0:T(8,128)(2,1)S(1)}, u32[]{:S(2)}, u32[]{:S(2)}) %collective-permute-start.4) | collective-permute-done | bytes 393248 | tf_op jit(solution)/shard_map/ppermute | solution.py:21
  57.9 5.1 %shard_map.86 = (f32[4,192,1024]{2,1,0:T(8,128)S(1)}, bf16[4,192,1024]{2,1,0:T(8,128)(2,1)S(1)}, bf16[4,8,48,1024]{3,2,1,0:T(8,128)(2,1)S(1)}) custom-call(s32[4]{0:T(128)S(1)} %pad_add_fusion.pos, bf16[4,2,48,512]{3,2,1,0:T(8,128)(2,1)S(1)} %pad_maximum_fusion.refs_0_, bf16[4,2,48,512]{3,2,1,0:T(8,128)(2,1)S(1)} %collective-permute-done.4.refs_1_, ...), custom_call_target="tpu_custom_call" | custom-call | flops 3221225472 | bytes 13107200 | tf_op jit(solution)/shard_map/pallas_call | solution.py:31
  63.2 3.4 %collective-permute-done.13 = bf16[4,192,1024]{2,1,0:T(8,128)(2,1)S(1)} collective-permute-done((bf16[4,192,1024]{2,1,0:T(8,128)(2,1)S(1)}, bf16[4,192,1024]{2,1,0:T(8,128)(2,1)S(1)}, u32[]{:S(2)}, u32[]{:S(2)}) %collective-permute-start.13) | collective-permute-done | bytes 1572896 | tf_op jit(solution)/shard_map/ppermute | solution.py:26
  71.2 8.5 %collective-permute-done.14 = bf16[192,1024]{1,0:T(8,128)(2,1)S(1)} collective-permute-done((bf16[192,1024]{1,0:T(8,128)(2,1)S(1)}, bf16[192,1024]{1,0:T(8,128)(2,1)S(1)}, u32[]{:S(2)}, u32[]{:S(2)}) %collective-permute-start.14) | collective-permute-done | bytes 393248 | tf_op jit(solution)/shard_map/ppermute | solution.py:26
  79.7 9.0 %collective-permute-done.16 = bf16[192,1024]{1,0:T(8,128)(2,1)S(1)} collective-permute-done((bf16[192,1024]{1,0:T(8,128)(2,1)S(1)}, bf16[192,1024]{1,0:T(8,128)(2,1)S(1)}, u32[]{:S(2)}, u32[]{:S(2)}) %collective-permute-start.16) | collective-permute-done | bytes 393248 | tf_op jit(solution)/shard_map/ppermute | solution.py:26
  93.3 14.3 %collective-permute-done.19.refs_3_ = bf16[192,1024]{1,0:T(8,128)(2,1)S(1)} collective-permute-done((bf16[192,1024]{1,0:T(8,128)(2,1)S(1)}, bf16[192,1024]{1,0:T(8,128)(2,1)S(1)}, u32[]{:S(2)}, u32[]{:S(2)}) %collective-permute-start.19) | collective-permute-done | bytes 393248 | tf_op jit(solution)/shard_map/ppermute | solution.py:21
  108.1 3.1 %collective-permute-done.17.refs_1_ = bf16[192,1024]{1,0:T(8,128)(2,1)S(1)} collective-permute-done((bf16[192,1024]{1,0:T(8,128)(2,1)S(1)}, bf16[192,1024]{1,0:T(8,128)(2,1)S(1)}, u32[]{:S(2)}, u32[]{:S(2)}) %collective-permute-start.17) | collective-permute-done | bytes 393248 | tf_op jit(solution)/shard_map/ppermute | solution.py:21
  111.2 1.7 collective-permute-done.21.refs_5_
  112.9 6.0 %shard_map.87 = (f32[4,2,48,512]{3,2,1,0:T(8,128)S(1)}, bf16[4,2,48,512]{3,2,1,0:T(8,128)(2,1)S(1)}, bf16[4,2,48,512]{3,2,1,0:T(8,128)(2,1)S(1)}, bf16[4,2,48,51...) custom-call(s32[4]{0:T(128)S(1)} %pad_add_fusion.pos, ...), custom_call_target="tpu_custom_call" | custom-call | flops 3221225472 | bytes 12320768 | tf_op jit(solution)/shard_map/pallas_call | solution.py:31
  119.4 2.8 %collective-permute-start.25 = (bf16[4,2,48,512]{3,2,1,0:T(8,128)(2,1)S(1)}, bf16[4,2,48,512]{3,2,1,0:T(8,128)(2,1)S(1)}, u32[]{:S(2)}, u32[]{:S(2)}) collective-permute-start(bf16[4,2,48,512]{3,2,1,0:T(8,128)(2,1)S(1)} %get-tuple-element.26), channel_id=1, source_target_pairs={{0,16},{8,24},{16,32},{24,40},{32,48},{40,56},{48,0},{56,8},{1,17}... | collective-permute-start | bytes 1179656 | tf_op jit(solution)/shard_map/ppermute | solution.py:26
  124.3 3.3 %collective-permute-start.28 = (bf16[4,2,48,512]{3,2,1,0:T(8,128)(2,1)S(1)}, bf16[4,2,48,512]{3,2,1,0:T(8,128)(2,1)S(1)}, u32[]{:S(2)}, u32[]{:S(2)}) collective-permute-start(bf16[4,2,48,512]{3,2,1,0:T(8,128)(2,1)S(1)} %get-tuple-element.30), channel_id=1, source_target_pairs={{0,128},{64,192},{128,0},{192,64},{1,129},{65,193},{129,1},{193,65... | collective-permute-start | bytes 1179656 | tf_op jit(solution)/shard_map/ppermute | solution.py:26
  127.7 4.9 %collective-permute-done.24 = bf16[4,2,48,512]{3,2,1,0:T(8,128)(2,1)S(1)} collective-permute-done((bf16[4,2,48,512]{3,2,1,0:T(8,128)(2,1)S(1)}, bf16[4,2,48,512]{3,2,1,0:T(8,128)(2,1)S(1)}, u32[]{:S(2)}, u32[]{:S(2)}) %collective-permute-start.24) | collective-permute-done | bytes 393248 | tf_op jit(solution)/shard_map/ppermute | solution.py:26
  132.5 2.5 %collective-permute-start.29 = (bf16[4,2,48,512]{3,2,1,0:T(8,128)(2,1)S(1)}, bf16[4,2,48,512]{3,2,1,0:T(8,128)(2,1)S(1)}, u32[]{:S(2)}, u32[]{:S(2)}) collective-permute-start(bf16[4,2,48,512]{3,2,1,0:T(8,128)(2,1)S(1)} %get-tuple-element.31), channel_id=1, source_target_pairs={{0,192},{64,0},{128,64},{192,128},{1,193},{65,1},{129,65},{193,129... | collective-permute-start | bytes 1179656 | tf_op jit(solution)/shard_map/ppermute | solution.py:26
  135.1 7.9 %shard_map.88 = bf16[1024,1024]{1,0:T(8,128)(2,1)} custom-call(s32[32]{0:T(128)S(1)} %get-tuple-element.53.rows, s32[32]{0:T(128)S(1)} %get-tuple-element.52.cols, s32[1]{0:T(128)} %bitcast.70.count, bf16[4,8,48,1024]{3,2,1,0:T(8,128)(2,1)S(1)} %get-tuple-element.32.toks, bf16[4,2,192,1024]{3,2,1,0:T(8,128)(2,1)S(1)} %get-tuple-element.33.grads), custom_call_target="tpu_custom_call" | custom-call | flops 3221225472 | bytes 8388608 | tf_op jit(solution)/shard_map/pallas_call | solution.py:31
  144.7 6.8 %collective-permute-start.30 = (bf16[2,48,512]{2,1,0:T(8,128)(2,1)S(1)}, bf16[2,48,512]{2,1,0:T(8,128)(2,1)S(1)}, u32[]{:S(2)}, u32[]{:S(2)}) collective-permute-start(bf16[2,48,512]{2,1,0:T(8,128)(2,1)S(1)} %get-tuple-element.47), channel_id=1, source_target_pairs={{0,64},{64,128},{128,192},{192,0},{1,65},{65,129},{129,193},{193,1... | collective-permute-start | bytes 294920 | tf_op jit(solution)/shard_map/ppermute | solution.py:26
  151.5 3.7 %collective-permute-start.31 = (bf16[2,48,512]{2,1,0:T(8,128)(2,1)S(1)}, bf16[2,48,512]{2,1,0:T(8,128)(2,1)S(1)}, u32[]{:S(2)}, u32[]{:S(2)}) collective-permute-start(bf16[2,48,512]{2,1,0:T(8,128)(2,1)S(1)} %get-tuple-element.49), channel_id=1, source_target_pairs={{0,128},{64,192},{128,0},{192,64},{1,129},{65,193},{129,1},{193,65... | collective-permute-start | bytes 294920 | tf_op jit(solution)/shard_map/ppermute | solution.py:26
  155.4 3.2 %collective-permute-start.35 = (bf16[2,48,512]{2,1,0:T(8,128)(2,1)S(1)}, bf16[2,48,512]{2,1,0:T(8,128)(2,1)S(1)}, u32[]{:S(2)}, u32[]{:S(2)}) collective-permute-start(bf16[2,48,512]{2,1,0:T(8,128)(2,1)S(1)} %get-tuple-element.45), channel_id=1, source_target_pairs={{0,56},{8,0},{16,8},{24,16},{32,24},{40,32},{48,40},{56,48},{1,57}... | collective-permute-start | bytes 294920 | tf_op jit(solution)/shard_map/ppermute | solution.py:26
  158.7 3.3 %collective-permute-done.33 = bf16[2,48,512]{2,1,0:T(8,128)(2,1)S(1)} collective-permute-done((bf16[2,48,512]{2,1,0:T(8,128)(2,1)S(1)}, bf16[2,48,512]{2,1,0:T(8,128)(2,1)S(1)}, u32[]{:S(2)}, u32[]{:S(2)}) %collective-permute-start.33) | collective-permute-done | bytes 98336 | tf_op jit(solution)/shard_map/ppermute | solution.py:26
  162.0 4.7 %collective-permute-done.34 = bf16[2,48,512]{2,1,0:T(8,128)(2,1)S(1)} collective-permute-done((bf16[2,48,512]{2,1,0:T(8,128)(2,1)S(1)}, bf16[2,48,512]{2,1,0:T(8,128)(2,1)S(1)}, u32[]{:S(2)}, u32[]{:S(2)}) %collective-permute-start.34) | collective-permute-done | bytes 98336 | tf_op jit(solution)/shard_map/ppermute | solution.py:26
  166.9 9.3 %collective-permute-done.36 = bf16[48,1024]{1,0:T(8,128)(2,1)S(1)} collective-permute-done((bf16[48,1024]{1,0:T(8,128)(2,1)S(1)}, bf16[48,1024]{1,0:T(8,128)(2,1)S(1)}, u32[]{:S(2)}, u32[]{:S(2)}) %collective-permute-start.36) | collective-permute-done | bytes 98336 | tf_op jit(solution)/shard_map/ppermute | solution.py:26
  (68 shorter events, 27.8 us)
Async XLA Ops:
  0.6 10.4 %collective-permute-start = (bf16[48,1024]{1,0:T(8,128)(2,1)}, bf16[48,1024]{1,0:T(8,128)(2,1)S(1)}, u32[]{:S(2)}, u32[]{:S(2)}) collective-permute-start(bf16[48,1024]{1,0:T(8,128)(2,1)} %param.6), channel_id=1, source_target_pairs={{32,0},{40,8},{48,16},{56,24},{0,32},{8,40},{16,48},{24,56},{33,1}... | collective-permute-start | bytes 294920 | tf_op jit(solution)/shard_map/ppermute | solution.py:21
  11.9 7.0 %collective-permute-start.3 = (bf16[2,48,512]{2,1,0:T(8,128)(2,1)S(1)}, bf16[2,48,512]{2,1,0:T(8,128)(2,1)S(1)}, u32[]{:S(2)}, u32[]{:S(2)}) collective-permute-start(bf16[2,48,512]{2,1,0:T(8,128)(2,1)S(1)} %get-tuple-element.51), channel_id=1, source_target_pairs={{192,0},{0,64},{64,128},{128,192},{193,1},{1,65},{65,129},{129,193... | collective-permute-start | bytes 294920 | tf_op jit(solution)/shard_map/ppermute | solution.py:21
  13.5 6.9 %collective-permute-start.2 = (bf16[2,48,512]{2,1,0:T(8,128)(2,1)S(1)}, bf16[2,48,512]{2,1,0:T(8,128)(2,1)S(1)}, u32[]{:S(2)}, u32[]{:S(2)}) collective-permute-start(bf16[2,48,512]{2,1,0:T(8,128)(2,1)S(1)} %get-tuple-element.51), channel_id=1, source_target_pairs={{128,0},{192,64},{0,128},{64,192},{129,1},{193,65},{1,129},{65,193... | collective-permute-start | bytes 294920 | tf_op jit(solution)/shard_map/ppermute | solution.py:21
  21.1 19.4 %collective-permute-start.6 = (bf16[4,2,48,512]{3,2,1,0:T(8,128)(2,1)S(1)}, bf16[4,2,48,512]{3,2,1,0:T(8,128)(2,1)S(1)}, u32[]{:S(2)}, u32[]{:S(2)}) collective-permute-start(bf16[4,2,48,512]{3,2,1,0:T(8,128)(2,1)S(1)} %pad_maximum_fusion.refs_0_), channel_id=1, source_target_pairs={{56,0},{0,8},{8,16},{16,24},{24,32},{32,40},{40,48},{48,56},{57,1}... | collective-permute-start | bytes 1179656 | tf_op jit(solution)/shard_map/ppermute | solution.py:21
  23.6 8.8 %collective-permute-start.8 = (bf16[2,48,512]{2,1,0:T(8,128)(2,1)S(1)}, bf16[2,48,512]{2,1,0:T(8,128)(2,1)S(1)}, u32[]{:S(2)}, u32[]{:S(2)}) collective-permute-start(bf16[2,48,512]{2,1,0:T(8,128)(2,1)S(1)} %get-tuple-element.50), channel_id=1, source_target_pairs={{16,0},{24,8},{32,16},{40,24},{48,32},{56,40},{0,48},{8,56},{17,1}... | collective-permute-start | bytes 294920 | tf_op jit(solution)/shard_map/ppermute | solution.py:21
  27.9 7.0 %collective-permute-start.7 = (bf16[2,48,512]{2,1,0:T(8,128)(2,1)S(1)}, bf16[2,48,512]{2,1,0:T(8,128)(2,1)S(1)}, u32[]{:S(2)}, u32[]{:S(2)}) collective-permute-start(bf16[2,48,512]{2,1,0:T(8,128)(2,1)S(1)} %get-tuple-element.50), channel_id=1, source_target_pairs={{8,0},{16,8},{24,16},{32,24},{40,32},{48,40},{56,48},{0,56},{9,1},... | collective-permute-start | bytes 294920 | tf_op jit(solution)/shard_map/ppermute | solution.py:21
  29.8 6.6 %collective-permute-start.9 = (bf16[2,48,512]{2,1,0:T(8,128)(2,1)S(1)}, bf16[2,48,512]{2,1,0:T(8,128)(2,1)S(1)}, u32[]{:S(2)}, u32[]{:S(2)}) collective-permute-start(bf16[2,48,512]{2,1,0:T(8,128)(2,1)S(1)} %get-tuple-element.50), channel_id=1, source_target_pairs={{56,0},{0,8},{8,16},{16,24},{24,32},{32,40},{40,48},{48,56},{57,1}... | collective-permute-start | bytes 294920 | tf_op jit(solution)/shard_map/ppermute | solution.py:21
  29.9 21.1 %collective-permute-start.5 = (bf16[4,2,48,512]{3,2,1,0:T(8,128)(2,1)S(1)}, bf16[4,2,48,512]{3,2,1,0:T(8,128)(2,1)S(1)}, u32[]{:S(2)}, u32[]{:S(2)}) collective-permute-start(bf16[4,2,48,512]{3,2,1,0:T(8,128)(2,1)S(1)} %pad_maximum_fusion.refs_0_), channel_id=1, source_target_pairs={{16,0},{24,8},{32,16},{40,24},{48,32},{56,40},{0,48},{8,56},{17,1}... | collective-permute-start | bytes 1179656 | tf_op jit(solution)/shard_map/ppermute | solution.py:21
  32.5 25.4 %collective-permute-start.4 = (bf16[4,2,48,512]{3,2,1,0:T(8,128)(2,1)S(1)}, bf16[4,2,48,512]{3,2,1,0:T(8,128)(2,1)S(1)}, u32[]{:S(2)}, u32[]{:S(2)}) collective-permute-start(bf16[4,2,48,512]{3,2,1,0:T(8,128)(2,1)S(1)} %pad_maximum_fusion.refs_0_), channel_id=1, source_target_pairs={{8,0},{16,8},{24,16},{32,24},{40,32},{48,40},{56,48},{0,56},{9,1},... | collective-permute-start | bytes 1179656 | tf_op jit(solution)/shard_map/ppermute | solution.py:21
  36.4 21.5 %collective-permute-start.12 = (bf16[4,2,48,512]{3,2,1,0:T(8,128)(2,1)S(1)}, bf16[4,2,48,512]{3,2,1,0:T(8,128)(2,1)S(1)}, u32[]{:S(2)}, u32[]{:S(2)}) collective-permute-start(bf16[4,2,48,512]{3,2,1,0:T(8,128)(2,1)S(1)} %pad_maximum_fusion.1.refs_4_), channel_id=1, source_target_pairs={{192,0},{0,64},{64,128},{128,192},{193,1},{1,65},{65,129},{129,193... | collective-permute-start | bytes 1179656 | tf_op jit(solution)/shard_map/ppermute | solution.py:21
  37.7 20.2 %collective-permute-start.11 = (bf16[4,2,48,512]{3,2,1,0:T(8,128)(2,1)S(1)}, bf16[4,2,48,512]{3,2,1,0:T(8,128)(2,1)S(1)}, u32[]{:S(2)}, u32[]{:S(2)}) collective-permute-start(bf16[4,2,48,512]{3,2,1,0:T(8,128)(2,1)S(1)} %pad_maximum_fusion.1.refs_4_), channel_id=1, source_target_pairs={{128,0},{192,64},{0,128},{64,192},{129,1},{193,65},{1,129},{65,193... | collective-permute-start | bytes 1179656 | tf_op jit(solution)/shard_map/ppermute | solution.py:21
  40.5 17.4 %collective-permute-start.10 = (bf16[4,2,48,512]{3,2,1,0:T(8,128)(2,1)S(1)}, bf16[4,2,48,512]{3,2,1,0:T(8,128)(2,1)S(1)}, u32[]{:S(2)}, u32[]{:S(2)}) collective-permute-start(bf16[4,2,48,512]{3,2,1,0:T(8,128)(2,1)S(1)} %pad_maximum_fusion.1.refs_4_), channel_id=1, source_target_pairs={{64,0},{128,64},{192,128},{0,192},{65,1},{129,65},{193,129},{1,193... | collective-permute-start | bytes 1179656 | tf_op jit(solution)/shard_map/ppermute | solution.py:21
  67.5 12.2 %collective-permute-start.14 = (bf16[192,1024]{1,0:T(8,128)(2,1)S(1)}, bf16[192,1024]{1,0:T(8,128)(2,1)S(1)}, u32[]{:S(2)}, u32[]{:S(2)}) collective-permute-start(bf16[192,1024]{1,0:T(8,128)(2,1)S(1)} %get-tuple-element.41), channel_id=1, source_target_pairs={{0,2},{2,4},{4,6},{6,0},{1,3},{3,5},{5,7},{7,1},{8,10},{10,12},{12... | collective-permute-start | bytes 1179656 | tf_op jit(solution)/shard_map/ppermute | solution.py:26
  68.2 20.5 %collective-permute-start.16 = (bf16[192,1024]{1,0:T(8,128)(2,1)S(1)}, bf16[192,1024]{1,0:T(8,128)(2,1)S(1)}, u32[]{:S(2)}, u32[]{:S(2)}) collective-permute-start(bf16[192,1024]{1,0:T(8,128)(2,1)S(1)} %get-tuple-element.42), channel_id=1, source_target_pairs={{0,6},{2,0},{4,2},{6,4},{1,7},{3,1},{5,3},{7,5},{8,14},{10,8},{12,... | collective-permute-start | bytes 1179656 | tf_op jit(solution)/shard_map/ppermute | solution.py:26
  69.8 18.9 %collective-permute-start.15 = (bf16[192,1024]{1,0:T(8,128)(2,1)S(1)}, bf16[192,1024]{1,0:T(8,128)(2,1)S(1)}, u32[]{:S(2)}, u32[]{:S(2)}) collective-permute-start(bf16[192,1024]{1,0:T(8,128)(2,1)S(1)} %get-tuple-element.43), channel_id=1, source_target_pairs={{0,4},{2,6},{4,0},{6,2},{1,5},{3,7},{5,1},{7,3},{8,12},{10,14},{12... | collective-permute-start | bytes 1179656 | tf_op jit(solution)/shard_map/ppermute | solution.py:26
  90.0 17.6 %collective-permute-start.19 = (bf16[192,1024]{1,0:T(8,128)(2,1)S(1)}, bf16[192,1024]{1,0:T(8,128)(2,1)S(1)}, u32[]{:S(2)}, u32[]{:S(2)}) collective-permute-start(bf16[192,1024]{1,0:T(8,128)(2,1)S(1)} %get-tuple-element.39.refs_0_), channel_id=1, source_target_pairs={{6,0},{0,2},{2,4},{4,6},{7,1},{1,3},{3,5},{5,7},{14,8},{8,10},{10,... | collective-permute-start | bytes 1179656 | tf_op jit(solution)/shard_map/ppermute | solution.py:21
  91.3 16.3 %collective-permute-start.18 = (bf16[192,1024]{1,0:T(8,128)(2,1)S(1)}, bf16[192,1024]{1,0:T(8,128)(2,1)S(1)}, u32[]{:S(2)}, u32[]{:S(2)}) collective-permute-start(bf16[192,1024]{1,0:T(8,128)(2,1)S(1)} %get-tuple-element.39.refs_0_), channel_id=1, source_target_pairs={{4,0},{6,2},{0,4},{2,6},{5,1},{7,3},{1,5},{3,7},{12,8},{14,10},{8,... | collective-permute-start | bytes 1179656 | tf_op jit(solution)/shard_map/ppermute | solution.py:21
  91.9 19.4 %collective-permute-start.17 = (bf16[192,1024]{1,0:T(8,128)(2,1)S(1)}, bf16[192,1024]{1,0:T(8,128)(2,1)S(1)}, u32[]{:S(2)}, u32[]{:S(2)}) collective-permute-start(bf16[192,1024]{1,0:T(8,128)(2,1)S(1)} %get-tuple-element.39.refs_0_), channel_id=1, source_target_pairs={{2,0},{4,2},{6,4},{0,6},{3,1},{5,3},{7,5},{1,7},{10,8},{12,10},{14... | collective-permute-start | bytes 1179656 | tf_op jit(solution)/shard_map/ppermute | solution.py:21
  93.3 17.9 %collective-permute-start.20 = (bf16[192,1024]{1,0:T(8,128)(2,1)S(1)}, bf16[192,1024]{1,0:T(8,128)(2,1)S(1)}, u32[]{:S(2)}, u32[]{:S(2)}) collective-permute-start(bf16[192,1024]{1,0:T(8,128)(2,1)S(1)} %get-tuple-element.39.refs_0_), channel_id=1, source_target_pairs={{0,1},{1,0},{2,3},{3,2},{4,5},{5,4},{6,7},{7,6},{8,9},{9,8},{10,11... | collective-permute-start | bytes 1179656 | tf_op jit(solution)/shard_map/ppermute | solution.py:26
  119.0 13.6 %collective-permute-start.24 = (bf16[4,2,48,512]{3,2,1,0:T(8,128)(2,1)S(1)}, bf16[4,2,48,512]{3,2,1,0:T(8,128)(2,1)S(1)}, u32[]{:S(2)}, u32[]{:S(2)}) collective-permute-start(bf16[4,2,48,512]{3,2,1,0:T(8,128)(2,1)S(1)} %get-tuple-element.25), channel_id=1, source_target_pairs={{0,8},{8,16},{16,24},{24,32},{32,40},{40,48},{48,56},{56,0},{1,9},... | collective-permute-start | bytes 1179656 | tf_op jit(solution)/shard_map/ppermute | solution.py:26
  119.4 23.6 %collective-permute-start.25 = (bf16[4,2,48,512]{3,2,1,0:T(8,128)(2,1)S(1)}, bf16[4,2,48,512]{3,2,1,0:T(8,128)(2,1)S(1)}, u32[]{:S(2)}, u32[]{:S(2)}) collective-permute-start(bf16[4,2,48,512]{3,2,1,0:T(8,128)(2,1)S(1)} %get-tuple-element.26), channel_id=1, source_target_pairs={{0,16},{8,24},{16,32},{24,40},{32,48},{40,56},{48,0},{56,8},{1,17}... | collective-permute-start | bytes 1179656 | tf_op jit(solution)/shard_map/ppermute | solution.py:26
  122.2 20.8 %collective-permute-start.26 = (bf16[4,2,48,512]{3,2,1,0:T(8,128)(2,1)S(1)}, bf16[4,2,48,512]{3,2,1,0:T(8,128)(2,1)S(1)}, u32[]{:S(2)}, u32[]{:S(2)}) collective-permute-start(bf16[4,2,48,512]{3,2,1,0:T(8,128)(2,1)S(1)} %get-tuple-element.27), channel_id=1, source_target_pairs={{0,56},{8,0},{16,8},{24,16},{32,24},{40,32},{48,40},{56,48},{1,57}... | collective-permute-start | bytes 1179656 | tf_op jit(solution)/shard_map/ppermute | solution.py:26
  123.6 19.5 %collective-permute-start.27 = (bf16[4,2,48,512]{3,2,1,0:T(8,128)(2,1)S(1)}, bf16[4,2,48,512]{3,2,1,0:T(8,128)(2,1)S(1)}, u32[]{:S(2)}, u32[]{:S(2)}) collective-permute-start(bf16[4,2,48,512]{3,2,1,0:T(8,128)(2,1)S(1)} %get-tuple-element.29), channel_id=1, source_target_pairs={{0,64},{64,128},{128,192},{192,0},{1,65},{65,129},{129,193},{193,1... | collective-permute-start | bytes 1179656 | tf_op jit(solution)/shard_map/ppermute | solution.py:26
  124.3 20.1 %collective-permute-start.28 = (bf16[4,2,48,512]{3,2,1,0:T(8,128)(2,1)S(1)}, bf16[4,2,48,512]{3,2,1,0:T(8,128)(2,1)S(1)}, u32[]{:S(2)}, u32[]{:S(2)}) collective-permute-start(bf16[4,2,48,512]{3,2,1,0:T(8,128)(2,1)S(1)} %get-tuple-element.30), channel_id=1, source_target_pairs={{0,128},{64,192},{128,0},{192,64},{1,129},{65,193},{129,1},{193,65... | collective-permute-start | bytes 1179656 | tf_op jit(solution)/shard_map/ppermute | solution.py:26
  132.5 11.9 %collective-permute-start.29 = (bf16[4,2,48,512]{3,2,1,0:T(8,128)(2,1)S(1)}, bf16[4,2,48,512]{3,2,1,0:T(8,128)(2,1)S(1)}, u32[]{:S(2)}, u32[]{:S(2)}) collective-permute-start(bf16[4,2,48,512]{3,2,1,0:T(8,128)(2,1)S(1)} %get-tuple-element.31), channel_id=1, source_target_pairs={{0,192},{64,0},{128,64},{192,128},{1,193},{65,1},{129,65},{193,129... | collective-permute-start | bytes 1179656 | tf_op jit(solution)/shard_map/ppermute | solution.py:26
  144.7 13.9 %collective-permute-start.30 = (bf16[2,48,512]{2,1,0:T(8,128)(2,1)S(1)}, bf16[2,48,512]{2,1,0:T(8,128)(2,1)S(1)}, u32[]{:S(2)}, u32[]{:S(2)}) collective-permute-start(bf16[2,48,512]{2,1,0:T(8,128)(2,1)S(1)} %get-tuple-element.47), channel_id=1, source_target_pairs={{0,64},{64,128},{128,192},{192,0},{1,65},{65,129},{129,193},{193,1... | collective-permute-start | bytes 294920 | tf_op jit(solution)/shard_map/ppermute | solution.py:26
  151.5 7.1 %collective-permute-start.32 = (bf16[2,48,512]{2,1,0:T(8,128)(2,1)S(1)}, bf16[2,48,512]{2,1,0:T(8,128)(2,1)S(1)}, u32[]{:S(2)}, u32[]{:S(2)}) collective-permute-start(bf16[2,48,512]{2,1,0:T(8,128)(2,1)S(1)} %get-tuple-element.48), channel_id=1, source_target_pairs={{0,192},{64,0},{128,64},{192,128},{1,193},{65,1},{129,65},{193,129... | collective-permute-start | bytes 294920 | tf_op jit(solution)/shard_map/ppermute | solution.py:26
  151.5 7.1 %collective-permute-start.31 = (bf16[2,48,512]{2,1,0:T(8,128)(2,1)S(1)}, bf16[2,48,512]{2,1,0:T(8,128)(2,1)S(1)}, u32[]{:S(2)}, u32[]{:S(2)}) collective-permute-start(bf16[2,48,512]{2,1,0:T(8,128)(2,1)S(1)} %get-tuple-element.49), channel_id=1, source_target_pairs={{0,128},{64,192},{128,0},{192,64},{1,129},{65,193},{129,1},{193,65... | collective-permute-start | bytes 294920 | tf_op jit(solution)/shard_map/ppermute | solution.py:26
  155.3 6.7 %collective-permute-start.33 = (bf16[2,48,512]{2,1,0:T(8,128)(2,1)S(1)}, bf16[2,48,512]{2,1,0:T(8,128)(2,1)S(1)}, u32[]{:S(2)}, u32[]{:S(2)}) collective-permute-start(bf16[2,48,512]{2,1,0:T(8,128)(2,1)S(1)} %get-tuple-element.44), channel_id=1, source_target_pairs={{0,8},{8,16},{16,24},{24,32},{32,40},{40,48},{48,56},{56,0},{1,9},... | collective-permute-start | bytes 294920 | tf_op jit(solution)/shard_map/ppermute | solution.py:26
  155.4 6.6 %collective-permute-start.35 = (bf16[2,48,512]{2,1,0:T(8,128)(2,1)S(1)}, bf16[2,48,512]{2,1,0:T(8,128)(2,1)S(1)}, u32[]{:S(2)}, u32[]{:S(2)}) collective-permute-start(bf16[2,48,512]{2,1,0:T(8,128)(2,1)S(1)} %get-tuple-element.45), channel_id=1, source_target_pairs={{0,56},{8,0},{16,8},{24,16},{32,24},{40,32},{48,40},{56,48},{1,57}... | collective-permute-start | bytes 294920 | tf_op jit(solution)/shard_map/ppermute | solution.py:26
  158.6 8.1 %collective-permute-start.34 = (bf16[2,48,512]{2,1,0:T(8,128)(2,1)S(1)}, bf16[2,48,512]{2,1,0:T(8,128)(2,1)S(1)}, u32[]{:S(2)}, u32[]{:S(2)}) collective-permute-start(bf16[2,48,512]{2,1,0:T(8,128)(2,1)S(1)} %get-tuple-element.46), channel_id=1, source_target_pairs={{0,16},{8,24},{16,32},{24,40},{32,48},{40,56},{48,0},{56,8},{1,17}... | collective-permute-start | bytes 294920 | tf_op jit(solution)/shard_map/ppermute | solution.py:26
  166.8 9.4 %collective-permute-start.36 = (bf16[48,1024]{1,0:T(8,128)(2,1)S(1)}, bf16[48,1024]{1,0:T(8,128)(2,1)S(1)}, u32[]{:S(2)}, u32[]{:S(2)}) collective-permute-start(bf16[48,1024]{1,0:T(8,128)(2,1)S(1)} %fusion.13), channel_id=1, source_target_pairs={{0,32},{8,40},{16,48},{24,56},{32,0},{40,8},{48,16},{56,24},{1,33}... | collective-permute-start | bytes 294920 | tf_op jit(solution)/shard_map/ppermute | solution.py:26
  (7 other events, 40.0 us)

commit v3 on v2

v3 whole, which is shorter than its diff:
```python
import jax
import jax.numpy as jnp
from jax import lax
from jax.experimental import pallas as pl
from jax.experimental.pallas import tpu as pltpu
from jax.sharding import Mesh
from jax.sharding import PartitionSpec as P

TILE = 128
SIZES = {"y": 4, "z": 8, "x": 4, "core": 2}
ROW = ("y", "z")
COL = ("x", "core")
VM = pltpu.VMEM
F32 = jnp.float32
BF16 = jnp.bfloat16
STEPS = (0, 1, 2, -1)


def from_ahead(value, axis, k):
    n = SIZES[axis]
    return lax.ppermute(value, axis, [((i + k) % n, i) for i in range(n)])


def to_ahead(value, axis, k):
    n = SIZES[axis]
    return lax.ppermute(value, axis, [(i, (i + k) % n) for i in range(n)])


def call(body, outs, smem, vmem, flops=0, scratch=(), limit=24):
    outs = [jax.ShapeDtypeStruct(s, d) for s, d in outs]
    return pl.pallas_call(
        body,
        out_shape=outs,
        in_specs=[pl.BlockSpec(memory_space=pltpu.SMEM)] * len(smem)
        + [pl.BlockSpec(memory_space=VM)] * len(vmem),
        out_specs=[pl.BlockSpec(memory_space=VM)] * len(outs),
        scratch_shapes=list(scratch),
        compiler_params=pltpu.CompilerParams(vmem_limit_bytes=limit * 2**20),
        cost_estimate=pl.CostEstimate(
            flops=flops,
            transcendentals=0,
            bytes_accessed=sum(v.size * v.dtype.itemsize for v in vmem)
            + sum(o.size * o.dtype.itemsize for o in outs),
        ),
    )(*smem, *vmem)


def tile_ref(ref, r, c):
    return ref.at[
        pl.ds(pl.multiple_of(r * TILE, TILE), TILE), pl.ds(pl.multiple_of(c * TILE, TILE), TILE)
    ]


def mask_body(rows, cols, count, w, out, flipped):
    out[...] = jnp.zeros_like(out)
    flipped[...] = jnp.zeros_like(flipped)

    @pl.loop(0, count[0])
    def _(k):
        tile = tile_ref(w, rows[k], cols[k])[...]
        tile_ref(out, rows[k], cols[k])[...] = tile
        tile_ref(flipped, cols[k], rows[k])[...] = tile.T


def zpos(pos, i, hi):
    return (pos[1] + i + 4 * hi + 8) % 8


def up_part(pos, toks, w, at, keep, send, acc):
    core = pos[3]

    @pl.loop(0, 4)
    def _(d):
        part = jnp.dot(
            toks[d].reshape(-1, toks.shape[-1]), w[:, at], preferred_element_type=F32
        )
        acc[...] = part.reshape(acc.shape)
        keep[d] = acc[core]
        send[d] = acc[1 - core].astype(BF16)


def up_first_body(pos, *refs):
    a3, b3, w = refs[:4], refs[4:8], refs[8]
    keep, send, toks, acc = refs[9:]
    cut = a3[0].shape[-1]
    back = pos[0] - pos[2] + 4
    for j in range(4):
        d = (j + back) % 4
        for i in range(4):
            for hi in range(2):
                at = zpos(pos, STEPS[i], hi)
                toks[d, at, :, :cut] = a3[i][j, hi]
                toks[d, at, :, cut:] = b3[j][i, hi]
    up_part(pos, toks, w, slice(0, keep.shape[-1]), keep, send, acc)


def up_second_body(pos, toks, w, keep, send, acc):
    n = keep.shape[-1]
    up_part(pos, toks, w, slice(n, 2 * n), keep, send, acc)


def collect(pos, mine, other, slots, sems):
    core = pos[3]
    copies = [
        pltpu.make_async_copy(g, slots(side), sems.at[s])
        for s, (side, g) in enumerate(((core, mine), (1 - core, other)))
    ]
    for c in copies:
        c.start()
    for c in copies:
        c.wait()


def back_first_body(pos, *refs):
    mine, other, w, total, grads, sems = refs
    collect(pos, mine, other, lambda side: grads.at[:, side], sems)

    @pl.loop(0, 4)
    def _(d):
        g = grads[d].reshape(-1, grads.shape[-1])
        part = jnp.dot(g, w[: g.shape[1]], preferred_element_type=F32)
        total[d] = part.reshape(total.shape[1:])


def back_second_body(pos, *refs):
    mine, other, w, total, first = refs[:5]
    a3, b3, grads = refs[5:9], refs[9:13], refs[13]
    acc, sems, first_sem = refs[14:]
    cut = first.shape[-1]
    kept = pltpu.make_async_copy(first, grads.at[:, :, :, pl.ds(0, cut)], first_sem)
    kept.start()
    collect(pos, mine, other, lambda side: grads.at[:, side, :, pl.ds(cut, cut)], sems)
    back = pos[0] - pos[2] + 4

    @pl.loop(0, 4)
    def _(j):
        d = (j + back) % 4
        g = grads[d, :, :, cut:].reshape(-1, cut)
        part = jnp.dot(g, w[cut:], preferred_element_type=F32)
        acc[j] = total[d] + part.reshape(total.shape[1:])

    kept.wait()
    cut = a3[0].shape[-1]
    for hi in range(2):
        for k in range(4):

            @pl.loop(0, 4)
            def _(j, k=k, hi=hi):
                piece = acc[j, zpos(pos, STEPS[k], hi), :, :cut]
                a3[k][j, hi] = piece.astype(a3[k].dtype)

            @pl.loop(0, 4)
            def _(i, k=k, hi=hi):
                piece = acc[k, zpos(pos, jnp.where(i == 3, -1, i), hi), :, cut:]
                b3[k][i, hi] = piece.astype(b3[k].dtype)


def add_body(keep, recv, *out):
    for d in range(4):

        @pl.loop(0, keep.shape[1] // 32)
        def _(i, d=d):
            at = pl.ds(pl.multiple_of(i * 32, 32), 32)
            total = keep[d, at] + recv[d, at].astype(F32)
            out[d][at] = total.astype(out[d].dtype)


def act_body(own, r1, r2, r3, cot, hidden, grad_pre):
    @pl.loop(0, own.shape[0] // 32)
    def _(i):
        at = pl.ds(pl.multiple_of(i * 32, 32), 32)
        pre_act = own[at] + r1[at].astype(F32) + r2[at].astype(F32) + r3[at].astype(F32)
        gate = jax.nn.sigmoid(pre_act)
        hidden[at] = (pre_act * gate).astype(BF16)
        slope = gate * (1.0 + pre_act * (1.0 - gate))
        grad_pre[at] = (cot[at].astype(F32) * slope).astype(BF16)


def wgrad_body(rows, cols, count, toks, grads, out, acc):
    acc[...] = jnp.zeros_like(acc)
    step = 256

    @pl.loop(0, 4)
    def _(d):
        t = toks[d].reshape(-1, toks.shape[-1])

        @pl.loop(0, acc.shape[1] // step)
        def _(k):
            at = pl.ds(pl.multiple_of(k * step, step), step)
            g = grads[d, :, :, at].reshape(-1, step)
            acc[:, at] += lax.dot_general(
                t, g, (((0,), (0,)), ((), ())), preferred_element_type=F32
            )

    out[...] = jnp.zeros_like(out)

    @pl.loop(0, count[0])
    def _(k):
        tile_ref(out, rows[k], cols[k])[...] = tile_ref(acc, rows[k], cols[k])[...].astype(BF16)


def gather_four(piece, axis):
    return [piece] + [from_ahead(piece, axis, k) for k in STEPS[1:]]


def gather_tokens(tokens):
    pair = jnp.stack([tokens, from_ahead(tokens, "z", 4)])
    cut = tokens.shape[1] // 2
    a2 = gather_four(pair[:, :, :cut], "y")
    b2 = gather_four(pair[:, :, cut:], "z")
    a2, b2 = lax.optimization_barrier((a2, b2))
    return gather_four(jnp.stack(a2), "z"), gather_four(jnp.stack(b2), "y")


def partial_sums(keep, send):
    shape = keep.shape[1:]
    return call(
        add_body, [(shape, F32)] + [(shape, BF16)] * 3, [], [keep, to_ahead(send, "core", 1)]
    )


def shares(sends):
    return [to_ahead(s, "x", d + 1) for d, s in enumerate(sends)]


def activation(own, recvs, cot):
    return call(act_body, [(own.shape, BF16)] * 2, [], [own] + recvs + [cot])


def gather_grads(grad_pre):
    mine = jnp.stack([grad_pre] + [from_ahead(grad_pre, "x", d) for d in range(1, 4)])
    return [mine, to_ahead(mine, "core", 1)]


def reduce_four(own, sends, axis):
    total = own
    for k, s in zip(STEPS[1:], sends):
        total = total + to_ahead(s.astype(BF16), axis, k).astype(F32)
    return total


def middle(a3, b3, wm, flipped, pos, cot):
    rows = a3[0].shape[2] * 4
    depth, width = wm.shape
    cut = width // 2
    flops = 8 * rows * depth * width
    pair = [((4, rows, cut), F32), ((4, rows, cut), BF16)]
    tok_shape = ((4, 8, rows // 4, depth), BF16)
    acc = VM((2, rows, cut), F32)
    keep1, send1, toks = call(
        up_first_body, pair + [tok_shape], [pos], a3 + b3 + [wm], flops, [acc]
    )
    own1, *sends1 = partial_sums(keep1, send1)
    keep2, send2 = call(up_second_body, pair, [pos], [toks, wm], flops, [acc])
    own2, *sends2 = partial_sums(keep2, send2)
    hidden1, grad1 = activation(own1, shares(sends1), cot[:, :cut])
    hidden2, grad2 = activation(own2, shares(sends2), cot[:, cut:])
    parts1 = gather_grads(grad1)
    parts2 = gather_grads(grad2)
    g_shape = ((4, 2, rows, cut), BF16)
    sems = pltpu.SemaphoreType.DMA((2,))
    sums = (4, 8, rows // 4, depth)
    total, g1 = call(
        back_first_body, [(sums, F32), g_shape], [pos], parts1 + [flipped], flops, [sems]
    )
    shape = (4, 2, rows // 4, depth // 2)
    outs = [(shape, F32)] + [(shape, BF16)] * 3
    *sends, grads = call(
        back_second_body,
        outs + outs + [((4, 2, rows, width), BF16)],
        [pos],
        parts2 + [flipped, total, g1],
        flops,
        [VM(sums, F32), sems, pltpu.SemaphoreType.DMA],
    )
    hidden = jnp.concatenate([hidden1, hidden2], axis=1)
    return hidden, sends, toks, grads


def reduce_inputs(sends, weight_grad):
    a2 = reduce_four(sends[0], sends[1:4], "z")
    b2 = reduce_four(sends[4], sends[5:], "y")
    a2, b2, weight_grad = lax.optimization_barrier((a2, b2, weight_grad))
    a1 = reduce_four(a2[0], a2[1:], "y")
    b1 = reduce_four(b2[0], b2[1:], "z")
    both = jnp.concatenate([a1, b1], axis=-1)
    total = both[0] + to_ahead(both[1].astype(BF16), "z", 4).astype(F32)
    return total.astype(BF16), weight_grad


def on_device(tokens, weight, tile_rows, tile_cols, tile_count, hidden_cotangent):
    y, z, x, core = (lax.axis_index(a) for a in ("y", "z", "x", "core"))
    pos = jnp.stack([y, z, x, core]).astype(jnp.int32)
    row_blocks = weight.shape[0] // TILE
    col_blocks = weight.shape[1] // TILE
    rows = tile_rows.reshape(-1) - (x * 2 + core) * row_blocks
    cols = tile_cols.reshape(-1) - (y * 8 + z) * col_blocks
    count = tile_count.reshape(1)
    shapes = [(weight.shape, BF16), (weight.shape[::-1], BF16)]
    wm, flipped = call(mask_body, shapes, [rows, cols, count], [weight])
    a3, b3 = gather_tokens(tokens)
    hidden, sends, toks, grads = middle(a3, b3, wm, flipped, pos, hidden_cotangent)
    (weight_grad,) = call(
        wgrad_body,
        [(weight.shape, BF16)],
        [rows, cols, count],
        [toks, grads],
        2 * 1536 * weight.size,
        [VM(weight.shape, F32)],
    )
    input_grad, weight_grad = reduce_inputs(sends, weight_grad)
    return hidden, input_grad, weight_grad


def solution(mesh):
    split = Mesh(mesh.devices.reshape(4, 8, 4, 2), ("y", "z", "x", "core"))
    return jax.shard_map(
        on_device,
        mesh=split,
        in_specs=(
            P(ROW, COL),
            P(COL, ROW),
            P(ROW, COL, None),
            P(ROW, COL, None),
            P(ROW, COL),
            P(COL, ROW),
        ),
        out_specs=(P(COL, ROW), P(ROW, COL), P(COL, ROW)),
        check_vma=False,
    )
```

time: 177 us -> 176 us (level)
  Pallas kernels: 21.9 us -> 28.4 us
  starting transfers between devices: 64.6 us -> 60.9 us
  waiting for transfers between devices: 82.1 us -> 78.4 us
    pallas_call x4 -> x10, Pallas kernels: 21.9 us -> 28.4 us  [call(): pl.pallas_call(body, out_shape=outs, in_specs=[pl.BlockSpec(memory_space=...]
    ppermute x21 -> x23, starting transfers between devices: 29.4 us -> 24.5 us  [to_ahead(): return lax.ppermute(value, axis, [(i, (i + k) % n) for i in range(n)])]
    ppermute x16 -> x19, waiting for transfers between devices: 35.9 us -> 34.1 us  [from_ahead(): return lax.ppermute(value, axis, [((i + k) % n, i) for i in range(n)])]
    ppermute x21 -> x23, waiting for transfers between devices: 46.1 us -> 44.3 us  [to_ahead(): return lax.ppermute(value, axis, [(i, (i + k) % n) for i in range(n)])]
    ppermute x16 -> x19, starting transfers between devices: 35.2 us -> 36.5 us  [from_ahead(): return lax.ppermute(value, axis, [((i + k) % n, i) for i in range(n)])]
  transfers between devices with their start and end apart: 37 -> 42, of which waited for: 19 -> 22; matrix products, arithmetic and copies ran while one was open for 1% -> 1% of each run, Pallas kernels for 6% -> 10%
where the time goes in v3:
time: 176 us; the launch traced here: 175 us
  waiting for transfers between devices  78.4 us (45%)
  starting transfers between devices  60.9 us (35%)
  Pallas kernels  28.4 us (16%)
  other arithmetic  4.03 us (2%)
    ppermute x23, waiting for transfers between devices, to_ahead(): return lax.ppermute(value, axis, [(i, (i + k) % n) for i in range(n)])  44.3 us
    ppermute x19, starting transfers between devices, from_ahead(): return lax.ppermute(value, axis, [((i + k) % n, i) for i in range(n)])  36.5 us
    ppermute x19, waiting for transfers between devices, from_ahead(): return lax.ppermute(value, axis, [((i + k) % n, i) for i in range(n)])  34.1 us
    pallas_call x10, Pallas kernels, call(): pl.pallas_call(body, out_shape=outs, in_specs=[pl.BlockSpec(memory_space=...  28.4 us
    ppermute x23, starting transfers between devices, to_ahead(): return lax.ppermute(value, axis, [(i, (i + k) % n) for i in range(n)])  24.5 us
  transfers between devices with their start and end apart: 42, of which 22 were waited for; matrix products, arithmetic and copies ran while one was open for 1% of the time, Pallas kernels for 10%

profile of v3, /device:TPU:6, one launch (start us, length us, event | category | flops | bytes accessed | tf_op | source)
XLA Modules:
  0.0 175.0 jit_solution(17507271647011126962)
XLA Ops:
  0.6 7.3 %collective-permute-start = (bf16[48,1024]{1,0:T(8,128)(2,1)}, bf16[48,1024]{1,0:T(8,128)(2,1)S(1)}, u32[]{:S(2)}, u32[]{:S(2)}) collective-permute-start(bf16[48,1024]{1,0:T(8,128)(2,1)} %param.6), channel_id=1, source_target_pairs={{32,0},{40,8},{48,16},{56,24},{0,32},{8,40},{16,48},{24,56},{33,1}... | collective-permute-start | bytes 294920 | tf_op jit(solution)/shard_map/ppermute | solution.py:21
  7.9 3.1 %collective-permute-done = bf16[48,1024]{1,0:T(8,128)(2,1)S(1)} collective-permute-done((bf16[48,1024]{1,0:T(8,128)(2,1)}, bf16[48,1024]{1,0:T(8,128)(2,1)S(1)}, u32[]{:S(2)}, u32[]{:S(2)}) %collective-permute-start) | collective-permute-done | bytes 98336 | tf_op jit(solution)/shard_map/ppermute | solution.py:21
  11.9 2.6 %collective-permute-start.6 = (bf16[2,48,512]{2,1,0:T(8,128)(2,1)S(1)}, bf16[2,48,512]{2,1,0:T(8,128)(2,1)S(1)}, u32[]{:S(2)}, u32[]{:S(2)}) collective-permute-start(bf16[2,48,512]{2,1,0:T(8,128)(2,1)S(1)} %get-tuple-element.48), channel_id=1, source_target_pairs={{56,0},{0,8},{8,16},{16,24},{24,32},{32,40},{40,48},{48,56},{57,1}... | collective-permute-start | bytes 294920 | tf_op jit(solution)/shard_map/ppermute | solution.py:21
  14.4 4.2 %collective-permute-start.5 = (bf16[2,48,512]{2,1,0:T(8,128)(2,1)S(1)}, bf16[2,48,512]{2,1,0:T(8,128)(2,1)S(1)}, u32[]{:S(2)}, u32[]{:S(2)}) collective-permute-start(bf16[2,48,512]{2,1,0:T(8,128)(2,1)S(1)} %get-tuple-element.48), channel_id=1, source_target_pairs={{16,0},{24,8},{32,16},{40,24},{48,32},{56,40},{0,48},{8,56},{17,1}... | collective-permute-start | bytes 294920 | tf_op jit(solution)/shard_map/ppermute | solution.py:21
  22.1 2.9 %collective-permute-start.2 = (bf16[2,48,512]{2,1,0:T(8,128)(2,1)S(1)}, bf16[2,48,512]{2,1,0:T(8,128)(2,1)S(1)}, u32[]{:S(2)}, u32[]{:S(2)}) collective-permute-start(bf16[2,48,512]{2,1,0:T(8,128)(2,1)S(1)} %get-tuple-element.44), channel_id=1, source_target_pairs={{128,0},{192,64},{0,128},{64,192},{129,1},{193,65},{1,129},{65,193... | collective-permute-start | bytes 294920 | tf_op jit(solution)/shard_map/ppermute | solution.py:21
  30.5 3.4 %collective-permute-start.11 = (bf16[4,2,48,512]{3,2,1,0:T(8,128)(2,1)S(1)}, bf16[4,2,48,512]{3,2,1,0:T(8,128)(2,1)S(1)}, u32[]{:S(2)}, u32[]{:S(2)}) collective-permute-start(bf16[4,2,48,512]{3,2,1,0:T(8,128)(2,1)S(1)} %pad_maximum_fusion.3.refs_4_), channel_id=1, source_target_pairs={{128,0},{192,64},{0,128},{64,192},{129,1},{193,65},{1,129},{65,193... | collective-permute-start | bytes 1179656 | tf_op jit(solution)/shard_map/ppermute | solution.py:21
  34.5 2.8 %collective-permute-start.8 = (bf16[4,2,48,512]{3,2,1,0:T(8,128)(2,1)S(1)}, bf16[4,2,48,512]{3,2,1,0:T(8,128)(2,1)S(1)}, u32[]{:S(2)}, u32[]{:S(2)}) collective-permute-start(bf16[4,2,48,512]{3,2,1,0:T(8,128)(2,1)S(1)} %pad_maximum_fusion.2.refs_0_), channel_id=1, source_target_pairs={{16,0},{24,8},{32,16},{40,24},{48,32},{56,40},{0,48},{8,56},{17,1}... | collective-permute-start | bytes 1179656 | tf_op jit(solution)/shard_map/ppermute | solution.py:21
  37.4 5.3 %collective-permute-done.12.refs_7_ = bf16[4,2,48,512]{3,2,1,0:T(8,128)(2,1)S(1)} collective-permute-done((bf16[4,2,48,512]{3,2,1,0:T(8,128)(2,1)S(1)}, bf16[4,2,48,512]{3,2,1,0:T(8,128)(2,1)S(1)}, u32[]{:S(2)}, u32[]{:S(2)}) %collective-permute-start.12) | collective-permute-done | bytes 393248 | tf_op jit(solution)/shard_map/ppermute | solution.py:21
  47.1 2.8 %shard_map.85 = (bf16[1024,1024]{1,0:T(8,128)(2,1)S(1)}, bf16[1024,1024]{1,0:T(8,128)(2,1)S(1)}) custom-call(s32[32]{0:T(128)S(1)} %get-tuple-element.96.rows, s32[32]{0:T(128)S(1)} %get-tuple-element.95.cols, s32[1]{0:T(128)} %bitcast.59.count, bf16[1024,1024]{1,0:T(8,128)(2,1)S(1)} %copy-done), custom_call_target="tpu_custom_call" | custom-call | bytes 6291456 | tf_op jit(solution)/shard_map/pallas_call | solution.py:31
  50.0 3.6 %collective-permute-done.8.refs_2_ = bf16[4,2,48,512]{3,2,1,0:T(8,128)(2,1)S(1)} collective-permute-done((bf16[4,2,48,512]{3,2,1,0:T(8,128)(2,1)S(1)}, bf16[4,2,48,512]{3,2,1,0:T(8,128)(2,1)S(1)}, u32[]{:S(2)}, u32[]{:S(2)}) %collective-permute-start.8) | collective-permute-done | bytes 393248 | tf_op jit(solution)/shard_map/ppermute | solution.py:21
  53.7 7.6 %collective-permute-done.7.refs_1_ = bf16[4,2,48,512]{3,2,1,0:T(8,128)(2,1)S(1)} collective-permute-done((bf16[4,2,48,512]{3,2,1,0:T(8,128)(2,1)S(1)}, bf16[4,2,48,512]{3,2,1,0:T(8,128)(2,1)S(1)}, u32[]{:S(2)}, u32[]{:S(2)}) %collective-permute-start.7) | collective-permute-done | bytes 393248 | tf_op jit(solution)/shard_map/ppermute | solution.py:21
  61.3 3.3 %shard_map.86 = (f32[4,192,512]{2,1,0:T(8,128)S(1)}, bf16[4,192,512]{2,1,0:T(8,128)(2,1)S(1)}, bf16[4,8,48,1024]{3,2,1,0:T(8,128)(2,1)S(1)}) custom-call(s32[4]{0:T(128)S(1)} %pad_add_fusion.pos, bf16[4,2,48,512]{3,2,1,0:T(8,128)(2,1)S(1)} %pad_maximum_fusion.2.refs_0_, bf16[4,2,48,512]{3,2,1,0:T(8,128)(2,1)S(1)} %collective-permute-done.7.refs_1_, ...), custom_call_target="tpu_custom_call" | custom-call | flops 1610612736 | bytes 10747904 | tf_op jit(solution)/shard_map/pallas_call | solution.py:31
  64.6 3.0 %shard_map.89 = (f32[4,192,512]{2,1,0:T(8,128)S(1)}, bf16[4,192,512]{2,1,0:T(8,128)(2,1)S(1)}) custom-call(s32[4]{0:T(128)S(1)} %pad_add_fusion.pos, bf16[4,8,48,1024]{3,2,1,0:T(8,128)(2,1)S(1)} %get-tuple-element.60.toks, bf16[1024,1024]{1,0:T(8,128)(2,1)S(1)} %get-tuple-element.52.refs_8_.w), custom_call_target="tpu_custom_call" | custom-call | flops 1610612736 | bytes 7602176 | tf_op jit(solution)/shard_map/pallas_call | solution.py:31
  72.9 2.1 %collective-permute-start.15 = (bf16[192,512]{1,0:T(8,128)(2,1)S(1)}, bf16[192,512]{1,0:T(8,128)(2,1)S(1)}, u32[]{:S(2)}, u32[]{:S(2)}) collective-permute-start(bf16[192,512]{1,0:T(8,128)(2,1)S(1)} %get-tuple-element.57), channel_id=1, source_target_pairs={{0,4},{2,6},{4,0},{6,2},{1,5},{3,7},{5,1},{7,3},{8,12},{10,14},{12... | collective-permute-start | bytes 589832 | tf_op jit(solution)/shard_map/ppermute | solution.py:26
  75.2 2.5 %collective-permute-start.19 = (bf16[192,512]{1,0:T(8,128)(2,1)S(1)}, bf16[192,512]{1,0:T(8,128)(2,1)S(1)}, u32[]{:S(2)}, u32[]{:S(2)}) collective-permute-start(bf16[192,512]{1,0:T(8,128)(2,1)S(1)} %get-tuple-element.65), channel_id=1, source_target_pairs={{0,4},{2,6},{4,0},{6,2},{1,5},{3,7},{5,1},{7,3},{8,12},{10,14},{12... | collective-permute-start | bytes 589832 | tf_op jit(solution)/shard_map/ppermute | solution.py:26
  77.8 4.7 %collective-permute-done.14.r1 = bf16[192,512]{1,0:T(8,128)(2,1)S(1)} collective-permute-done((bf16[192,512]{1,0:T(8,128)(2,1)S(1)}, bf16[192,512]{1,0:T(8,128)(2,1)S(1)}, u32[]{:S(2)}, u32[]{:S(2)}) %collective-permute-start.14) | collective-permute-done | bytes 196640 | tf_op jit(solution)/shard_map/ppermute | solution.py:26
  83.3 4.8 %collective-permute-done.16.r3 = bf16[192,512]{1,0:T(8,128)(2,1)S(1)} collective-permute-done((bf16[192,512]{1,0:T(8,128)(2,1)S(1)}, bf16[192,512]{1,0:T(8,128)(2,1)S(1)}, u32[]{:S(2)}, u32[]{:S(2)}) %collective-permute-start.16) | collective-permute-done | bytes 196640 | tf_op jit(solution)/shard_map/ppermute | solution.py:26
  91.9 4.7 %collective-permute-done.20.r3 = bf16[192,512]{1,0:T(8,128)(2,1)S(1)} collective-permute-done((bf16[192,512]{1,0:T(8,128)(2,1)S(1)}, bf16[192,512]{1,0:T(8,128)(2,1)S(1)}, u32[]{:S(2)}, u32[]{:S(2)}) %collective-permute-start.20) | collective-permute-done | bytes 196640 | tf_op jit(solution)/shard_map/ppermute | solution.py:26
  99.1 5.8 %collective-permute-done.25 = bf16[192,512]{1,0:T(8,128)(2,1)S(1)} collective-permute-done((bf16[192,512]{1,0:T(8,128)(2,1)S(1)}, bf16[192,512]{1,0:T(8,128)(2,1)S(1)}, u32[]{:S(2)}, u32[]{:S(2)}) %collective-permute-start.25) | collective-permute-done | bytes 196640 | tf_op jit(solution)/shard_map/ppermute | solution.py:21
  105.1 2.4 %collective-permute-done.22 = bf16[192,512]{1,0:T(8,128)(2,1)S(1)} collective-permute-done((bf16[192,512]{1,0:T(8,128)(2,1)S(1)}, bf16[192,512]{1,0:T(8,128)(2,1)S(1)}, u32[]{:S(2)}, u32[]{:S(2)}) %collective-permute-start.22) | collective-permute-done | bytes 196640 | tf_op jit(solution)/shard_map/ppermute | solution.py:21
  107.6 2.7 %collective-permute-done.21 = bf16[192,512]{1,0:T(8,128)(2,1)S(1)} collective-permute-done((bf16[192,512]{1,0:T(8,128)(2,1)S(1)}, bf16[192,512]{1,0:T(8,128)(2,1)S(1)}, u32[]{:S(2)}, u32[]{:S(2)}) %collective-permute-start.21) | collective-permute-done | bytes 196640 | tf_op jit(solution)/shard_map/ppermute | solution.py:21
  110.4 3.0 %shard_map.92 = (f32[4,8,48,1024]{3,2,1,0:T(8,128)S(1)}, bf16[4,2,192,512]{3,2,1,0:T(8,128)(2,1)S(1)}) custom-call(s32[4]{0:T(128)S(1)} %pad_add_fusion.pos, bf16[4,192,512]{2,1,0:T(8,128)(2,1)S(1)} %pad_maximum_fusion.1.refs_0_, bf16[4,192,512]{2,1,0:T(8,128)(2,1)S(1)} %collective-permute-done.28.refs_1_, bf16[1024,1024]{1,0:T(8,128)(2,1)S(1)} %get-tuple-element.69.refs_2_), custom_call_target="tpu_custom_call" | custom-call | flops 1610612736 | bytes 11534336 | tf_op jit(solution)/shard_map/pallas_call | solution.py:31
  113.5 4.4 %shard_map.93 = (f32[4,2,48,512]{3,2,1,0:T(8,128)S(1)}, bf16[4,2,48,512]{3,2,1,0:T(8,128)(2,1)S(1)}, bf16[4,2,48,512]{3,2,1,0:T(8,128)(2,1)S(1)}, bf16[4,2,48,51...) custom-call(s32[4]{0:T(128)S(1)} %pad_add_fusion.pos, ...), custom_call_target="tpu_custom_call" | custom-call | flops 1610612736 | bytes 18612224 | tf_op jit(solution)/shard_map/pallas_call | solution.py:31
  119.1 2.1 %collective-permute-start.31 = (bf16[4,2,48,512]{3,2,1,0:T(8,128)(2,1)S(1)}, bf16[4,2,48,512]{3,2,1,0:T(8,128)(2,1)S(1)}, u32[]{:S(2)}, u32[]{:S(2)}) collective-permute-start(bf16[4,2,48,512]{3,2,1,0:T(8,128)(2,1)S(1)} %get-tuple-element.76), channel_id=1, source_target_pairs={{0,56},{8,0},{16,8},{24,16},{32,24},{40,32},{48,40},{56,48},{1,57}... | collective-permute-start | bytes 1179656 | tf_op jit(solution)/shard_map/ppermute | solution.py:26
  123.0 9.8 %collective-permute-done.29 = bf16[4,2,48,512]{3,2,1,0:T(8,128)(2,1)S(1)} collective-permute-done((bf16[4,2,48,512]{3,2,1,0:T(8,128)(2,1)S(1)}, bf16[4,2,48,512]{3,2,1,0:T(8,128)(2,1)S(1)}, u32[]{:S(2)}, u32[]{:S(2)}) %collective-permute-start.29) | collective-permute-done | bytes 393248 | tf_op jit(solution)/shard_map/ppermute | solution.py:26
  132.9 10.8 %shard_map.94 = bf16[1024,1024]{1,0:T(8,128)(2,1)} custom-call(s32[32]{0:T(128)S(1)} %get-tuple-element.96.rows, s32[32]{0:T(128)S(1)} %get-tuple-element.95.cols, s32[1]{0:T(128)} %bitcast.60.count, bf16[4,8,48,1024]{3,2,1,0:T(8,128)(2,1)S(1)} %get-tuple-element.60.toks, bf16[4,2,192,1024]{3,2,1,0:T(8,128)(2,1)S(1)} %get-tuple-element.81.grads), custom_call_target="tpu_custom_call" | custom-call | flops 3221225472 | bytes 8388608 | tf_op jit(solution)/shard_map/pallas_call | solution.py:31
  143.8 3.2 %collective-permute-done.30 = bf16[4,2,48,512]{3,2,1,0:T(8,128)(2,1)S(1)} collective-permute-done((bf16[4,2,48,512]{3,2,1,0:T(8,128)(2,1)S(1)}, bf16[4,2,48,512]{3,2,1,0:T(8,128)(2,1)S(1)}, u32[]{:S(2)}, u32[]{:S(2)}) %collective-permute-start.30) | collective-permute-done | bytes 393248 | tf_op jit(solution)/shard_map/ppermute | solution.py:26
  147.6 3.1 %collective-permute-start.35 = (bf16[2,48,512]{2,1,0:T(8,128)(2,1)S(1)}, bf16[2,48,512]{2,1,0:T(8,128)(2,1)S(1)}, u32[]{:S(2)}, u32[]{:S(2)}) collective-permute-start(bf16[2,48,512]{2,1,0:T(8,128)(2,1)S(1)} %get-tuple-element.88), channel_id=1, source_target_pairs={{0,64},{64,128},{128,192},{192,0},{1,65},{65,129},{129,193},{193,1... | collective-permute-start | bytes 294920 | tf_op jit(solution)/shard_map/ppermute | solution.py:26
  150.6 2.1 %collective-permute-start.37 = (bf16[2,48,512]{2,1,0:T(8,128)(2,1)S(1)}, bf16[2,48,512]{2,1,0:T(8,128)(2,1)S(1)}, u32[]{:S(2)}, u32[]{:S(2)}) collective-permute-start(bf16[2,48,512]{2,1,0:T(8,128)(2,1)S(1)} %get-tuple-element.89), channel_id=1, source_target_pairs={{0,192},{64,0},{128,64},{192,128},{1,193},{65,1},{129,65},{193,129... | collective-permute-start | bytes 294920 | tf_op jit(solution)/shard_map/ppermute | solution.py:26
  154.9 3.2 %collective-permute-start.40 = (bf16[2,48,512]{2,1,0:T(8,128)(2,1)S(1)}, bf16[2,48,512]{2,1,0:T(8,128)(2,1)S(1)}, u32[]{:S(2)}, u32[]{:S(2)}) collective-permute-start(bf16[2,48,512]{2,1,0:T(8,128)(2,1)S(1)} %get-tuple-element.86), channel_id=1, source_target_pairs={{0,56},{8,0},{16,8},{24,16},{32,24},{40,32},{48,40},{56,48},{1,57}... | collective-permute-start | bytes 294920 | tf_op jit(solution)/shard_map/ppermute | solution.py:26
  160.7 4.5 %collective-permute-done.39 = bf16[2,48,512]{2,1,0:T(8,128)(2,1)S(1)} collective-permute-done((bf16[2,48,512]{2,1,0:T(8,128)(2,1)S(1)}, bf16[2,48,512]{2,1,0:T(8,128)(2,1)S(1)}, u32[]{:S(2)}, u32[]{:S(2)}) %collective-permute-start.39) | collective-permute-done | bytes 98336 | tf_op jit(solution)/shard_map/ppermute | solution.py:26
  166.1 8.2 %collective-permute-done.41 = bf16[48,1024]{1,0:T(8,128)(2,1)S(1)} collective-permute-done((bf16[48,1024]{1,0:T(8,128)(2,1)S(1)}, bf16[48,1024]{1,0:T(8,128)(2,1)S(1)}, u32[]{:S(2)}, u32[]{:S(2)}) %collective-permute-start.41) | collective-permute-done | bytes 98336 | tf_op jit(solution)/shard_map/ppermute | solution.py:26
  (85 shorter events, 37.3 us)
Async XLA Ops:
  0.6 10.4 %collective-permute-start = (bf16[48,1024]{1,0:T(8,128)(2,1)}, bf16[48,1024]{1,0:T(8,128)(2,1)S(1)}, u32[]{:S(2)}, u32[]{:S(2)}) collective-permute-start(bf16[48,1024]{1,0:T(8,128)(2,1)} %param.6), channel_id=1, source_target_pairs={{32,0},{40,8},{48,16},{56,24},{0,32},{8,40},{16,48},{24,56},{33,1}... | collective-permute-start | bytes 294920 | tf_op jit(solution)/shard_map/ppermute | solution.py:21
  11.9 13.2 %collective-permute-start.6 = (bf16[2,48,512]{2,1,0:T(8,128)(2,1)S(1)}, bf16[2,48,512]{2,1,0:T(8,128)(2,1)S(1)}, u32[]{:S(2)}, u32[]{:S(2)}) collective-permute-start(bf16[2,48,512]{2,1,0:T(8,128)(2,1)S(1)} %get-tuple-element.48), channel_id=1, source_target_pairs={{56,0},{0,8},{8,16},{16,24},{24,32},{32,40},{40,48},{48,56},{57,1}... | collective-permute-start | bytes 294920 | tf_op jit(solution)/shard_map/ppermute | solution.py:21
  14.4 12.0 %collective-permute-start.5 = (bf16[2,48,512]{2,1,0:T(8,128)(2,1)S(1)}, bf16[2,48,512]{2,1,0:T(8,128)(2,1)S(1)}, u32[]{:S(2)}, u32[]{:S(2)}) collective-permute-start(bf16[2,48,512]{2,1,0:T(8,128)(2,1)S(1)} %get-tuple-element.48), channel_id=1, source_target_pairs={{16,0},{24,8},{32,16},{40,24},{48,32},{56,40},{0,48},{8,56},{17,1}... | collective-permute-start | bytes 294920 | tf_op jit(solution)/shard_map/ppermute | solution.py:21
  18.6 7.8 %collective-permute-start.4 = (bf16[2,48,512]{2,1,0:T(8,128)(2,1)S(1)}, bf16[2,48,512]{2,1,0:T(8,128)(2,1)S(1)}, u32[]{:S(2)}, u32[]{:S(2)}) collective-permute-start(bf16[2,48,512]{2,1,0:T(8,128)(2,1)S(1)} %get-tuple-element.48), channel_id=1, source_target_pairs={{8,0},{16,8},{24,16},{32,24},{40,32},{48,40},{56,48},{0,56},{9,1},... | collective-permute-start | bytes 294920 | tf_op jit(solution)/shard_map/ppermute | solution.py:21
  29.7 13.0 %collective-permute-start.12 = (bf16[4,2,48,512]{3,2,1,0:T(8,128)(2,1)S(1)}, bf16[4,2,48,512]{3,2,1,0:T(8,128)(2,1)S(1)}, u32[]{:S(2)}, u32[]{:S(2)}) collective-permute-start(bf16[4,2,48,512]{3,2,1,0:T(8,128)(2,1)S(1)} %pad_maximum_fusion.3.refs_4_), channel_id=1, source_target_pairs={{192,0},{0,64},{64,128},{128,192},{193,1},{1,65},{65,129},{129,193... | collective-permute-start | bytes 1179656 | tf_op jit(solution)/shard_map/ppermute | solution.py:21
  30.5 19.5 %collective-permute-start.11 = (bf16[4,2,48,512]{3,2,1,0:T(8,128)(2,1)S(1)}, bf16[4,2,48,512]{3,2,1,0:T(8,128)(2,1)S(1)}, u32[]{:S(2)}, u32[]{:S(2)}) collective-permute-start(bf16[4,2,48,512]{3,2,1,0:T(8,128)(2,1)S(1)} %pad_maximum_fusion.3.refs_4_), channel_id=1, source_target_pairs={{128,0},{192,64},{0,128},{64,192},{129,1},{193,65},{1,129},{65,193... | collective-permute-start | bytes 1179656 | tf_op jit(solution)/shard_map/ppermute | solution.py:21
  33.8 16.2 %collective-permute-start.10 = (bf16[4,2,48,512]{3,2,1,0:T(8,128)(2,1)S(1)}, bf16[4,2,48,512]{3,2,1,0:T(8,128)(2,1)S(1)}, u32[]{:S(2)}, u32[]{:S(2)}) collective-permute-start(bf16[4,2,48,512]{3,2,1,0:T(8,128)(2,1)S(1)} %pad_maximum_fusion.3.refs_4_), channel_id=1, source_target_pairs={{64,0},{128,64},{192,128},{0,192},{65,1},{129,65},{193,129},{1,193... | collective-permute-start | bytes 1179656 | tf_op jit(solution)/shard_map/ppermute | solution.py:21
  34.4 15.6 %collective-permute-start.9 = (bf16[4,2,48,512]{3,2,1,0:T(8,128)(2,1)S(1)}, bf16[4,2,48,512]{3,2,1,0:T(8,128)(2,1)S(1)}, u32[]{:S(2)}, u32[]{:S(2)}) collective-permute-start(bf16[4,2,48,512]{3,2,1,0:T(8,128)(2,1)S(1)} %pad_maximum_fusion.2.refs_0_), channel_id=1, source_target_pairs={{56,0},{0,8},{8,16},{16,24},{24,32},{32,40},{40,48},{48,56},{57,1}... | collective-permute-start | bytes 1179656 | tf_op jit(solution)/shard_map/ppermute | solution.py:21
  34.5 19.1 %collective-permute-start.8 = (bf16[4,2,48,512]{3,2,1,0:T(8,128)(2,1)S(1)}, bf16[4,2,48,512]{3,2,1,0:T(8,128)(2,1)S(1)}, u32[]{:S(2)}, u32[]{:S(2)}) collective-permute-start(bf16[4,2,48,512]{3,2,1,0:T(8,128)(2,1)S(1)} %pad_maximum_fusion.2.refs_0_), channel_id=1, source_target_pairs={{16,0},{24,8},{32,16},{40,24},{48,32},{56,40},{0,48},{8,56},{17,1}... | collective-permute-start | bytes 1179656 | tf_op jit(solution)/shard_map/ppermute | solution.py:21
  42.7 18.6 %collective-permute-start.7 = (bf16[4,2,48,512]{3,2,1,0:T(8,128)(2,1)S(1)}, bf16[4,2,48,512]{3,2,1,0:T(8,128)(2,1)S(1)}, u32[]{:S(2)}, u32[]{:S(2)}) collective-permute-start(bf16[4,2,48,512]{3,2,1,0:T(8,128)(2,1)S(1)} %pad_maximum_fusion.2.refs_0_), channel_id=1, source_target_pairs={{8,0},{16,8},{24,16},{32,24},{40,32},{48,40},{56,48},{0,56},{9,1},... | collective-permute-start | bytes 1179656 | tf_op jit(solution)/shard_map/ppermute | solution.py:21
  70.3 20.3 %collective-permute-start.18 = (bf16[192,512]{1,0:T(8,128)(2,1)S(1)}, bf16[192,512]{1,0:T(8,128)(2,1)S(1)}, u32[]{:S(2)}, u32[]{:S(2)}) collective-permute-start(bf16[192,512]{1,0:T(8,128)(2,1)S(1)} %get-tuple-element.64), channel_id=1, source_target_pairs={{0,2},{2,4},{4,6},{6,0},{1,3},{3,5},{5,7},{7,1},{8,10},{10,12},{12... | collective-permute-start | bytes 589832 | tf_op jit(solution)/shard_map/ppermute | solution.py:26
  71.4 11.1 %collective-permute-start.14 = (bf16[192,512]{1,0:T(8,128)(2,1)S(1)}, bf16[192,512]{1,0:T(8,128)(2,1)S(1)}, u32[]{:S(2)}, u32[]{:S(2)}) collective-permute-start(bf16[192,512]{1,0:T(8,128)(2,1)S(1)} %get-tuple-element.56), channel_id=1, source_target_pairs={{0,2},{2,4},{4,6},{6,0},{1,3},{3,5},{5,7},{7,1},{8,10},{10,12},{12... | collective-permute-start | bytes 589832 | tf_op jit(solution)/shard_map/ppermute | solution.py:26
  72.9 10.5 %collective-permute-start.15 = (bf16[192,512]{1,0:T(8,128)(2,1)S(1)}, bf16[192,512]{1,0:T(8,128)(2,1)S(1)}, u32[]{:S(2)}, u32[]{:S(2)}) collective-permute-start(bf16[192,512]{1,0:T(8,128)(2,1)S(1)} %get-tuple-element.57), channel_id=1, source_target_pairs={{0,4},{2,6},{4,0},{6,2},{1,5},{3,7},{5,1},{7,3},{8,12},{10,14},{12... | collective-permute-start | bytes 589832 | tf_op jit(solution)/shard_map/ppermute | solution.py:26
  75.0 13.1 %collective-permute-start.16 = (bf16[192,512]{1,0:T(8,128)(2,1)S(1)}, bf16[192,512]{1,0:T(8,128)(2,1)S(1)}, u32[]{:S(2)}, u32[]{:S(2)}) collective-permute-start(bf16[192,512]{1,0:T(8,128)(2,1)S(1)} %get-tuple-element.58), channel_id=1, source_target_pairs={{0,6},{2,0},{4,2},{6,4},{1,7},{3,1},{5,3},{7,5},{8,14},{10,8},{12,... | collective-permute-start | bytes 589832 | tf_op jit(solution)/shard_map/ppermute | solution.py:26
  75.2 16.6 %collective-permute-start.19 = (bf16[192,512]{1,0:T(8,128)(2,1)S(1)}, bf16[192,512]{1,0:T(8,128)(2,1)S(1)}, u32[]{:S(2)}, u32[]{:S(2)}) collective-permute-start(bf16[192,512]{1,0:T(8,128)(2,1)S(1)} %get-tuple-element.65), channel_id=1, source_target_pairs={{0,4},{2,6},{4,0},{6,2},{1,5},{3,7},{5,1},{7,3},{8,12},{10,14},{12... | collective-permute-start | bytes 589832 | tf_op jit(solution)/shard_map/ppermute | solution.py:26
  82.5 14.0 %collective-permute-start.20 = (bf16[192,512]{1,0:T(8,128)(2,1)S(1)}, bf16[192,512]{1,0:T(8,128)(2,1)S(1)}, u32[]{:S(2)}, u32[]{:S(2)}) collective-permute-start(bf16[192,512]{1,0:T(8,128)(2,1)S(1)} %get-tuple-element.66), channel_id=1, source_target_pairs={{0,6},{2,0},{4,2},{6,4},{1,7},{3,1},{5,3},{7,5},{8,14},{10,8},{12,... | collective-permute-start | bytes 589832 | tf_op jit(solution)/shard_map/ppermute | solution.py:26
  88.4 9.5 %collective-permute-start.27 = (bf16[192,512]{1,0:T(8,128)(2,1)S(1)}, bf16[192,512]{1,0:T(8,128)(2,1)S(1)}, u32[]{:S(2)}, u32[]{:S(2)}) collective-permute-start(bf16[192,512]{1,0:T(8,128)(2,1)S(1)} %get-tuple-element.70), channel_id=1, source_target_pairs={{6,0},{0,2},{2,4},{4,6},{7,1},{1,3},{3,5},{5,7},{14,8},{8,10},{10,... | collective-permute-start | bytes 589832 | tf_op jit(solution)/shard_map/ppermute | solution.py:21
  89.7 9.4 %collective-permute-start.26 = (bf16[192,512]{1,0:T(8,128)(2,1)S(1)}, bf16[192,512]{1,0:T(8,128)(2,1)S(1)}, u32[]{:S(2)}, u32[]{:S(2)}) collective-permute-start(bf16[192,512]{1,0:T(8,128)(2,1)S(1)} %get-tuple-element.70), channel_id=1, source_target_pairs={{4,0},{6,2},{0,4},{2,6},{5,1},{7,3},{1,5},{3,7},{12,8},{14,10},{8,... | collective-permute-start | bytes 589832 | tf_op jit(solution)/shard_map/ppermute | solution.py:21
  90.5 14.4 %collective-permute-start.25 = (bf16[192,512]{1,0:T(8,128)(2,1)S(1)}, bf16[192,512]{1,0:T(8,128)(2,1)S(1)}, u32[]{:S(2)}, u32[]{:S(2)}) collective-permute-start(bf16[192,512]{1,0:T(8,128)(2,1)S(1)} %get-tuple-element.70), channel_id=1, source_target_pairs={{2,0},{4,2},{6,4},{0,6},{3,1},{5,3},{7,5},{1,7},{10,8},{12,10},{14... | collective-permute-start | bytes 589832 | tf_op jit(solution)/shard_map/ppermute | solution.py:21
  96.8 8.3 %collective-permute-start.23 = (bf16[192,512]{1,0:T(8,128)(2,1)S(1)}, bf16[192,512]{1,0:T(8,128)(2,1)S(1)}, u32[]{:S(2)}, u32[]{:S(2)}) collective-permute-start(bf16[192,512]{1,0:T(8,128)(2,1)S(1)} %get-tuple-element.68), channel_id=1, source_target_pairs={{6,0},{0,2},{2,4},{4,6},{7,1},{1,3},{3,5},{5,7},{14,8},{8,10},{10,... | collective-permute-start | bytes 589832 | tf_op jit(solution)/shard_map/ppermute | solution.py:21
  96.9 10.7 %collective-permute-start.22 = (bf16[192,512]{1,0:T(8,128)(2,1)S(1)}, bf16[192,512]{1,0:T(8,128)(2,1)S(1)}, u32[]{:S(2)}, u32[]{:S(2)}) collective-permute-start(bf16[192,512]{1,0:T(8,128)(2,1)S(1)} %get-tuple-element.68), channel_id=1, source_target_pairs={{4,0},{6,2},{0,4},{2,6},{5,1},{7,3},{1,5},{3,7},{12,8},{14,10},{8,... | collective-permute-start | bytes 589832 | tf_op jit(solution)/shard_map/ppermute | solution.py:21
  97.9 12.3 %collective-permute-start.21 = (bf16[192,512]{1,0:T(8,128)(2,1)S(1)}, bf16[192,512]{1,0:T(8,128)(2,1)S(1)}, u32[]{:S(2)}, u32[]{:S(2)}) collective-permute-start(bf16[192,512]{1,0:T(8,128)(2,1)S(1)} %get-tuple-element.68), channel_id=1, source_target_pairs={{2,0},{4,2},{6,4},{0,6},{3,1},{5,3},{7,5},{1,7},{10,8},{12,10},{14... | collective-permute-start | bytes 589832 | tf_op jit(solution)/shard_map/ppermute | solution.py:21
  117.9 14.8 %collective-permute-start.29 = (bf16[4,2,48,512]{3,2,1,0:T(8,128)(2,1)S(1)}, bf16[4,2,48,512]{3,2,1,0:T(8,128)(2,1)S(1)}, u32[]{:S(2)}, u32[]{:S(2)}) collective-permute-start(bf16[4,2,48,512]{3,2,1,0:T(8,128)(2,1)S(1)} %get-tuple-element.74), channel_id=1, source_target_pairs={{0,8},{8,16},{16,24},{24,32},{32,40},{40,48},{48,56},{56,0},{1,9},... | collective-permute-start | bytes 1179656 | tf_op jit(solution)/shard_map/ppermute | solution.py:26
  118.0 29.0 %collective-permute-start.30 = (bf16[4,2,48,512]{3,2,1,0:T(8,128)(2,1)S(1)}, bf16[4,2,48,512]{3,2,1,0:T(8,128)(2,1)S(1)}, u32[]{:S(2)}, u32[]{:S(2)}) collective-permute-start(bf16[4,2,48,512]{3,2,1,0:T(8,128)(2,1)S(1)} %get-tuple-element.75), channel_id=1, source_target_pairs={{0,16},{8,24},{16,32},{24,40},{32,48},{40,56},{48,0},{56,8},{1,17}... | collective-permute-start | bytes 1179656 | tf_op jit(solution)/shard_map/ppermute | solution.py:26
  119.1 27.9 %collective-permute-start.31 = (bf16[4,2,48,512]{3,2,1,0:T(8,128)(2,1)S(1)}, bf16[4,2,48,512]{3,2,1,0:T(8,128)(2,1)S(1)}, u32[]{:S(2)}, u32[]{:S(2)}) collective-permute-start(bf16[4,2,48,512]{3,2,1,0:T(8,128)(2,1)S(1)} %get-tuple-element.76), channel_id=1, source_target_pairs={{0,56},{8,0},{16,8},{24,16},{32,24},{40,32},{48,40},{56,48},{1,57}... | collective-permute-start | bytes 1179656 | tf_op jit(solution)/shard_map/ppermute | solution.py:26
  121.2 26.0 %collective-permute-start.32 = (bf16[4,2,48,512]{3,2,1,0:T(8,128)(2,1)S(1)}, bf16[4,2,48,512]{3,2,1,0:T(8,128)(2,1)S(1)}, u32[]{:S(2)}, u32[]{:S(2)}) collective-permute-start(bf16[4,2,48,512]{3,2,1,0:T(8,128)(2,1)S(1)} %get-tuple-element.78), channel_id=1, source_target_pairs={{0,64},{64,128},{128,192},{192,0},{1,65},{65,129},{129,193},{193,1... | collective-permute-start | bytes 1179656 | tf_op jit(solution)/shard_map/ppermute | solution.py:26
  122.5 24.7 %collective-permute-start.33 = (bf16[4,2,48,512]{3,2,1,0:T(8,128)(2,1)S(1)}, bf16[4,2,48,512]{3,2,1,0:T(8,128)(2,1)S(1)}, u32[]{:S(2)}, u32[]{:S(2)}) collective-permute-start(bf16[4,2,48,512]{3,2,1,0:T(8,128)(2,1)S(1)} %get-tuple-element.79), channel_id=1, source_target_pairs={{0,128},{64,192},{128,0},{192,64},{1,129},{65,193},{129,1},{193,65... | collective-permute-start | bytes 1179656 | tf_op jit(solution)/shard_map/ppermute | solution.py:26
  132.7 14.5 %collective-permute-start.34 = (bf16[4,2,48,512]{3,2,1,0:T(8,128)(2,1)S(1)}, bf16[4,2,48,512]{3,2,1,0:T(8,128)(2,1)S(1)}, u32[]{:S(2)}, u32[]{:S(2)}) collective-permute-start(bf16[4,2,48,512]{3,2,1,0:T(8,128)(2,1)S(1)} %get-tuple-element.80), channel_id=1, source_target_pairs={{0,192},{64,0},{128,64},{192,128},{1,193},{65,1},{129,65},{193,129... | collective-permute-start | bytes 1179656 | tf_op jit(solution)/shard_map/ppermute | solution.py:26
  147.6 10.5 %collective-permute-start.35 = (bf16[2,48,512]{2,1,0:T(8,128)(2,1)S(1)}, bf16[2,48,512]{2,1,0:T(8,128)(2,1)S(1)}, u32[]{:S(2)}, u32[]{:S(2)}) collective-permute-start(bf16[2,48,512]{2,1,0:T(8,128)(2,1)S(1)} %get-tuple-element.88), channel_id=1, source_target_pairs={{0,64},{64,128},{128,192},{192,0},{1,65},{65,129},{129,193},{193,1... | collective-permute-start | bytes 294920 | tf_op jit(solution)/shard_map/ppermute | solution.py:26
  150.6 7.5 %collective-permute-start.37 = (bf16[2,48,512]{2,1,0:T(8,128)(2,1)S(1)}, bf16[2,48,512]{2,1,0:T(8,128)(2,1)S(1)}, u32[]{:S(2)}, u32[]{:S(2)}) collective-permute-start(bf16[2,48,512]{2,1,0:T(8,128)(2,1)S(1)} %get-tuple-element.89), channel_id=1, source_target_pairs={{0,192},{64,0},{128,64},{192,128},{1,193},{65,1},{129,65},{193,129... | collective-permute-start | bytes 294920 | tf_op jit(solution)/shard_map/ppermute | solution.py:26
  158.1 7.1 %collective-permute-start.39 = (bf16[2,48,512]{2,1,0:T(8,128)(2,1)S(1)}, bf16[2,48,512]{2,1,0:T(8,128)(2,1)S(1)}, u32[]{:S(2)}, u32[]{:S(2)}) collective-permute-start(bf16[2,48,512]{2,1,0:T(8,128)(2,1)S(1)} %get-tuple-element.87), channel_id=1, source_target_pairs={{0,16},{8,24},{16,32},{24,40},{32,48},{40,56},{48,0},{56,8},{1,17}... | collective-permute-start | bytes 294920 | tf_op jit(solution)/shard_map/ppermute | solution.py:26
  165.2 9.1 %collective-permute-start.41 = (bf16[48,1024]{1,0:T(8,128)(2,1)S(1)}, bf16[48,1024]{1,0:T(8,128)(2,1)S(1)}, u32[]{:S(2)}, u32[]{:S(2)}) collective-permute-start(bf16[48,1024]{1,0:T(8,128)(2,1)S(1)} %fusion.10), channel_id=1, source_target_pairs={{0,32},{8,40},{16,48},{24,56},{32,0},{40,8},{48,16},{56,24},{1,33}... | collective-permute-start | bytes 294920 | tf_op jit(solution)/shard_map/ppermute | solution.py:26
  (12 other events, 56.6 us)

commit v4 on v3

--- a/solution.py
+++ b/solution.py
@@ -1,3 +1,5 @@
+import functools
+
 import jax
 import jax.numpy as jnp
 from jax import lax
@@ -66,37 +68,41 @@
     return (pos[1] + i + 4 * hi + 8) % 8
 
 
-def up_part(pos, toks, w, at, keep, send, acc):
+def z_step(i, j):
+    return -2 if i == 2 and j >= 2 else STEPS[i]
+
+
+def at_step(pieces, step, k):
+    if step == 2:
+        return pieces[2 + k // 2], k % 2
+    return pieces[step + step // 3], k
+
+
+def up_body(pos, *refs):
+    a3, b3, w = refs[:5], refs[5:10], refs[10]
+    keep, send, toks, acc = refs[11:]
     core = pos[3]
-
-    @pl.loop(0, 4)
-    def _(d):
-        part = jnp.dot(
-            toks[d].reshape(-1, toks.shape[-1]), w[:, at], preferred_element_type=F32
-        )
-        acc[...] = part.reshape(acc.shape)
-        keep[d] = acc[core]
-        send[d] = acc[1 - core].astype(BF16)
-
-
-def up_first_body(pos, *refs):
-    a3, b3, w = refs[:4], refs[4:8], refs[8]
-    keep, send, toks, acc = refs[9:]
     cut = a3[0].shape[-1]
     back = pos[0] - pos[2] + 4
     for j in range(4):
         d = (j + back) % 4
         for i in range(4):
+            a_ref, a_at = at_step(a3, i, j)
+            b_ref, b_at = at_step(b3, j, i)
             for hi in range(2):
                 at = zpos(pos, STEPS[i], hi)
-                toks[d, at, :, :cut] = a3[i][j, hi]
-                toks[d, at, :, cut:] = b3[j][i, hi]
-    up_part(pos, toks, w, slice(0, keep.shape[-1]), keep, send, acc)
-
-
-def up_second_body(pos, toks, w, keep, send, acc):
-    n = keep.shape[-1]
-    up_part(pos, toks, w, slice(n, 2 * n), keep, send, acc)
+                low = zpos(pos, z_step(i, j), hi)
+                toks[d, low, :, :cut] = a_ref[a_at, hi]
+                toks[d, at, :, cut:] = b_ref[b_at, hi]
+
+    @pl.loop(0, 4)
+    def _(d):
+        part = jnp.dot(
+            toks[d].reshape(-1, toks.shape[-1]), w[...], preferred_element_type=F32
+        )
+        acc[...] = part.reshape(acc.shape)
+        keep[d] = acc[core]
+        send[d] = acc[1 - core].astype(BF16)
 
 
 def collect(pos, mine, other, slots, sems):
@@ -146,7 +152,8 @@
 
             @pl.loop(0, 4)
             def _(j, k=k, hi=hi):
-                piece = acc[j, zpos(pos, STEPS[k], hi), :, :cut]
+                step = jnp.where(j >= 2, z_step(k, 2), z_step(k, 0))
+                piece = acc[j, zpos(pos, step, hi), :, :cut]
                 a3[k][j, hi] = piece.astype(a3[k].dtype)
 
             @pl.loop(0, 4)
@@ -155,13 +162,13 @@
                 b3[k][i, hi] = piece.astype(b3[k].dtype)
 
 
-def add_body(keep, recv, *out):
+def add_body(cols, keep, recv, *out):
     for d in range(4):
 
         @pl.loop(0, keep.shape[1] // 32)
         def _(i, d=d):
             at = pl.ds(pl.multiple_of(i * 32, 32), 32)
-            total = keep[d, at] + recv[d, at].astype(F32)
+            total = keep[d, at, cols] + recv[d, at, cols].astype(F32)
             out[d][at] = total.astype(out[d].dtype)
 
 
@@ -178,7 +185,7 @@
 
 def wgrad_body(rows, cols, count, toks, grads, out, acc):
     acc[...] = jnp.zeros_like(acc)
-    step = 256
+    step = 512
 
     @pl.loop(0, 4)
     def _(d):
@@ -203,20 +210,26 @@
     return [piece] + [from_ahead(piece, axis, k) for k in STEPS[1:]]
 
 
+def ring_gather(piece, axis):
+    ahead, behind = from_ahead(piece, axis, 1), from_ahead(piece, axis, -1)
+    half = piece.shape[0] // 2
+    far = [from_ahead(ahead[:half], axis, 1), from_ahead(behind[half:], axis, -1)]
+    return [piece, ahead] + far + [behind]
+
+
 def gather_tokens(tokens):
     pair = jnp.stack([tokens, from_ahead(tokens, "z", 4)])
     cut = tokens.shape[1] // 2
     a2 = gather_four(pair[:, :, :cut], "y")
     b2 = gather_four(pair[:, :, cut:], "z")
     a2, b2 = lax.optimization_barrier((a2, b2))
-    return gather_four(jnp.stack(a2), "z"), gather_four(jnp.stack(b2), "y")
-
-
-def partial_sums(keep, send):
-    shape = keep.shape[1:]
-    return call(
-        add_body, [(shape, F32)] + [(shape, BF16)] * 3, [], [keep, to_ahead(send, "core", 1)]
-    )
+    return ring_gather(jnp.stack(a2), "z"), ring_gather(jnp.stack(b2), "y")
+
+
+def partial_sums(keep, recv, cols):
+    shape = (keep.shape[1], cols.stop - cols.start)
+    body = functools.partial(add_body, cols)
+    return call(body, [(shape, F32)] + [(shape, BF16)] * 3, [], [keep, recv])
 
 
 def shares(sends):
@@ -239,20 +252,36 @@
     return total
 
 
+def ring_reduce(own, ahead, far, behind, axis):
+    half = own.shape[0] // 2
+    lo = to_ahead(far[:half], axis, 1).astype(F32)
+    hi = to_ahead(far[half:], axis, -1).astype(F32)
+    ahead = jnp.concatenate([ahead[:half] + lo, ahead[half:]])
+    behind = jnp.concatenate([behind[:half], behind[half:] + hi])
+    total = own + to_ahead(ahead.astype(BF16), axis, 1).astype(F32)
+    return total + to_ahead(behind.astype(BF16), axis, -1).astype(F32)
+
+
 def middle(a3, b3, wm, flipped, pos, cot):
     rows = a3[0].shape[2] * 4
     depth, width = wm.shape
     cut = width // 2
     flops = 8 * rows * depth * width
-    pair = [((4, rows, cut), F32), ((4, rows, cut), BF16)]
-    tok_shape = ((4, 8, rows // 4, depth), BF16)
-    acc = VM((2, rows, cut), F32)
-    keep1, send1, toks = call(
-        up_first_body, pair + [tok_shape], [pos], a3 + b3 + [wm], flops, [acc]
-    )
-    own1, *sends1 = partial_sums(keep1, send1)
-    keep2, send2 = call(up_second_body, pair, [pos], [toks, wm], flops, [acc])
-    own2, *sends2 = partial_sums(keep2, send2)
+    keep, send, toks = call(
+        up_body,
+        [
+            ((4, rows, width), F32),
+            ((4, rows, width), BF16),
+            ((4, 8, rows // 4, depth), BF16),
+        ],
+        [pos],
+        a3 + b3 + [wm],
+        2 * flops,
+        [VM((2, rows, width), F32)],
+    )
+    recv = to_ahead(send, "core", 1)
+    own1, *sends1 = partial_sums(keep, recv, slice(0, cut))
+    own2, *sends2 = partial_sums(keep, recv, slice(cut, width))
     hidden1, grad1 = activation(own1, shares(sends1), cot[:, :cut])
     hidden2, grad2 = activation(own2, shares(sends2), cot[:, cut:])
     parts1 = gather_grads(grad1)
@@ -264,7 +293,7 @@
         back_first_body, [(sums, F32), g_shape], [pos], parts1 + [flipped], flops, [sems]
     )
     shape = (4, 2, rows // 4, depth // 2)
-    outs = [(shape, F32)] + [(shape, BF16)] * 3
+    outs = [(shape, d) for d in (F32, F32, BF16, F32)]
     *sends, grads = call(
         back_second_body,
         outs + outs + [((4, 2, rows, width), BF16)],
@@ -277,15 +306,15 @@
     return hidden, sends, toks, grads
 
 
-def reduce_inputs(sends, weight_grad):
-    a2 = reduce_four(sends[0], sends[1:4], "z")
-    b2 = reduce_four(sends[4], sends[5:], "y")
-    a2, b2, weight_grad = lax.optimization_barrier((a2, b2, weight_grad))
+def reduce_inputs(sends):
+    a2 = ring_reduce(*sends[:4], "z")
+    b2 = ring_reduce(*sends[4:], "y")
+    a2, b2 = lax.optimization_barrier((a2, b2))
     a1 = reduce_four(a2[0], a2[1:], "y")
     b1 = reduce_four(b2[0], b2[1:], "z")
     both = jnp.concatenate([a1, b1], axis=-1)
     total = both[0] + to_ahead(both[1].astype(BF16), "z", 4).astype(F32)
-    return total.astype(BF16), weight_grad
+    return total.astype(BF16)
 
 
 def on_device(tokens, weight, tile_rows, tile_cols, tile_count, hidden_cotangent):
@@ -308,7 +337,7 @@
         2 * 1536 * weight.size,
         [VM(weight.shape, F32)],
     )
-    input_grad, weight_grad = reduce_inputs(sends, weight_grad)
+    input_grad = reduce_inputs(sends)
     return hidden, input_grad, weight_grad
 
 

time: 176 us -> 178 us (1.011)
  the two profiles are of different devices: /device:TPU:6 before, /device:TPU:10 now
where the time goes in v4:
time: 178 us; the launch traced here: 175 us
  starting transfers between devices  84.8 us (48%)
  waiting for transfers between devices  55.1 us (31%)
  Pallas kernels  26.2 us (15%)
  other arithmetic  3.54 us (2%)
  local copies, waits for them, and re-layouts  3.08 us (2%)
  between operations  1.87 us (1%)
    ppermute x21, starting transfers between devices, from_ahead(): return lax.ppermute(value, axis, [((i + k) % n, i) for i in range(n)])  42.5 us
    ppermute x24, starting transfers between devices, to_ahead(): return lax.ppermute(value, axis, [(i, (i + k) % n) for i in range(n)])  42.3 us
    ppermute x24, waiting for transfers between devices, to_ahead(): return lax.ppermute(value, axis, [(i, (i + k) % n) for i in range(n)])  37.3 us
    pallas_call x9, Pallas kernels, call(): pl.pallas_call(body, out_shape=outs, in_specs=[pl.BlockSpec(memory_space=...  26.2 us
    ppermute x21, waiting for transfers between devices, from_ahead(): return lax.ppermute(value, axis, [((i + k) % n, i) for i in range(n)])  17.8 us
  transfers between devices with their start and end apart: 45, of which 21 were waited for; matrix products, arithmetic and copies ran while one was open for 3% of the time, Pallas kernels for 9%

profile of v4, /device:TPU:10, one launch (start us, length us, event | category | flops | bytes accessed | tf_op | source)
XLA Modules:
  0.0 174.6 jit_solution(10004266991694034964)
XLA Ops:
  0.7 7.3 %collective-permute-start = (bf16[48,1024]{1,0:T(8,128)(2,1)}, bf16[48,1024]{1,0:T(8,128)(2,1)S(1)}, u32[]{:S(2)}, u32[]{:S(2)}) collective-permute-start(bf16[48,1024]{1,0:T(8,128)(2,1)} %param.6), channel_id=1, source_target_pairs={{32,0},{40,8},{48,16},{56,24},{0,32},{8,40},{16,48},{24,56},{33,1}... | collective-permute-start | bytes 294920 | tf_op jit(solution)/shard_map/ppermute | solution.py:23
  7.9 3.1 %collective-permute-done = bf16[48,1024]{1,0:T(8,128)(2,1)S(1)} collective-permute-done((bf16[48,1024]{1,0:T(8,128)(2,1)}, bf16[48,1024]{1,0:T(8,128)(2,1)S(1)}, u32[]{:S(2)}, u32[]{:S(2)}) %collective-permute-start) | collective-permute-done | bytes 98336 | tf_op jit(solution)/shard_map/ppermute | solution.py:23
  11.9 2.6 %collective-permute-start.6 = (bf16[2,48,512]{2,1,0:T(8,128)(2,1)S(1)}, bf16[2,48,512]{2,1,0:T(8,128)(2,1)S(1)}, u32[]{:S(2)}, u32[]{:S(2)}) collective-permute-start(bf16[2,48,512]{2,1,0:T(8,128)(2,1)S(1)} %get-tuple-element.45), channel_id=1, source_target_pairs={{56,0},{0,8},{8,16},{16,24},{24,32},{32,40},{40,48},{48,56},{57,1}... | collective-permute-start | bytes 294920 | tf_op jit(solution)/shard_map/ppermute | solution.py:23
  14.4 4.2 %collective-permute-start.5 = (bf16[2,48,512]{2,1,0:T(8,128)(2,1)S(1)}, bf16[2,48,512]{2,1,0:T(8,128)(2,1)S(1)}, u32[]{:S(2)}, u32[]{:S(2)}) collective-permute-start(bf16[2,48,512]{2,1,0:T(8,128)(2,1)S(1)} %get-tuple-element.45), channel_id=1, source_target_pairs={{16,0},{24,8},{32,16},{40,24},{48,32},{56,40},{0,48},{8,56},{17,1}... | collective-permute-start | bytes 294920 | tf_op jit(solution)/shard_map/ppermute | solution.py:23
  23.1 2.4 %collective-permute-start.1 = (bf16[2,48,512]{2,1,0:T(8,128)(2,1)S(1)}, bf16[2,48,512]{2,1,0:T(8,128)(2,1)S(1)}, u32[]{:S(2)}, u32[]{:S(2)}) collective-permute-start(bf16[2,48,512]{2,1,0:T(8,128)(2,1)S(1)} %get-tuple-element.41), channel_id=1, source_target_pairs={{64,0},{128,64},{192,128},{0,192},{65,1},{129,65},{193,129},{1,193... | collective-permute-start | bytes 294920 | tf_op jit(solution)/shard_map/ppermute | solution.py:23
  31.2 3.1 %collective-permute-start.7 = (bf16[4,2,48,512]{3,2,1,0:T(8,128)(2,1)S(1)}, bf16[4,2,48,512]{3,2,1,0:T(8,128)(2,1)}, u32[]{:S(2)}, u32[]{:S(2)}) collective-permute-start(bf16[4,2,48,512]{3,2,1,0:T(8,128)(2,1)S(1)} %pad_maximum_fusion.2.refs_0_), channel_id=1, source_target_pairs={{8,0},{16,8},{24,16},{32,24},{40,32},{48,40},{56,48},{0,56},{9,1},... | collective-permute-start | bytes 1179656 | tf_op jit(solution)/shard_map/ppermute | solution.py:23
  34.3 2.6 %collective-permute-done.13.refs_9_ = bf16[4,2,48,512]{3,2,1,0:T(8,128)(2,1)S(1)} collective-permute-done((bf16[4,2,48,512]{3,2,1,0:T(8,128)(2,1)S(1)}, bf16[4,2,48,512]{3,2,1,0:T(8,128)(2,1)S(1)}, u32[]{:S(2)}, u32[]{:S(2)}) %collective-permute-start.13) | collective-permute-done | bytes 393248 | tf_op jit(solution)/shard_map/ppermute | solution.py:23
  46.7 3.1 %shard_map.85 = (bf16[1024,1024]{1,0:T(8,128)(2,1)S(1)}, bf16[1024,1024]{1,0:T(8,128)(2,1)S(1)}) custom-call(s32[32]{0:T(128)S(1)} %get-tuple-element.94.rows, s32[32]{0:T(128)S(1)} %get-tuple-element.93.cols, s32[1]{0:T(128)} %bitcast.59.count, bf16[1024,1024]{1,0:T(8,128)(2,1)S(1)} %copy-done), custom_call_target="tpu_custom_call" | custom-call | bytes 6291456 | tf_op jit(solution)/shard_map/pallas_call | solution.py:33
  49.9 5.8 %shard_map.86 = (f32[4,192,1024]{2,1,0:T(8,128)S(1)}, bf16[4,192,1024]{2,1,0:T(8,128)(2,1)S(1)}, bf16[4,8,48,1024]{3,2,1,0:T(8,128)(2,1)S(1)}) custom-call(s32[4]{0:T(128)S(1)} %pad_add_fusion.pos, bf16[4,2,48,512]{3,2,1,0:T(8,128)(2,1)S(1)} %pad_maximum_fusion.2.refs_0_, bf16[4,2,48,512]{3,2,1,0:T(8,128)(2,1)} %collective-permute-done.7.refs_1_, ...), custom_call_target="tpu_custom_call" | custom-call | flops 3221225472 | bytes 13107200 | tf_op jit(solution)/shard_map/pallas_call | solution.py:33
  55.8 3.4 %collective-permute-done.15.recv = bf16[4,192,1024]{2,1,0:T(8,128)(2,1)S(1)} collective-permute-done((bf16[4,192,1024]{2,1,0:T(8,128)(2,1)S(1)}, bf16[4,192,1024]{2,1,0:T(8,128)(2,1)S(1)}, u32[]{:S(2)}, u32[]{:S(2)}) %collective-permute-start.15) | collective-permute-done | bytes 1572896 | tf_op jit(solution)/shard_map/ppermute | solution.py:28
  66.5 5.1 %collective-permute-done.16.r1 = bf16[192,512]{1,0:T(8,128)(2,1)S(1)} collective-permute-done((bf16[192,512]{1,0:T(8,128)(2,1)S(1)}, bf16[192,512]{1,0:T(8,128)(2,1)S(1)}, u32[]{:S(2)}, u32[]{:S(2)}) %collective-permute-start.16) | collective-permute-done | bytes 196640 | tf_op jit(solution)/shard_map/ppermute | solution.py:28
  72.4 5.3 %collective-permute-done.18.r3 = bf16[192,512]{1,0:T(8,128)(2,1)S(1)} collective-permute-done((bf16[192,512]{1,0:T(8,128)(2,1)S(1)}, bf16[192,512]{1,0:T(8,128)(2,1)S(1)}, u32[]{:S(2)}, u32[]{:S(2)}) %collective-permute-start.18) | collective-permute-done | bytes 196640 | tf_op jit(solution)/shard_map/ppermute | solution.py:28
  78.1 2.8 %collective-permute-start.27 = (bf16[192,512]{1,0:T(8,128)(2,1)S(1)}, bf16[192,512]{1,0:T(8,128)(2,1)S(1)}, u32[]{:S(2)}, u32[]{:S(2)}) collective-permute-start(bf16[192,512]{1,0:T(8,128)(2,1)S(1)} %get-tuple-element.64), channel_id=1, source_target_pairs={{4,0},{6,2},{0,4},{2,6},{5,1},{7,3},{1,5},{3,7},{12,8},{14,10},{8,... | collective-permute-start | bytes 589832 | tf_op jit(solution)/shard_map/ppermute | solution.py:23
  82.2 2.5 %collective-permute-done.21.r3 = bf16[192,512]{1,0:T(8,128)(2,1)S(1)} collective-permute-done((bf16[192,512]{1,0:T(8,128)(2,1)S(1)}, bf16[192,512]{1,0:T(8,128)(2,1)S(1)}, u32[]{:S(2)}, u32[]{:S(2)}) %collective-permute-start.21) | collective-permute-done | bytes 196640 | tf_op jit(solution)/shard_map/ppermute | solution.py:28
  85.5 2.6 %collective-permute-start.23 = (bf16[192,512]{1,0:T(8,128)(2,1)S(1)}, bf16[192,512]{1,0:T(8,128)(2,1)S(1)}, u32[]{:S(2)}, u32[]{:S(2)}) collective-permute-start(bf16[192,512]{1,0:T(8,128)(2,1)S(1)} %get-tuple-element.62), channel_id=1, source_target_pairs={{4,0},{6,2},{0,4},{2,6},{5,1},{7,3},{1,5},{3,7},{12,8},{14,10},{8,... | collective-permute-start | bytes 589832 | tf_op jit(solution)/shard_map/ppermute | solution.py:23
  88.1 2.5 %collective-permute-start.22 = (bf16[192,512]{1,0:T(8,128)(2,1)S(1)}, bf16[192,512]{1,0:T(8,128)(2,1)S(1)}, u32[]{:S(2)}, u32[]{:S(2)}) collective-permute-start(bf16[192,512]{1,0:T(8,128)(2,1)S(1)} %get-tuple-element.62), channel_id=1, source_target_pairs={{2,0},{4,2},{6,4},{0,6},{3,1},{5,3},{7,5},{1,7},{10,8},{12,10},{14... | collective-permute-start | bytes 589832 | tf_op jit(solution)/shard_map/ppermute | solution.py:23
  90.7 2.5 %collective-permute-done.26 = bf16[192,512]{1,0:T(8,128)(2,1)S(1)} collective-permute-done((bf16[192,512]{1,0:T(8,128)(2,1)S(1)}, bf16[192,512]{1,0:T(8,128)(2,1)S(1)}, u32[]{:S(2)}, u32[]{:S(2)}) %collective-permute-start.26) | collective-permute-done | bytes 196640 | tf_op jit(solution)/shard_map/ppermute | solution.py:23
  93.7 3.7 %collective-permute-done.23 = bf16[192,512]{1,0:T(8,128)(2,1)S(1)} collective-permute-done((bf16[192,512]{1,0:T(8,128)(2,1)S(1)}, bf16[192,512]{1,0:T(8,128)(2,1)S(1)}, u32[]{:S(2)}, u32[]{:S(2)}) %collective-permute-start.23) | collective-permute-done | bytes 196640 | tf_op jit(solution)/shard_map/ppermute | solution.py:23
  99.7 10.2 %collective-permute-start.25 = (bf16[4,192,512]{2,1,0:T(8,128)(2,1)S(1)}, bf16[4,192,512]{2,1,0:T(8,128)(2,1)S(1)}, u32[]{:S(2)}, u32[]{:S(2)}) collective-permute-start(bf16[4,192,512]{2,1,0:T(8,128)(2,1)S(1)} %pad_maximum_fusion.refs_0_), channel_id=1, source_target_pairs={{0,1},{1,0},{2,3},{3,2},{4,5},{5,4},{6,7},{7,6},{8,9},{9,8},{10,11... | collective-permute-start | bytes 2359304 | tf_op jit(solution)/shard_map/ppermute | solution.py:28
  109.9 3.0 %shard_map.91 = (f32[4,8,48,1024]{3,2,1,0:T(8,128)S(1)}, bf16[4,2,192,512]{3,2,1,0:T(8,128)(2,1)S(1)}) custom-call(s32[4]{0:T(128)S(1)} %pad_add_fusion.pos, bf16[4,192,512]{2,1,0:T(8,128)(2,1)S(1)} %pad_maximum_fusion.1.refs_0_, bf16[4,192,512]{2,1,0:T(8,128)(2,1)S(1)} %collective-permute-done.29.refs_1_, bf16[1024,1024]{1,0:T(8,128)(2,1)S(1)} %get-tuple-element.63.refs_2_), custom_call_target="tpu_custom_call" | custom-call | flops 1610612736 | bytes 11534336 | tf_op jit(solution)/shard_map/pallas_call | solution.py:33
  112.9 4.4 %shard_map.92 = (f32[4,2,48,512]{3,2,1,0:T(8,128)S(1)}, f32[4,2,48,512]{3,2,1,0:T(8,128)S(1)}, bf16[4,2,48,512]{3,2,1,0:T(8,128)(2,1)S(1)}, f32[4,2,48,512]{3,2,...) custom-call(s32[4]{0:T(128)S(1)} %pad_add_fusion.pos, ...), custom_call_target="tpu_custom_call" | custom-call | flops 1610612736 | bytes 20185088 | tf_op jit(solution)/shard_map/pallas_call | solution.py:33
  117.6 3.3 %collective-permute-start.36 = (bf16[2,2,48,512]{3,2,1,0:T(8,128)(2,1)S(1)}, bf16[2,2,48,512]{3,2,1,0:T(8,128)(2,1)S(1)}, u32[]{:S(2)}, u32[]{:S(2)}) collective-permute-start(bf16[2,2,48,512]{3,2,1,0:T(8,128)(2,1)S(1)} %get-tuple-element.86), channel_id=1, source_target_pairs={{0,192},{64,0},{128,64},{192,128},{1,193},{65,1},{129,65},{193,129... | collective-permute-start | bytes 589832 | tf_op jit(solution)/shard_map/ppermute | solution.py:28
  121.5 2.7 %collective-permute-start.32 = (bf16[2,2,48,512]{3,2,1,0:T(8,128)(2,1)S(1)}, bf16[2,2,48,512]{3,2,1,0:T(8,128)(2,1)S(1)}, u32[]{:S(2)}, u32[]{:S(2)}) collective-permute-start(bf16[2,2,48,512]{3,2,1,0:T(8,128)(2,1)S(1)} %get-tuple-element.88), channel_id=1, source_target_pairs={{0,56},{8,0},{16,8},{24,16},{32,24},{40,32},{48,40},{56,48},{1,57}... | collective-permute-start | bytes 589832 | tf_op jit(solution)/shard_map/ppermute | solution.py:28
  125.7 2.6 %collective-permute-start.37 = (bf16[4,2,48,512]{3,2,1,0:T(8,128)(2,1)S(1)}, bf16[4,2,48,512]{3,2,1,0:T(8,128)(2,1)S(1)}, u32[]{:S(2)}, u32[]{:S(2)}) collective-permute-start(bf16[4,2,48,512]{3,2,1,0:T(8,128)(2,1)S(1)} %pad_maximum_fusion.8), channel_id=1, source_target_pairs={{0,192},{64,0},{128,64},{192,128},{1,193},{65,1},{129,65},{193,129... | collective-permute-start | bytes 1179656 | tf_op jit(solution)/shard_map/ppermute | solution.py:28
  128.3 2.5 %collective-permute-done.34 = bf16[2,2,48,512]{3,2,1,0:T(8,128)(2,1)S(1)} collective-permute-done((bf16[2,2,48,512]{3,2,1,0:T(8,128)(2,1)S(1)}, bf16[2,2,48,512]{3,2,1,0:T(8,128)(2,1)S(1)}, u32[]{:S(2)}, u32[]{:S(2)}) %collective-permute-start.34) | collective-permute-done | bytes 196640 | tf_op jit(solution)/shard_map/ppermute | solution.py:28
  136.5 5.2 %collective-permute-done.35 = bf16[4,2,48,512]{3,2,1,0:T(8,128)(2,1)S(1)} collective-permute-done((bf16[4,2,48,512]{3,2,1,0:T(8,128)(2,1)S(1)}, bf16[4,2,48,512]{3,2,1,0:T(8,128)(2,1)S(1)}, u32[]{:S(2)}, u32[]{:S(2)}) %collective-permute-start.35) | collective-permute-done | bytes 393248 | tf_op jit(solution)/shard_map/ppermute | solution.py:28
  146.5 3.7 %collective-permute-start.39 = (bf16[2,48,512]{2,1,0:T(8,128)(2,1)S(1)}, bf16[2,48,512]{2,1,0:T(8,128)(2,1)S(1)}, u32[]{:S(2)}, u32[]{:S(2)}) collective-permute-start(bf16[2,48,512]{2,1,0:T(8,128)(2,1)S(1)} %get-tuple-element.84), channel_id=1, source_target_pairs={{0,128},{64,192},{128,0},{192,64},{1,129},{65,193},{129,1},{193,65... | collective-permute-start | bytes 294920 | tf_op jit(solution)/shard_map/ppermute | solution.py:28
  150.4 3.2 %collective-permute-start.43 = (bf16[2,48,512]{2,1,0:T(8,128)(2,1)S(1)}, bf16[2,48,512]{2,1,0:T(8,128)(2,1)S(1)}, u32[]{:S(2)}, u32[]{:S(2)}) collective-permute-start(bf16[2,48,512]{2,1,0:T(8,128)(2,1)S(1)} %get-tuple-element.80), channel_id=1, source_target_pairs={{0,56},{8,0},{16,8},{24,16},{32,24},{40,32},{48,40},{56,48},{1,57}... | collective-permute-start | bytes 294920 | tf_op jit(solution)/shard_map/ppermute | solution.py:28
  153.9 2.8 %collective-permute-done.41 = bf16[2,48,512]{2,1,0:T(8,128)(2,1)S(1)} collective-permute-done((bf16[2,48,512]{2,1,0:T(8,128)(2,1)S(1)}, bf16[2,48,512]{2,1,0:T(8,128)(2,1)S(1)}, u32[]{:S(2)}, u32[]{:S(2)}) %collective-permute-start.41) | collective-permute-done | bytes 98336 | tf_op jit(solution)/shard_map/ppermute | solution.py:28
  156.8 4.6 %collective-permute-done.42 = bf16[2,48,512]{2,1,0:T(8,128)(2,1)S(1)} collective-permute-done((bf16[2,48,512]{2,1,0:T(8,128)(2,1)S(1)}, bf16[2,48,512]{2,1,0:T(8,128)(2,1)S(1)}, u32[]{:S(2)}, u32[]{:S(2)}) %collective-permute-start.42) | collective-permute-done | bytes 98336 | tf_op jit(solution)/shard_map/ppermute | solution.py:28
  161.4 3.5 %collective-permute-start.44 = (bf16[48,1024]{1,0:T(8,128)(2,1)S(1)}, bf16[48,1024]{1,0:T(8,128)(2,1)S(1)}, u32[]{:S(2)}, u32[]{:S(2)}) collective-permute-start(bf16[48,1024]{1,0:T(8,128)(2,1)S(1)} %fusion.10), channel_id=1, source_target_pairs={{0,32},{8,40},{16,48},{24,56},{32,0},{40,8},{48,16},{56,24},{1,33}... | collective-permute-start | bytes 294920 | tf_op jit(solution)/shard_map/ppermute | solution.py:28
  164.9 8.9 %shard_map.93 = bf16[1024,1024]{1,0:T(8,128)(2,1)} custom-call(s32[32]{0:T(128)S(1)} %get-tuple-element.94.rows, s32[32]{0:T(128)S(1)} %get-tuple-element.93.cols, s32[1]{0:T(128)} %bitcast.60.count, bf16[4,8,48,1024]{3,2,1,0:T(8,128)(2,1)S(1)} %get-tuple-element.77.toks, bf16[4,2,192,1024]{3,2,1,0:T(8,128)(2,1)S(1)} %get-tuple-element.78.grads), custom_call_target="tpu_custom_call" | custom-call | flops 3221225472 | bytes 8388608 | tf_op jit(solution)/shard_map/pallas_call | solution.py:33
  (112 shorter events, 47.6 us)
Async XLA Ops:
  0.7 10.4 %collective-permute-start = (bf16[48,1024]{1,0:T(8,128)(2,1)}, bf16[48,1024]{1,0:T(8,128)(2,1)S(1)}, u32[]{:S(2)}, u32[]{:S(2)}) collective-permute-start(bf16[48,1024]{1,0:T(8,128)(2,1)} %param.6), channel_id=1, source_target_pairs={{32,0},{40,8},{48,16},{56,24},{0,32},{8,40},{16,48},{24,56},{33,1}... | collective-permute-start | bytes 294920 | tf_op jit(solution)/shard_map/ppermute | solution.py:23
  11.9 11.2 %collective-permute-start.6 = (bf16[2,48,512]{2,1,0:T(8,128)(2,1)S(1)}, bf16[2,48,512]{2,1,0:T(8,128)(2,1)S(1)}, u32[]{:S(2)}, u32[]{:S(2)}) collective-permute-start(bf16[2,48,512]{2,1,0:T(8,128)(2,1)S(1)} %get-tuple-element.45), channel_id=1, source_target_pairs={{56,0},{0,8},{8,16},{16,24},{24,32},{32,40},{40,48},{48,56},{57,1}... | collective-permute-start | bytes 294920 | tf_op jit(solution)/shard_map/ppermute | solution.py:23
  14.4 11.1 %collective-permute-start.5 = (bf16[2,48,512]{2,1,0:T(8,128)(2,1)S(1)}, bf16[2,48,512]{2,1,0:T(8,128)(2,1)S(1)}, u32[]{:S(2)}, u32[]{:S(2)}) collective-permute-start(bf16[2,48,512]{2,1,0:T(8,128)(2,1)S(1)} %get-tuple-element.45), channel_id=1, source_target_pairs={{16,0},{24,8},{32,16},{40,24},{48,32},{56,40},{0,48},{8,56},{17,1}... | collective-permute-start | bytes 294920 | tf_op jit(solution)/shard_map/ppermute | solution.py:23
  30.1 9.3 %collective-permute-start.11 = (bf16[4,2,48,512]{3,2,1,0:T(8,128)(2,1)S(1)}, bf16[4,2,48,512]{3,2,1,0:T(8,128)(2,1)}, u32[]{:S(2)}, u32[]{:S(2)}) collective-permute-start(bf16[4,2,48,512]{3,2,1,0:T(8,128)(2,1)S(1)} %pad_maximum_fusion.3.refs_5_), channel_id=1, source_target_pairs={{64,0},{128,64},{192,128},{0,192},{65,1},{129,65},{193,129},{1,193... | collective-permute-start | bytes 1179656 | tf_op jit(solution)/shard_map/ppermute | solution.py:23
  31.0 9.7 %collective-permute-start.9 = (bf16[4,2,48,512]{3,2,1,0:T(8,128)(2,1)S(1)}, bf16[4,2,48,512]{3,2,1,0:T(8,128)(2,1)}, u32[]{:S(2)}, u32[]{:S(2)}) collective-permute-start(bf16[4,2,48,512]{3,2,1,0:T(8,128)(2,1)S(1)} %pad_maximum_fusion.2.refs_0_), channel_id=1, source_target_pairs={{56,0},{0,8},{8,16},{16,24},{24,32},{32,40},{40,48},{48,56},{57,1}... | collective-permute-start | bytes 1179656 | tf_op jit(solution)/shard_map/ppermute | solution.py:23
  31.2 12.0 %collective-permute-start.7 = (bf16[4,2,48,512]{3,2,1,0:T(8,128)(2,1)S(1)}, bf16[4,2,48,512]{3,2,1,0:T(8,128)(2,1)}, u32[]{:S(2)}, u32[]{:S(2)}) collective-permute-start(bf16[4,2,48,512]{3,2,1,0:T(8,128)(2,1)S(1)} %pad_maximum_fusion.2.refs_0_), channel_id=1, source_target_pairs={{8,0},{16,8},{24,16},{32,24},{40,32},{48,40},{56,48},{0,56},{9,1},... | collective-permute-start | bytes 1179656 | tf_op jit(solution)/shard_map/ppermute | solution.py:23
  37.0 12.9 %collective-permute-start.14 = (bf16[2,2,48,512]{3,2,1,0:T(8,128)(2,1)S(1)}, bf16[2,2,48,512]{3,2,1,0:T(8,128)(2,1)S(1)}, u32[]{:S(2)}, u32[]{:S(2)}) collective-permute-start(bf16[2,2,48,512]{3,2,1,0:T(8,128)(2,1)S(1)} %slice.114), channel_id=1, source_target_pairs={{192,0},{0,64},{64,128},{128,192},{193,1},{1,65},{65,129},{129,193... | collective-permute-start | bytes 589832 | tf_op jit(solution)/shard_map/ppermute | solution.py:23
  40.3 9.6 %collective-permute-start.12 = (bf16[2,2,48,512]{3,2,1,0:T(8,128)(2,1)S(1)}, bf16[2,2,48,512]{3,2,1,0:T(8,128)(2,1)S(1)}, u32[]{:S(2)}, u32[]{:S(2)}) collective-permute-start(bf16[2,2,48,512]{3,2,1,0:T(8,128)(2,1)S(1)} %slice.113), channel_id=1, source_target_pairs={{64,0},{128,64},{192,128},{0,192},{65,1},{129,65},{193,129},{1,193... | collective-permute-start | bytes 589832 | tf_op jit(solution)/shard_map/ppermute | solution.py:23
  41.7 8.2 %collective-permute-start.10 = (bf16[2,2,48,512]{3,2,1,0:T(8,128)(2,1)S(1)}, bf16[2,2,48,512]{3,2,1,0:T(8,128)(2,1)S(1)}, u32[]{:S(2)}, u32[]{:S(2)}) collective-permute-start(bf16[2,2,48,512]{3,2,1,0:T(8,128)(2,1)S(1)} %slice.112), channel_id=1, source_target_pairs={{56,0},{0,8},{8,16},{16,24},{24,32},{32,40},{40,48},{48,56},{57,1}... | collective-permute-start | bytes 589832 | tf_op jit(solution)/shard_map/ppermute | solution.py:23
  59.5 21.4 %collective-permute-start.19 = (bf16[192,512]{1,0:T(8,128)(2,1)S(1)}, bf16[192,512]{1,0:T(8,128)(2,1)S(1)}, u32[]{:S(2)}, u32[]{:S(2)}) collective-permute-start(bf16[192,512]{1,0:T(8,128)(2,1)S(1)} %get-tuple-element.58), channel_id=1, source_target_pairs={{0,2},{2,4},{4,6},{6,0},{1,3},{3,5},{5,7},{7,1},{8,10},{10,12},{12... | collective-permute-start | bytes 589832 | tf_op jit(solution)/shard_map/ppermute | solution.py:28
  61.3 10.2 %collective-permute-start.16 = (bf16[192,512]{1,0:T(8,128)(2,1)S(1)}, bf16[192,512]{1,0:T(8,128)(2,1)S(1)}, u32[]{:S(2)}, u32[]{:S(2)}) collective-permute-start(bf16[192,512]{1,0:T(8,128)(2,1)S(1)} %get-tuple-element.53), channel_id=1, source_target_pairs={{0,2},{2,4},{4,6},{6,0},{1,3},{3,5},{5,7},{7,1},{8,10},{10,12},{12... | collective-permute-start | bytes 589832 | tf_op jit(solution)/shard_map/ppermute | solution.py:28
  62.6 9.8 %collective-permute-start.17 = (bf16[192,512]{1,0:T(8,128)(2,1)S(1)}, bf16[192,512]{1,0:T(8,128)(2,1)S(1)}, u32[]{:S(2)}, u32[]{:S(2)}) collective-permute-start(bf16[192,512]{1,0:T(8,128)(2,1)S(1)} %get-tuple-element.54), channel_id=1, source_target_pairs={{0,4},{2,6},{4,0},{6,2},{1,5},{3,7},{5,1},{7,3},{8,12},{10,14},{12... | collective-permute-start | bytes 589832 | tf_op jit(solution)/shard_map/ppermute | solution.py:28
  64.0 13.7 %collective-permute-start.18 = (bf16[192,512]{1,0:T(8,128)(2,1)S(1)}, bf16[192,512]{1,0:T(8,128)(2,1)S(1)}, u32[]{:S(2)}, u32[]{:S(2)}) collective-permute-start(bf16[192,512]{1,0:T(8,128)(2,1)S(1)} %get-tuple-element.55), channel_id=1, source_target_pairs={{0,6},{2,0},{4,2},{6,4},{1,7},{3,1},{5,3},{7,5},{8,14},{10,8},{12,... | collective-permute-start | bytes 589832 | tf_op jit(solution)/shard_map/ppermute | solution.py:28
  65.1 17.1 %collective-permute-start.20 = (bf16[192,512]{1,0:T(8,128)(2,1)S(1)}, bf16[192,512]{1,0:T(8,128)(2,1)S(1)}, u32[]{:S(2)}, u32[]{:S(2)}) collective-permute-start(bf16[192,512]{1,0:T(8,128)(2,1)S(1)} %get-tuple-element.59), channel_id=1, source_target_pairs={{0,4},{2,6},{4,0},{6,2},{1,5},{3,7},{5,1},{7,3},{8,12},{10,14},{12... | collective-permute-start | bytes 589832 | tf_op jit(solution)/shard_map/ppermute | solution.py:28
  71.6 13.1 %collective-permute-start.21 = (bf16[192,512]{1,0:T(8,128)(2,1)S(1)}, bf16[192,512]{1,0:T(8,128)(2,1)S(1)}, u32[]{:S(2)}, u32[]{:S(2)}) collective-permute-start(bf16[192,512]{1,0:T(8,128)(2,1)S(1)} %get-tuple-element.60), channel_id=1, source_target_pairs={{0,6},{2,0},{4,2},{6,4},{1,7},{3,1},{5,3},{7,5},{8,14},{10,8},{12,... | collective-permute-start | bytes 589832 | tf_op jit(solution)/shard_map/ppermute | solution.py:28
  78.0 10.1 %collective-permute-start.28 = (bf16[192,512]{1,0:T(8,128)(2,1)S(1)}, bf16[192,512]{1,0:T(8,128)(2,1)S(1)}, u32[]{:S(2)}, u32[]{:S(2)}) collective-permute-start(bf16[192,512]{1,0:T(8,128)(2,1)S(1)} %get-tuple-element.64), channel_id=1, source_target_pairs={{6,0},{0,2},{2,4},{4,6},{7,1},{1,3},{3,5},{5,7},{14,8},{8,10},{10,... | collective-permute-start | bytes 589832 | tf_op jit(solution)/shard_map/ppermute | solution.py:23
  78.1 12.6 %collective-permute-start.27 = (bf16[192,512]{1,0:T(8,128)(2,1)S(1)}, bf16[192,512]{1,0:T(8,128)(2,1)S(1)}, u32[]{:S(2)}, u32[]{:S(2)}) collective-permute-start(bf16[192,512]{1,0:T(8,128)(2,1)S(1)} %get-tuple-element.64), channel_id=1, source_target_pairs={{4,0},{6,2},{0,4},{2,6},{5,1},{7,3},{1,5},{3,7},{12,8},{14,10},{8,... | collective-permute-start | bytes 589832 | tf_op jit(solution)/shard_map/ppermute | solution.py:23
  80.9 12.2 %collective-permute-start.26 = (bf16[192,512]{1,0:T(8,128)(2,1)S(1)}, bf16[192,512]{1,0:T(8,128)(2,1)S(1)}, u32[]{:S(2)}, u32[]{:S(2)}) collective-permute-start(bf16[192,512]{1,0:T(8,128)(2,1)S(1)} %get-tuple-element.64), channel_id=1, source_target_pairs={{2,0},{4,2},{6,4},{0,6},{3,1},{5,3},{7,5},{1,7},{10,8},{12,10},{14... | collective-permute-start | bytes 589832 | tf_op jit(solution)/shard_map/ppermute | solution.py:23
  85.0 8.7 %collective-permute-start.24 = (bf16[192,512]{1,0:T(8,128)(2,1)S(1)}, bf16[192,512]{1,0:T(8,128)(2,1)S(1)}, u32[]{:S(2)}, u32[]{:S(2)}) collective-permute-start(bf16[192,512]{1,0:T(8,128)(2,1)S(1)} %get-tuple-element.62), channel_id=1, source_target_pairs={{6,0},{0,2},{2,4},{4,6},{7,1},{1,3},{3,5},{5,7},{14,8},{8,10},{10,... | collective-permute-start | bytes 589832 | tf_op jit(solution)/shard_map/ppermute | solution.py:23
  85.5 11.8 %collective-permute-start.23 = (bf16[192,512]{1,0:T(8,128)(2,1)S(1)}, bf16[192,512]{1,0:T(8,128)(2,1)S(1)}, u32[]{:S(2)}, u32[]{:S(2)}) collective-permute-start(bf16[192,512]{1,0:T(8,128)(2,1)S(1)} %get-tuple-element.62), channel_id=1, source_target_pairs={{4,0},{6,2},{0,4},{2,6},{5,1},{7,3},{1,5},{3,7},{12,8},{14,10},{8,... | collective-permute-start | bytes 589832 | tf_op jit(solution)/shard_map/ppermute | solution.py:23
  88.1 11.5 %collective-permute-start.22 = (bf16[192,512]{1,0:T(8,128)(2,1)S(1)}, bf16[192,512]{1,0:T(8,128)(2,1)S(1)}, u32[]{:S(2)}, u32[]{:S(2)}) collective-permute-start(bf16[192,512]{1,0:T(8,128)(2,1)S(1)} %get-tuple-element.62), channel_id=1, source_target_pairs={{2,0},{4,2},{6,4},{0,6},{3,1},{5,3},{7,5},{1,7},{10,8},{12,10},{14... | collective-permute-start | bytes 589832 | tf_op jit(solution)/shard_map/ppermute | solution.py:23
  93.2 16.7 %collective-permute-start.29 = (bf16[4,192,512]{2,1,0:T(8,128)(2,1)S(1)}, bf16[4,192,512]{2,1,0:T(8,128)(2,1)S(1)}, u32[]{:S(2)}, u32[]{:S(2)}) collective-permute-start(bf16[4,192,512]{2,1,0:T(8,128)(2,1)S(1)} %pad_maximum_fusion.1.refs_0_), channel_id=1, source_target_pairs={{0,1},{1,0},{2,3},{3,2},{4,5},{5,4},{6,7},{7,6},{8,9},{9,8},{10,11... | collective-permute-start | bytes 2359304 | tf_op jit(solution)/shard_map/ppermute | solution.py:28
  99.7 13.2 %collective-permute-start.25 = (bf16[4,192,512]{2,1,0:T(8,128)(2,1)S(1)}, bf16[4,192,512]{2,1,0:T(8,128)(2,1)S(1)}, u32[]{:S(2)}, u32[]{:S(2)}) collective-permute-start(bf16[4,192,512]{2,1,0:T(8,128)(2,1)S(1)} %pad_maximum_fusion.refs_0_), channel_id=1, source_target_pairs={{0,1},{1,0},{2,3},{3,2},{4,5},{5,4},{6,7},{7,6},{8,9},{9,8},{10,11... | collective-permute-start | bytes 2359304 | tf_op jit(solution)/shard_map/ppermute | solution.py:28
  120.9 12.2 %collective-permute-start.30 = (bf16[2,2,48,512]{3,2,1,0:T(8,128)(2,1)S(1)}, bf16[2,2,48,512]{3,2,1,0:T(8,128)(2,1)S(1)}, u32[]{:S(2)}, u32[]{:S(2)}) collective-permute-start(bf16[2,2,48,512]{3,2,1,0:T(8,128)(2,1)S(1)} %get-tuple-element.87), channel_id=1, source_target_pairs={{0,8},{8,16},{16,24},{24,32},{32,40},{40,48},{48,56},{56,0},{1,9},... | collective-permute-start | bytes 589832 | tf_op jit(solution)/shard_map/ppermute | solution.py:28
  121.5 9.8 %collective-permute-start.32 = (bf16[2,2,48,512]{3,2,1,0:T(8,128)(2,1)S(1)}, bf16[2,2,48,512]{3,2,1,0:T(8,128)(2,1)S(1)}, u32[]{:S(2)}, u32[]{:S(2)}) collective-permute-start(bf16[2,2,48,512]{3,2,1,0:T(8,128)(2,1)S(1)} %get-tuple-element.88), channel_id=1, source_target_pairs={{0,56},{8,0},{16,8},{24,16},{32,24},{40,32},{48,40},{56,48},{1,57}... | collective-permute-start | bytes 589832 | tf_op jit(solution)/shard_map/ppermute | solution.py:28
  125.7 10.8 %collective-permute-start.37 = (bf16[4,2,48,512]{3,2,1,0:T(8,128)(2,1)S(1)}, bf16[4,2,48,512]{3,2,1,0:T(8,128)(2,1)S(1)}, u32[]{:S(2)}, u32[]{:S(2)}) collective-permute-start(bf16[4,2,48,512]{3,2,1,0:T(8,128)(2,1)S(1)} %pad_maximum_fusion.8), channel_id=1, source_target_pairs={{0,192},{64,0},{128,64},{192,128},{1,193},{65,1},{129,65},{193,129... | collective-permute-start | bytes 1179656 | tf_op jit(solution)/shard_map/ppermute | solution.py:28
  130.9 10.8 %collective-permute-start.35 = (bf16[4,2,48,512]{3,2,1,0:T(8,128)(2,1)S(1)}, bf16[4,2,48,512]{3,2,1,0:T(8,128)(2,1)S(1)}, u32[]{:S(2)}, u32[]{:S(2)}) collective-permute-start(bf16[4,2,48,512]{3,2,1,0:T(8,128)(2,1)S(1)} %pad_maximum_fusion.7), channel_id=1, source_target_pairs={{0,64},{64,128},{128,192},{192,0},{1,65},{65,129},{129,193},{193,1... | collective-permute-start | bytes 1179656 | tf_op jit(solution)/shard_map/ppermute | solution.py:28
  131.3 10.6 %collective-permute-start.33 = (bf16[4,2,48,512]{3,2,1,0:T(8,128)(2,1)S(1)}, bf16[4,2,48,512]{3,2,1,0:T(8,128)(2,1)S(1)}, u32[]{:S(2)}, u32[]{:S(2)}) collective-permute-start(bf16[4,2,48,512]{3,2,1,0:T(8,128)(2,1)S(1)} %pad_maximum_fusion.6), channel_id=1, source_target_pairs={{0,56},{8,0},{16,8},{24,16},{32,24},{40,32},{48,40},{56,48},{1,57}... | collective-permute-start | bytes 1179656 | tf_op jit(solution)/shard_map/ppermute | solution.py:28
  133.1 10.8 %collective-permute-start.31 = (bf16[4,2,48,512]{3,2,1,0:T(8,128)(2,1)S(1)}, bf16[4,2,48,512]{3,2,1,0:T(8,128)(2,1)S(1)}, u32[]{:S(2)}, u32[]{:S(2)}) collective-permute-start(bf16[4,2,48,512]{3,2,1,0:T(8,128)(2,1)S(1)} %pad_maximum_fusion.5), channel_id=1, source_target_pairs={{0,8},{8,16},{16,24},{24,32},{32,40},{40,48},{48,56},{56,0},{1,9},... | collective-permute-start | bytes 1179656 | tf_op jit(solution)/shard_map/ppermute | solution.py:28
  144.2 9.4 %collective-permute-start.38 = (bf16[2,48,512]{2,1,0:T(8,128)(2,1)S(1)}, bf16[2,48,512]{2,1,0:T(8,128)(2,1)S(1)}, u32[]{:S(2)}, u32[]{:S(2)}) collective-permute-start(bf16[2,48,512]{2,1,0:T(8,128)(2,1)S(1)} %get-tuple-element.82), channel_id=1, source_target_pairs={{0,64},{64,128},{128,192},{192,0},{1,65},{65,129},{129,193},{193,1... | collective-permute-start | bytes 294920 | tf_op jit(solution)/shard_map/ppermute | solution.py:28
  145.4 8.2 %collective-permute-start.40 = (bf16[2,48,512]{2,1,0:T(8,128)(2,1)S(1)}, bf16[2,48,512]{2,1,0:T(8,128)(2,1)S(1)}, u32[]{:S(2)}, u32[]{:S(2)}) collective-permute-start(bf16[2,48,512]{2,1,0:T(8,128)(2,1)S(1)} %get-tuple-element.83), channel_id=1, source_target_pairs={{0,192},{64,0},{128,64},{192,128},{1,193},{65,1},{129,65},{193,129... | collective-permute-start | bytes 294920 | tf_op jit(solution)/shard_map/ppermute | solution.py:28
  161.4 12.3 %collective-permute-start.44 = (bf16[48,1024]{1,0:T(8,128)(2,1)S(1)}, bf16[48,1024]{1,0:T(8,128)(2,1)S(1)}, u32[]{:S(2)}, u32[]{:S(2)}) collective-permute-start(bf16[48,1024]{1,0:T(8,128)(2,1)S(1)} %fusion.10), channel_id=1, source_target_pairs={{0,32},{8,40},{16,48},{24,56},{32,0},{40,8},{48,16},{56,24},{1,33}... | collective-permute-start | bytes 294920 | tf_op jit(solution)/shard_map/ppermute | solution.py:28
  (17 other events, 226.6 us)

commit v5 on v2

v5 whole, which is shorter than its diff:
```python
import functools

import jax
import jax.numpy as jnp
from jax import lax
from jax.experimental import pallas as pl
from jax.experimental.pallas import tpu as pltpu
from jax.sharding import Mesh
from jax.sharding import PartitionSpec as P

TILE = 128
SIZES = {"y": 4, "z": 8, "x": 4, "core": 2}
ROW = ("y", "z")
COL = ("x", "core")
VM = pltpu.VMEM
F32 = jnp.float32
BF16 = jnp.bfloat16
STEPS = (0, 1, 2, -1)


def from_ahead(value, axis, k):
    n = SIZES[axis]
    return lax.ppermute(value, axis, [((i + k) % n, i) for i in range(n)])


def to_ahead(value, axis, k):
    n = SIZES[axis]
    return lax.ppermute(value, axis, [(i, (i + k) % n) for i in range(n)])


def call(body, outs, smem, vmem, flops=0, scratch=(), limit=24):
    outs = [jax.ShapeDtypeStruct(s, d) for s, d in outs]
    return pl.pallas_call(
        body,
        out_shape=outs,
        in_specs=[pl.BlockSpec(memory_space=pltpu.SMEM)] * len(smem)
        + [pl.BlockSpec(memory_space=VM)] * len(vmem),
        out_specs=[pl.BlockSpec(memory_space=VM)] * len(outs),
        scratch_shapes=list(scratch),
        compiler_params=pltpu.CompilerParams(vmem_limit_bytes=limit * 2**20),
        cost_estimate=pl.CostEstimate(
            flops=flops,
            transcendentals=0,
            bytes_accessed=sum(v.size * v.dtype.itemsize for v in vmem)
            + sum(o.size * o.dtype.itemsize for o in outs),
        ),
    )(*smem, *vmem)


def tile_ref(ref, r, c):
    return ref.at[
        pl.ds(pl.multiple_of(r * TILE, TILE), TILE), pl.ds(pl.multiple_of(c * TILE, TILE), TILE)
    ]


def mask_body(rows, cols, count, w, out, flipped):
    out[...] = jnp.zeros_like(out)
    flipped[...] = jnp.zeros_like(flipped)

    @pl.loop(0, count[0])
    def _(k):
        tile = tile_ref(w, rows[k], cols[k])[...]
        tile_ref(out, rows[k], cols[k])[...] = tile
        tile_ref(flipped, cols[k], rows[k])[...] = tile.T


def z_half(pos, step):
    return ((pos[1] + step + 8) % 8) // 4


def turned(pos):
    return pos[0] - pos[2] + 4


def up_body(steps, pos, *refs):
    pieces, w = refs[:5], refs[5]
    keep, send, toks = refs[6:]
    core = pos[3]
    for j in range(4):
        d = (j + turned(pos)) % 4
        for i, step in enumerate(steps):
            ref, at = (pieces[2 + i], 0) if j == 2 else (pieces[j + j // 3], i)
            for hi in range(2):
                side = (z_half(pos, step) + hi + core) % 2
                toks[d, side, i] = ref[at, hi]

    @pl.loop(0, 2)
    def _(k):
        at = pl.ds(k * 2, 2)
        part = jnp.dot(
            toks[at].reshape(-1, toks.shape[-1]), w[...], preferred_element_type=F32
        )
        part = part.reshape(2, 2, keep.shape[1], keep.shape[2])
        keep[at] = part[:, 0]
        send[at] = part[:, 1].astype(BF16)


def add_body(keep, recv, *out):
    for d in range(4):

        @pl.loop(0, keep.shape[1] // 16)
        def _(i, d=d):
            at = pl.ds(pl.multiple_of(i * 16, 16), 16)
            total = keep[d, at] + recv[d, at].astype(F32)
            out[d][at] = total.astype(out[d].dtype)


def act_body(steps, pos, own, r1, r2, r3, cot, *refs):
    hidden, grad_pre = refs[-2:]
    whole = len(refs) == 3
    size = cot.shape[1]
    for i, step in enumerate(steps):
        block = (pos[1] + step + 8) % 4

        @pl.loop(0, size // 16)
        def _(k, i=i, block=block):
            here = pl.ds(pl.multiple_of(k * 16, 16), 16)
            at = pl.ds(pl.multiple_of(i * size + k * 16, 16), 16)
            pre_act = own[at] + r1[at].astype(F32) + r2[at].astype(F32) + r3[at].astype(F32)
            gate = jax.nn.sigmoid(pre_act)
            hidden[block if whole else i, here] = (pre_act * gate).astype(BF16)
            slope = gate * (1.0 + pre_act * (1.0 - gate))
            grad_pre[at] = (cot[block, here].astype(F32) * slope).astype(BF16)

    if whole:
        for i, step in enumerate(STEPS[:2]):
            hidden[(pos[1] + step + 8) % 4] = refs[0][i]


def back_body(steps, pos, mine, other, w, own, ahead, far, behind, grads, acc, sems):
    core = pos[3]
    copies = [
        pltpu.make_async_copy(g, grads.at[:, side], sems.at[side])
        for side, g in enumerate((mine, other))
    ]
    for c in copies:
        c.start()
    for c in copies:
        c.wait()

    @pl.loop(0, 2)
    def _(k):
        at = pl.ds(k * 2, 2)
        part = jnp.dot(
            grads[at].reshape(-1, grads.shape[-1]), w[...], preferred_element_type=F32
        )
        acc[at] = part.reshape(2, 2, 2, acc.shape[3], acc.shape[4])

    for j, out in enumerate((own, ahead, far, behind)):
        d = (j + turned(pos)) % 4
        for i, step in enumerate(steps):

            @pl.loop(0, 2)
            def _(side, i=i, step=step, d=d, out=out):
                part = acc[d, side, i]
                out[i, (z_half(pos, step) + side + core) % 2] = part.astype(out.dtype)


def wgrad_body(rows, cols, count, t1, g1, t2, g2, out, acc):
    acc[...] = jnp.zeros_like(acc)
    for toks, grads in ((t1, g1), (t2, g2)):

        @pl.loop(0, 2)
        def _(k, toks=toks, grads=grads):
            at = pl.ds(k * 2, 2)
            t = toks[at].reshape(-1, toks.shape[-1])
            g = grads[at].reshape(-1, grads.shape[-1])
            acc[...] += lax.dot_general(
                t, g, (((0,), (0,)), ((), ())), preferred_element_type=F32
            )

    out[...] = jnp.zeros_like(out)

    @pl.loop(0, count[0])
    def _(k):
        tile_ref(out, rows[k], cols[k])[...] = tile_ref(acc, rows[k], cols[k])[...].astype(BF16)


def both_sides(piece, axis):
    return [from_ahead(piece, axis, 1), from_ahead(piece, axis, -1)]


def far_halves(ahead, behind, axis):
    half = ahead.shape[0] // 2
    return [from_ahead(ahead[:half], axis, 1), from_ahead(behind[half:], axis, -1)]


def after(values, *others):
    return lax.optimization_barrier((values, others))[0]


def far_shares(far, axis):
    half = far.shape[0] // 2
    return [to_ahead(far[:half], axis, 1), to_ahead(far[half:], axis, -1)]


def ring_reduce(own, ahead, behind, shares, axis):
    half = own.shape[0] // 2
    lo, hi = (s.astype(F32) for s in shares)
    ahead = jnp.concatenate([ahead[:half] + lo, ahead[half:]])
    behind = jnp.concatenate([behind[:half], behind[half:] + hi])
    total = own + to_ahead(ahead.astype(BF16), axis, 1).astype(F32)
    return total + to_ahead(behind.astype(BF16), axis, -1).astype(F32)


def up(pieces, steps, wm, pos):
    rows = 2 * pieces[0].shape[2]
    depth, width = wm.shape
    keep, send, toks = call(
        functools.partial(up_body, steps),
        [
            ((4, rows, width), F32),
            ((4, rows, width), BF16),
            ((4, 2, 2, rows // 2, depth), BF16),
        ],
        [pos],
        pieces + [wm],
        16 * rows * depth * width,
    )
    shape = (rows, width)
    recv = to_ahead(send, "core", 1)
    own, *sends = call(add_body, [(shape, F32)] + [(shape, BF16)] * 3, [], [keep, recv])
    return own, sends, toks


def activation(own, sends, cot, steps, pos, before):
    recvs = [to_ahead(s, "x", d + 1) for d, s in enumerate(sends)]
    out = (4 if before else 2,) + cot.shape[1:]
    return call(
        functools.partial(act_body, steps),
        [(out, BF16), (own.shape, BF16)],
        [pos],
        [own] + recvs + [cot] + before,
    )


def gather_grads(grad_pre):
    mine = jnp.stack([grad_pre] + [from_ahead(grad_pre, "x", d) for d in range(1, 4)])
    return mine, to_ahead(mine, "core", 1)


def back(mine, other, steps, flipped, pos):
    rows, width = mine.shape[1:]
    depth = flipped.shape[1]
    shape = (2, 2, rows // 2, depth)
    *sends, grads = call(
        functools.partial(back_body, steps),
        [(shape, d) for d in (F32, F32, BF16, F32)] + [((4, 2, rows, width), BF16)],
        [pos],
        [mine, other, flipped],
        16 * rows * depth * width,
        [VM((4,) + shape, F32), pltpu.SemaphoreType.DMA((2,))],
    )
    return sends, grads


def on_device(tokens, weight, tile_rows, tile_cols, tile_count, hidden_cotangent):
    y, z, x, core = (lax.axis_index(a) for a in ("y", "z", "x", "core"))
    pos = jnp.stack([y, z, x, core]).astype(jnp.int32)
    row_blocks = weight.shape[0] // TILE
    col_blocks = weight.shape[1] // TILE
    rows = tile_rows.reshape(-1) - (x * 2 + core) * row_blocks
    cols = tile_cols.reshape(-1) - (y * 8 + z) * col_blocks
    count = tile_count.reshape(1)
    shapes = [(weight.shape, BF16), (weight.shape[::-1], BF16)]
    wm, flipped = call(mask_body, shapes, [rows, cols, count], [weight])
    pair = jnp.stack([tokens, from_ahead(tokens, "z", 4)])
    pairs = [pair] + [from_ahead(pair, "z", k) for k in STEPS[1:]]
    cot = hidden_cotangent.reshape(4, tokens.shape[0], -1)
    first, second = STEPS[:2], STEPS[2:]
    piece1, piece2 = jnp.stack(pairs[:2]), jnp.stack(pairs[2:])
    ahead1, behind1 = both_sides(piece1, "y")
    far1 = far_halves(*after((ahead1, behind1), piece2), "y")
    ahead2, behind2 = both_sides(after(piece2, ahead1, behind1), "y")
    own1, sends1, toks1 = up([piece1, ahead1] + far1 + [behind1], first, wm, pos)
    ahead2, behind2 = after((ahead2, behind2), toks1)
    far2 = far_halves(ahead2, behind2, "y")
    own2, sends2, toks2 = up([piece2, ahead2] + far2 + [behind2], second, wm, pos)
    hidden1, grad1 = activation(own1, sends1, cot, first, pos, [])
    sends2 = after(sends2, grad1)
    parts1, grads1 = back(*gather_grads(grad1), first, flipped, pos)
    shares1 = far_shares(parts1[2], "y")
    own2 = after(own2, shares1)
    hidden, grad2 = activation(own2, sends2, cot, second, pos, [hidden1])
    sums1 = ring_reduce(parts1[0], parts1[1], parts1[3], shares1, "y")
    mine2, other2 = after(gather_grads(grad2), sums1)
    parts2, grads2 = back(mine2, other2, second, flipped, pos)
    sums2 = ring_reduce(parts2[0], parts2[1], parts2[3], far_shares(parts2[2], "y"), "y")
    total = sums1[0]
    for k, piece in zip(STEPS[1:], (sums1[1], sums2[0], sums2[1])):
        total = total + to_ahead(piece.astype(BF16), "z", k).astype(F32)
    input_grad = total[0] + to_ahead(total[1].astype(BF16), "z", 4).astype(F32)
    (weight_grad,) = call(
        wgrad_body,
        [(weight.shape, BF16)],
        [rows, cols, count],
        [
            toks1.reshape(4, -1, weight.shape[0]),
            grads1.reshape(4, -1, weight.shape[1]),
            toks2.reshape(4, -1, weight.shape[0]),
            grads2.reshape(4, -1, weight.shape[1]),
        ],
        2 * 1536 * weight.size,
        [VM(weight.shape, F32)],
    )
    return hidden.reshape(hidden_cotangent.shape), input_grad.astype(BF16), weight_grad


def solution(mesh):
    split = Mesh(mesh.devices.reshape(4, 8, 4, 2), ("y", "z", "x", "core"))
    return jax.shard_map(
        on_device,
        mesh=split,
        in_specs=(
            P(ROW, COL),
            P(COL, ROW),
            P(ROW, COL, None),
            P(ROW, COL, None),
            P(ROW, COL),
            P(COL, ROW),
        ),
        out_specs=(P(COL, ROW), P(ROW, COL), P(COL, ROW)),
        check_vma=False,
    )
```

time: 177 us -> 177 us (level)
  starting transfers between devices: 64.6 us -> 55.2 us
  waiting for transfers between devices: 82.1 us -> 90.8 us
  Pallas kernels: 21.9 us -> 25.2 us
    ppermute x21 -> x22, starting transfers between devices: 29.4 us -> 21 us  [to_ahead(): return lax.ppermute(value, axis, [(i, (i + k) % n) for i in range(n)])]
    ppermute x21 -> x22, waiting for transfers between devices: 46.1 us -> 50.6 us  [to_ahead(): return lax.ppermute(value, axis, [(i, (i + k) % n) for i in range(n)])]
    ppermute x16 -> x18, waiting for transfers between devices: 35.9 us -> 40.2 us  [from_ahead(): return lax.ppermute(value, axis, [((i + k) % n, i) for i in range(n)])]
    pallas_call x4 -> x10, Pallas kernels: 21.9 us -> 25.2 us  [call(): pl.pallas_call(body, out_shape=outs, in_specs=[pl.BlockSpec(memory_space=...]
    ppermute x16 -> x18, starting transfers between devices: 35.2 us -> 34.3 us  [from_ahead(): return lax.ppermute(value, axis, [((i + k) % n, i) for i in range(n)])]
  transfers between devices with their start and end apart: 37 -> 40, of which waited for: 19 -> 28; matrix products, arithmetic and copies ran while one was open for 1% -> 1% of each run, Pallas kernels for 6% -> 8%
where the time goes in v5:
time: 177 us
  waiting for transfers between devices  90.8 us (51%)
  starting transfers between devices  55.2 us (31%)
  Pallas kernels  25.2 us (14%)
  other arithmetic  3.71 us (2%)
    ppermute x22, waiting for transfers between devices, to_ahead(): return lax.ppermute(value, axis, [(i, (i + k) % n) for i in range(n)])  50.6 us
    ppermute x18, waiting for transfers between devices, from_ahead(): return lax.ppermute(value, axis, [((i + k) % n, i) for i in range(n)])  40.2 us
    ppermute x18, starting transfers between devices, from_ahead(): return lax.ppermute(value, axis, [((i + k) % n, i) for i in range(n)])  34.3 us
    pallas_call x10, Pallas kernels, call(): pl.pallas_call(body, out_shape=outs, in_specs=[pl.BlockSpec(memory_space=...  25.2 us
    ppermute x22, starting transfers between devices, to_ahead(): return lax.ppermute(value, axis, [(i, (i + k) % n) for i in range(n)])  21 us
  transfers between devices with their start and end apart: 40, of which 28 were waited for; matrix products, arithmetic and copies ran while one was open for 1% of the time, Pallas kernels for 8%

profile of v5, /device:TPU:6, one launch (start us, length us, event | category | flops | bytes accessed | tf_op | source)
XLA Modules:
  0.0 176.9 jit_solution(3355438649588346933)
XLA Ops:
  0.7 7.3 %collective-permute-start = (bf16[48,1024]{1,0:T(8,128)(2,1)}, bf16[48,1024]{1,0:T(8,128)(2,1)S(1)}, u32[]{:S(2)}, u32[]{:S(2)}) collective-permute-start(bf16[48,1024]{1,0:T(8,128)(2,1)} %param.6), channel_id=1, source_target_pairs={{32,0},{40,8},{48,16},{56,24},{0,32},{8,40},{16,48},{24,56},{33,1}... | collective-permute-start | bytes 294920 | tf_op jit(solution)/shard_map/ppermute | solution.py:23
  7.9 3.1 %collective-permute-done = bf16[48,1024]{1,0:T(8,128)(2,1)S(1)} collective-permute-done((bf16[48,1024]{1,0:T(8,128)(2,1)}, bf16[48,1024]{1,0:T(8,128)(2,1)S(1)}, u32[]{:S(2)}, u32[]{:S(2)}) %collective-permute-start) | collective-permute-done | bytes 98336 | tf_op jit(solution)/shard_map/ppermute | solution.py:23
  12.0 5.3 %collective-permute-start.3 = (bf16[2,48,1024]{2,1,0:T(8,128)(2,1)S(1)}, bf16[2,48,1024]{2,1,0:T(8,128)(2,1)S(1)}, u32[]{:S(2)}, u32[]{:S(2)}) collective-permute-start(bf16[2,48,1024]{2,1,0:T(8,128)(2,1)S(1)} %get-tuple-element.92), channel_id=1, source_target_pairs={{8,0},{16,8},{24,16},{32,24},{40,32},{48,40},{56,48},{0,56},{9,1},... | collective-permute-start | bytes 589832 | tf_op jit(solution)/shard_map/ppermute | solution.py:23
  17.3 4.1 %collective-permute-done.3 = bf16[2,48,1024]{2,1,0:T(8,128)(2,1)S(1)} collective-permute-done((bf16[2,48,1024]{2,1,0:T(8,128)(2,1)S(1)}, bf16[2,48,1024]{2,1,0:T(8,128)(2,1)S(1)}, u32[]{:S(2)}, u32[]{:S(2)}) %collective-permute-start.3) | collective-permute-done | bytes 196640 | tf_op jit(solution)/shard_map/ppermute | solution.py:23
  21.4 3.1 %collective-permute-start.4 = (bf16[2,2,48,1024]{3,2,1,0:T(8,128)(2,1)S(1)}, bf16[2,2,48,1024]{3,2,1,0:T(8,128)(2,1)S(1)}, u32[]{:S(2)}, u32[]{:S(2)}) collective-permute-start(bf16[2,2,48,1024]{3,2,1,0:T(8,128)(2,1)S(1)} %pad_maximum_fusion.3.refs_0_), channel_id=1, source_target_pairs={{64,0},{128,64},{192,128},{0,192},{65,1},{129,65},{193,129},{1,193... | collective-permute-start | bytes 1179656 | tf_op jit(solution)/shard_map/ppermute | solution.py:23
  24.5 5.2 %collective-permute-start.1 = (bf16[2,48,1024]{2,1,0:T(8,128)(2,1)S(1)}, bf16[2,48,1024]{2,1,0:T(8,128)(2,1)}, u32[]{:S(2)}, u32[]{:S(2)}) collective-permute-start(bf16[2,48,1024]{2,1,0:T(8,128)(2,1)S(1)} %get-tuple-element.92), channel_id=1, source_target_pairs={{16,0},{24,8},{32,16},{40,24},{48,32},{56,40},{0,48},{8,56},{17,1}... | collective-permute-start | bytes 589832 | tf_op jit(solution)/shard_map/ppermute | solution.py:23
  32.0 4.3 %collective-permute-done.1 = bf16[2,48,1024]{2,1,0:T(8,128)(2,1)} collective-permute-done((bf16[2,48,1024]{2,1,0:T(8,128)(2,1)S(1)}, bf16[2,48,1024]{2,1,0:T(8,128)(2,1)}, u32[]{:S(2)}, u32[]{:S(2)}) %collective-permute-start.1) | collective-permute-done | bytes 196640 | tf_op jit(solution)/shard_map/ppermute | solution.py:23
  37.4 3.0 %collective-permute-start.8 = (bf16[1,2,48,1024]{3,2,1,0:T(8,128)(2,1)S(1)}, bf16[1,2,48,1024]{3,2,1,0:T(8,128)(2,1)S(1)}, u32[]{:S(2)}, u32[]{:S(2)}) collective-permute-start(bf16[1,2,48,1024]{3,2,1,0:T(8,128)(2,1)S(1)} %slice.74), channel_id=1, source_target_pairs={{64,0},{128,64},{192,128},{0,192},{65,1},{129,65},{193,129},{1,193... | collective-permute-start | bytes 589832 | tf_op jit(solution)/shard_map/ppermute | solution.py:23
  41.2 2.9 %shard_map.85 = (bf16[1024,1024]{1,0:T(8,128)(2,1)S(1)}, bf16[1024,1024]{1,0:T(8,128)(2,1)S(1)}) custom-call(s32[32]{0:T(128)S(1)} %get-tuple-element.94.rows, s32[32]{0:T(128)S(1)} %get-tuple-element.93.cols, s32[1]{0:T(128)} %bitcast.52.count, bf16[1024,1024]{1,0:T(8,128)(2,1)S(1)} %copy-done), custom_call_target="tpu_custom_call" | custom-call | bytes 6291456 | tf_op jit(solution)/shard_map/pallas_call | solution.py:33
  44.2 3.2 %collective-permute-done.9.refs_3_ = bf16[1,2,48,1024]{3,2,1,0:T(8,128)(2,1)S(1)} collective-permute-done((bf16[1,2,48,1024]{3,2,1,0:T(8,128)(2,1)S(1)}, bf16[1,2,48,1024]{3,2,1,0:T(8,128)(2,1)S(1)}, u32[]{:S(2)}, u32[]{:S(2)}) %collective-permute-start.9) | collective-permute-done | bytes 196640 | tf_op jit(solution)/shard_map/ppermute | solution.py:23
  47.4 2.6 %shard_map.86 = (f32[4,96,1024]{2,1,0:T(8,128)S(1)}, bf16[4,96,1024]{2,1,0:T(8,128)(2,1)S(1)}, bf16[4,2,2,48,1024]{4,3,2,1,0:T(8,128)(2,1)S(1)}) custom-call(s32[4]{0:T(128)S(1)} %pad_add_fusion.pos, bf16[2,2,48,1024]{3,2,1,0:T(8,128)(2,1)S(1)} %pad_maximum_fusion.3.refs_0_, bf16[2,2,48,1024]{3,2,1,0:T(8,128)(2,1)S(1)} %collective-permute-done.4.refs_1_, ...), custom_call_target="tpu_custom_call" | custom-call | flops 1610612736 | bytes 7602176 | tf_op jit(solution)/shard_map/pallas_call | solution.py:33
  53.2 2.4 %collective-permute-start.15 = (bf16[96,1024]{1,0:T(8,128)(2,1)S(1)}, bf16[96,1024]{1,0:T(8,128)(2,1)S(1)}, u32[]{:S(2)}, u32[]{:S(2)}) collective-permute-start(bf16[96,1024]{1,0:T(8,128)(2,1)S(1)} %get-tuple-element.58), channel_id=1, source_target_pairs={{0,4},{2,6},{4,0},{6,2},{1,5},{3,7},{5,1},{7,3},{8,12},{10,14},{12... | collective-permute-start | bytes 589832 | tf_op jit(solution)/shard_map/ppermute | solution.py:28
  55.7 6.0 %collective-permute-done.6.refs_1_ = bf16[2,2,48,1024]{3,2,1,0:T(8,128)(2,1)S(1)} collective-permute-done((bf16[2,2,48,1024]{3,2,1,0:T(8,128)(2,1)S(1)}, bf16[2,2,48,1024]{3,2,1,0:T(8,128)(2,1)S(1)}, u32[]{:S(2)}, u32[]{:S(2)}) %collective-permute-start.6) | collective-permute-done | bytes 393248 | tf_op jit(solution)/shard_map/ppermute | solution.py:23
  71.1 2.6 %shard_map.87 = (f32[4,96,1024]{2,1,0:T(8,128)S(1)}, bf16[4,96,1024]{2,1,0:T(8,128)(2,1)S(1)}, bf16[4,2,2,48,1024]{4,3,2,1,0:T(8,128)(2,1)S(1)}) custom-call(s32[4]{0:T(128)S(1)} %pad_add_fusion.pos, bf16[2,2,48,1024]{3,2,1,0:T(8,128)(2,1)S(1)} %pad_maximum_fusion.2.refs_0_, bf16[2,2,48,1024]{3,2,1,0:T(8,128)(2,1)S(1)} %collective-permute-done.6.refs_1_, ...), custom_call_target="tpu_custom_call" | custom-call | flops 1610612736 | bytes 7602176 | tf_op jit(solution)/shard_map/pallas_call | solution.py:33
  74.3 2.6 %collective-permute-done.18 = bf16[96,1024]{1,0:T(8,128)(2,1)S(1)} collective-permute-done((bf16[96,1024]{1,0:T(8,128)(2,1)S(1)}, bf16[96,1024]{1,0:T(8,128)(2,1)S(1)}, u32[]{:S(2)}, u32[]{:S(2)}) %collective-permute-start.18) | collective-permute-done | bytes 196640 | tf_op jit(solution)/shard_map/ppermute | solution.py:23
  81.6 3.1 %shard_map.91 = (f32[2,2,48,1024]{3,2,1,0:T(8,128)S(1)}, f32[2,2,48,1024]{3,2,1,0:T(8,128)S(1)}, bf16[2,2,48,1024]{3,2,1,0:T(8,128)(2,1)S(1)}, f32[2,2,48,1024]{...) custom-call(s32[4]{0:T(128)S(1)} %pad_add_fusion.pos, bf16[4,96,1024]{2,1,0:T(8,128)(2,1)S(1)} %pad_maximum_fusion.mine, ...), custom_call_target="tpu_custom_call" | custom-call | flops 1610612736 | bytes 7995392 | tf_op jit(solution)/shard_map/pallas_call | solution.py:33
  84.9 3.2 %collective-permute-start.22 = (bf16[1,2,48,1024]{3,2,1,0:T(8,128)(2,1)S(1)}, bf16[1,2,48,1024]{3,2,1,0:T(8,128)(2,1)S(1)}, u32[]{:S(2)}, u32[]{:S(2)}) collective-permute-start(bf16[1,2,48,1024]{3,2,1,0:T(8,128)(2,1)S(1)} %get-tuple-element.89), channel_id=1, source_target_pairs={{0,192},{64,0},{128,64},{192,128},{1,193},{65,1},{129,65},{193,129... | collective-permute-start | bytes 589832 | tf_op jit(solution)/shard_map/ppermute | solution.py:28
  93.0 2.9 %collective-permute-done.23.r1 = bf16[96,1024]{1,0:T(8,128)(2,1)S(1)} collective-permute-done((bf16[96,1024]{1,0:T(8,128)(2,1)S(1)}, bf16[96,1024]{1,0:T(8,128)(2,1)S(1)}, u32[]{:S(2)}, u32[]{:S(2)}) %collective-permute-start.23) | collective-permute-done | bytes 196640 | tf_op jit(solution)/shard_map/ppermute | solution.py:28
  95.9 2.6 %collective-permute-done.24.r2 = bf16[96,1024]{1,0:T(8,128)(2,1)S(1)} collective-permute-done((bf16[96,1024]{1,0:T(8,128)(2,1)S(1)}, bf16[96,1024]{1,0:T(8,128)(2,1)S(1)}, u32[]{:S(2)}, u32[]{:S(2)}) %collective-permute-start.24) | collective-permute-done | bytes 196640 | tf_op jit(solution)/shard_map/ppermute | solution.py:28
  98.6 2.4 %collective-permute-done.25.r3 = bf16[96,1024]{1,0:T(8,128)(2,1)S(1)} collective-permute-done((bf16[96,1024]{1,0:T(8,128)(2,1)S(1)}, bf16[96,1024]{1,0:T(8,128)(2,1)S(1)}, u32[]{:S(2)}, u32[]{:S(2)}) %collective-permute-start.25) | collective-permute-done | bytes 196640 | tf_op jit(solution)/shard_map/ppermute | solution.py:28
  105.9 4.4 %collective-permute-done.31 = bf16[96,1024]{1,0:T(8,128)(2,1)S(1)} collective-permute-done((bf16[96,1024]{1,0:T(8,128)(2,1)S(1)}, bf16[96,1024]{1,0:T(8,128)(2,1)S(1)}, u32[]{:S(2)}, u32[]{:S(2)}) %collective-permute-start.31) | collective-permute-done | bytes 196640 | tf_op jit(solution)/shard_map/ppermute | solution.py:23
  112.5 2.6 %collective-permute-done.29 = bf16[96,1024]{1,0:T(8,128)(2,1)S(1)} collective-permute-done((bf16[96,1024]{1,0:T(8,128)(2,1)S(1)}, bf16[96,1024]{1,0:T(8,128)(2,1)S(1)}, u32[]{:S(2)}, u32[]{:S(2)}) %collective-permute-start.29) | collective-permute-done | bytes 196640 | tf_op jit(solution)/shard_map/ppermute | solution.py:23
  115.8 12.4 %collective-permute-done.26 = bf16[2,2,48,1024]{3,2,1,0:T(8,128)(2,1)S(1)} collective-permute-done((bf16[2,2,48,1024]{3,2,1,0:T(8,128)(2,1)S(1)}, bf16[2,2,48,1024]{3,2,1,0:T(8,128)(2,1)S(1)}, u32[]{:S(2)}, u32[]{:S(2)}) %collective-permute-start.26) | collective-permute-done | bytes 393248 | tf_op jit(solution)/shard_map/ppermute | solution.py:28
  128.3 3.1 %shard_map.93 = (f32[2,2,48,1024]{3,2,1,0:T(8,128)S(1)}, f32[2,2,48,1024]{3,2,1,0:T(8,128)S(1)}, bf16[2,2,48,1024]{3,2,1,0:T(8,128)(2,1)S(1)}, f32[2,2,48,1024]{...) custom-call(s32[4]{0:T(128)S(1)} %pad_add_fusion.pos, bf16[4,96,1024]{2,1,0:T(8,128)(2,1)S(1)} %pad_maximum_fusion.1.mine, ...), custom_call_target="tpu_custom_call" | custom-call | flops 1610612736 | bytes 7995392 | tf_op jit(solution)/shard_map/pallas_call | solution.py:33
  133.8 4.4 %collective-permute-done.35 = bf16[1,2,48,1024]{3,2,1,0:T(8,128)(2,1)S(1)} collective-permute-done((bf16[1,2,48,1024]{3,2,1,0:T(8,128)(2,1)S(1)}, bf16[1,2,48,1024]{3,2,1,0:T(8,128)(2,1)S(1)}, u32[]{:S(2)}, u32[]{:S(2)}) %collective-permute-start.35) | collective-permute-done | bytes 196640 | tf_op jit(solution)/shard_map/ppermute | solution.py:28
  140.6 7.5 %collective-permute-done.36 = bf16[2,2,48,1024]{3,2,1,0:T(8,128)(2,1)S(1)} collective-permute-done((bf16[2,2,48,1024]{3,2,1,0:T(8,128)(2,1)S(1)}, bf16[2,2,48,1024]{3,2,1,0:T(8,128)(2,1)S(1)}, u32[]{:S(2)}, u32[]{:S(2)}) %collective-permute-start.36) | collective-permute-done | bytes 393248 | tf_op jit(solution)/shard_map/ppermute | solution.py:28
  148.1 2.9 %collective-permute-done.34 = bf16[2,2,48,1024]{3,2,1,0:T(8,128)(2,1)S(1)} collective-permute-done((bf16[2,2,48,1024]{3,2,1,0:T(8,128)(2,1)S(1)}, bf16[2,2,48,1024]{3,2,1,0:T(8,128)(2,1)S(1)}, u32[]{:S(2)}, u32[]{:S(2)}) %collective-permute-start.34) | collective-permute-done | bytes 393248 | tf_op jit(solution)/shard_map/ppermute | solution.py:28
  151.3 2.5 %collective-permute-start.38 = (bf16[2,48,1024]{2,1,0:T(8,128)(2,1)S(1)}, bf16[2,48,1024]{2,1,0:T(8,128)(2,1)S(1)}, u32[]{:S(2)}, u32[]{:S(2)}) collective-permute-start(bf16[2,48,1024]{2,1,0:T(8,128)(2,1)S(1)} %get-tuple-element.86), channel_id=1, source_target_pairs={{0,56},{8,0},{16,8},{24,16},{32,24},{40,32},{48,40},{56,48},{1,57}... | collective-permute-start | bytes 589832 | tf_op jit(solution)/shard_map/ppermute | solution.py:28
  153.8 3.2 %collective-permute-done.38 = bf16[2,48,1024]{2,1,0:T(8,128)(2,1)S(1)} collective-permute-done((bf16[2,48,1024]{2,1,0:T(8,128)(2,1)S(1)}, bf16[2,48,1024]{2,1,0:T(8,128)(2,1)S(1)}, u32[]{:S(2)}, u32[]{:S(2)}) %collective-permute-start.38) | collective-permute-done | bytes 196640 | tf_op jit(solution)/shard_map/ppermute | solution.py:28
  157.0 7.6 %collective-permute-done.37 = bf16[2,48,1024]{2,1,0:T(8,128)(2,1)S(1)} collective-permute-done((bf16[2,48,1024]{2,1,0:T(8,128)(2,1)S(1)}, bf16[2,48,1024]{2,1,0:T(8,128)(2,1)S(1)}, u32[]{:S(2)}, u32[]{:S(2)}) %collective-permute-start.37) | collective-permute-done | bytes 196640 | tf_op jit(solution)/shard_map/ppermute | solution.py:28
  164.7 3.6 %collective-permute-start.39 = (bf16[48,1024]{1,0:T(8,128)(2,1)S(1)}, bf16[48,1024]{1,0:T(8,128)(2,1)S(1)}, u32[]{:S(2)}, u32[]{:S(2)}) collective-permute-start(bf16[48,1024]{1,0:T(8,128)(2,1)S(1)} %fusion.6), channel_id=1, source_target_pairs={{0,32},{8,40},{16,48},{24,56},{32,0},{40,8},{48,16},{56,24},{1,33}... | collective-permute-start | bytes 294920 | tf_op jit(solution)/shard_map/ppermute | solution.py:28
  168.4 7.9 %shard_map.94 = bf16[1024,1024]{1,0:T(8,128)(2,1)} custom-call(s32[32]{0:T(128)S(1)} %get-tuple-element.94.rows, s32[32]{0:T(128)S(1)} %get-tuple-element.93.cols, s32[1]{0:T(128)} %bitcast.53.count, bf16[4,192,1024]{2,1,0:T(8,128)(2,1)S(1)} %bitcast.58, bf16[4,192,1024]{2,1,0:T(8,128)(2,1)S(1)} %bitcast.60, bf16[4,192,1024]{2,1,0:T(8,128)(2,1)S(1)} %bitcast.59, ...), custom_call_target="tpu_custom_call" | custom-call | flops 3221225472 | bytes 8388608 | tf_op jit(solution)/shard_map/pallas_call | solution.py:33
  (98 shorter events, 41.0 us)
Async XLA Ops:
  0.7 10.4 %collective-permute-start = (bf16[48,1024]{1,0:T(8,128)(2,1)}, bf16[48,1024]{1,0:T(8,128)(2,1)S(1)}, u32[]{:S(2)}, u32[]{:S(2)}) collective-permute-start(bf16[48,1024]{1,0:T(8,128)(2,1)} %param.6), channel_id=1, source_target_pairs={{32,0},{40,8},{48,16},{56,24},{0,32},{8,40},{16,48},{24,56},{33,1}... | collective-permute-start | bytes 294920 | tf_op jit(solution)/shard_map/ppermute | solution.py:23
  12.0 9.4 %collective-permute-start.3 = (bf16[2,48,1024]{2,1,0:T(8,128)(2,1)S(1)}, bf16[2,48,1024]{2,1,0:T(8,128)(2,1)S(1)}, u32[]{:S(2)}, u32[]{:S(2)}) collective-permute-start(bf16[2,48,1024]{2,1,0:T(8,128)(2,1)S(1)} %get-tuple-element.92), channel_id=1, source_target_pairs={{8,0},{16,8},{24,16},{32,24},{40,32},{48,40},{56,48},{0,56},{9,1},... | collective-permute-start | bytes 589832 | tf_op jit(solution)/shard_map/ppermute | solution.py:23
  21.4 15.9 %collective-permute-start.4 = (bf16[2,2,48,1024]{3,2,1,0:T(8,128)(2,1)S(1)}, bf16[2,2,48,1024]{3,2,1,0:T(8,128)(2,1)S(1)}, u32[]{:S(2)}, u32[]{:S(2)}) collective-permute-start(bf16[2,2,48,1024]{3,2,1,0:T(8,128)(2,1)S(1)} %pad_maximum_fusion.3.refs_0_), channel_id=1, source_target_pairs={{64,0},{128,64},{192,128},{0,192},{65,1},{129,65},{193,129},{1,193... | collective-permute-start | bytes 1179656 | tf_op jit(solution)/shard_map/ppermute | solution.py:23
  24.5 12.8 %collective-permute-start.5 = (bf16[2,2,48,1024]{3,2,1,0:T(8,128)(2,1)S(1)}, bf16[2,2,48,1024]{3,2,1,0:T(8,128)(2,1)S(1)}, u32[]{:S(2)}, u32[]{:S(2)}) collective-permute-start(bf16[2,2,48,1024]{3,2,1,0:T(8,128)(2,1)S(1)} %pad_maximum_fusion.3.refs_0_), channel_id=1, source_target_pairs={{192,0},{0,64},{64,128},{128,192},{193,1},{1,65},{65,129},{129,193... | collective-permute-start | bytes 1179656 | tf_op jit(solution)/shard_map/ppermute | solution.py:23
  24.5 7.5 %collective-permute-start.2 = (bf16[2,48,1024]{2,1,0:T(8,128)(2,1)S(1)}, bf16[2,48,1024]{2,1,0:T(8,128)(2,1)}, u32[]{:S(2)}, u32[]{:S(2)}) collective-permute-start(bf16[2,48,1024]{2,1,0:T(8,128)(2,1)S(1)} %get-tuple-element.92), channel_id=1, source_target_pairs={{56,0},{0,8},{8,16},{16,24},{24,32},{32,40},{40,48},{48,56},{57,1}... | collective-permute-start | bytes 589832 | tf_op jit(solution)/shard_map/ppermute | solution.py:23
  24.5 11.8 %collective-permute-start.1 = (bf16[2,48,1024]{2,1,0:T(8,128)(2,1)S(1)}, bf16[2,48,1024]{2,1,0:T(8,128)(2,1)}, u32[]{:S(2)}, u32[]{:S(2)}) collective-permute-start(bf16[2,48,1024]{2,1,0:T(8,128)(2,1)S(1)} %get-tuple-element.92), channel_id=1, source_target_pairs={{16,0},{24,8},{32,16},{40,24},{48,32},{56,40},{0,48},{8,56},{17,1}... | collective-permute-start | bytes 589832 | tf_op jit(solution)/shard_map/ppermute | solution.py:23
  50.1 11.5 %collective-permute-start.6 = (bf16[2,2,48,1024]{3,2,1,0:T(8,128)(2,1)S(1)}, bf16[2,2,48,1024]{3,2,1,0:T(8,128)(2,1)S(1)}, u32[]{:S(2)}, u32[]{:S(2)}) collective-permute-start(bf16[2,2,48,1024]{3,2,1,0:T(8,128)(2,1)S(1)} %pad_maximum_fusion.2.refs_0_), channel_id=1, source_target_pairs={{64,0},{128,64},{192,128},{0,192},{65,1},{129,65},{193,129},{1,193... | collective-permute-start | bytes 1179656 | tf_op jit(solution)/shard_map/ppermute | solution.py:23
  50.2 12.6 %collective-permute-start.7 = (bf16[2,2,48,1024]{3,2,1,0:T(8,128)(2,1)S(1)}, bf16[2,2,48,1024]{3,2,1,0:T(8,128)(2,1)S(1)}, u32[]{:S(2)}, u32[]{:S(2)}) collective-permute-start(bf16[2,2,48,1024]{3,2,1,0:T(8,128)(2,1)S(1)} %pad_maximum_fusion.2.refs_0_), channel_id=1, source_target_pairs={{192,0},{0,64},{64,128},{128,192},{193,1},{1,65},{65,129},{129,193... | collective-permute-start | bytes 1179656 | tf_op jit(solution)/shard_map/ppermute | solution.py:23
  52.7 12.6 %collective-permute-start.14 = (bf16[96,1024]{1,0:T(8,128)(2,1)S(1)}, bf16[96,1024]{1,0:T(8,128)(2,1)S(1)}, u32[]{:S(2)}, u32[]{:S(2)}) collective-permute-start(bf16[96,1024]{1,0:T(8,128)(2,1)S(1)} %get-tuple-element.57), channel_id=1, source_target_pairs={{0,2},{2,4},{4,6},{6,0},{1,3},{3,5},{5,7},{7,1},{8,10},{10,12},{12... | collective-permute-start | bytes 589832 | tf_op jit(solution)/shard_map/ppermute | solution.py:28
  53.2 12.0 %collective-permute-start.15 = (bf16[96,1024]{1,0:T(8,128)(2,1)S(1)}, bf16[96,1024]{1,0:T(8,128)(2,1)S(1)}, u32[]{:S(2)}, u32[]{:S(2)}) collective-permute-start(bf16[96,1024]{1,0:T(8,128)(2,1)S(1)} %get-tuple-element.58), channel_id=1, source_target_pairs={{0,4},{2,6},{4,0},{6,2},{1,5},{3,7},{5,1},{7,3},{8,12},{10,14},{12... | collective-permute-start | bytes 589832 | tf_op jit(solution)/shard_map/ppermute | solution.py:28
  55.7 10.0 %collective-permute-start.16 = (bf16[96,1024]{1,0:T(8,128)(2,1)S(1)}, bf16[96,1024]{1,0:T(8,128)(2,1)S(1)}, u32[]{:S(2)}, u32[]{:S(2)}) collective-permute-start(bf16[96,1024]{1,0:T(8,128)(2,1)S(1)} %get-tuple-element.59), channel_id=1, source_target_pairs={{0,6},{2,0},{4,2},{6,4},{1,7},{3,1},{5,3},{7,5},{8,14},{10,8},{12,... | collective-permute-start | bytes 589832 | tf_op jit(solution)/shard_map/ppermute | solution.py:28
  63.5 7.7 %collective-permute-start.11 = (bf16[1,2,48,1024]{3,2,1,0:T(8,128)(2,1)S(1)}, bf16[1,2,48,1024]{3,2,1,0:T(8,128)(2,1)S(1)}, u32[]{:S(2)}, u32[]{:S(2)}) collective-permute-start(bf16[1,2,48,1024]{3,2,1,0:T(8,128)(2,1)S(1)} %slice.77), channel_id=1, source_target_pairs={{192,0},{0,64},{64,128},{128,192},{193,1},{1,65},{65,129},{129,193... | collective-permute-start | bytes 589832 | tf_op jit(solution)/shard_map/ppermute | solution.py:23
  66.4 7.8 %collective-permute-start.19 = (bf16[96,1024]{1,0:T(8,128)(2,1)S(1)}, bf16[96,1024]{1,0:T(8,128)(2,1)S(1)}, u32[]{:S(2)}, u32[]{:S(2)}) collective-permute-start(bf16[96,1024]{1,0:T(8,128)(2,1)S(1)} %get-tuple-element.60), channel_id=1, source_target_pairs={{6,0},{0,2},{2,4},{4,6},{7,1},{1,3},{3,5},{5,7},{14,8},{8,10},{10,... | collective-permute-start | bytes 589832 | tf_op jit(solution)/shard_map/ppermute | solution.py:23
  67.5 9.3 %collective-permute-start.18 = (bf16[96,1024]{1,0:T(8,128)(2,1)S(1)}, bf16[96,1024]{1,0:T(8,128)(2,1)S(1)}, u32[]{:S(2)}, u32[]{:S(2)}) collective-permute-start(bf16[96,1024]{1,0:T(8,128)(2,1)S(1)} %get-tuple-element.60), channel_id=1, source_target_pairs={{4,0},{6,2},{0,4},{2,6},{5,1},{7,3},{1,5},{3,7},{12,8},{14,10},{8,... | collective-permute-start | bytes 589832 | tf_op jit(solution)/shard_map/ppermute | solution.py:23
  69.5 9.6 %collective-permute-start.17 = (bf16[96,1024]{1,0:T(8,128)(2,1)S(1)}, bf16[96,1024]{1,0:T(8,128)(2,1)S(1)}, u32[]{:S(2)}, u32[]{:S(2)}) collective-permute-start(bf16[96,1024]{1,0:T(8,128)(2,1)S(1)} %get-tuple-element.60), channel_id=1, source_target_pairs={{2,0},{4,2},{6,4},{0,6},{3,1},{5,3},{7,5},{1,7},{10,8},{12,10},{14... | collective-permute-start | bytes 589832 | tf_op jit(solution)/shard_map/ppermute | solution.py:23
  84.8 8.2 %collective-permute-start.21 = (bf16[1,2,48,1024]{3,2,1,0:T(8,128)(2,1)S(1)}, bf16[1,2,48,1024]{3,2,1,0:T(8,128)(2,1)S(1)}, u32[]{:S(2)}, u32[]{:S(2)}) collective-permute-start(bf16[1,2,48,1024]{3,2,1,0:T(8,128)(2,1)S(1)} %get-tuple-element.90), channel_id=1, source_target_pairs={{0,64},{64,128},{128,192},{192,0},{1,65},{65,129},{129,193},{193,1... | collective-permute-start | bytes 589832 | tf_op jit(solution)/shard_map/ppermute | solution.py:28
  84.9 8.1 %collective-permute-start.22 = (bf16[1,2,48,1024]{3,2,1,0:T(8,128)(2,1)S(1)}, bf16[1,2,48,1024]{3,2,1,0:T(8,128)(2,1)S(1)}, u32[]{:S(2)}, u32[]{:S(2)}) collective-permute-start(bf16[1,2,48,1024]{3,2,1,0:T(8,128)(2,1)S(1)} %get-tuple-element.89), channel_id=1, source_target_pairs={{0,192},{64,0},{128,64},{192,128},{1,193},{65,1},{129,65},{193,129... | collective-permute-start | bytes 589832 | tf_op jit(solution)/shard_map/ppermute | solution.py:28
  88.1 7.8 %collective-permute-start.23 = (bf16[96,1024]{1,0:T(8,128)(2,1)S(1)}, bf16[96,1024]{1,0:T(8,128)(2,1)S(1)}, u32[]{:S(2)}, u32[]{:S(2)}) collective-permute-start(bf16[96,1024]{1,0:T(8,128)(2,1)S(1)} %get-tuple-element.67), channel_id=1, source_target_pairs={{0,2},{2,4},{4,6},{6,0},{1,3},{3,5},{5,7},{7,1},{8,10},{10,12},{12... | collective-permute-start | bytes 589832 | tf_op jit(solution)/shard_map/ppermute | solution.py:28
  89.2 9.4 %collective-permute-start.24 = (bf16[96,1024]{1,0:T(8,128)(2,1)S(1)}, bf16[96,1024]{1,0:T(8,128)(2,1)S(1)}, u32[]{:S(2)}, u32[]{:S(2)}) collective-permute-start(bf16[96,1024]{1,0:T(8,128)(2,1)S(1)} %get-tuple-element.68), channel_id=1, source_target_pairs={{0,4},{2,6},{4,0},{6,2},{1,5},{3,7},{5,1},{7,3},{8,12},{10,14},{12... | collective-permute-start | bytes 589832 | tf_op jit(solution)/shard_map/ppermute | solution.py:28
  90.4 10.6 %collective-permute-start.25 = (bf16[96,1024]{1,0:T(8,128)(2,1)S(1)}, bf16[96,1024]{1,0:T(8,128)(2,1)S(1)}, u32[]{:S(2)}, u32[]{:S(2)}) collective-permute-start(bf16[96,1024]{1,0:T(8,128)(2,1)S(1)} %get-tuple-element.69), channel_id=1, source_target_pairs={{0,6},{2,0},{4,2},{6,4},{1,7},{3,1},{5,3},{7,5},{8,14},{10,8},{12,... | collective-permute-start | bytes 589832 | tf_op jit(solution)/shard_map/ppermute | solution.py:28
  102.6 7.8 %collective-permute-start.31 = (bf16[96,1024]{1,0:T(8,128)(2,1)S(1)}, bf16[96,1024]{1,0:T(8,128)(2,1)S(1)}, u32[]{:S(2)}, u32[]{:S(2)}) collective-permute-start(bf16[96,1024]{1,0:T(8,128)(2,1)S(1)} %get-tuple-element.75), channel_id=1, source_target_pairs={{6,0},{0,2},{2,4},{4,6},{7,1},{1,3},{3,5},{5,7},{14,8},{8,10},{10,... | collective-permute-start | bytes 589832 | tf_op jit(solution)/shard_map/ppermute | solution.py:23
  103.2 9.4 %collective-permute-start.30 = (bf16[96,1024]{1,0:T(8,128)(2,1)S(1)}, bf16[96,1024]{1,0:T(8,128)(2,1)S(1)}, u32[]{:S(2)}, u32[]{:S(2)}) collective-permute-start(bf16[96,1024]{1,0:T(8,128)(2,1)S(1)} %get-tuple-element.75), channel_id=1, source_target_pairs={{4,0},{6,2},{0,4},{2,6},{5,1},{7,3},{1,5},{3,7},{12,8},{14,10},{8,... | collective-permute-start | bytes 589832 | tf_op jit(solution)/shard_map/ppermute | solution.py:23
  104.4 10.7 %collective-permute-start.29 = (bf16[96,1024]{1,0:T(8,128)(2,1)S(1)}, bf16[96,1024]{1,0:T(8,128)(2,1)S(1)}, u32[]{:S(2)}, u32[]{:S(2)}) collective-permute-start(bf16[96,1024]{1,0:T(8,128)(2,1)S(1)} %get-tuple-element.75), channel_id=1, source_target_pairs={{2,0},{4,2},{6,4},{0,6},{3,1},{5,3},{7,5},{1,7},{10,8},{12,10},{14... | collective-permute-start | bytes 589832 | tf_op jit(solution)/shard_map/ppermute | solution.py:23
  105.3 10.5 %collective-permute-start.27 = (bf16[2,2,48,1024]{3,2,1,0:T(8,128)(2,1)S(1)}, bf16[2,2,48,1024]{3,2,1,0:T(8,128)(2,1)S(1)}, u32[]{:S(2)}, u32[]{:S(2)}) collective-permute-start(bf16[2,2,48,1024]{3,2,1,0:T(8,128)(2,1)S(1)} %pad_maximum_fusion.5), channel_id=1, source_target_pairs={{0,192},{64,0},{128,64},{192,128},{1,193},{65,1},{129,65},{193,129... | collective-permute-start | bytes 1179656 | tf_op jit(solution)/shard_map/ppermute | solution.py:28
  115.2 13.1 %collective-permute-start.32 = (bf16[4,96,1024]{2,1,0:T(8,128)(2,1)S(1)}, bf16[4,96,1024]{2,1,0:T(8,128)(2,1)S(1)}, u32[]{:S(2)}, u32[]{:S(2)}) collective-permute-start(bf16[4,96,1024]{2,1,0:T(8,128)(2,1)S(1)} %pad_maximum_fusion.1.mine), channel_id=1, source_target_pairs={{0,1},{1,0},{2,3},{3,2},{4,5},{5,4},{6,7},{7,6},{8,9},{9,8},{10,11... | collective-permute-start | bytes 2359304 | tf_op jit(solution)/shard_map/ppermute | solution.py:28
  115.3 12.8 %collective-permute-start.26 = (bf16[2,2,48,1024]{3,2,1,0:T(8,128)(2,1)S(1)}, bf16[2,2,48,1024]{3,2,1,0:T(8,128)(2,1)S(1)}, u32[]{:S(2)}, u32[]{:S(2)}) collective-permute-start(bf16[2,2,48,1024]{3,2,1,0:T(8,128)(2,1)S(1)} %pad_maximum_fusion.4), channel_id=1, source_target_pairs={{0,64},{64,128},{128,192},{192,0},{1,65},{65,129},{129,193},{193,1... | collective-permute-start | bytes 1179656 | tf_op jit(solution)/shard_map/ppermute | solution.py:28
  131.7 8.1 %collective-permute-start.33 = (bf16[1,2,48,1024]{3,2,1,0:T(8,128)(2,1)S(1)}, bf16[1,2,48,1024]{3,2,1,0:T(8,128)(2,1)S(1)}, u32[]{:S(2)}, u32[]{:S(2)}) collective-permute-start(bf16[1,2,48,1024]{3,2,1,0:T(8,128)(2,1)S(1)} %get-tuple-element.87), channel_id=1, source_target_pairs={{0,64},{64,128},{128,192},{192,0},{1,65},{65,129},{129,193},{193,1... | collective-permute-start | bytes 589832 | tf_op jit(solution)/shard_map/ppermute | solution.py:28
  138.2 9.9 %collective-permute-start.36 = (bf16[2,2,48,1024]{3,2,1,0:T(8,128)(2,1)S(1)}, bf16[2,2,48,1024]{3,2,1,0:T(8,128)(2,1)S(1)}, u32[]{:S(2)}, u32[]{:S(2)}) collective-permute-start(bf16[2,2,48,1024]{3,2,1,0:T(8,128)(2,1)S(1)} %pad_maximum_fusion.7), channel_id=1, source_target_pairs={{0,192},{64,0},{128,64},{192,128},{1,193},{65,1},{129,65},{193,129... | collective-permute-start | bytes 1179656 | tf_op jit(solution)/shard_map/ppermute | solution.py:28
  139.9 11.2 %collective-permute-start.34 = (bf16[2,2,48,1024]{3,2,1,0:T(8,128)(2,1)S(1)}, bf16[2,2,48,1024]{3,2,1,0:T(8,128)(2,1)S(1)}, u32[]{:S(2)}, u32[]{:S(2)}) collective-permute-start(bf16[2,2,48,1024]{3,2,1,0:T(8,128)(2,1)S(1)} %pad_maximum_fusion.6), channel_id=1, source_target_pairs={{0,64},{64,128},{128,192},{192,0},{1,65},{65,129},{129,193},{193,1... | collective-permute-start | bytes 1179656 | tf_op jit(solution)/shard_map/ppermute | solution.py:28
  140.5 13.3 %collective-permute-start.28 = (bf16[2,48,1024]{2,1,0:T(8,128)(2,1)S(1)}, bf16[2,48,1024]{2,1,0:T(8,128)(2,1)S(1)}, u32[]{:S(2)}, u32[]{:S(2)}) collective-permute-start(bf16[2,48,1024]{2,1,0:T(8,128)(2,1)S(1)} %fusion.3), channel_id=1, source_target_pairs={{0,8},{8,16},{16,24},{24,32},{32,40},{40,48},{48,56},{56,0},{1,9},... | collective-permute-start | bytes 589832 | tf_op jit(solution)/shard_map/ppermute | solution.py:28
  153.8 10.9 %collective-permute-start.37 = (bf16[2,48,1024]{2,1,0:T(8,128)(2,1)S(1)}, bf16[2,48,1024]{2,1,0:T(8,128)(2,1)S(1)}, u32[]{:S(2)}, u32[]{:S(2)}) collective-permute-start(bf16[2,48,1024]{2,1,0:T(8,128)(2,1)S(1)} %get-tuple-element.85), channel_id=1, source_target_pairs={{0,16},{8,24},{16,32},{24,40},{32,48},{40,56},{48,0},{56,8},{1,17}... | collective-permute-start | bytes 589832 | tf_op jit(solution)/shard_map/ppermute | solution.py:28
  164.7 11.5 %collective-permute-start.39 = (bf16[48,1024]{1,0:T(8,128)(2,1)S(1)}, bf16[48,1024]{1,0:T(8,128)(2,1)S(1)}, u32[]{:S(2)}, u32[]{:S(2)}) collective-permute-start(bf16[48,1024]{1,0:T(8,128)(2,1)S(1)} %fusion.6), channel_id=1, source_target_pairs={{0,32},{8,40},{16,48},{24,56},{32,0},{40,8},{48,16},{56,24},{1,33}... | collective-permute-start | bytes 294920 | tf_op jit(solution)/shard_map/ppermute | solution.py:28
  (12 other events, 176.9 us)

commit v6 on v4

--- a/solution.py
+++ b/solution.py
@@ -1,5 +1,3 @@
-import functools
-
 import jax
 import jax.numpy as jnp
 from jax import lax
@@ -89,7 +87,9 @@
         for i in range(4):
             a_ref, a_at = at_step(a3, i, j)
             b_ref, b_at = at_step(b3, j, i)
-            for hi in range(2):
+
+            @pl.loop(0, 2)
+            def _(hi, i=i, j=j, d=d, a_ref=a_ref, a_at=a_at, b_ref=b_ref, b_at=b_at):
                 at = zpos(pos, STEPS[i], hi)
                 low = zpos(pos, z_step(i, j), hi)
                 toks[d, low, :, :cut] = a_ref[a_at, hi]
@@ -162,25 +162,29 @@
                 b3[k][i, hi] = piece.astype(b3[k].dtype)
 
 
-def add_body(cols, keep, recv, *out):
+def add_body(keep, recv, *out):
     for d in range(4):
 
-        @pl.loop(0, keep.shape[1] // 32)
+        @pl.loop(0, keep.shape[1] // 16)
         def _(i, d=d):
-            at = pl.ds(pl.multiple_of(i * 32, 32), 32)
-            total = keep[d, at, cols] + recv[d, at, cols].astype(F32)
+            at = pl.ds(pl.multiple_of(i * 16, 16), 16)
+            total = keep[d, at] + recv[d, at].astype(F32)
             out[d][at] = total.astype(out[d].dtype)
 
 
-def act_body(own, r1, r2, r3, cot, hidden, grad_pre):
-    @pl.loop(0, own.shape[0] // 32)
+def act_body(own, r1, r2, r3, cot, hidden, *grads):
+    step = grads[0].shape[1]
+
+    @pl.loop(0, own.shape[0] // 16)
     def _(i):
-        at = pl.ds(pl.multiple_of(i * 32, 32), 32)
-        pre_act = own[at] + r1[at].astype(F32) + r2[at].astype(F32) + r3[at].astype(F32)
-        gate = jax.nn.sigmoid(pre_act)
-        hidden[at] = (pre_act * gate).astype(BF16)
-        slope = gate * (1.0 + pre_act * (1.0 - gate))
-        grad_pre[at] = (cot[at].astype(F32) * slope).astype(BF16)
+        rows = pl.ds(pl.multiple_of(i * 16, 16), 16)
+        for k, grad_pre in enumerate(grads):
+            at = (rows, slice(k * step, (k + 1) * step))
+            pre_act = own[at] + r1[at].astype(F32) + r2[at].astype(F32) + r3[at].astype(F32)
+            gate = jax.nn.sigmoid(pre_act)
+            hidden[at] = (pre_act * gate).astype(BF16)
+            slope = gate * (1.0 + pre_act * (1.0 - gate))
+            grad_pre[rows] = (cot[at].astype(F32) * slope).astype(BF16)
 
 
 def wgrad_body(rows, cols, count, toks, grads, out, acc):
@@ -226,18 +230,13 @@
     return ring_gather(jnp.stack(a2), "z"), ring_gather(jnp.stack(b2), "y")
 
 
-def partial_sums(keep, recv, cols):
-    shape = (keep.shape[1], cols.stop - cols.start)
-    body = functools.partial(add_body, cols)
-    return call(body, [(shape, F32)] + [(shape, BF16)] * 3, [], [keep, recv])
-
-
-def shares(sends):
-    return [to_ahead(s, "x", d + 1) for d, s in enumerate(sends)]
-
-
-def activation(own, recvs, cot):
-    return call(act_body, [(own.shape, BF16)] * 2, [], [own] + recvs + [cot])
+def activation(keep, recv, cot):
+    shape = keep.shape[1:]
+    own, *sends = call(add_body, [(shape, F32)] + [(shape, BF16)] * 3, [], [keep, recv])
+    recvs = [to_ahead(s, "x", d + 1) for d, s in enumerate(sends)]
+    cut = shape[1] // 2
+    outs = [(shape, BF16)] + [((shape[0], cut), BF16)] * 2
+    return call(act_body, outs, [], [own] + recvs + [cot])
 
 
 def gather_grads(grad_pre):
@@ -280,10 +279,7 @@
         [VM((2, rows, width), F32)],
     )
     recv = to_ahead(send, "core", 1)
-    own1, *sends1 = partial_sums(keep, recv, slice(0, cut))
-    own2, *sends2 = partial_sums(keep, recv, slice(cut, width))
-    hidden1, grad1 = activation(own1, shares(sends1), cot[:, :cut])
-    hidden2, grad2 = activation(own2, shares(sends2), cot[:, cut:])
+    hidden, grad1, grad2 = activation(keep, recv, cot)
     parts1 = gather_grads(grad1)
     parts2 = gather_grads(grad2)
     g_shape = ((4, 2, rows, cut), BF16)
@@ -302,19 +298,18 @@
         flops,
         [VM(sums, F32), sems, pltpu.SemaphoreType.DMA],
     )
-    hidden = jnp.concatenate([hidden1, hidden2], axis=1)
     return hidden, sends, toks, grads
 
 
-def reduce_inputs(sends):
+def reduce_inputs(sends, weight_grad):
     a2 = ring_reduce(*sends[:4], "z")
     b2 = ring_reduce(*sends[4:], "y")
-    a2, b2 = lax.optimization_barrier((a2, b2))
+    a2, b2, weight_grad = lax.optimization_barrier((a2, b2, weight_grad))
     a1 = reduce_four(a2[0], a2[1:], "y")
     b1 = reduce_four(b2[0], b2[1:], "z")
     both = jnp.concatenate([a1, b1], axis=-1)
     total = both[0] + to_ahead(both[1].astype(BF16), "z", 4).astype(F32)
-    return total.astype(BF16)
+    return total.astype(BF16), weight_grad
 
 
 def on_device(tokens, weight, tile_rows, tile_cols, tile_count, hidden_cotangent):
@@ -337,7 +332,7 @@
         2 * 1536 * weight.size,
         [VM(weight.shape, F32)],
     )
-    input_grad = reduce_inputs(sends)
+    input_grad, weight_grad = reduce_inputs(sends, weight_grad)
     return hidden, input_grad, weight_grad
 
 

time: 178 us -> 166 us (0.933)
  the two profiles are of different devices: /device:TPU:10 before, /device:TPU:6 now
where the time goes in v6:
time: 166 us; the launch traced here: 165 us
  starting transfers between devices  69.8 us (42%)
  waiting for transfers between devices  60.4 us (36%)
  Pallas kernels  27.3 us (16%)
  local copies, waits for them, and re-layouts  3.05 us (2%)
  other arithmetic  2.8 us (2%)
  between operations  1.68 us (1%)
    ppermute x21, starting transfers between devices, from_ahead(): return lax.ppermute(value, axis, [((i + k) % n, i) for i in range(n)])  45.2 us
    ppermute x21, waiting for transfers between devices, to_ahead(): return lax.ppermute(value, axis, [(i, (i + k) % n) for i in range(n)])  40.4 us
    pallas_call x7, Pallas kernels, call(): pl.pallas_call(body, out_shape=outs, in_specs=[pl.BlockSpec(memory_space=...  27.3 us
    ppermute x21, starting transfers between devices, to_ahead(): return lax.ppermute(value, axis, [(i, (i + k) % n) for i in range(n)])  24.6 us
    ppermute x21, waiting for transfers between devices, from_ahead(): return lax.ppermute(value, axis, [((i + k) % n, i) for i in range(n)])  20 us
  transfers between devices with their start and end apart: 42, of which 20 were waited for; matrix products, arithmetic and copies ran while one was open for 2% of the time, Pallas kernels for 9%

profile of v6, /device:TPU:6, one launch (start us, length us, event | category | flops | bytes accessed | tf_op | source)
XLA Modules:
  0.0 165.0 jit_solution(3744995604382999203)
XLA Ops:
  0.7 7.3 %collective-permute-start = (bf16[48,1024]{1,0:T(8,128)(2,1)}, bf16[48,1024]{1,0:T(8,128)(2,1)S(1)}, u32[]{:S(2)}, u32[]{:S(2)}) collective-permute-start(bf16[48,1024]{1,0:T(8,128)(2,1)} %param.6), channel_id=1, source_target_pairs={{32,0},{40,8},{48,16},{56,24},{0,32},{8,40},{16,48},{24,56},{33,1}... | collective-permute-start | bytes 294920 | tf_op jit(solution)/shard_map/ppermute | solution.py:21
  7.9 3.1 %collective-permute-done = bf16[48,1024]{1,0:T(8,128)(2,1)S(1)} collective-permute-done((bf16[48,1024]{1,0:T(8,128)(2,1)}, bf16[48,1024]{1,0:T(8,128)(2,1)S(1)}, u32[]{:S(2)}, u32[]{:S(2)}) %collective-permute-start) | collective-permute-done | bytes 98336 | tf_op jit(solution)/shard_map/ppermute | solution.py:21
  11.9 2.6 %collective-permute-start.6 = (bf16[2,48,512]{2,1,0:T(8,128)(2,1)S(1)}, bf16[2,48,512]{2,1,0:T(8,128)(2,1)S(1)}, u32[]{:S(2)}, u32[]{:S(2)}) collective-permute-start(bf16[2,48,512]{2,1,0:T(8,128)(2,1)S(1)} %get-tuple-element.41), channel_id=1, source_target_pairs={{56,0},{0,8},{8,16},{16,24},{24,32},{32,40},{40,48},{48,56},{57,1}... | collective-permute-start | bytes 294920 | tf_op jit(solution)/shard_map/ppermute | solution.py:21
  14.4 4.2 %collective-permute-start.5 = (bf16[2,48,512]{2,1,0:T(8,128)(2,1)S(1)}, bf16[2,48,512]{2,1,0:T(8,128)(2,1)S(1)}, u32[]{:S(2)}, u32[]{:S(2)}) collective-permute-start(bf16[2,48,512]{2,1,0:T(8,128)(2,1)S(1)} %get-tuple-element.41), channel_id=1, source_target_pairs={{16,0},{24,8},{32,16},{40,24},{48,32},{56,40},{0,48},{8,56},{17,1}... | collective-permute-start | bytes 294920 | tf_op jit(solution)/shard_map/ppermute | solution.py:21
  22.2 2.9 %collective-permute-start.2 = (bf16[2,48,512]{2,1,0:T(8,128)(2,1)S(1)}, bf16[2,48,512]{2,1,0:T(8,128)(2,1)S(1)}, u32[]{:S(2)}, u32[]{:S(2)}) collective-permute-start(bf16[2,48,512]{2,1,0:T(8,128)(2,1)S(1)} %get-tuple-element.37), channel_id=1, source_target_pairs={{128,0},{192,64},{0,128},{64,192},{129,1},{193,65},{1,129},{65,193... | collective-permute-start | bytes 294920 | tf_op jit(solution)/shard_map/ppermute | solution.py:21
  30.5 2.6 %collective-permute-start.11 = (bf16[4,2,48,512]{3,2,1,0:T(8,128)(2,1)S(1)}, bf16[4,2,48,512]{3,2,1,0:T(8,128)(2,1)}, u32[]{:S(2)}, u32[]{:S(2)}) collective-permute-start(bf16[4,2,48,512]{3,2,1,0:T(8,128)(2,1)S(1)} %pad_maximum_fusion.3.refs_5_), channel_id=1, source_target_pairs={{64,0},{128,64},{192,128},{0,192},{65,1},{129,65},{193,129},{1,193... | collective-permute-start | bytes 1179656 | tf_op jit(solution)/shard_map/ppermute | solution.py:21
  33.3 3.1 %collective-permute-start.7 = (bf16[4,2,48,512]{3,2,1,0:T(8,128)(2,1)S(1)}, bf16[4,2,48,512]{3,2,1,0:T(8,128)(2,1)}, u32[]{:S(2)}, u32[]{:S(2)}) collective-permute-start(bf16[4,2,48,512]{3,2,1,0:T(8,128)(2,1)S(1)} %pad_maximum_fusion.2.refs_0_), channel_id=1, source_target_pairs={{8,0},{16,8},{24,16},{32,24},{40,32},{48,40},{56,48},{0,56},{9,1},... | collective-permute-start | bytes 1179656 | tf_op jit(solution)/shard_map/ppermute | solution.py:21
  36.4 2.7 %collective-permute-done.13.refs_9_ = bf16[4,2,48,512]{3,2,1,0:T(8,128)(2,1)S(1)} collective-permute-done((bf16[4,2,48,512]{3,2,1,0:T(8,128)(2,1)S(1)}, bf16[4,2,48,512]{3,2,1,0:T(8,128)(2,1)S(1)}, u32[]{:S(2)}, u32[]{:S(2)}) %collective-permute-start.13) | collective-permute-done | bytes 393248 | tf_op jit(solution)/shard_map/ppermute | solution.py:21
  40.2 3.3 %collective-permute-start.12 = (bf16[2,2,48,512]{3,2,1,0:T(8,128)(2,1)S(1)}, bf16[2,2,48,512]{3,2,1,0:T(8,128)(2,1)S(1)}, u32[]{:S(2)}, u32[]{:S(2)}) collective-permute-start(bf16[2,2,48,512]{3,2,1,0:T(8,128)(2,1)S(1)} %slice.105), channel_id=1, source_target_pairs={{64,0},{128,64},{192,128},{0,192},{65,1},{129,65},{193,129},{1,193... | collective-permute-start | bytes 589832 | tf_op jit(solution)/shard_map/ppermute | solution.py:21
  49.5 3.1 %shard_map.85 = (bf16[1024,1024]{1,0:T(8,128)(2,1)S(1)}, bf16[1024,1024]{1,0:T(8,128)(2,1)S(1)}) custom-call(s32[32]{0:T(128)S(1)} %get-tuple-element.84.rows, s32[32]{0:T(128)S(1)} %get-tuple-element.83.cols, s32[1]{0:T(128)} %bitcast.59.count, bf16[1024,1024]{1,0:T(8,128)(2,1)S(1)} %copy-done), custom_call_target="tpu_custom_call" | custom-call | bytes 6291456 | tf_op jit(solution)/shard_map/pallas_call | solution.py:31
  52.7 6.1 %shard_map.86 = (f32[4,192,1024]{2,1,0:T(8,128)S(1)}, bf16[4,192,1024]{2,1,0:T(8,128)(2,1)S(1)}, bf16[4,8,48,1024]{3,2,1,0:T(8,128)(2,1)S(1)}) custom-call(s32[4]{0:T(128)S(1)} %pad_add_fusion.pos, bf16[4,2,48,512]{3,2,1,0:T(8,128)(2,1)S(1)} %pad_maximum_fusion.2.refs_0_, bf16[4,2,48,512]{3,2,1,0:T(8,128)(2,1)} %collective-permute-done.7.refs_1_, ...), custom_call_target="tpu_custom_call" | custom-call | flops 3221225472 | bytes 13107200 | tf_op jit(solution)/shard_map/pallas_call | solution.py:31
  58.9 3.4 %collective-permute-done.15.recv = bf16[4,192,1024]{2,1,0:T(8,128)(2,1)S(1)} collective-permute-done((bf16[4,192,1024]{2,1,0:T(8,128)(2,1)S(1)}, bf16[4,192,1024]{2,1,0:T(8,128)(2,1)S(1)}, u32[]{:S(2)}, u32[]{:S(2)}) %collective-permute-start.15) | collective-permute-done | bytes 1572896 | tf_op jit(solution)/shard_map/ppermute | solution.py:26
  63.3 2.5 %collective-permute-start.17 = (bf16[192,1024]{1,0:T(8,128)(2,1)S(1)}, bf16[192,1024]{1,0:T(8,128)(2,1)S(1)}, u32[]{:S(2)}, u32[]{:S(2)}) collective-permute-start(bf16[192,1024]{1,0:T(8,128)(2,1)S(1)} %get-tuple-element.50), channel_id=1, source_target_pairs={{0,4},{2,6},{4,0},{6,2},{1,5},{3,7},{5,1},{7,3},{8,12},{10,14},{12... | collective-permute-start | bytes 1179656 | tf_op jit(solution)/shard_map/ppermute | solution.py:26
  65.8 9.1 %collective-permute-done.16.r1 = bf16[192,1024]{1,0:T(8,128)(2,1)S(1)} collective-permute-done((bf16[192,1024]{1,0:T(8,128)(2,1)S(1)}, bf16[192,1024]{1,0:T(8,128)(2,1)S(1)}, u32[]{:S(2)}, u32[]{:S(2)}) %collective-permute-start.16) | collective-permute-done | bytes 393248 | tf_op jit(solution)/shard_map/ppermute | solution.py:26
  76.8 7.3 %collective-permute-done.18.r3 = bf16[192,1024]{1,0:T(8,128)(2,1)S(1)} collective-permute-done((bf16[192,1024]{1,0:T(8,128)(2,1)S(1)}, bf16[192,1024]{1,0:T(8,128)(2,1)S(1)}, u32[]{:S(2)}, u32[]{:S(2)}) %collective-permute-start.18) | collective-permute-done | bytes 393248 | tf_op jit(solution)/shard_map/ppermute | solution.py:26
  86.4 2.0 %collective-permute-start.24 = (bf16[192,512]{1,0:T(8,128)(2,1)S(1)}, bf16[192,512]{1,0:T(8,128)(2,1)S(1)}, u32[]{:S(2)}, u32[]{:S(2)}) collective-permute-start(bf16[192,512]{1,0:T(8,128)(2,1)S(1)} %get-tuple-element.55), channel_id=1, source_target_pairs={{4,0},{6,2},{0,4},{2,6},{5,1},{7,3},{1,5},{3,7},{12,8},{14,10},{8,... | collective-permute-start | bytes 589832 | tf_op jit(solution)/shard_map/ppermute | solution.py:21
  88.5 3.2 %collective-permute-start.21 = (bf16[192,512]{1,0:T(8,128)(2,1)S(1)}, bf16[192,512]{1,0:T(8,128)(2,1)S(1)}, u32[]{:S(2)}, u32[]{:S(2)}) collective-permute-start(bf16[192,512]{1,0:T(8,128)(2,1)S(1)} %get-tuple-element.53), channel_id=1, source_target_pairs={{6,0},{0,2},{2,4},{4,6},{7,1},{1,3},{3,5},{5,7},{14,8},{8,10},{10,... | collective-permute-start | bytes 589832 | tf_op jit(solution)/shard_map/ppermute | solution.py:21
  93.1 3.3 %collective-permute-start.19 = (bf16[192,512]{1,0:T(8,128)(2,1)S(1)}, bf16[192,512]{1,0:T(8,128)(2,1)S(1)}, u32[]{:S(2)}, u32[]{:S(2)}) collective-permute-start(bf16[192,512]{1,0:T(8,128)(2,1)S(1)} %get-tuple-element.53), channel_id=1, source_target_pairs={{2,0},{4,2},{6,4},{0,6},{3,1},{5,3},{7,5},{1,7},{10,8},{12,10},{14... | collective-permute-start | bytes 589832 | tf_op jit(solution)/shard_map/ppermute | solution.py:21
  96.4 5.3 %collective-permute-done.23 = bf16[192,512]{1,0:T(8,128)(2,1)S(1)} collective-permute-done((bf16[192,512]{1,0:T(8,128)(2,1)S(1)}, bf16[192,512]{1,0:T(8,128)(2,1)S(1)}, u32[]{:S(2)}, u32[]{:S(2)}) %collective-permute-start.23) | collective-permute-done | bytes 196640 | tf_op jit(solution)/shard_map/ppermute | solution.py:21
  102.0 2.2 %collective-permute-done.20 = bf16[192,512]{1,0:T(8,128)(2,1)S(1)} collective-permute-done((bf16[192,512]{1,0:T(8,128)(2,1)S(1)}, bf16[192,512]{1,0:T(8,128)(2,1)S(1)}, u32[]{:S(2)}, u32[]{:S(2)}) %collective-permute-start.20) | collective-permute-done | bytes 196640 | tf_op jit(solution)/shard_map/ppermute | solution.py:21
  104.2 2.2 %collective-permute-done.19 = bf16[192,512]{1,0:T(8,128)(2,1)S(1)} collective-permute-done((bf16[192,512]{1,0:T(8,128)(2,1)S(1)}, bf16[192,512]{1,0:T(8,128)(2,1)S(1)}, u32[]{:S(2)}, u32[]{:S(2)}) %collective-permute-start.19) | collective-permute-done | bytes 196640 | tf_op jit(solution)/shard_map/ppermute | solution.py:21
  106.6 3.0 %shard_map.89 = (f32[4,8,48,1024]{3,2,1,0:T(8,128)S(1)}, bf16[4,2,192,512]{3,2,1,0:T(8,128)(2,1)S(1)}) custom-call(s32[4]{0:T(128)S(1)} %pad_add_fusion.pos, bf16[4,192,512]{2,1,0:T(8,128)(2,1)S(1)} %pad_maximum_fusion.1.refs_0_, bf16[4,192,512]{2,1,0:T(8,128)(2,1)S(1)} %collective-permute-done.26.refs_1_, bf16[1024,1024]{1,0:T(8,128)(2,1)S(1)} %get-tuple-element.54.refs_2_), custom_call_target="tpu_custom_call" | custom-call | flops 1610612736 | bytes 11534336 | tf_op jit(solution)/shard_map/pallas_call | solution.py:31
  109.6 4.4 %shard_map.90 = (f32[4,2,48,512]{3,2,1,0:T(8,128)S(1)}, f32[4,2,48,512]{3,2,1,0:T(8,128)S(1)}, bf16[4,2,48,512]{3,2,1,0:T(8,128)(2,1)S(1)}, f32[4,2,48,512]{3,2,...) custom-call(s32[4]{0:T(128)S(1)} %pad_add_fusion.pos, ...), custom_call_target="tpu_custom_call" | custom-call | flops 1610612736 | bytes 20185088 | tf_op jit(solution)/shard_map/pallas_call | solution.py:31
  115.3 3.7 %collective-permute-start.29 = (bf16[2,2,48,512]{3,2,1,0:T(8,128)(2,1)S(1)}, bf16[2,2,48,512]{3,2,1,0:T(8,128)(2,1)S(1)}, u32[]{:S(2)}, u32[]{:S(2)}) collective-permute-start(bf16[2,2,48,512]{3,2,1,0:T(8,128)(2,1)S(1)} %get-tuple-element.80), channel_id=1, source_target_pairs={{0,56},{8,0},{16,8},{24,16},{32,24},{40,32},{48,40},{56,48},{1,57}... | collective-permute-start | bytes 589832 | tf_op jit(solution)/shard_map/ppermute | solution.py:26
  121.7 2.2 %collective-permute-start.34 = (bf16[4,2,48,512]{3,2,1,0:T(8,128)(2,1)S(1)}, bf16[4,2,48,512]{3,2,1,0:T(8,128)(2,1)S(1)}, u32[]{:S(2)}, u32[]{:S(2)}) collective-permute-start(bf16[4,2,48,512]{3,2,1,0:T(8,128)(2,1)S(1)} %pad_maximum_fusion.7), channel_id=1, source_target_pairs={{0,192},{64,0},{128,64},{192,128},{1,193},{65,1},{129,65},{193,129... | collective-permute-start | bytes 1179656 | tf_op jit(solution)/shard_map/ppermute | solution.py:26
  123.8 3.0 %collective-permute-done.31 = bf16[2,2,48,512]{3,2,1,0:T(8,128)(2,1)S(1)} collective-permute-done((bf16[2,2,48,512]{3,2,1,0:T(8,128)(2,1)S(1)}, bf16[2,2,48,512]{3,2,1,0:T(8,128)(2,1)S(1)}, u32[]{:S(2)}, u32[]{:S(2)}) %collective-permute-start.31) | collective-permute-done | bytes 196640 | tf_op jit(solution)/shard_map/ppermute | solution.py:26
  129.4 8.9 %shard_map.91 = bf16[1024,1024]{1,0:T(8,128)(2,1)} custom-call(s32[32]{0:T(128)S(1)} %get-tuple-element.84.rows, s32[32]{0:T(128)S(1)} %get-tuple-element.83.cols, s32[1]{0:T(128)} %bitcast.60.count, bf16[4,8,48,1024]{3,2,1,0:T(8,128)(2,1)S(1)} %get-tuple-element.66.toks, bf16[4,2,192,1024]{3,2,1,0:T(8,128)(2,1)S(1)} %get-tuple-element.67.grads), custom_call_target="tpu_custom_call" | custom-call | flops 3221225472 | bytes 8388608 | tf_op jit(solution)/shard_map/pallas_call | solution.py:31
  140.0 3.1 %collective-permute-start.37 = (bf16[2,48,512]{2,1,0:T(8,128)(2,1)S(1)}, bf16[2,48,512]{2,1,0:T(8,128)(2,1)S(1)}, u32[]{:S(2)}, u32[]{:S(2)}) collective-permute-start(bf16[2,48,512]{2,1,0:T(8,128)(2,1)S(1)} %get-tuple-element.75), channel_id=1, source_target_pairs={{0,192},{64,0},{128,64},{192,128},{1,193},{65,1},{129,65},{193,129... | collective-permute-start | bytes 294920 | tf_op jit(solution)/shard_map/ppermute | solution.py:26
  144.5 3.2 %collective-permute-start.40 = (bf16[2,48,512]{2,1,0:T(8,128)(2,1)S(1)}, bf16[2,48,512]{2,1,0:T(8,128)(2,1)S(1)}, u32[]{:S(2)}, u32[]{:S(2)}) collective-permute-start(bf16[2,48,512]{2,1,0:T(8,128)(2,1)S(1)} %get-tuple-element.72), channel_id=1, source_target_pairs={{0,56},{8,0},{16,8},{24,16},{32,24},{40,32},{48,40},{56,48},{1,57}... | collective-permute-start | bytes 294920 | tf_op jit(solution)/shard_map/ppermute | solution.py:26
  150.6 4.7 %collective-permute-done.39 = bf16[2,48,512]{2,1,0:T(8,128)(2,1)S(1)} collective-permute-done((bf16[2,48,512]{2,1,0:T(8,128)(2,1)S(1)}, bf16[2,48,512]{2,1,0:T(8,128)(2,1)S(1)}, u32[]{:S(2)}, u32[]{:S(2)}) %collective-permute-start.39) | collective-permute-done | bytes 98336 | tf_op jit(solution)/shard_map/ppermute | solution.py:26
  155.4 3.7 %collective-permute-start.41 = (bf16[48,1024]{1,0:T(8,128)(2,1)S(1)}, bf16[48,1024]{1,0:T(8,128)(2,1)S(1)}, u32[]{:S(2)}, u32[]{:S(2)}) collective-permute-start(bf16[48,1024]{1,0:T(8,128)(2,1)S(1)} %fusion.10), channel_id=1, source_target_pairs={{0,32},{8,40},{16,48},{24,56},{32,0},{40,8},{48,16},{56,24},{1,33}... | collective-permute-start | bytes 294920 | tf_op jit(solution)/shard_map/ppermute | solution.py:26
  159.1 5.2 %collective-permute-done.41 = bf16[48,1024]{1,0:T(8,128)(2,1)S(1)} collective-permute-done((bf16[48,1024]{1,0:T(8,128)(2,1)S(1)}, bf16[48,1024]{1,0:T(8,128)(2,1)S(1)}, u32[]{:S(2)}, u32[]{:S(2)}) %collective-permute-start.41) | collective-permute-done | bytes 98336 | tf_op jit(solution)/shard_map/ppermute | solution.py:26
  (102 shorter events, 36.6 us)
Async XLA Ops:
  0.7 10.4 %collective-permute-start = (bf16[48,1024]{1,0:T(8,128)(2,1)}, bf16[48,1024]{1,0:T(8,128)(2,1)S(1)}, u32[]{:S(2)}, u32[]{:S(2)}) collective-permute-start(bf16[48,1024]{1,0:T(8,128)(2,1)} %param.6), channel_id=1, source_target_pairs={{32,0},{40,8},{48,16},{56,24},{0,32},{8,40},{16,48},{24,56},{33,1}... | collective-permute-start | bytes 294920 | tf_op jit(solution)/shard_map/ppermute | solution.py:21
  11.9 13.2 %collective-permute-start.6 = (bf16[2,48,512]{2,1,0:T(8,128)(2,1)S(1)}, bf16[2,48,512]{2,1,0:T(8,128)(2,1)S(1)}, u32[]{:S(2)}, u32[]{:S(2)}) collective-permute-start(bf16[2,48,512]{2,1,0:T(8,128)(2,1)S(1)} %get-tuple-element.41), channel_id=1, source_target_pairs={{56,0},{0,8},{8,16},{16,24},{24,32},{32,40},{40,48},{48,56},{57,1}... | collective-permute-start | bytes 294920 | tf_op jit(solution)/shard_map/ppermute | solution.py:21
  14.4 12.0 %collective-permute-start.5 = (bf16[2,48,512]{2,1,0:T(8,128)(2,1)S(1)}, bf16[2,48,512]{2,1,0:T(8,128)(2,1)S(1)}, u32[]{:S(2)}, u32[]{:S(2)}) collective-permute-start(bf16[2,48,512]{2,1,0:T(8,128)(2,1)S(1)} %get-tuple-element.41), channel_id=1, source_target_pairs={{16,0},{24,8},{32,16},{40,24},{48,32},{56,40},{0,48},{8,56},{17,1}... | collective-permute-start | bytes 294920 | tf_op jit(solution)/shard_map/ppermute | solution.py:21
  18.7 7.8 %collective-permute-start.4 = (bf16[2,48,512]{2,1,0:T(8,128)(2,1)S(1)}, bf16[2,48,512]{2,1,0:T(8,128)(2,1)S(1)}, u32[]{:S(2)}, u32[]{:S(2)}) collective-permute-start(bf16[2,48,512]{2,1,0:T(8,128)(2,1)S(1)} %get-tuple-element.41), channel_id=1, source_target_pairs={{8,0},{16,8},{24,16},{32,24},{40,32},{48,40},{56,48},{0,56},{9,1},... | collective-permute-start | bytes 294920 | tf_op jit(solution)/shard_map/ppermute | solution.py:21
  29.8 9.4 %collective-permute-start.13 = (bf16[4,2,48,512]{3,2,1,0:T(8,128)(2,1)S(1)}, bf16[4,2,48,512]{3,2,1,0:T(8,128)(2,1)S(1)}, u32[]{:S(2)}, u32[]{:S(2)}) collective-permute-start(bf16[4,2,48,512]{3,2,1,0:T(8,128)(2,1)S(1)} %pad_maximum_fusion.3.refs_5_), channel_id=1, source_target_pairs={{192,0},{0,64},{64,128},{128,192},{193,1},{1,65},{65,129},{129,193... | collective-permute-start | bytes 1179656 | tf_op jit(solution)/shard_map/ppermute | solution.py:21
  30.5 8.8 %collective-permute-start.11 = (bf16[4,2,48,512]{3,2,1,0:T(8,128)(2,1)S(1)}, bf16[4,2,48,512]{3,2,1,0:T(8,128)(2,1)}, u32[]{:S(2)}, u32[]{:S(2)}) collective-permute-start(bf16[4,2,48,512]{3,2,1,0:T(8,128)(2,1)S(1)} %pad_maximum_fusion.3.refs_5_), channel_id=1, source_target_pairs={{64,0},{128,64},{192,128},{0,192},{65,1},{129,65},{193,129},{1,193... | collective-permute-start | bytes 1179656 | tf_op jit(solution)/shard_map/ppermute | solution.py:21
  33.1 10.4 %collective-permute-start.9 = (bf16[4,2,48,512]{3,2,1,0:T(8,128)(2,1)S(1)}, bf16[4,2,48,512]{3,2,1,0:T(8,128)(2,1)}, u32[]{:S(2)}, u32[]{:S(2)}) collective-permute-start(bf16[4,2,48,512]{3,2,1,0:T(8,128)(2,1)S(1)} %pad_maximum_fusion.2.refs_0_), channel_id=1, source_target_pairs={{56,0},{0,8},{8,16},{16,24},{24,32},{32,40},{40,48},{48,56},{57,1}... | collective-permute-start | bytes 1179656 | tf_op jit(solution)/shard_map/ppermute | solution.py:21
  33.3 12.7 %collective-permute-start.7 = (bf16[4,2,48,512]{3,2,1,0:T(8,128)(2,1)S(1)}, bf16[4,2,48,512]{3,2,1,0:T(8,128)(2,1)}, u32[]{:S(2)}, u32[]{:S(2)}) collective-permute-start(bf16[4,2,48,512]{3,2,1,0:T(8,128)(2,1)S(1)} %pad_maximum_fusion.2.refs_0_), channel_id=1, source_target_pairs={{8,0},{16,8},{24,16},{32,24},{40,32},{48,40},{56,48},{0,56},{9,1},... | collective-permute-start | bytes 1179656 | tf_op jit(solution)/shard_map/ppermute | solution.py:21
  39.2 13.5 %collective-permute-start.14 = (bf16[2,2,48,512]{3,2,1,0:T(8,128)(2,1)S(1)}, bf16[2,2,48,512]{3,2,1,0:T(8,128)(2,1)S(1)}, u32[]{:S(2)}, u32[]{:S(2)}) collective-permute-start(bf16[2,2,48,512]{3,2,1,0:T(8,128)(2,1)S(1)} %slice.106), channel_id=1, source_target_pairs={{192,0},{0,64},{64,128},{128,192},{193,1},{1,65},{65,129},{129,193... | collective-permute-start | bytes 589832 | tf_op jit(solution)/shard_map/ppermute | solution.py:21
  40.2 12.4 %collective-permute-start.12 = (bf16[2,2,48,512]{3,2,1,0:T(8,128)(2,1)S(1)}, bf16[2,2,48,512]{3,2,1,0:T(8,128)(2,1)S(1)}, u32[]{:S(2)}, u32[]{:S(2)}) collective-permute-start(bf16[2,2,48,512]{3,2,1,0:T(8,128)(2,1)S(1)} %slice.105), channel_id=1, source_target_pairs={{64,0},{128,64},{192,128},{0,192},{65,1},{129,65},{193,129},{1,193... | collective-permute-start | bytes 589832 | tf_op jit(solution)/shard_map/ppermute | solution.py:21
  44.4 8.2 %collective-permute-start.10 = (bf16[2,2,48,512]{3,2,1,0:T(8,128)(2,1)S(1)}, bf16[2,2,48,512]{3,2,1,0:T(8,128)(2,1)S(1)}, u32[]{:S(2)}, u32[]{:S(2)}) collective-permute-start(bf16[2,2,48,512]{3,2,1,0:T(8,128)(2,1)S(1)} %slice.104), channel_id=1, source_target_pairs={{56,0},{0,8},{8,16},{16,24},{24,32},{32,40},{40,48},{48,56},{57,1}... | collective-permute-start | bytes 589832 | tf_op jit(solution)/shard_map/ppermute | solution.py:21
  62.8 12.0 %collective-permute-start.16 = (bf16[192,1024]{1,0:T(8,128)(2,1)S(1)}, bf16[192,1024]{1,0:T(8,128)(2,1)S(1)}, u32[]{:S(2)}, u32[]{:S(2)}) collective-permute-start(bf16[192,1024]{1,0:T(8,128)(2,1)S(1)} %get-tuple-element.49), channel_id=1, source_target_pairs={{0,2},{2,4},{4,6},{6,0},{1,3},{3,5},{5,7},{7,1},{8,10},{10,12},{12... | collective-permute-start | bytes 1179656 | tf_op jit(solution)/shard_map/ppermute | solution.py:26
  63.3 13.5 %collective-permute-start.17 = (bf16[192,1024]{1,0:T(8,128)(2,1)S(1)}, bf16[192,1024]{1,0:T(8,128)(2,1)S(1)}, u32[]{:S(2)}, u32[]{:S(2)}) collective-permute-start(bf16[192,1024]{1,0:T(8,128)(2,1)S(1)} %get-tuple-element.50), channel_id=1, source_target_pairs={{0,4},{2,6},{4,0},{6,2},{1,5},{3,7},{5,1},{7,3},{8,12},{10,14},{12... | collective-permute-start | bytes 1179656 | tf_op jit(solution)/shard_map/ppermute | solution.py:26
  65.8 18.3 %collective-permute-start.18 = (bf16[192,1024]{1,0:T(8,128)(2,1)S(1)}, bf16[192,1024]{1,0:T(8,128)(2,1)S(1)}, u32[]{:S(2)}, u32[]{:S(2)}) collective-permute-start(bf16[192,1024]{1,0:T(8,128)(2,1)S(1)} %get-tuple-element.51), channel_id=1, source_target_pairs={{0,6},{2,0},{4,2},{6,4},{1,7},{3,1},{5,3},{7,5},{8,14},{10,8},{12,... | collective-permute-start | bytes 1179656 | tf_op jit(solution)/shard_map/ppermute | solution.py:26
  85.3 7.8 %collective-permute-start.25 = (bf16[192,512]{1,0:T(8,128)(2,1)S(1)}, bf16[192,512]{1,0:T(8,128)(2,1)S(1)}, u32[]{:S(2)}, u32[]{:S(2)}) collective-permute-start(bf16[192,512]{1,0:T(8,128)(2,1)S(1)} %get-tuple-element.55), channel_id=1, source_target_pairs={{6,0},{0,2},{2,4},{4,6},{7,1},{1,3},{3,5},{5,7},{14,8},{8,10},{10,... | collective-permute-start | bytes 589832 | tf_op jit(solution)/shard_map/ppermute | solution.py:21
  86.4 10.0 %collective-permute-start.24 = (bf16[192,512]{1,0:T(8,128)(2,1)S(1)}, bf16[192,512]{1,0:T(8,128)(2,1)S(1)}, u32[]{:S(2)}, u32[]{:S(2)}) collective-permute-start(bf16[192,512]{1,0:T(8,128)(2,1)S(1)} %get-tuple-element.55), channel_id=1, source_target_pairs={{4,0},{6,2},{0,4},{2,6},{5,1},{7,3},{1,5},{3,7},{12,8},{14,10},{8,... | collective-permute-start | bytes 589832 | tf_op jit(solution)/shard_map/ppermute | solution.py:21
  88.4 13.3 %collective-permute-start.23 = (bf16[192,512]{1,0:T(8,128)(2,1)S(1)}, bf16[192,512]{1,0:T(8,128)(2,1)S(1)}, u32[]{:S(2)}, u32[]{:S(2)}) collective-permute-start(bf16[192,512]{1,0:T(8,128)(2,1)S(1)} %get-tuple-element.55), channel_id=1, source_target_pairs={{2,0},{4,2},{6,4},{0,6},{3,1},{5,3},{7,5},{1,7},{10,8},{12,10},{14... | collective-permute-start | bytes 589832 | tf_op jit(solution)/shard_map/ppermute | solution.py:21
  88.5 13.5 %collective-permute-start.21 = (bf16[192,512]{1,0:T(8,128)(2,1)S(1)}, bf16[192,512]{1,0:T(8,128)(2,1)S(1)}, u32[]{:S(2)}, u32[]{:S(2)}) collective-permute-start(bf16[192,512]{1,0:T(8,128)(2,1)S(1)} %get-tuple-element.53), channel_id=1, source_target_pairs={{6,0},{0,2},{2,4},{4,6},{7,1},{1,3},{3,5},{5,7},{14,8},{8,10},{10,... | collective-permute-start | bytes 589832 | tf_op jit(solution)/shard_map/ppermute | solution.py:21
  91.7 12.5 %collective-permute-start.20 = (bf16[192,512]{1,0:T(8,128)(2,1)S(1)}, bf16[192,512]{1,0:T(8,128)(2,1)S(1)}, u32[]{:S(2)}, u32[]{:S(2)}) collective-permute-start(bf16[192,512]{1,0:T(8,128)(2,1)S(1)} %get-tuple-element.53), channel_id=1, source_target_pairs={{4,0},{6,2},{0,4},{2,6},{5,1},{7,3},{1,5},{3,7},{12,8},{14,10},{8,... | collective-permute-start | bytes 589832 | tf_op jit(solution)/shard_map/ppermute | solution.py:21
  93.1 13.3 %collective-permute-start.19 = (bf16[192,512]{1,0:T(8,128)(2,1)S(1)}, bf16[192,512]{1,0:T(8,128)(2,1)S(1)}, u32[]{:S(2)}, u32[]{:S(2)}) collective-permute-start(bf16[192,512]{1,0:T(8,128)(2,1)S(1)} %get-tuple-element.53), channel_id=1, source_target_pairs={{2,0},{4,2},{6,4},{0,6},{3,1},{5,3},{7,5},{1,7},{10,8},{12,10},{14... | collective-permute-start | bytes 589832 | tf_op jit(solution)/shard_map/ppermute | solution.py:21
  114.2 7.4 %collective-permute-start.33 = (bf16[2,2,48,512]{3,2,1,0:T(8,128)(2,1)S(1)}, bf16[2,2,48,512]{3,2,1,0:T(8,128)(2,1)S(1)}, u32[]{:S(2)}, u32[]{:S(2)}) collective-permute-start(bf16[2,2,48,512]{3,2,1,0:T(8,128)(2,1)S(1)} %get-tuple-element.78), channel_id=1, source_target_pairs={{0,192},{64,0},{128,64},{192,128},{1,193},{65,1},{129,65},{193,129... | collective-permute-start | bytes 589832 | tf_op jit(solution)/shard_map/ppermute | solution.py:26
  115.2 13.5 %collective-permute-start.27 = (bf16[2,2,48,512]{3,2,1,0:T(8,128)(2,1)S(1)}, bf16[2,2,48,512]{3,2,1,0:T(8,128)(2,1)S(1)}, u32[]{:S(2)}, u32[]{:S(2)}) collective-permute-start(bf16[2,2,48,512]{3,2,1,0:T(8,128)(2,1)S(1)} %get-tuple-element.79), channel_id=1, source_target_pairs={{0,8},{8,16},{16,24},{24,32},{32,40},{40,48},{48,56},{56,0},{1,9},... | collective-permute-start | bytes 589832 | tf_op jit(solution)/shard_map/ppermute | solution.py:26
  115.3 11.8 %collective-permute-start.29 = (bf16[2,2,48,512]{3,2,1,0:T(8,128)(2,1)S(1)}, bf16[2,2,48,512]{3,2,1,0:T(8,128)(2,1)S(1)}, u32[]{:S(2)}, u32[]{:S(2)}) collective-permute-start(bf16[2,2,48,512]{3,2,1,0:T(8,128)(2,1)S(1)} %get-tuple-element.80), channel_id=1, source_target_pairs={{0,56},{8,0},{16,8},{24,16},{32,24},{40,32},{48,40},{56,48},{1,57}... | collective-permute-start | bytes 589832 | tf_op jit(solution)/shard_map/ppermute | solution.py:26
  118.9 7.9 %collective-permute-start.31 = (bf16[2,2,48,512]{3,2,1,0:T(8,128)(2,1)S(1)}, bf16[2,2,48,512]{3,2,1,0:T(8,128)(2,1)S(1)}, u32[]{:S(2)}, u32[]{:S(2)}) collective-permute-start(bf16[2,2,48,512]{3,2,1,0:T(8,128)(2,1)S(1)} %get-tuple-element.77), channel_id=1, source_target_pairs={{0,64},{64,128},{128,192},{192,0},{1,65},{65,129},{129,193},{193,1... | collective-permute-start | bytes 589832 | tf_op jit(solution)/shard_map/ppermute | solution.py:26
  121.7 16.6 %collective-permute-start.34 = (bf16[4,2,48,512]{3,2,1,0:T(8,128)(2,1)S(1)}, bf16[4,2,48,512]{3,2,1,0:T(8,128)(2,1)S(1)}, u32[]{:S(2)}, u32[]{:S(2)}) collective-permute-start(bf16[4,2,48,512]{3,2,1,0:T(8,128)(2,1)S(1)} %pad_maximum_fusion.7), channel_id=1, source_target_pairs={{0,192},{64,0},{128,64},{192,128},{1,193},{65,1},{129,65},{193,129... | collective-permute-start | bytes 1179656 | tf_op jit(solution)/shard_map/ppermute | solution.py:26
  127.0 11.4 %collective-permute-start.32 = (bf16[4,2,48,512]{3,2,1,0:T(8,128)(2,1)S(1)}, bf16[4,2,48,512]{3,2,1,0:T(8,128)(2,1)S(1)}, u32[]{:S(2)}, u32[]{:S(2)}) collective-permute-start(bf16[4,2,48,512]{3,2,1,0:T(8,128)(2,1)S(1)} %pad_maximum_fusion.6), channel_id=1, source_target_pairs={{0,64},{64,128},{128,192},{192,0},{1,65},{65,129},{129,193},{193,1... | collective-permute-start | bytes 1179656 | tf_op jit(solution)/shard_map/ppermute | solution.py:26
  127.2 11.4 %collective-permute-start.30 = (bf16[4,2,48,512]{3,2,1,0:T(8,128)(2,1)S(1)}, bf16[4,2,48,512]{3,2,1,0:T(8,128)(2,1)S(1)}, u32[]{:S(2)}, u32[]{:S(2)}) collective-permute-start(bf16[4,2,48,512]{3,2,1,0:T(8,128)(2,1)S(1)} %pad_maximum_fusion.5), channel_id=1, source_target_pairs={{0,56},{8,0},{16,8},{24,16},{32,24},{40,32},{48,40},{56,48},{1,57}... | collective-permute-start | bytes 1179656 | tf_op jit(solution)/shard_map/ppermute | solution.py:26
  128.8 10.8 %collective-permute-start.28 = (bf16[4,2,48,512]{3,2,1,0:T(8,128)(2,1)S(1)}, bf16[4,2,48,512]{3,2,1,0:T(8,128)(2,1)S(1)}, u32[]{:S(2)}, u32[]{:S(2)}) collective-permute-start(bf16[4,2,48,512]{3,2,1,0:T(8,128)(2,1)S(1)} %pad_maximum_fusion.4), channel_id=1, source_target_pairs={{0,8},{8,16},{16,24},{24,32},{32,40},{40,48},{48,56},{56,0},{1,9},... | collective-permute-start | bytes 1179656 | tf_op jit(solution)/shard_map/ppermute | solution.py:26
  139.8 7.9 %collective-permute-start.35 = (bf16[2,48,512]{2,1,0:T(8,128)(2,1)S(1)}, bf16[2,48,512]{2,1,0:T(8,128)(2,1)S(1)}, u32[]{:S(2)}, u32[]{:S(2)}) collective-permute-start(bf16[2,48,512]{2,1,0:T(8,128)(2,1)S(1)} %get-tuple-element.74), channel_id=1, source_target_pairs={{0,64},{64,128},{128,192},{192,0},{1,65},{65,129},{129,193},{193,1... | collective-permute-start | bytes 294920 | tf_op jit(solution)/shard_map/ppermute | solution.py:26
  140.0 7.7 %collective-permute-start.37 = (bf16[2,48,512]{2,1,0:T(8,128)(2,1)S(1)}, bf16[2,48,512]{2,1,0:T(8,128)(2,1)S(1)}, u32[]{:S(2)}, u32[]{:S(2)}) collective-permute-start(bf16[2,48,512]{2,1,0:T(8,128)(2,1)S(1)} %get-tuple-element.75), channel_id=1, source_target_pairs={{0,192},{64,0},{128,64},{192,128},{1,193},{65,1},{129,65},{193,129... | collective-permute-start | bytes 294920 | tf_op jit(solution)/shard_map/ppermute | solution.py:26
  147.7 7.6 %collective-permute-start.39 = (bf16[2,48,512]{2,1,0:T(8,128)(2,1)S(1)}, bf16[2,48,512]{2,1,0:T(8,128)(2,1)S(1)}, u32[]{:S(2)}, u32[]{:S(2)}) collective-permute-start(bf16[2,48,512]{2,1,0:T(8,128)(2,1)S(1)} %get-tuple-element.73), channel_id=1, source_target_pairs={{0,16},{8,24},{16,32},{24,40},{32,48},{40,56},{48,0},{56,8},{1,17}... | collective-permute-start | bytes 294920 | tf_op jit(solution)/shard_map/ppermute | solution.py:26
  155.4 8.9 %collective-permute-start.41 = (bf16[48,1024]{1,0:T(8,128)(2,1)S(1)}, bf16[48,1024]{1,0:T(8,128)(2,1)S(1)}, u32[]{:S(2)}, u32[]{:S(2)}) collective-permute-start(bf16[48,1024]{1,0:T(8,128)(2,1)S(1)} %fusion.10), channel_id=1, source_target_pairs={{0,32},{8,40},{16,48},{24,56},{32,0},{40,8},{48,16},{56,24},{1,33}... | collective-permute-start | bytes 294920 | tf_op jit(solution)/shard_map/ppermute | solution.py:26
  (14 other events, 220.1 us)

commit v7 on v4

--- a/solution.py
+++ b/solution.py
@@ -68,32 +68,21 @@
     return (pos[1] + i + 4 * hi + 8) % 8
 
 
-def z_step(i, j):
-    return -2 if i == 2 and j >= 2 else STEPS[i]
-
-
-def at_step(pieces, step, k):
-    if step == 2:
-        return pieces[2 + k // 2], k % 2
-    return pieces[step + step // 3], k
-
-
 def up_body(pos, *refs):
-    a3, b3, w = refs[:5], refs[5:10], refs[10]
-    keep, send, toks, acc = refs[11:]
+    a3, b3, w = refs[:4], refs[4:8], refs[8]
+    keep, send, toks, acc = refs[9:]
     core = pos[3]
     cut = a3[0].shape[-1]
     back = pos[0] - pos[2] + 4
     for j in range(4):
         d = (j + back) % 4
         for i in range(4):
-            a_ref, a_at = at_step(a3, i, j)
-            b_ref, b_at = at_step(b3, j, i)
-            for hi in range(2):
+
+            @pl.loop(0, 2)
+            def _(hi, i=i, j=j, d=d):
                 at = zpos(pos, STEPS[i], hi)
-                low = zpos(pos, z_step(i, j), hi)
-                toks[d, low, :, :cut] = a_ref[a_at, hi]
-                toks[d, at, :, cut:] = b_ref[b_at, hi]
+                toks[d, at, :, :cut] = a3[i][j, hi]
+                toks[d, at, :, cut:] = b3[j][i, hi]
 
     @pl.loop(0, 4)
     def _(d):
@@ -152,8 +141,7 @@
 
             @pl.loop(0, 4)
             def _(j, k=k, hi=hi):
-                step = jnp.where(j >= 2, z_step(k, 2), z_step(k, 0))
-                piece = acc[j, zpos(pos, step, hi), :, :cut]
+                piece = acc[j, zpos(pos, STEPS[k], hi), :, :cut]
                 a3[k][j, hi] = piece.astype(a3[k].dtype)
 
             @pl.loop(0, 4)
@@ -165,22 +153,22 @@
 def add_body(cols, keep, recv, *out):
     for d in range(4):
 
-        @pl.loop(0, keep.shape[1] // 32)
+        @pl.loop(0, keep.shape[1] // 16)
         def _(i, d=d):
-            at = pl.ds(pl.multiple_of(i * 32, 32), 32)
+            at = pl.ds(pl.multiple_of(i * 16, 16), 16)
             total = keep[d, at, cols] + recv[d, at, cols].astype(F32)
             out[d][at] = total.astype(out[d].dtype)
 
 
-def act_body(own, r1, r2, r3, cot, hidden, grad_pre):
-    @pl.loop(0, own.shape[0] // 32)
+def act_body(cols, own, r1, r2, r3, cot, hidden, grad_pre):
+    @pl.loop(0, own.shape[0] // 16)
     def _(i):
-        at = pl.ds(pl.multiple_of(i * 32, 32), 32)
+        at = pl.ds(pl.multiple_of(i * 16, 16), 16)
         pre_act = own[at] + r1[at].astype(F32) + r2[at].astype(F32) + r3[at].astype(F32)
         gate = jax.nn.sigmoid(pre_act)
         hidden[at] = (pre_act * gate).astype(BF16)
         slope = gate * (1.0 + pre_act * (1.0 - gate))
-        grad_pre[at] = (cot[at].astype(F32) * slope).astype(BF16)
+        grad_pre[at] = (cot[at, cols].astype(F32) * slope).astype(BF16)
 
 
 def wgrad_body(rows, cols, count, toks, grads, out, acc):
@@ -211,10 +199,9 @@
 
 
 def ring_gather(piece, axis):
-    ahead, behind = from_ahead(piece, axis, 1), from_ahead(piece, axis, -1)
-    half = piece.shape[0] // 2
-    far = [from_ahead(ahead[:half], axis, 1), from_ahead(behind[half:], axis, -1)]
-    return [piece, ahead] + far + [behind]
+    ahead = from_ahead(piece, axis, 1)
+    behind = from_ahead(piece, axis, -1)
+    return [piece, ahead, from_ahead(ahead, axis, 1), behind]
 
 
 def gather_tokens(tokens):
@@ -232,12 +219,10 @@
     return call(body, [(shape, F32)] + [(shape, BF16)] * 3, [], [keep, recv])
 
 
-def shares(sends):
-    return [to_ahead(s, "x", d + 1) for d, s in enumerate(sends)]
-
-
-def activation(own, recvs, cot):
-    return call(act_body, [(own.shape, BF16)] * 2, [], [own] + recvs + [cot])
+def activation(own, sends, cot, cols):
+    recvs = [to_ahead(s, "x", d + 1) for d, s in enumerate(sends)]
+    body = functools.partial(act_body, cols)
+    return call(body, [(own.shape, BF16)] * 2, [], [own] + recvs + [cot])
 
 
 def gather_grads(grad_pre):
@@ -253,13 +238,9 @@
 
 
 def ring_reduce(own, ahead, far, behind, axis):
-    half = own.shape[0] // 2
-    lo = to_ahead(far[:half], axis, 1).astype(F32)
-    hi = to_ahead(far[half:], axis, -1).astype(F32)
-    ahead = jnp.concatenate([ahead[:half] + lo, ahead[half:]])
-    behind = jnp.concatenate([behind[:half], behind[half:] + hi])
-    total = own + to_ahead(ahead.astype(BF16), axis, 1).astype(F32)
-    return total + to_ahead(behind.astype(BF16), axis, -1).astype(F32)
+    through = to_ahead(far, axis, 1).astype(F32)
+    total = own + to_ahead(behind, axis, -1).astype(F32)
+    return total + to_ahead((ahead + through).astype(BF16), axis, 1).astype(F32)
 
 
 def middle(a3, b3, wm, flipped, pos, cot):
@@ -280,10 +261,12 @@
         [VM((2, rows, width), F32)],
     )
     recv = to_ahead(send, "core", 1)
-    own1, *sends1 = partial_sums(keep, recv, slice(0, cut))
-    own2, *sends2 = partial_sums(keep, recv, slice(cut, width))
-    hidden1, grad1 = activation(own1, shares(sends1), cot[:, :cut])
-    hidden2, grad2 = activation(own2, shares(sends2), cot[:, cut:])
+    cols1, cols2 = slice(0, cut), slice(cut, width)
+    own1, *sends1 = partial_sums(keep, recv, cols1)
+    own2, *sends2 = partial_sums(keep, recv, cols2)
+    hidden1, grad1 = activation(own1, sends1, cot, cols1)
+    hidden2, grad2 = activation(own2, sends2, cot, cols2)
+    hidden = jnp.concatenate([hidden1, hidden2], axis=1)
     parts1 = gather_grads(grad1)
     parts2 = gather_grads(grad2)
     g_shape = ((4, 2, rows, cut), BF16)
@@ -293,7 +276,7 @@
         back_first_body, [(sums, F32), g_shape], [pos], parts1 + [flipped], flops, [sems]
     )
     shape = (4, 2, rows // 4, depth // 2)
-    outs = [(shape, d) for d in (F32, F32, BF16, F32)]
+    outs = [(shape, d) for d in (F32, F32, BF16, BF16)]
     *sends, grads = call(
         back_second_body,
         outs + outs + [((4, 2, rows, width), BF16)],
@@ -302,19 +285,18 @@
         flops,
         [VM(sums, F32), sems, pltpu.SemaphoreType.DMA],
     )
-    hidden = jnp.concatenate([hidden1, hidden2], axis=1)
     return hidden, sends, toks, grads
 
 
-def reduce_inputs(sends):
+def reduce_inputs(sends, weight_grad):
     a2 = ring_reduce(*sends[:4], "z")
     b2 = ring_reduce(*sends[4:], "y")
-    a2, b2 = lax.optimization_barrier((a2, b2))
+    a2, b2, weight_grad = lax.optimization_barrier((a2, b2, weight_grad))
     a1 = reduce_four(a2[0], a2[1:], "y")
     b1 = reduce_four(b2[0], b2[1:], "z")
     both = jnp.concatenate([a1, b1], axis=-1)
     total = both[0] + to_ahead(both[1].astype(BF16), "z", 4).astype(F32)
-    return total.astype(BF16)
+    return total.astype(BF16), weight_grad
 
 
 def on_device(tokens, weight, tile_rows, tile_cols, tile_count, hidden_cotangent):
@@ -337,7 +319,7 @@
         2 * 1536 * weight.size,
         [VM(weight.shape, F32)],
     )
-    input_grad = reduce_inputs(sends)
+    input_grad, weight_grad = reduce_inputs(sends, weight_grad)
     return hidden, input_grad, weight_grad
 
 

time: 178 us -> 157 us (0.88)
  the two profiles are of different devices: /device:TPU:10 before, /device:TPU:6 now
where the time goes in v7:
time: 157 us; the launch traced here: 154 us
  starting transfers between devices  73.5 us (47%)
  waiting for transfers between devices  48.4 us (31%)
  Pallas kernels  24.9 us (16%)
  other arithmetic  4.17 us (3%)
  local copies, waits for them, and re-layouts  1.64 us (1%)
    ppermute x19, starting transfers between devices, from_ahead(): return lax.ppermute(value, axis, [((i + k) % n, i) for i in range(n)])  39.1 us
    ppermute x22, starting transfers between devices, to_ahead(): return lax.ppermute(value, axis, [(i, (i + k) % n) for i in range(n)])  34.4 us
    ppermute x22, waiting for transfers between devices, to_ahead(): return lax.ppermute(value, axis, [(i, (i + k) % n) for i in range(n)])  28.3 us
    pallas_call x9, Pallas kernels, call(): pl.pallas_call(body, out_shape=outs, in_specs=[pl.BlockSpec(memory_space=...  24.9 us
    ppermute x19, waiting for transfers between devices, from_ahead(): return lax.ppermute(value, axis, [((i + k) % n, i) for i in range(n)])  20.1 us
  transfers between devices with their start and end apart: 41, of which 21 were waited for; matrix products, arithmetic and copies ran while one was open for 2% of the time, Pallas kernels for 10%

profile of v7, /device:TPU:6, one launch (start us, length us, event | category | flops | bytes accessed | tf_op | source)
XLA Modules:
  0.0 154.2 jit_solution(11049099775432648504)
XLA Ops:
  0.6 7.3 %collective-permute-start = (bf16[48,1024]{1,0:T(8,128)(2,1)}, bf16[48,1024]{1,0:T(8,128)(2,1)S(1)}, u32[]{:S(2)}, u32[]{:S(2)}) collective-permute-start(bf16[48,1024]{1,0:T(8,128)(2,1)} %param.6), channel_id=1, source_target_pairs={{32,0},{40,8},{48,16},{56,24},{0,32},{8,40},{16,48},{24,56},{33,1}... | collective-permute-start | bytes 294920 | tf_op jit(solution)/shard_map/ppermute | solution.py:23
  7.9 3.1 %collective-permute-done = bf16[48,1024]{1,0:T(8,128)(2,1)S(1)} collective-permute-done((bf16[48,1024]{1,0:T(8,128)(2,1)}, bf16[48,1024]{1,0:T(8,128)(2,1)S(1)}, u32[]{:S(2)}, u32[]{:S(2)}) %collective-permute-start) | collective-permute-done | bytes 98336 | tf_op jit(solution)/shard_map/ppermute | solution.py:23
  11.9 2.6 %collective-permute-start.6 = (bf16[2,48,512]{2,1,0:T(8,128)(2,1)S(1)}, bf16[2,48,512]{2,1,0:T(8,128)(2,1)S(1)}, u32[]{:S(2)}, u32[]{:S(2)}) collective-permute-start(bf16[2,48,512]{2,1,0:T(8,128)(2,1)S(1)} %get-tuple-element.46), channel_id=1, source_target_pairs={{56,0},{0,8},{8,16},{16,24},{24,32},{32,40},{40,48},{48,56},{57,1}... | collective-permute-start | bytes 294920 | tf_op jit(solution)/shard_map/ppermute | solution.py:23
  14.4 4.2 %collective-permute-start.5 = (bf16[2,48,512]{2,1,0:T(8,128)(2,1)S(1)}, bf16[2,48,512]{2,1,0:T(8,128)(2,1)S(1)}, u32[]{:S(2)}, u32[]{:S(2)}) collective-permute-start(bf16[2,48,512]{2,1,0:T(8,128)(2,1)S(1)} %get-tuple-element.46), channel_id=1, source_target_pairs={{16,0},{24,8},{32,16},{40,24},{48,32},{56,40},{0,48},{8,56},{17,1}... | collective-permute-start | bytes 294920 | tf_op jit(solution)/shard_map/ppermute | solution.py:23
  18.6 1.9 %collective-permute-start.4 = (bf16[2,48,512]{2,1,0:T(8,128)(2,1)S(1)}, bf16[2,48,512]{2,1,0:T(8,128)(2,1)S(1)}, u32[]{:S(2)}, u32[]{:S(2)}) collective-permute-start(bf16[2,48,512]{2,1,0:T(8,128)(2,1)S(1)} %get-tuple-element.46), channel_id=1, source_target_pairs={{8,0},{16,8},{24,16},{32,24},{40,32},{48,40},{56,48},{0,56},{9,1},... | collective-permute-start | bytes 294920 | tf_op jit(solution)/shard_map/ppermute | solution.py:23
  22.1 2.9 %collective-permute-start.2 = (bf16[2,48,512]{2,1,0:T(8,128)(2,1)S(1)}, bf16[2,48,512]{2,1,0:T(8,128)(2,1)S(1)}, u32[]{:S(2)}, u32[]{:S(2)}) collective-permute-start(bf16[2,48,512]{2,1,0:T(8,128)(2,1)S(1)} %get-tuple-element.42), channel_id=1, source_target_pairs={{128,0},{192,64},{0,128},{64,192},{129,1},{193,65},{1,129},{65,193... | collective-permute-start | bytes 294920 | tf_op jit(solution)/shard_map/ppermute | solution.py:23
  29.9 2.4 %collective-permute-start.10 = (bf16[4,2,48,512]{3,2,1,0:T(8,128)(2,1)S(1)}, bf16[4,2,48,512]{3,2,1,0:T(8,128)(2,1)S(1)}, u32[]{:S(2)}, u32[]{:S(2)}) collective-permute-start(bf16[4,2,48,512]{3,2,1,0:T(8,128)(2,1)S(1)} %pad_maximum_fusion.3.refs_4_), channel_id=1, source_target_pairs={{64,0},{128,64},{192,128},{0,192},{65,1},{129,65},{193,129},{1,193... | collective-permute-start | bytes 1179656 | tf_op jit(solution)/shard_map/ppermute | solution.py:23
  34.5 4.8 %collective-permute-done.10.refs_5_ = bf16[4,2,48,512]{3,2,1,0:T(8,128)(2,1)S(1)} collective-permute-done((bf16[4,2,48,512]{3,2,1,0:T(8,128)(2,1)S(1)}, bf16[4,2,48,512]{3,2,1,0:T(8,128)(2,1)S(1)}, u32[]{:S(2)}, u32[]{:S(2)}) %collective-permute-start.10) | collective-permute-done | bytes 393248 | tf_op jit(solution)/shard_map/ppermute | solution.py:23
  39.3 2.3 %collective-permute-start.11 = (bf16[4,2,48,512]{3,2,1,0:T(8,128)(2,1)S(1)}, bf16[4,2,48,512]{3,2,1,0:T(8,128)(2,1)S(1)}, u32[]{:S(2)}, u32[]{:S(2)}) collective-permute-start(bf16[4,2,48,512]{3,2,1,0:T(8,128)(2,1)S(1)} %collective-permute-done.10.refs_5_), channel_id=1, source_target_pairs={{64,0},{128,64},{192,128},{0,192},{65,1},{129,65},{193,129},{1,193... | collective-permute-start | bytes 1179656 | tf_op jit(solution)/shard_map/ppermute | solution.py:23
  41.6 2.3 %collective-permute-start.8 = (bf16[4,2,48,512]{3,2,1,0:T(8,128)(2,1)S(1)}, bf16[4,2,48,512]{3,2,1,0:T(8,128)(2,1)S(1)}, u32[]{:S(2)}, u32[]{:S(2)}) collective-permute-start(bf16[4,2,48,512]{3,2,1,0:T(8,128)(2,1)S(1)} %collective-permute-done.7.refs_1_), channel_id=1, source_target_pairs={{8,0},{16,8},{24,16},{32,24},{40,32},{48,40},{56,48},{0,56},{9,1},... | collective-permute-start | bytes 1179656 | tf_op jit(solution)/shard_map/ppermute | solution.py:23
  46.9 2.0 %shard_map.85 = (bf16[1024,1024]{1,0:T(8,128)(2,1)S(1)}, bf16[1024,1024]{1,0:T(8,128)(2,1)S(1)}) custom-call(s32[32]{0:T(128)S(1)} %get-tuple-element.90.rows, s32[32]{0:T(128)S(1)} %get-tuple-element.89.cols, s32[1]{0:T(128)} %bitcast.59.count, bf16[1024,1024]{1,0:T(8,128)(2,1)S(1)} %copy-done), custom_call_target="tpu_custom_call" | custom-call | bytes 6291456 | tf_op jit(solution)/shard_map/pallas_call | solution.py:33
  49.4 5.4 %shard_map.86 = (f32[4,192,1024]{2,1,0:T(8,128)S(1)}, bf16[4,192,1024]{2,1,0:T(8,128)(2,1)S(1)}, bf16[4,8,48,1024]{3,2,1,0:T(8,128)(2,1)S(1)}) custom-call(s32[4]{0:T(128)S(1)} %pad_add_fusion.pos, bf16[4,2,48,512]{3,2,1,0:T(8,128)(2,1)S(1)} %pad_maximum_fusion.2.refs_0_, bf16[4,2,48,512]{3,2,1,0:T(8,128)(2,1)S(1)} %collective-permute-done.7.refs_1_, ...), custom_call_target="tpu_custom_call" | custom-call | flops 3221225472 | bytes 13107200 | tf_op jit(solution)/shard_map/pallas_call | solution.py:33
  55.0 3.4 %collective-permute-done.13.recv = bf16[4,192,1024]{2,1,0:T(8,128)(2,1)S(1)} collective-permute-done((bf16[4,192,1024]{2,1,0:T(8,128)(2,1)S(1)}, bf16[4,192,1024]{2,1,0:T(8,128)(2,1)S(1)}, u32[]{:S(2)}, u32[]{:S(2)}) %collective-permute-start.13) | collective-permute-done | bytes 1572896 | tf_op jit(solution)/shard_map/ppermute | solution.py:28
  59.5 3.1 %collective-permute-start.15 = (bf16[192,512]{1,0:T(8,128)(2,1)S(1)}, bf16[192,512]{1,0:T(8,128)(2,1)S(1)}, u32[]{:S(2)}, u32[]{:S(2)}) collective-permute-start(bf16[192,512]{1,0:T(8,128)(2,1)S(1)} %get-tuple-element.55), channel_id=1, source_target_pairs={{0,4},{2,6},{4,0},{6,2},{1,5},{3,7},{5,1},{7,3},{8,12},{10,14},{12... | collective-permute-start | bytes 589832 | tf_op jit(solution)/shard_map/ppermute | solution.py:28
  63.0 3.3 %collective-permute-start.17 = (bf16[192,512]{1,0:T(8,128)(2,1)S(1)}, bf16[192,512]{1,0:T(8,128)(2,1)S(1)}, u32[]{:S(2)}, u32[]{:S(2)}) collective-permute-start(bf16[192,512]{1,0:T(8,128)(2,1)S(1)} %get-tuple-element.59), channel_id=1, source_target_pairs={{0,2},{2,4},{4,6},{6,0},{1,3},{3,5},{5,7},{7,1},{8,10},{10,12},{12... | collective-permute-start | bytes 589832 | tf_op jit(solution)/shard_map/ppermute | solution.py:28
  66.8 5.7 %collective-permute-start.19 = (bf16[192,512]{1,0:T(8,128)(2,1)S(1)}, bf16[192,512]{1,0:T(8,128)(2,1)S(1)}, u32[]{:S(2)}, u32[]{:S(2)}) collective-permute-start(bf16[192,512]{1,0:T(8,128)(2,1)S(1)} %get-tuple-element.61), channel_id=1, source_target_pairs={{0,6},{2,0},{4,2},{6,4},{1,7},{3,1},{5,3},{7,5},{8,14},{10,8},{12,... | collective-permute-start | bytes 589832 | tf_op jit(solution)/shard_map/ppermute | solution.py:28
  72.5 3.4 %collective-permute-done.16.r3 = bf16[192,512]{1,0:T(8,128)(2,1)S(1)} collective-permute-done((bf16[192,512]{1,0:T(8,128)(2,1)S(1)}, bf16[192,512]{1,0:T(8,128)(2,1)S(1)}, u32[]{:S(2)}, u32[]{:S(2)}) %collective-permute-start.16) | collective-permute-done | bytes 196640 | tf_op jit(solution)/shard_map/ppermute | solution.py:28
  77.1 3.2 %collective-permute-start.24 = (bf16[192,512]{1,0:T(8,128)(2,1)S(1)}, bf16[192,512]{1,0:T(8,128)(2,1)S(1)}, u32[]{:S(2)}, u32[]{:S(2)}) collective-permute-start(bf16[192,512]{1,0:T(8,128)(2,1)S(1)} %get-tuple-element.65), channel_id=1, source_target_pairs={{2,0},{4,2},{6,4},{0,6},{3,1},{5,3},{7,5},{1,7},{10,8},{12,10},{14... | collective-permute-start | bytes 589832 | tf_op jit(solution)/shard_map/ppermute | solution.py:23
  80.2 4.0 %collective-permute-done.19.r3 = bf16[192,512]{1,0:T(8,128)(2,1)S(1)} collective-permute-done((bf16[192,512]{1,0:T(8,128)(2,1)S(1)}, bf16[192,512]{1,0:T(8,128)(2,1)S(1)}, u32[]{:S(2)}, u32[]{:S(2)}) %collective-permute-start.19) | collective-permute-done | bytes 196640 | tf_op jit(solution)/shard_map/ppermute | solution.py:28
  85.5 3.1 %collective-permute-start.20 = (bf16[192,512]{1,0:T(8,128)(2,1)S(1)}, bf16[192,512]{1,0:T(8,128)(2,1)S(1)}, u32[]{:S(2)}, u32[]{:S(2)}) collective-permute-start(bf16[192,512]{1,0:T(8,128)(2,1)S(1)} %get-tuple-element.63), channel_id=1, source_target_pairs={{2,0},{4,2},{6,4},{0,6},{3,1},{5,3},{7,5},{1,7},{10,8},{12,10},{14... | collective-permute-start | bytes 589832 | tf_op jit(solution)/shard_map/ppermute | solution.py:23
  88.6 4.0 %collective-permute-done.24 = bf16[192,512]{1,0:T(8,128)(2,1)S(1)} collective-permute-done((bf16[192,512]{1,0:T(8,128)(2,1)S(1)}, bf16[192,512]{1,0:T(8,128)(2,1)S(1)}, u32[]{:S(2)}, u32[]{:S(2)}) %collective-permute-start.24) | collective-permute-done | bytes 196640 | tf_op jit(solution)/shard_map/ppermute | solution.py:23
  94.2 3.0 %collective-permute-done.20 = bf16[192,512]{1,0:T(8,128)(2,1)S(1)} collective-permute-done((bf16[192,512]{1,0:T(8,128)(2,1)S(1)}, bf16[192,512]{1,0:T(8,128)(2,1)S(1)}, u32[]{:S(2)}, u32[]{:S(2)}) %collective-permute-start.20) | collective-permute-done | bytes 196640 | tf_op jit(solution)/shard_map/ppermute | solution.py:23
  97.4 3.0 %shard_map.91 = (f32[4,8,48,1024]{3,2,1,0:T(8,128)S(1)}, bf16[4,2,192,512]{3,2,1,0:T(8,128)(2,1)S(1)}) custom-call(s32[4]{0:T(128)S(1)} %pad_add_fusion.pos, bf16[4,192,512]{2,1,0:T(8,128)(2,1)S(1)} %pad_maximum_fusion.1.refs_0_, bf16[4,192,512]{2,1,0:T(8,128)(2,1)S(1)} %collective-permute-done.27.refs_1_, bf16[1024,1024]{1,0:T(8,128)(2,1)S(1)} %get-tuple-element.64.refs_2_), custom_call_target="tpu_custom_call" | custom-call | flops 1610612736 | bytes 11534336 | tf_op jit(solution)/shard_map/pallas_call | solution.py:33
  100.4 4.4 %shard_map.92 = (f32[4,2,48,512]{3,2,1,0:T(8,128)S(1)}, f32[4,2,48,512]{3,2,1,0:T(8,128)S(1)}, bf16[4,2,48,512]{3,2,1,0:T(8,128)(2,1)S(1)}, bf16[4,2,48,512]{3,2...) custom-call(s32[4]{0:T(128)S(1)} %pad_add_fusion.pos, ...), custom_call_target="tpu_custom_call" | custom-call | flops 1610612736 | bytes 19398656 | tf_op jit(solution)/shard_map/pallas_call | solution.py:33
  107.0 3.2 %collective-permute-start.28 = (bf16[4,2,48,512]{3,2,1,0:T(8,128)(2,1)S(1)}, bf16[4,2,48,512]{3,2,1,0:T(8,128)(2,1)S(1)}, u32[]{:S(2)}, u32[]{:S(2)}) collective-permute-start(bf16[4,2,48,512]{3,2,1,0:T(8,128)(2,1)S(1)} %get-tuple-element.69), channel_id=1, source_target_pairs={{0,56},{8,0},{16,8},{24,16},{32,24},{40,32},{48,40},{56,48},{1,57}... | collective-permute-start | bytes 1179656 | tf_op jit(solution)/shard_map/ppermute | solution.py:28
  111.8 6.4 %collective-permute-done.29 = bf16[4,2,48,512]{3,2,1,0:T(8,128)(2,1)S(1)} collective-permute-done((bf16[4,2,48,512]{3,2,1,0:T(8,128)(2,1)S(1)}, bf16[4,2,48,512]{3,2,1,0:T(8,128)(2,1)S(1)}, u32[]{:S(2)}, u32[]{:S(2)}) %collective-permute-start.29) | collective-permute-done | bytes 393248 | tf_op jit(solution)/shard_map/ppermute | solution.py:28
  120.2 8.7 %shard_map.93 = bf16[1024,1024]{1,0:T(8,128)(2,1)} custom-call(s32[32]{0:T(128)S(1)} %get-tuple-element.90.rows, s32[32]{0:T(128)S(1)} %get-tuple-element.89.cols, s32[1]{0:T(128)} %bitcast.60.count, bf16[4,8,48,1024]{3,2,1,0:T(8,128)(2,1)S(1)} %get-tuple-element.76.toks, bf16[4,2,192,1024]{3,2,1,0:T(8,128)(2,1)S(1)} %get-tuple-element.77.grads), custom_call_target="tpu_custom_call" | custom-call | flops 3221225472 | bytes 8388608 | tf_op jit(solution)/shard_map/pallas_call | solution.py:33
  132.5 1.9 %collective-permute-start.36 = (bf16[2,48,512]{2,1,0:T(8,128)(2,1)S(1)}, bf16[2,48,512]{2,1,0:T(8,128)(2,1)S(1)}, u32[]{:S(2)}, u32[]{:S(2)}) collective-permute-start(bf16[2,48,512]{2,1,0:T(8,128)(2,1)S(1)} %get-tuple-element.85), channel_id=1, source_target_pairs={{0,192},{64,0},{128,64},{192,128},{1,193},{65,1},{129,65},{193,129... | collective-permute-start | bytes 294920 | tf_op jit(solution)/shard_map/ppermute | solution.py:28
  135.6 2.5 %collective-permute-start.39 = (bf16[2,48,512]{2,1,0:T(8,128)(2,1)S(1)}, bf16[2,48,512]{2,1,0:T(8,128)(2,1)S(1)}, u32[]{:S(2)}, u32[]{:S(2)}) collective-permute-start(bf16[2,48,512]{2,1,0:T(8,128)(2,1)S(1)} %get-tuple-element.82), channel_id=1, source_target_pairs={{0,56},{8,0},{16,8},{24,16},{32,24},{40,32},{48,40},{56,48},{1,57}... | collective-permute-start | bytes 294920 | tf_op jit(solution)/shard_map/ppermute | solution.py:28
  140.7 4.2 %collective-permute-done.38 = bf16[2,48,512]{2,1,0:T(8,128)(2,1)S(1)} collective-permute-done((bf16[2,48,512]{2,1,0:T(8,128)(2,1)S(1)}, bf16[2,48,512]{2,1,0:T(8,128)(2,1)S(1)}, u32[]{:S(2)}, u32[]{:S(2)}) %collective-permute-start.38) | collective-permute-done | bytes 98336 | tf_op jit(solution)/shard_map/ppermute | solution.py:28
  145.0 5.1 %collective-permute-start.40 = (bf16[48,1024]{1,0:T(8,128)(2,1)S(1)}, bf16[48,1024]{1,0:T(8,128)(2,1)S(1)}, u32[]{:S(2)}, u32[]{:S(2)}) collective-permute-start(bf16[48,1024]{1,0:T(8,128)(2,1)S(1)} %fusion.10), channel_id=1, source_target_pairs={{0,32},{8,40},{16,48},{24,56},{32,0},{40,8},{48,16},{56,24},{1,33}... | collective-permute-start | bytes 294920 | tf_op jit(solution)/shard_map/ppermute | solution.py:28
  150.8 2.7 %collective-permute-done.40 = bf16[48,1024]{1,0:T(8,128)(2,1)S(1)} collective-permute-done((bf16[48,1024]{1,0:T(8,128)(2,1)S(1)}, bf16[48,1024]{1,0:T(8,128)(2,1)S(1)}, u32[]{:S(2)}, u32[]{:S(2)}) %collective-permute-start.40) | collective-permute-done | bytes 98336 | tf_op jit(solution)/shard_map/ppermute | solution.py:28
  (83 shorter events, 33.2 us)
Async XLA Ops:
  0.6 10.4 %collective-permute-start = (bf16[48,1024]{1,0:T(8,128)(2,1)}, bf16[48,1024]{1,0:T(8,128)(2,1)S(1)}, u32[]{:S(2)}, u32[]{:S(2)}) collective-permute-start(bf16[48,1024]{1,0:T(8,128)(2,1)} %param.6), channel_id=1, source_target_pairs={{32,0},{40,8},{48,16},{56,24},{0,32},{8,40},{16,48},{24,56},{33,1}... | collective-permute-start | bytes 294920 | tf_op jit(solution)/shard_map/ppermute | solution.py:23
  11.9 13.2 %collective-permute-start.6 = (bf16[2,48,512]{2,1,0:T(8,128)(2,1)S(1)}, bf16[2,48,512]{2,1,0:T(8,128)(2,1)S(1)}, u32[]{:S(2)}, u32[]{:S(2)}) collective-permute-start(bf16[2,48,512]{2,1,0:T(8,128)(2,1)S(1)} %get-tuple-element.46), channel_id=1, source_target_pairs={{56,0},{0,8},{8,16},{16,24},{24,32},{32,40},{40,48},{48,56},{57,1}... | collective-permute-start | bytes 294920 | tf_op jit(solution)/shard_map/ppermute | solution.py:23
  14.4 12.0 %collective-permute-start.5 = (bf16[2,48,512]{2,1,0:T(8,128)(2,1)S(1)}, bf16[2,48,512]{2,1,0:T(8,128)(2,1)S(1)}, u32[]{:S(2)}, u32[]{:S(2)}) collective-permute-start(bf16[2,48,512]{2,1,0:T(8,128)(2,1)S(1)} %get-tuple-element.46), channel_id=1, source_target_pairs={{16,0},{24,8},{32,16},{40,24},{48,32},{56,40},{0,48},{8,56},{17,1}... | collective-permute-start | bytes 294920 | tf_op jit(solution)/shard_map/ppermute | solution.py:23
  18.6 7.8 %collective-permute-start.4 = (bf16[2,48,512]{2,1,0:T(8,128)(2,1)S(1)}, bf16[2,48,512]{2,1,0:T(8,128)(2,1)S(1)}, u32[]{:S(2)}, u32[]{:S(2)}) collective-permute-start(bf16[2,48,512]{2,1,0:T(8,128)(2,1)S(1)} %get-tuple-element.46), channel_id=1, source_target_pairs={{8,0},{16,8},{24,16},{32,24},{40,32},{48,40},{56,48},{0,56},{9,1},... | collective-permute-start | bytes 294920 | tf_op jit(solution)/shard_map/ppermute | solution.py:23
  29.9 9.4 %collective-permute-start.10 = (bf16[4,2,48,512]{3,2,1,0:T(8,128)(2,1)S(1)}, bf16[4,2,48,512]{3,2,1,0:T(8,128)(2,1)S(1)}, u32[]{:S(2)}, u32[]{:S(2)}) collective-permute-start(bf16[4,2,48,512]{3,2,1,0:T(8,128)(2,1)S(1)} %pad_maximum_fusion.3.refs_4_), channel_id=1, source_target_pairs={{64,0},{128,64},{192,128},{0,192},{65,1},{129,65},{193,129},{1,193... | collective-permute-start | bytes 1179656 | tf_op jit(solution)/shard_map/ppermute | solution.py:23
  32.4 9.2 %collective-permute-start.7 = (bf16[4,2,48,512]{3,2,1,0:T(8,128)(2,1)S(1)}, bf16[4,2,48,512]{3,2,1,0:T(8,128)(2,1)S(1)}, u32[]{:S(2)}, u32[]{:S(2)}) collective-permute-start(bf16[4,2,48,512]{3,2,1,0:T(8,128)(2,1)S(1)} %pad_maximum_fusion.2.refs_0_), channel_id=1, source_target_pairs={{8,0},{16,8},{24,16},{32,24},{40,32},{48,40},{56,48},{0,56},{9,1},... | collective-permute-start | bytes 1179656 | tf_op jit(solution)/shard_map/ppermute | solution.py:23
  33.7 15.3 %collective-permute-start.12 = (bf16[4,2,48,512]{3,2,1,0:T(8,128)(2,1)S(1)}, bf16[4,2,48,512]{3,2,1,0:T(8,128)(2,1)S(1)}, u32[]{:S(2)}, u32[]{:S(2)}) collective-permute-start(bf16[4,2,48,512]{3,2,1,0:T(8,128)(2,1)S(1)} %pad_maximum_fusion.3.refs_4_), channel_id=1, source_target_pairs={{192,0},{0,64},{64,128},{128,192},{193,1},{1,65},{65,129},{129,193... | collective-permute-start | bytes 1179656 | tf_op jit(solution)/shard_map/ppermute | solution.py:23
  34.2 14.8 %collective-permute-start.9 = (bf16[4,2,48,512]{3,2,1,0:T(8,128)(2,1)S(1)}, bf16[4,2,48,512]{3,2,1,0:T(8,128)(2,1)S(1)}, u32[]{:S(2)}, u32[]{:S(2)}) collective-permute-start(bf16[4,2,48,512]{3,2,1,0:T(8,128)(2,1)S(1)} %pad_maximum_fusion.2.refs_0_), channel_id=1, source_target_pairs={{56,0},{0,8},{8,16},{16,24},{24,32},{32,40},{40,48},{48,56},{57,1}... | collective-permute-start | bytes 1179656 | tf_op jit(solution)/shard_map/ppermute | solution.py:23
  39.3 9.7 %collective-permute-start.11 = (bf16[4,2,48,512]{3,2,1,0:T(8,128)(2,1)S(1)}, bf16[4,2,48,512]{3,2,1,0:T(8,128)(2,1)S(1)}, u32[]{:S(2)}, u32[]{:S(2)}) collective-permute-start(bf16[4,2,48,512]{3,2,1,0:T(8,128)(2,1)S(1)} %collective-permute-done.10.refs_5_), channel_id=1, source_target_pairs={{64,0},{128,64},{192,128},{0,192},{65,1},{129,65},{193,129},{1,193... | collective-permute-start | bytes 1179656 | tf_op jit(solution)/shard_map/ppermute | solution.py:23
  41.6 7.8 %collective-permute-start.8 = (bf16[4,2,48,512]{3,2,1,0:T(8,128)(2,1)S(1)}, bf16[4,2,48,512]{3,2,1,0:T(8,128)(2,1)S(1)}, u32[]{:S(2)}, u32[]{:S(2)}) collective-permute-start(bf16[4,2,48,512]{3,2,1,0:T(8,128)(2,1)S(1)} %collective-permute-done.7.refs_1_), channel_id=1, source_target_pairs={{8,0},{16,8},{24,16},{32,24},{40,32},{48,40},{56,48},{0,56},{9,1},... | collective-permute-start | bytes 1179656 | tf_op jit(solution)/shard_map/ppermute | solution.py:23
  58.8 8.0 %collective-permute-start.14 = (bf16[192,512]{1,0:T(8,128)(2,1)S(1)}, bf16[192,512]{1,0:T(8,128)(2,1)S(1)}, u32[]{:S(2)}, u32[]{:S(2)}) collective-permute-start(bf16[192,512]{1,0:T(8,128)(2,1)S(1)} %get-tuple-element.54), channel_id=1, source_target_pairs={{0,2},{2,4},{4,6},{6,0},{1,3},{3,5},{5,7},{7,1},{8,10},{10,12},{12... | collective-permute-start | bytes 589832 | tf_op jit(solution)/shard_map/ppermute | solution.py:28
  59.5 12.9 %collective-permute-start.15 = (bf16[192,512]{1,0:T(8,128)(2,1)S(1)}, bf16[192,512]{1,0:T(8,128)(2,1)S(1)}, u32[]{:S(2)}, u32[]{:S(2)}) collective-permute-start(bf16[192,512]{1,0:T(8,128)(2,1)S(1)} %get-tuple-element.55), channel_id=1, source_target_pairs={{0,4},{2,6},{4,0},{6,2},{1,5},{3,7},{5,1},{7,3},{8,12},{10,14},{12... | collective-permute-start | bytes 589832 | tf_op jit(solution)/shard_map/ppermute | solution.py:28
  62.6 13.3 %collective-permute-start.16 = (bf16[192,512]{1,0:T(8,128)(2,1)S(1)}, bf16[192,512]{1,0:T(8,128)(2,1)S(1)}, u32[]{:S(2)}, u32[]{:S(2)}) collective-permute-start(bf16[192,512]{1,0:T(8,128)(2,1)S(1)} %get-tuple-element.56), channel_id=1, source_target_pairs={{0,6},{2,0},{4,2},{6,4},{1,7},{3,1},{5,3},{7,5},{8,14},{10,8},{12,... | collective-permute-start | bytes 589832 | tf_op jit(solution)/shard_map/ppermute | solution.py:28
  63.0 14.1 %collective-permute-start.17 = (bf16[192,512]{1,0:T(8,128)(2,1)S(1)}, bf16[192,512]{1,0:T(8,128)(2,1)S(1)}, u32[]{:S(2)}, u32[]{:S(2)}) collective-permute-start(bf16[192,512]{1,0:T(8,128)(2,1)S(1)} %get-tuple-element.59), channel_id=1, source_target_pairs={{0,2},{2,4},{4,6},{6,0},{1,3},{3,5},{5,7},{7,1},{8,10},{10,12},{12... | collective-permute-start | bytes 589832 | tf_op jit(solution)/shard_map/ppermute | solution.py:28
  66.3 13.9 %collective-permute-start.18 = (bf16[192,512]{1,0:T(8,128)(2,1)S(1)}, bf16[192,512]{1,0:T(8,128)(2,1)S(1)}, u32[]{:S(2)}, u32[]{:S(2)}) collective-permute-start(bf16[192,512]{1,0:T(8,128)(2,1)S(1)} %get-tuple-element.60), channel_id=1, source_target_pairs={{0,4},{2,6},{4,0},{6,2},{1,5},{3,7},{5,1},{7,3},{8,12},{10,14},{12... | collective-permute-start | bytes 589832 | tf_op jit(solution)/shard_map/ppermute | solution.py:28
  66.8 17.5 %collective-permute-start.19 = (bf16[192,512]{1,0:T(8,128)(2,1)S(1)}, bf16[192,512]{1,0:T(8,128)(2,1)S(1)}, u32[]{:S(2)}, u32[]{:S(2)}) collective-permute-start(bf16[192,512]{1,0:T(8,128)(2,1)S(1)} %get-tuple-element.61), channel_id=1, source_target_pairs={{0,6},{2,0},{4,2},{6,4},{1,7},{3,1},{5,3},{7,5},{8,14},{10,8},{12,... | collective-permute-start | bytes 589832 | tf_op jit(solution)/shard_map/ppermute | solution.py:28
  76.2 9.4 %collective-permute-start.26 = (bf16[192,512]{1,0:T(8,128)(2,1)S(1)}, bf16[192,512]{1,0:T(8,128)(2,1)S(1)}, u32[]{:S(2)}, u32[]{:S(2)}) collective-permute-start(bf16[192,512]{1,0:T(8,128)(2,1)S(1)} %get-tuple-element.65), channel_id=1, source_target_pairs={{6,0},{0,2},{2,4},{4,6},{7,1},{1,3},{3,5},{5,7},{14,8},{8,10},{10,... | collective-permute-start | bytes 589832 | tf_op jit(solution)/shard_map/ppermute | solution.py:23
  76.3 12.4 %collective-permute-start.25 = (bf16[192,512]{1,0:T(8,128)(2,1)S(1)}, bf16[192,512]{1,0:T(8,128)(2,1)S(1)}, u32[]{:S(2)}, u32[]{:S(2)}) collective-permute-start(bf16[192,512]{1,0:T(8,128)(2,1)S(1)} %get-tuple-element.65), channel_id=1, source_target_pairs={{4,0},{6,2},{0,4},{2,6},{5,1},{7,3},{1,5},{3,7},{12,8},{14,10},{8,... | collective-permute-start | bytes 589832 | tf_op jit(solution)/shard_map/ppermute | solution.py:23
  77.1 15.5 %collective-permute-start.24 = (bf16[192,512]{1,0:T(8,128)(2,1)S(1)}, bf16[192,512]{1,0:T(8,128)(2,1)S(1)}, u32[]{:S(2)}, u32[]{:S(2)}) collective-permute-start(bf16[192,512]{1,0:T(8,128)(2,1)S(1)} %get-tuple-element.65), channel_id=1, source_target_pairs={{2,0},{4,2},{6,4},{0,6},{3,1},{5,3},{7,5},{1,7},{10,8},{12,10},{14... | collective-permute-start | bytes 589832 | tf_op jit(solution)/shard_map/ppermute | solution.py:23
  84.5 8.3 %collective-permute-start.22 = (bf16[192,512]{1,0:T(8,128)(2,1)S(1)}, bf16[192,512]{1,0:T(8,128)(2,1)S(1)}, u32[]{:S(2)}, u32[]{:S(2)}) collective-permute-start(bf16[192,512]{1,0:T(8,128)(2,1)S(1)} %get-tuple-element.63), channel_id=1, source_target_pairs={{6,0},{0,2},{2,4},{4,6},{7,1},{1,3},{3,5},{5,7},{14,8},{8,10},{10,... | collective-permute-start | bytes 589832 | tf_op jit(solution)/shard_map/ppermute | solution.py:23
  84.6 9.6 %collective-permute-start.21 = (bf16[192,512]{1,0:T(8,128)(2,1)S(1)}, bf16[192,512]{1,0:T(8,128)(2,1)S(1)}, u32[]{:S(2)}, u32[]{:S(2)}) collective-permute-start(bf16[192,512]{1,0:T(8,128)(2,1)S(1)} %get-tuple-element.63), channel_id=1, source_target_pairs={{4,0},{6,2},{0,4},{2,6},{5,1},{7,3},{1,5},{3,7},{12,8},{14,10},{8,... | collective-permute-start | bytes 589832 | tf_op jit(solution)/shard_map/ppermute | solution.py:23
  85.5 11.7 %collective-permute-start.20 = (bf16[192,512]{1,0:T(8,128)(2,1)S(1)}, bf16[192,512]{1,0:T(8,128)(2,1)S(1)}, u32[]{:S(2)}, u32[]{:S(2)}) collective-permute-start(bf16[192,512]{1,0:T(8,128)(2,1)S(1)} %get-tuple-element.63), channel_id=1, source_target_pairs={{2,0},{4,2},{6,4},{0,6},{3,1},{5,3},{7,5},{1,7},{10,8},{12,10},{14... | collective-permute-start | bytes 589832 | tf_op jit(solution)/shard_map/ppermute | solution.py:23
  104.8 13.4 %collective-permute-start.29 = (bf16[4,2,48,512]{3,2,1,0:T(8,128)(2,1)S(1)}, bf16[4,2,48,512]{3,2,1,0:T(8,128)(2,1)S(1)}, u32[]{:S(2)}, u32[]{:S(2)}) collective-permute-start(bf16[4,2,48,512]{3,2,1,0:T(8,128)(2,1)S(1)} %get-tuple-element.71), channel_id=1, source_target_pairs={{0,8},{8,16},{16,24},{24,32},{32,40},{40,48},{48,56},{56,0},{1,9},... | collective-permute-start | bytes 1179656 | tf_op jit(solution)/shard_map/ppermute | solution.py:28
  106.5 12.4 %collective-permute-start.32 = (bf16[4,2,48,512]{3,2,1,0:T(8,128)(2,1)S(1)}, bf16[4,2,48,512]{3,2,1,0:T(8,128)(2,1)S(1)}, u32[]{:S(2)}, u32[]{:S(2)}) collective-permute-start(bf16[4,2,48,512]{3,2,1,0:T(8,128)(2,1)S(1)} %get-tuple-element.75), channel_id=1, source_target_pairs={{0,64},{64,128},{128,192},{192,0},{1,65},{65,129},{129,193},{193,1... | collective-permute-start | bytes 1179656 | tf_op jit(solution)/shard_map/ppermute | solution.py:28
  107.0 21.9 %collective-permute-start.28 = (bf16[4,2,48,512]{3,2,1,0:T(8,128)(2,1)S(1)}, bf16[4,2,48,512]{3,2,1,0:T(8,128)(2,1)S(1)}, u32[]{:S(2)}, u32[]{:S(2)}) collective-permute-start(bf16[4,2,48,512]{3,2,1,0:T(8,128)(2,1)S(1)} %get-tuple-element.69), channel_id=1, source_target_pairs={{0,56},{8,0},{16,8},{24,16},{32,24},{40,32},{48,40},{56,48},{1,57}... | collective-permute-start | bytes 1179656 | tf_op jit(solution)/shard_map/ppermute | solution.py:28
  110.2 20.6 %collective-permute-start.31 = (bf16[4,2,48,512]{3,2,1,0:T(8,128)(2,1)S(1)}, bf16[4,2,48,512]{3,2,1,0:T(8,128)(2,1)S(1)}, u32[]{:S(2)}, u32[]{:S(2)}) collective-permute-start(bf16[4,2,48,512]{3,2,1,0:T(8,128)(2,1)S(1)} %get-tuple-element.73), channel_id=1, source_target_pairs={{0,192},{64,0},{128,64},{192,128},{1,193},{65,1},{129,65},{193,129... | collective-permute-start | bytes 1179656 | tf_op jit(solution)/shard_map/ppermute | solution.py:28
  118.4 12.2 %collective-permute-start.30 = (bf16[4,2,48,512]{3,2,1,0:T(8,128)(2,1)S(1)}, bf16[4,2,48,512]{3,2,1,0:T(8,128)(2,1)S(1)}, u32[]{:S(2)}, u32[]{:S(2)}) collective-permute-start(bf16[4,2,48,512]{3,2,1,0:T(8,128)(2,1)S(1)} %add_convert_fusion.1), channel_id=1, source_target_pairs={{0,8},{8,16},{16,24},{24,32},{32,40},{40,48},{48,56},{56,0},{1,9},... | collective-permute-start | bytes 1179656 | tf_op jit(solution)/shard_map/ppermute | solution.py:28
  119.0 11.8 %collective-permute-start.33 = (bf16[4,2,48,512]{3,2,1,0:T(8,128)(2,1)S(1)}, bf16[4,2,48,512]{3,2,1,0:T(8,128)(2,1)S(1)}, u32[]{:S(2)}, u32[]{:S(2)}) collective-permute-start(bf16[4,2,48,512]{3,2,1,0:T(8,128)(2,1)S(1)} %add_convert_fusion), channel_id=1, source_target_pairs={{0,64},{64,128},{128,192},{192,0},{1,65},{65,129},{129,193},{193,1... | collective-permute-start | bytes 1179656 | tf_op jit(solution)/shard_map/ppermute | solution.py:28
  131.1 7.0 %collective-permute-start.34 = (bf16[2,48,512]{2,1,0:T(8,128)(2,1)S(1)}, bf16[2,48,512]{2,1,0:T(8,128)(2,1)S(1)}, u32[]{:S(2)}, u32[]{:S(2)}) collective-permute-start(bf16[2,48,512]{2,1,0:T(8,128)(2,1)S(1)} %get-tuple-element.84), channel_id=1, source_target_pairs={{0,64},{64,128},{128,192},{192,0},{1,65},{65,129},{129,193},{193,1... | collective-permute-start | bytes 294920 | tf_op jit(solution)/shard_map/ppermute | solution.py:28
  132.5 6.7 %collective-permute-start.36 = (bf16[2,48,512]{2,1,0:T(8,128)(2,1)S(1)}, bf16[2,48,512]{2,1,0:T(8,128)(2,1)S(1)}, u32[]{:S(2)}, u32[]{:S(2)}) collective-permute-start(bf16[2,48,512]{2,1,0:T(8,128)(2,1)S(1)} %get-tuple-element.85), channel_id=1, source_target_pairs={{0,192},{64,0},{128,64},{192,128},{1,193},{65,1},{129,65},{193,129... | collective-permute-start | bytes 294920 | tf_op jit(solution)/shard_map/ppermute | solution.py:28
  138.1 6.8 %collective-permute-start.38 = (bf16[2,48,512]{2,1,0:T(8,128)(2,1)S(1)}, bf16[2,48,512]{2,1,0:T(8,128)(2,1)S(1)}, u32[]{:S(2)}, u32[]{:S(2)}) collective-permute-start(bf16[2,48,512]{2,1,0:T(8,128)(2,1)S(1)} %get-tuple-element.83), channel_id=1, source_target_pairs={{0,16},{8,24},{16,32},{24,40},{32,48},{40,56},{48,0},{56,8},{1,17}... | collective-permute-start | bytes 294920 | tf_op jit(solution)/shard_map/ppermute | solution.py:28
  145.0 8.6 %collective-permute-start.40 = (bf16[48,1024]{1,0:T(8,128)(2,1)S(1)}, bf16[48,1024]{1,0:T(8,128)(2,1)S(1)}, u32[]{:S(2)}, u32[]{:S(2)}) collective-permute-start(bf16[48,1024]{1,0:T(8,128)(2,1)S(1)} %fusion.10), channel_id=1, source_target_pairs={{0,32},{8,40},{16,48},{24,56},{32,0},{40,8},{48,16},{56,24},{1,33}... | collective-permute-start | bytes 294920 | tf_op jit(solution)/shard_map/ppermute | solution.py:28
  (11 other events, 61.1 us)

commit v8 on v7

--- a/solution.py
+++ b/solution.py
@@ -194,10 +194,6 @@
         tile_ref(out, rows[k], cols[k])[...] = tile_ref(acc, rows[k], cols[k])[...].astype(BF16)
 
 
-def gather_four(piece, axis):
-    return [piece] + [from_ahead(piece, axis, k) for k in STEPS[1:]]
-
-
 def ring_gather(piece, axis):
     ahead = from_ahead(piece, axis, 1)
     behind = from_ahead(piece, axis, -1)
@@ -207,8 +203,8 @@
 def gather_tokens(tokens):
     pair = jnp.stack([tokens, from_ahead(tokens, "z", 4)])
     cut = tokens.shape[1] // 2
-    a2 = gather_four(pair[:, :, :cut], "y")
-    b2 = gather_four(pair[:, :, cut:], "z")
+    a2 = ring_gather(pair[:, :, :cut], "y")
+    b2 = ring_gather(pair[:, :, cut:], "z")
     a2, b2 = lax.optimization_barrier((a2, b2))
     return ring_gather(jnp.stack(a2), "z"), ring_gather(jnp.stack(b2), "y")
 
@@ -230,16 +226,9 @@
     return [mine, to_ahead(mine, "core", 1)]
 
 
-def reduce_four(own, sends, axis):
-    total = own
-    for k, s in zip(STEPS[1:], sends):
-        total = total + to_ahead(s.astype(BF16), axis, k).astype(F32)
-    return total
-
-
 def ring_reduce(own, ahead, far, behind, axis):
-    through = to_ahead(far, axis, 1).astype(F32)
-    total = own + to_ahead(behind, axis, -1).astype(F32)
+    through = to_ahead(far.astype(BF16), axis, 1).astype(F32)
+    total = own + to_ahead(behind.astype(BF16), axis, -1).astype(F32)
     return total + to_ahead((ahead + through).astype(BF16), axis, 1).astype(F32)
 
 
@@ -292,8 +281,8 @@
     a2 = ring_reduce(*sends[:4], "z")
     b2 = ring_reduce(*sends[4:], "y")
     a2, b2, weight_grad = lax.optimization_barrier((a2, b2, weight_grad))
-    a1 = reduce_four(a2[0], a2[1:], "y")
-    b1 = reduce_four(b2[0], b2[1:], "z")
+    a1 = ring_reduce(*a2, "y")
+    b1 = ring_reduce(*b2, "z")
     both = jnp.concatenate([a1, b1], axis=-1)
     total = both[0] + to_ahead(both[1].astype(BF16), "z", 4).astype(F32)
     return total.astype(BF16), weight_grad

time: 157 us -> 159 us (1.013); the launches traced: 154 us -> 158 us
  waiting for transfers between devices: 48.4 us -> 52.4 us
    ppermute x22, starting transfers between devices: 34.4 us -> 27.4 us  [to_ahead(): return lax.ppermute(value, axis, [(i, (i + k) % n) for i in range(n)])]
    ppermute x19, starting transfers between devices: 39.1 us -> 44.7 us  [from_ahead(): return lax.ppermute(value, axis, [((i + k) % n, i) for i in range(n)])]
    ppermute x22, waiting for transfers between devices: 28.3 us -> 33.7 us  [to_ahead(): return lax.ppermute(value, axis, [(i, (i + k) % n) for i in range(n)])]
  transfers between devices with their start and end apart: 41 -> 41, of which waited for: 21 -> 19; matrix products, arithmetic and copies ran while one was open for 2% -> 2% of each run, Pallas kernels for 10% -> 10%
where the time goes in v8:
time: 159 us; the launch traced here: 158 us
  starting transfers between devices  72 us (45%)
  waiting for transfers between devices  52.4 us (33%)
  Pallas kernels  26.2 us (16%)
  other arithmetic  4.19 us (3%)
  local copies, waits for them, and re-layouts  1.62 us (1%)
  between operations  1.59 us (1%)
    ppermute x19, starting transfers between devices, from_ahead(): return lax.ppermute(value, axis, [((i + k) % n, i) for i in range(n)])  44.7 us
    ppermute x22, waiting for transfers between devices, to_ahead(): return lax.ppermute(value, axis, [(i, (i + k) % n) for i in range(n)])  33.7 us
    ppermute x22, starting transfers between devices, to_ahead(): return lax.ppermute(value, axis, [(i, (i + k) % n) for i in range(n)])  27.4 us
    pallas_call x9, Pallas kernels, call(): pl.pallas_call(body, out_shape=outs, in_specs=[pl.BlockSpec(memory_space=...  26.2 us
    ppermute x19, waiting for transfers between devices, from_ahead(): return lax.ppermute(value, axis, [((i + k) % n, i) for i in range(n)])  18.7 us
  transfers between devices with their start and end apart: 41, of which 19 were waited for; matrix products, arithmetic and copies ran while one was open for 2% of the time, Pallas kernels for 10%

profile of v8, /device:TPU:6, one launch (start us, length us, event | category | flops | bytes accessed | tf_op | source)
XLA Modules:
  0.0 158.0 jit_solution(17799013991617698682)
XLA Ops:
  0.6 7.3 %collective-permute-start = (bf16[48,1024]{1,0:T(8,128)(2,1)}, bf16[48,1024]{1,0:T(8,128)(2,1)S(1)}, u32[]{:S(2)}, u32[]{:S(2)}) collective-permute-start(bf16[48,1024]{1,0:T(8,128)(2,1)} %param.6), channel_id=1, source_target_pairs={{32,0},{40,8},{48,16},{56,24},{0,32},{8,40},{16,48},{24,56},{33,1}... | collective-permute-start | bytes 294920 | tf_op jit(solution)/shard_map/ppermute | solution.py:23
  7.9 3.1 %collective-permute-done = bf16[48,1024]{1,0:T(8,128)(2,1)S(1)} collective-permute-done((bf16[48,1024]{1,0:T(8,128)(2,1)}, bf16[48,1024]{1,0:T(8,128)(2,1)S(1)}, u32[]{:S(2)}, u32[]{:S(2)}) %collective-permute-start) | collective-permute-done | bytes 98336 | tf_op jit(solution)/shard_map/ppermute | solution.py:23
  11.9 5.3 %collective-permute-start.4 = (bf16[2,48,512]{2,1,0:T(8,128)(2,1)S(1)}, bf16[2,48,512]{2,1,0:T(8,128)(2,1)S(1)}, u32[]{:S(2)}, u32[]{:S(2)}) collective-permute-start(bf16[2,48,512]{2,1,0:T(8,128)(2,1)S(1)} %get-tuple-element.46), channel_id=1, source_target_pairs={{8,0},{16,8},{24,16},{32,24},{40,32},{48,40},{56,48},{0,56},{9,1},... | collective-permute-start | bytes 294920 | tf_op jit(solution)/shard_map/ppermute | solution.py:23
  17.2 3.0 %collective-permute-start.1 = (bf16[2,48,512]{2,1,0:T(8,128)(2,1)S(1)}, bf16[2,48,512]{2,1,0:T(8,128)(2,1)S(1)}, u32[]{:S(2)}, u32[]{:S(2)}) collective-permute-start(bf16[2,48,512]{2,1,0:T(8,128)(2,1)S(1)} %get-tuple-element.42), channel_id=1, source_target_pairs={{64,0},{128,64},{192,128},{0,192},{65,1},{129,65},{193,129},{1,193... | collective-permute-start | bytes 294920 | tf_op jit(solution)/shard_map/ppermute | solution.py:23
  20.2 3.2 %collective-permute-start.5 = (bf16[2,48,512]{2,1,0:T(8,128)(2,1)S(1)}, bf16[2,48,512]{2,1,0:T(8,128)(2,1)S(1)}, u32[]{:S(2)}, u32[]{:S(2)}) collective-permute-start(bf16[2,48,512]{2,1,0:T(8,128)(2,1)S(1)} %collective-permute-done.4), channel_id=1, source_target_pairs={{8,0},{16,8},{24,16},{32,24},{40,32},{48,40},{56,48},{0,56},{9,1},... | collective-permute-start | bytes 294920 | tf_op jit(solution)/shard_map/ppermute | solution.py:23
  23.4 3.2 %collective-permute-start.2 = (bf16[2,48,512]{2,1,0:T(8,128)(2,1)S(1)}, bf16[2,48,512]{2,1,0:T(8,128)(2,1)S(1)}, u32[]{:S(2)}, u32[]{:S(2)}) collective-permute-start(bf16[2,48,512]{2,1,0:T(8,128)(2,1)S(1)} %collective-permute-done.1), channel_id=1, source_target_pairs={{64,0},{128,64},{192,128},{0,192},{65,1},{129,65},{193,129},{1,193... | collective-permute-start | bytes 294920 | tf_op jit(solution)/shard_map/ppermute | solution.py:23
  28.9 3.7 %collective-permute-start.10 = (bf16[4,2,48,512]{3,2,1,0:T(8,128)(2,1)S(1)}, bf16[4,2,48,512]{3,2,1,0:T(8,128)(2,1)S(1)}, u32[]{:S(2)}, u32[]{:S(2)}) collective-permute-start(bf16[4,2,48,512]{3,2,1,0:T(8,128)(2,1)S(1)} %pad_maximum_fusion.3.refs_4_), channel_id=1, source_target_pairs={{64,0},{128,64},{192,128},{0,192},{65,1},{129,65},{193,129},{1,193... | collective-permute-start | bytes 1179656 | tf_op jit(solution)/shard_map/ppermute | solution.py:23
  34.8 3.6 %collective-permute-done.10.refs_5_ = bf16[4,2,48,512]{3,2,1,0:T(8,128)(2,1)S(1)} collective-permute-done((bf16[4,2,48,512]{3,2,1,0:T(8,128)(2,1)S(1)}, bf16[4,2,48,512]{3,2,1,0:T(8,128)(2,1)S(1)}, u32[]{:S(2)}, u32[]{:S(2)}) %collective-permute-start.10) | collective-permute-done | bytes 393248 | tf_op jit(solution)/shard_map/ppermute | solution.py:23
  38.4 3.7 %collective-permute-start.11 = (bf16[4,2,48,512]{3,2,1,0:T(8,128)(2,1)S(1)}, bf16[4,2,48,512]{3,2,1,0:T(8,128)(2,1)S(1)}, u32[]{:S(2)}, u32[]{:S(2)}) collective-permute-start(bf16[4,2,48,512]{3,2,1,0:T(8,128)(2,1)S(1)} %collective-permute-done.10.refs_5_), channel_id=1, source_target_pairs={{64,0},{128,64},{192,128},{0,192},{65,1},{129,65},{193,129},{1,193... | collective-permute-start | bytes 1179656 | tf_op jit(solution)/shard_map/ppermute | solution.py:23
  46.7 3.0 %shard_map.85 = (bf16[1024,1024]{1,0:T(8,128)(2,1)S(1)}, bf16[1024,1024]{1,0:T(8,128)(2,1)S(1)}) custom-call(s32[32]{0:T(128)S(1)} %get-tuple-element.88.rows, s32[32]{0:T(128)S(1)} %get-tuple-element.87.cols, s32[1]{0:T(128)} %bitcast.59.count, bf16[1024,1024]{1,0:T(8,128)(2,1)S(1)} %copy-done), custom_call_target="tpu_custom_call" | custom-call | bytes 6291456 | tf_op jit(solution)/shard_map/pallas_call | solution.py:33
  49.9 5.4 %shard_map.86 = (f32[4,192,1024]{2,1,0:T(8,128)S(1)}, bf16[4,192,1024]{2,1,0:T(8,128)(2,1)S(1)}, bf16[4,8,48,1024]{3,2,1,0:T(8,128)(2,1)S(1)}) custom-call(s32[4]{0:T(128)S(1)} %pad_add_fusion.pos, bf16[4,2,48,512]{3,2,1,0:T(8,128)(2,1)S(1)} %pad_maximum_fusion.2.refs_0_, bf16[4,2,48,512]{3,2,1,0:T(8,128)(2,1)S(1)} %collective-permute-done.7.refs_1_, ...), custom_call_target="tpu_custom_call" | custom-call | flops 3221225472 | bytes 13107200 | tf_op jit(solution)/shard_map/pallas_call | solution.py:33
  55.4 3.4 %collective-permute-done.13.recv = bf16[4,192,1024]{2,1,0:T(8,128)(2,1)S(1)} collective-permute-done((bf16[4,192,1024]{2,1,0:T(8,128)(2,1)S(1)}, bf16[4,192,1024]{2,1,0:T(8,128)(2,1)S(1)}, u32[]{:S(2)}, u32[]{:S(2)}) %collective-permute-start.13) | collective-permute-done | bytes 1572896 | tf_op jit(solution)/shard_map/ppermute | solution.py:28
  59.9 2.4 %collective-permute-start.15 = (bf16[192,512]{1,0:T(8,128)(2,1)S(1)}, bf16[192,512]{1,0:T(8,128)(2,1)S(1)}, u32[]{:S(2)}, u32[]{:S(2)}) collective-permute-start(bf16[192,512]{1,0:T(8,128)(2,1)S(1)} %get-tuple-element.55), channel_id=1, source_target_pairs={{0,4},{2,6},{4,0},{6,2},{1,5},{3,7},{5,1},{7,3},{8,12},{10,14},{12... | collective-permute-start | bytes 589832 | tf_op jit(solution)/shard_map/ppermute | solution.py:28
  62.8 3.3 %collective-permute-start.17 = (bf16[192,512]{1,0:T(8,128)(2,1)S(1)}, bf16[192,512]{1,0:T(8,128)(2,1)S(1)}, u32[]{:S(2)}, u32[]{:S(2)}) collective-permute-start(bf16[192,512]{1,0:T(8,128)(2,1)S(1)} %get-tuple-element.59), channel_id=1, source_target_pairs={{0,2},{2,4},{4,6},{6,0},{1,3},{3,5},{5,7},{7,1},{8,10},{10,12},{12... | collective-permute-start | bytes 589832 | tf_op jit(solution)/shard_map/ppermute | solution.py:28
  67.2 5.0 %collective-permute-start.19 = (bf16[192,512]{1,0:T(8,128)(2,1)S(1)}, bf16[192,512]{1,0:T(8,128)(2,1)S(1)}, u32[]{:S(2)}, u32[]{:S(2)}) collective-permute-start(bf16[192,512]{1,0:T(8,128)(2,1)S(1)} %get-tuple-element.61), channel_id=1, source_target_pairs={{0,6},{2,0},{4,2},{6,4},{1,7},{3,1},{5,3},{7,5},{8,14},{10,8},{12,... | collective-permute-start | bytes 589832 | tf_op jit(solution)/shard_map/ppermute | solution.py:28
  74.5 4.0 %collective-permute-start.25 = (bf16[192,512]{1,0:T(8,128)(2,1)S(1)}, bf16[192,512]{1,0:T(8,128)(2,1)S(1)}, u32[]{:S(2)}, u32[]{:S(2)}) collective-permute-start(bf16[192,512]{1,0:T(8,128)(2,1)S(1)} %get-tuple-element.65), channel_id=1, source_target_pairs={{4,0},{6,2},{0,4},{2,6},{5,1},{7,3},{1,5},{3,7},{12,8},{14,10},{8,... | collective-permute-start | bytes 589832 | tf_op jit(solution)/shard_map/ppermute | solution.py:23
  83.0 2.3 %collective-permute-start.21 = (bf16[192,512]{1,0:T(8,128)(2,1)S(1)}, bf16[192,512]{1,0:T(8,128)(2,1)S(1)}, u32[]{:S(2)}, u32[]{:S(2)}) collective-permute-start(bf16[192,512]{1,0:T(8,128)(2,1)S(1)} %get-tuple-element.63), channel_id=1, source_target_pairs={{4,0},{6,2},{0,4},{2,6},{5,1},{7,3},{1,5},{3,7},{12,8},{14,10},{8,... | collective-permute-start | bytes 589832 | tf_op jit(solution)/shard_map/ppermute | solution.py:23
  85.3 2.4 %collective-permute-start.20 = (bf16[192,512]{1,0:T(8,128)(2,1)S(1)}, bf16[192,512]{1,0:T(8,128)(2,1)S(1)}, u32[]{:S(2)}, u32[]{:S(2)}) collective-permute-start(bf16[192,512]{1,0:T(8,128)(2,1)S(1)} %get-tuple-element.63), channel_id=1, source_target_pairs={{2,0},{4,2},{6,4},{0,6},{3,1},{5,3},{7,5},{1,7},{10,8},{12,10},{14... | collective-permute-start | bytes 589832 | tf_op jit(solution)/shard_map/ppermute | solution.py:23
  87.7 4.9 %collective-permute-done.24 = bf16[192,512]{1,0:T(8,128)(2,1)S(1)} collective-permute-done((bf16[192,512]{1,0:T(8,128)(2,1)S(1)}, bf16[192,512]{1,0:T(8,128)(2,1)S(1)}, u32[]{:S(2)}, u32[]{:S(2)}) %collective-permute-start.24) | collective-permute-done | bytes 196640 | tf_op jit(solution)/shard_map/ppermute | solution.py:23
  94.6 3.0 %collective-permute-done.20 = bf16[192,512]{1,0:T(8,128)(2,1)S(1)} collective-permute-done((bf16[192,512]{1,0:T(8,128)(2,1)S(1)}, bf16[192,512]{1,0:T(8,128)(2,1)S(1)}, u32[]{:S(2)}, u32[]{:S(2)}) %collective-permute-start.20) | collective-permute-done | bytes 196640 | tf_op jit(solution)/shard_map/ppermute | solution.py:23
  97.8 3.0 %shard_map.91 = (f32[4,8,48,1024]{3,2,1,0:T(8,128)S(1)}, bf16[4,2,192,512]{3,2,1,0:T(8,128)(2,1)S(1)}) custom-call(s32[4]{0:T(128)S(1)} %pad_add_fusion.pos, bf16[4,192,512]{2,1,0:T(8,128)(2,1)S(1)} %pad_maximum_fusion.1.refs_0_, bf16[4,192,512]{2,1,0:T(8,128)(2,1)S(1)} %collective-permute-done.27.refs_1_, bf16[1024,1024]{1,0:T(8,128)(2,1)S(1)} %get-tuple-element.64.refs_2_), custom_call_target="tpu_custom_call" | custom-call | flops 1610612736 | bytes 11534336 | tf_op jit(solution)/shard_map/pallas_call | solution.py:33
  100.8 4.4 %shard_map.92 = (f32[4,2,48,512]{3,2,1,0:T(8,128)S(1)}, f32[4,2,48,512]{3,2,1,0:T(8,128)S(1)}, bf16[4,2,48,512]{3,2,1,0:T(8,128)(2,1)S(1)}, bf16[4,2,48,512]{3,2...) custom-call(s32[4]{0:T(128)S(1)} %pad_add_fusion.pos, ...), custom_call_target="tpu_custom_call" | custom-call | flops 1610612736 | bytes 19398656 | tf_op jit(solution)/shard_map/pallas_call | solution.py:33
  105.6 3.0 %collective-permute-start.28 = (bf16[4,2,48,512]{3,2,1,0:T(8,128)(2,1)S(1)}, bf16[4,2,48,512]{3,2,1,0:T(8,128)(2,1)S(1)}, u32[]{:S(2)}, u32[]{:S(2)}) collective-permute-start(bf16[4,2,48,512]{3,2,1,0:T(8,128)(2,1)S(1)} %get-tuple-element.69), channel_id=1, source_target_pairs={{0,56},{8,0},{16,8},{24,16},{32,24},{40,32},{48,40},{56,48},{1,57}... | collective-permute-start | bytes 1179656 | tf_op jit(solution)/shard_map/ppermute | solution.py:28
  108.6 3.2 %collective-permute-start.31 = (bf16[4,2,48,512]{3,2,1,0:T(8,128)(2,1)S(1)}, bf16[4,2,48,512]{3,2,1,0:T(8,128)(2,1)S(1)}, u32[]{:S(2)}, u32[]{:S(2)}) collective-permute-start(bf16[4,2,48,512]{3,2,1,0:T(8,128)(2,1)S(1)} %get-tuple-element.73), channel_id=1, source_target_pairs={{0,192},{64,0},{128,64},{192,128},{1,193},{65,1},{129,65},{193,129... | collective-permute-start | bytes 1179656 | tf_op jit(solution)/shard_map/ppermute | solution.py:28
  111.8 6.2 %collective-permute-done.29 = bf16[4,2,48,512]{3,2,1,0:T(8,128)(2,1)S(1)} collective-permute-done((bf16[4,2,48,512]{3,2,1,0:T(8,128)(2,1)S(1)}, bf16[4,2,48,512]{3,2,1,0:T(8,128)(2,1)S(1)}, u32[]{:S(2)}, u32[]{:S(2)}) %collective-permute-start.29) | collective-permute-done | bytes 393248 | tf_op jit(solution)/shard_map/ppermute | solution.py:28
  118.5 8.9 %shard_map.93 = bf16[1024,1024]{1,0:T(8,128)(2,1)} custom-call(s32[32]{0:T(128)S(1)} %get-tuple-element.88.rows, s32[32]{0:T(128)S(1)} %get-tuple-element.87.cols, s32[1]{0:T(128)} %bitcast.60.count, bf16[4,8,48,1024]{3,2,1,0:T(8,128)(2,1)S(1)} %get-tuple-element.76.toks, bf16[4,2,192,1024]{3,2,1,0:T(8,128)(2,1)S(1)} %get-tuple-element.77.grads), custom_call_target="tpu_custom_call" | custom-call | flops 3221225472 | bytes 8388608 | tf_op jit(solution)/shard_map/pallas_call | solution.py:33
  127.4 2.8 %collective-permute-done.30 = bf16[4,2,48,512]{3,2,1,0:T(8,128)(2,1)S(1)} collective-permute-done((bf16[4,2,48,512]{3,2,1,0:T(8,128)(2,1)S(1)}, bf16[4,2,48,512]{3,2,1,0:T(8,128)(2,1)S(1)}, u32[]{:S(2)}, u32[]{:S(2)}) %collective-permute-start.30) | collective-permute-done | bytes 393248 | tf_op jit(solution)/shard_map/ppermute | solution.py:28
  132.9 3.0 %collective-permute-start.37 = (bf16[2,48,512]{2,1,0:T(8,128)(2,1)S(1)}, bf16[2,48,512]{2,1,0:T(8,128)(2,1)S(1)}, u32[]{:S(2)}, u32[]{:S(2)}) collective-permute-start(bf16[2,48,512]{2,1,0:T(8,128)(2,1)S(1)} %get-tuple-element.81), channel_id=1, source_target_pairs={{0,56},{8,0},{16,8},{24,16},{32,24},{40,32},{48,40},{56,48},{1,57}... | collective-permute-start | bytes 294920 | tf_op jit(solution)/shard_map/ppermute | solution.py:28
  137.9 3.8 %collective-permute-done.38 = bf16[2,48,512]{2,1,0:T(8,128)(2,1)S(1)} collective-permute-done((bf16[2,48,512]{2,1,0:T(8,128)(2,1)S(1)}, bf16[2,48,512]{2,1,0:T(8,128)(2,1)S(1)}, u32[]{:S(2)}, u32[]{:S(2)}) %collective-permute-start.38) | collective-permute-done | bytes 98336 | tf_op jit(solution)/shard_map/ppermute | solution.py:28
  143.8 5.0 %collective-permute-done.39 = bf16[2,48,512]{2,1,0:T(8,128)(2,1)S(1)} collective-permute-done((bf16[2,48,512]{2,1,0:T(8,128)(2,1)S(1)}, bf16[2,48,512]{2,1,0:T(8,128)(2,1)S(1)}, u32[]{:S(2)}, u32[]{:S(2)}) %collective-permute-start.39) | collective-permute-done | bytes 98336 | tf_op jit(solution)/shard_map/ppermute | solution.py:28
  148.8 3.5 %collective-permute-start.40 = (bf16[48,1024]{1,0:T(8,128)(2,1)S(1)}, bf16[48,1024]{1,0:T(8,128)(2,1)S(1)}, u32[]{:S(2)}, u32[]{:S(2)}) collective-permute-start(bf16[48,1024]{1,0:T(8,128)(2,1)S(1)} %fusion.10), channel_id=1, source_target_pairs={{0,32},{8,40},{16,48},{24,56},{32,0},{40,8},{48,16},{56,24},{1,33}... | collective-permute-start | bytes 294920 | tf_op jit(solution)/shard_map/ppermute | solution.py:28
  153.0 4.3 %collective-permute-done.40 = bf16[48,1024]{1,0:T(8,128)(2,1)S(1)} collective-permute-done((bf16[48,1024]{1,0:T(8,128)(2,1)S(1)}, bf16[48,1024]{1,0:T(8,128)(2,1)S(1)}, u32[]{:S(2)}, u32[]{:S(2)}) %collective-permute-start.40) | collective-permute-done | bytes 98336 | tf_op jit(solution)/shard_map/ppermute | solution.py:28
  (85 shorter events, 30.1 us)
Async XLA Ops:
  0.6 10.4 %collective-permute-start = (bf16[48,1024]{1,0:T(8,128)(2,1)}, bf16[48,1024]{1,0:T(8,128)(2,1)S(1)}, u32[]{:S(2)}, u32[]{:S(2)}) collective-permute-start(bf16[48,1024]{1,0:T(8,128)(2,1)} %param.6), channel_id=1, source_target_pairs={{32,0},{40,8},{48,16},{56,24},{0,32},{8,40},{16,48},{24,56},{33,1}... | collective-permute-start | bytes 294920 | tf_op jit(solution)/shard_map/ppermute | solution.py:23
  11.9 8.3 %collective-permute-start.4 = (bf16[2,48,512]{2,1,0:T(8,128)(2,1)S(1)}, bf16[2,48,512]{2,1,0:T(8,128)(2,1)S(1)}, u32[]{:S(2)}, u32[]{:S(2)}) collective-permute-start(bf16[2,48,512]{2,1,0:T(8,128)(2,1)S(1)} %get-tuple-element.46), channel_id=1, source_target_pairs={{8,0},{16,8},{24,16},{32,24},{40,32},{48,40},{56,48},{0,56},{9,1},... | collective-permute-start | bytes 294920 | tf_op jit(solution)/shard_map/ppermute | solution.py:23
  20.2 6.5 %collective-permute-start.6 = (bf16[2,48,512]{2,1,0:T(8,128)(2,1)S(1)}, bf16[2,48,512]{2,1,0:T(8,128)(2,1)S(1)}, u32[]{:S(2)}, u32[]{:S(2)}) collective-permute-start(bf16[2,48,512]{2,1,0:T(8,128)(2,1)S(1)} %get-tuple-element.46), channel_id=1, source_target_pairs={{56,0},{0,8},{8,16},{16,24},{24,32},{32,40},{40,48},{48,56},{57,1}... | collective-permute-start | bytes 294920 | tf_op jit(solution)/shard_map/ppermute | solution.py:23
  20.2 6.5 %collective-permute-start.3 = (bf16[2,48,512]{2,1,0:T(8,128)(2,1)S(1)}, bf16[2,48,512]{2,1,0:T(8,128)(2,1)S(1)}, u32[]{:S(2)}, u32[]{:S(2)}) collective-permute-start(bf16[2,48,512]{2,1,0:T(8,128)(2,1)S(1)} %get-tuple-element.42), channel_id=1, source_target_pairs={{192,0},{0,64},{64,128},{128,192},{193,1},{1,65},{65,129},{129,193... | collective-permute-start | bytes 294920 | tf_op jit(solution)/shard_map/ppermute | solution.py:23
  28.9 9.5 %collective-permute-start.10 = (bf16[4,2,48,512]{3,2,1,0:T(8,128)(2,1)S(1)}, bf16[4,2,48,512]{3,2,1,0:T(8,128)(2,1)S(1)}, u32[]{:S(2)}, u32[]{:S(2)}) collective-permute-start(bf16[4,2,48,512]{3,2,1,0:T(8,128)(2,1)S(1)} %pad_maximum_fusion.3.refs_4_), channel_id=1, source_target_pairs={{64,0},{128,64},{192,128},{0,192},{65,1},{129,65},{193,129},{1,193... | collective-permute-start | bytes 1179656 | tf_op jit(solution)/shard_map/ppermute | solution.py:23
  32.7 9.4 %collective-permute-start.7 = (bf16[4,2,48,512]{3,2,1,0:T(8,128)(2,1)S(1)}, bf16[4,2,48,512]{3,2,1,0:T(8,128)(2,1)S(1)}, u32[]{:S(2)}, u32[]{:S(2)}) collective-permute-start(bf16[4,2,48,512]{3,2,1,0:T(8,128)(2,1)S(1)} %pad_maximum_fusion.2.refs_0_), channel_id=1, source_target_pairs={{8,0},{16,8},{24,16},{32,24},{40,32},{48,40},{56,48},{0,56},{9,1},... | collective-permute-start | bytes 1179656 | tf_op jit(solution)/shard_map/ppermute | solution.py:23
  34.0 15.8 %collective-permute-start.12 = (bf16[4,2,48,512]{3,2,1,0:T(8,128)(2,1)S(1)}, bf16[4,2,48,512]{3,2,1,0:T(8,128)(2,1)S(1)}, u32[]{:S(2)}, u32[]{:S(2)}) collective-permute-start(bf16[4,2,48,512]{3,2,1,0:T(8,128)(2,1)S(1)} %pad_maximum_fusion.3.refs_4_), channel_id=1, source_target_pairs={{192,0},{0,64},{64,128},{128,192},{193,1},{1,65},{65,129},{129,193... | collective-permute-start | bytes 1179656 | tf_op jit(solution)/shard_map/ppermute | solution.py:23
  34.0 15.8 %collective-permute-start.9 = (bf16[4,2,48,512]{3,2,1,0:T(8,128)(2,1)S(1)}, bf16[4,2,48,512]{3,2,1,0:T(8,128)(2,1)S(1)}, u32[]{:S(2)}, u32[]{:S(2)}) collective-permute-start(bf16[4,2,48,512]{3,2,1,0:T(8,128)(2,1)S(1)} %pad_maximum_fusion.2.refs_0_), channel_id=1, source_target_pairs={{56,0},{0,8},{8,16},{16,24},{24,32},{32,40},{40,48},{48,56},{57,1}... | collective-permute-start | bytes 1179656 | tf_op jit(solution)/shard_map/ppermute | solution.py:23
  38.4 11.4 %collective-permute-start.11 = (bf16[4,2,48,512]{3,2,1,0:T(8,128)(2,1)S(1)}, bf16[4,2,48,512]{3,2,1,0:T(8,128)(2,1)S(1)}, u32[]{:S(2)}, u32[]{:S(2)}) collective-permute-start(bf16[4,2,48,512]{3,2,1,0:T(8,128)(2,1)S(1)} %collective-permute-done.10.refs_5_), channel_id=1, source_target_pairs={{64,0},{128,64},{192,128},{0,192},{65,1},{129,65},{193,129},{1,193... | collective-permute-start | bytes 1179656 | tf_op jit(solution)/shard_map/ppermute | solution.py:23
  42.1 7.8 %collective-permute-start.8 = (bf16[4,2,48,512]{3,2,1,0:T(8,128)(2,1)S(1)}, bf16[4,2,48,512]{3,2,1,0:T(8,128)(2,1)S(1)}, u32[]{:S(2)}, u32[]{:S(2)}) collective-permute-start(bf16[4,2,48,512]{3,2,1,0:T(8,128)(2,1)S(1)} %collective-permute-done.7.refs_1_), channel_id=1, source_target_pairs={{8,0},{16,8},{24,16},{32,24},{40,32},{48,40},{56,48},{0,56},{9,1},... | collective-permute-start | bytes 1179656 | tf_op jit(solution)/shard_map/ppermute | solution.py:23
  59.2 8.0 %collective-permute-start.14 = (bf16[192,512]{1,0:T(8,128)(2,1)S(1)}, bf16[192,512]{1,0:T(8,128)(2,1)S(1)}, u32[]{:S(2)}, u32[]{:S(2)}) collective-permute-start(bf16[192,512]{1,0:T(8,128)(2,1)S(1)} %get-tuple-element.54), channel_id=1, source_target_pairs={{0,2},{2,4},{4,6},{6,0},{1,3},{3,5},{5,7},{7,1},{8,10},{10,12},{12... | collective-permute-start | bytes 589832 | tf_op jit(solution)/shard_map/ppermute | solution.py:28
  59.9 12.3 %collective-permute-start.15 = (bf16[192,512]{1,0:T(8,128)(2,1)S(1)}, bf16[192,512]{1,0:T(8,128)(2,1)S(1)}, u32[]{:S(2)}, u32[]{:S(2)}) collective-permute-start(bf16[192,512]{1,0:T(8,128)(2,1)S(1)} %get-tuple-element.55), channel_id=1, source_target_pairs={{0,4},{2,6},{4,0},{6,2},{1,5},{3,7},{5,1},{7,3},{8,12},{10,14},{12... | collective-permute-start | bytes 589832 | tf_op jit(solution)/shard_map/ppermute | solution.py:28
  62.4 11.2 %collective-permute-start.16 = (bf16[192,512]{1,0:T(8,128)(2,1)S(1)}, bf16[192,512]{1,0:T(8,128)(2,1)S(1)}, u32[]{:S(2)}, u32[]{:S(2)}) collective-permute-start(bf16[192,512]{1,0:T(8,128)(2,1)S(1)} %get-tuple-element.56), channel_id=1, source_target_pairs={{0,6},{2,0},{4,2},{6,4},{1,7},{3,1},{5,3},{7,5},{8,14},{10,8},{12,... | collective-permute-start | bytes 589832 | tf_op jit(solution)/shard_map/ppermute | solution.py:28
  62.8 15.8 %collective-permute-start.17 = (bf16[192,512]{1,0:T(8,128)(2,1)S(1)}, bf16[192,512]{1,0:T(8,128)(2,1)S(1)}, u32[]{:S(2)}, u32[]{:S(2)}) collective-permute-start(bf16[192,512]{1,0:T(8,128)(2,1)S(1)} %get-tuple-element.59), channel_id=1, source_target_pairs={{0,2},{2,4},{4,6},{6,0},{1,3},{3,5},{5,7},{7,1},{8,10},{10,12},{12... | collective-permute-start | bytes 589832 | tf_op jit(solution)/shard_map/ppermute | solution.py:28
  66.1 13.9 %collective-permute-start.18 = (bf16[192,512]{1,0:T(8,128)(2,1)S(1)}, bf16[192,512]{1,0:T(8,128)(2,1)S(1)}, u32[]{:S(2)}, u32[]{:S(2)}) collective-permute-start(bf16[192,512]{1,0:T(8,128)(2,1)S(1)} %get-tuple-element.60), channel_id=1, source_target_pairs={{0,4},{2,6},{4,0},{6,2},{1,5},{3,7},{5,1},{7,3},{8,12},{10,14},{12... | collective-permute-start | bytes 589832 | tf_op jit(solution)/shard_map/ppermute | solution.py:28
  67.2 14.8 %collective-permute-start.19 = (bf16[192,512]{1,0:T(8,128)(2,1)S(1)}, bf16[192,512]{1,0:T(8,128)(2,1)S(1)}, u32[]{:S(2)}, u32[]{:S(2)}) collective-permute-start(bf16[192,512]{1,0:T(8,128)(2,1)S(1)} %get-tuple-element.61), channel_id=1, source_target_pairs={{0,6},{2,0},{4,2},{6,4},{1,7},{3,1},{5,3},{7,5},{8,14},{10,8},{12,... | collective-permute-start | bytes 589832 | tf_op jit(solution)/shard_map/ppermute | solution.py:28
  73.9 11.4 %collective-permute-start.26 = (bf16[192,512]{1,0:T(8,128)(2,1)S(1)}, bf16[192,512]{1,0:T(8,128)(2,1)S(1)}, u32[]{:S(2)}, u32[]{:S(2)}) collective-permute-start(bf16[192,512]{1,0:T(8,128)(2,1)S(1)} %get-tuple-element.65), channel_id=1, source_target_pairs={{6,0},{0,2},{2,4},{4,6},{7,1},{1,3},{3,5},{5,7},{14,8},{8,10},{10,... | collective-permute-start | bytes 589832 | tf_op jit(solution)/shard_map/ppermute | solution.py:23
  74.5 13.1 %collective-permute-start.25 = (bf16[192,512]{1,0:T(8,128)(2,1)S(1)}, bf16[192,512]{1,0:T(8,128)(2,1)S(1)}, u32[]{:S(2)}, u32[]{:S(2)}) collective-permute-start(bf16[192,512]{1,0:T(8,128)(2,1)S(1)} %get-tuple-element.65), channel_id=1, source_target_pairs={{4,0},{6,2},{0,4},{2,6},{5,1},{7,3},{1,5},{3,7},{12,8},{14,10},{8,... | collective-permute-start | bytes 589832 | tf_op jit(solution)/shard_map/ppermute | solution.py:23
  78.5 14.0 %collective-permute-start.24 = (bf16[192,512]{1,0:T(8,128)(2,1)S(1)}, bf16[192,512]{1,0:T(8,128)(2,1)S(1)}, u32[]{:S(2)}, u32[]{:S(2)}) collective-permute-start(bf16[192,512]{1,0:T(8,128)(2,1)S(1)} %get-tuple-element.65), channel_id=1, source_target_pairs={{2,0},{4,2},{6,4},{0,6},{3,1},{5,3},{7,5},{1,7},{10,8},{12,10},{14... | collective-permute-start | bytes 589832 | tf_op jit(solution)/shard_map/ppermute | solution.py:23
  82.3 10.4 %collective-permute-start.22 = (bf16[192,512]{1,0:T(8,128)(2,1)S(1)}, bf16[192,512]{1,0:T(8,128)(2,1)S(1)}, u32[]{:S(2)}, u32[]{:S(2)}) collective-permute-start(bf16[192,512]{1,0:T(8,128)(2,1)S(1)} %get-tuple-element.63), channel_id=1, source_target_pairs={{6,0},{0,2},{2,4},{4,6},{7,1},{1,3},{3,5},{5,7},{14,8},{8,10},{10,... | collective-permute-start | bytes 589832 | tf_op jit(solution)/shard_map/ppermute | solution.py:23
  83.0 11.6 %collective-permute-start.21 = (bf16[192,512]{1,0:T(8,128)(2,1)S(1)}, bf16[192,512]{1,0:T(8,128)(2,1)S(1)}, u32[]{:S(2)}, u32[]{:S(2)}) collective-permute-start(bf16[192,512]{1,0:T(8,128)(2,1)S(1)} %get-tuple-element.63), channel_id=1, source_target_pairs={{4,0},{6,2},{0,4},{2,6},{5,1},{7,3},{1,5},{3,7},{12,8},{14,10},{8,... | collective-permute-start | bytes 589832 | tf_op jit(solution)/shard_map/ppermute | solution.py:23
  85.3 12.3 %collective-permute-start.20 = (bf16[192,512]{1,0:T(8,128)(2,1)S(1)}, bf16[192,512]{1,0:T(8,128)(2,1)S(1)}, u32[]{:S(2)}, u32[]{:S(2)}) collective-permute-start(bf16[192,512]{1,0:T(8,128)(2,1)S(1)} %get-tuple-element.63), channel_id=1, source_target_pairs={{2,0},{4,2},{6,4},{0,6},{3,1},{5,3},{7,5},{1,7},{10,8},{12,10},{14... | collective-permute-start | bytes 589832 | tf_op jit(solution)/shard_map/ppermute | solution.py:23
  105.2 12.8 %collective-permute-start.29 = (bf16[4,2,48,512]{3,2,1,0:T(8,128)(2,1)S(1)}, bf16[4,2,48,512]{3,2,1,0:T(8,128)(2,1)S(1)}, u32[]{:S(2)}, u32[]{:S(2)}) collective-permute-start(bf16[4,2,48,512]{3,2,1,0:T(8,128)(2,1)S(1)} %get-tuple-element.71), channel_id=1, source_target_pairs={{0,8},{8,16},{16,24},{24,32},{32,40},{40,48},{48,56},{56,0},{1,9},... | collective-permute-start | bytes 1179656 | tf_op jit(solution)/shard_map/ppermute | solution.py:28
  105.6 12.7 %collective-permute-start.32 = (bf16[4,2,48,512]{3,2,1,0:T(8,128)(2,1)S(1)}, bf16[4,2,48,512]{3,2,1,0:T(8,128)(2,1)S(1)}, u32[]{:S(2)}, u32[]{:S(2)}) collective-permute-start(bf16[4,2,48,512]{3,2,1,0:T(8,128)(2,1)S(1)} %get-tuple-element.75), channel_id=1, source_target_pairs={{0,64},{64,128},{128,192},{192,0},{1,65},{65,129},{129,193},{193,1... | collective-permute-start | bytes 1179656 | tf_op jit(solution)/shard_map/ppermute | solution.py:28
  105.6 21.8 %collective-permute-start.28 = (bf16[4,2,48,512]{3,2,1,0:T(8,128)(2,1)S(1)}, bf16[4,2,48,512]{3,2,1,0:T(8,128)(2,1)S(1)}, u32[]{:S(2)}, u32[]{:S(2)}) collective-permute-start(bf16[4,2,48,512]{3,2,1,0:T(8,128)(2,1)S(1)} %get-tuple-element.69), channel_id=1, source_target_pairs={{0,56},{8,0},{16,8},{24,16},{32,24},{40,32},{48,40},{56,48},{1,57}... | collective-permute-start | bytes 1179656 | tf_op jit(solution)/shard_map/ppermute | solution.py:28
  108.6 21.8 %collective-permute-start.31 = (bf16[4,2,48,512]{3,2,1,0:T(8,128)(2,1)S(1)}, bf16[4,2,48,512]{3,2,1,0:T(8,128)(2,1)S(1)}, u32[]{:S(2)}, u32[]{:S(2)}) collective-permute-start(bf16[4,2,48,512]{3,2,1,0:T(8,128)(2,1)S(1)} %get-tuple-element.73), channel_id=1, source_target_pairs={{0,192},{64,0},{128,64},{192,128},{1,193},{65,1},{129,65},{193,129... | collective-permute-start | bytes 1179656 | tf_op jit(solution)/shard_map/ppermute | solution.py:28
  118.2 12.0 %collective-permute-start.30 = (bf16[4,2,48,512]{3,2,1,0:T(8,128)(2,1)S(1)}, bf16[4,2,48,512]{3,2,1,0:T(8,128)(2,1)S(1)}, u32[]{:S(2)}, u32[]{:S(2)}) collective-permute-start(bf16[4,2,48,512]{3,2,1,0:T(8,128)(2,1)S(1)} %add_convert_fusion.1), channel_id=1, source_target_pairs={{0,8},{8,16},{16,24},{24,32},{32,40},{40,48},{48,56},{56,0},{1,9},... | collective-permute-start | bytes 1179656 | tf_op jit(solution)/shard_map/ppermute | solution.py:28
  118.4 12.0 %collective-permute-start.33 = (bf16[4,2,48,512]{3,2,1,0:T(8,128)(2,1)S(1)}, bf16[4,2,48,512]{3,2,1,0:T(8,128)(2,1)S(1)}, u32[]{:S(2)}, u32[]{:S(2)}) collective-permute-start(bf16[4,2,48,512]{3,2,1,0:T(8,128)(2,1)S(1)} %add_convert_fusion), channel_id=1, source_target_pairs={{0,64},{64,128},{128,192},{192,0},{1,65},{65,129},{129,193},{193,1... | collective-permute-start | bytes 1179656 | tf_op jit(solution)/shard_map/ppermute | solution.py:28
  130.7 11.1 %collective-permute-start.34 = (bf16[2,48,512]{2,1,0:T(8,128)(2,1)S(1)}, bf16[2,48,512]{2,1,0:T(8,128)(2,1)S(1)}, u32[]{:S(2)}, u32[]{:S(2)}) collective-permute-start(bf16[2,48,512]{2,1,0:T(8,128)(2,1)S(1)} %get-tuple-element.83), channel_id=1, source_target_pairs={{0,192},{64,0},{128,64},{192,128},{1,193},{65,1},{129,65},{193,129... | collective-permute-start | bytes 294920 | tf_op jit(solution)/shard_map/ppermute | solution.py:28
  132.9 10.9 %collective-permute-start.37 = (bf16[2,48,512]{2,1,0:T(8,128)(2,1)S(1)}, bf16[2,48,512]{2,1,0:T(8,128)(2,1)S(1)}, u32[]{:S(2)}, u32[]{:S(2)}) collective-permute-start(bf16[2,48,512]{2,1,0:T(8,128)(2,1)S(1)} %get-tuple-element.81), channel_id=1, source_target_pairs={{0,56},{8,0},{16,8},{24,16},{32,24},{40,32},{48,40},{56,48},{1,57}... | collective-permute-start | bytes 294920 | tf_op jit(solution)/shard_map/ppermute | solution.py:28
  141.7 7.0 %collective-permute-start.39 = (bf16[2,48,512]{2,1,0:T(8,128)(2,1)S(1)}, bf16[2,48,512]{2,1,0:T(8,128)(2,1)S(1)}, u32[]{:S(2)}, u32[]{:S(2)}) collective-permute-start(bf16[2,48,512]{2,1,0:T(8,128)(2,1)S(1)} %fusion.5), channel_id=1, source_target_pairs={{0,8},{8,16},{16,24},{24,32},{32,40},{40,48},{48,56},{56,0},{1,9},... | collective-permute-start | bytes 294920 | tf_op jit(solution)/shard_map/ppermute | solution.py:28
  148.8 8.6 %collective-permute-start.40 = (bf16[48,1024]{1,0:T(8,128)(2,1)S(1)}, bf16[48,1024]{1,0:T(8,128)(2,1)S(1)}, u32[]{:S(2)}, u32[]{:S(2)}) collective-permute-start(bf16[48,1024]{1,0:T(8,128)(2,1)S(1)} %fusion.10), channel_id=1, source_target_pairs={{0,32},{8,40},{16,48},{24,56},{32,0},{40,8},{48,16},{56,24},{1,33}... | collective-permute-start | bytes 294920 | tf_op jit(solution)/shard_map/ppermute | solution.py:28
  (11 other events, 60.3 us)

commit v9 on v7

--- a/solution.py
+++ b/solution.py
@@ -70,7 +70,7 @@
 
 def up_body(pos, *refs):
     a3, b3, w = refs[:4], refs[4:8], refs[8]
-    keep, send, toks, acc = refs[9:]
+    keep, send1, send2, toks, acc = refs[9:]
     core = pos[3]
     cut = a3[0].shape[-1]
     back = pos[0] - pos[2] + 4
@@ -91,7 +91,10 @@
         )
         acc[...] = part.reshape(acc.shape)
         keep[d] = acc[core]
-        send[d] = acc[1 - core].astype(BF16)
+        away = acc[1 - core].astype(BF16)
+        half = send1.shape[2]
+        send1[d] = away[:, :half]
+        send2[d] = away[:, half:]
 
 
 def collect(pos, mine, other, slots, sems):
@@ -156,7 +159,7 @@
         @pl.loop(0, keep.shape[1] // 16)
         def _(i, d=d):
             at = pl.ds(pl.multiple_of(i * 16, 16), 16)
-            total = keep[d, at, cols] + recv[d, at, cols].astype(F32)
+            total = keep[d, at, cols] + recv[d, at].astype(F32)
             out[d][at] = total.astype(out[d].dtype)
 
 
@@ -248,11 +251,12 @@
     depth, width = wm.shape
     cut = width // 2
     flops = 8 * rows * depth * width
-    keep, send, toks = call(
+    keep, send1, send2, toks = call(
         up_body,
         [
             ((4, rows, width), F32),
-            ((4, rows, width), BF16),
+            ((4, rows, cut), BF16),
+            ((4, rows, cut), BF16),
             ((4, 8, rows // 4, depth), BF16),
         ],
         [pos],
@@ -260,10 +264,9 @@
         2 * flops,
         [VM((2, rows, width), F32)],
     )
-    recv = to_ahead(send, "core", 1)
     cols1, cols2 = slice(0, cut), slice(cut, width)
-    own1, *sends1 = partial_sums(keep, recv, cols1)
-    own2, *sends2 = partial_sums(keep, recv, cols2)
+    own1, *sends1 = partial_sums(keep, to_ahead(send1, "core", 1), cols1)
+    own2, *sends2 = partial_sums(keep, to_ahead(send2, "core", 1), cols2)
     hidden1, grad1 = activation(own1, sends1, cot, cols1)
     hidden2, grad2 = activation(own2, sends2, cot, cols2)
     hidden = jnp.concatenate([hidden1, hidden2], axis=1)

time: 157 us -> 156 us (level)
    ppermute x22 -> x23, waiting for transfers between devices: 28.3 us -> 25.6 us  [to_ahead(): return lax.ppermute(value, axis, [(i, (i + k) % n) for i in range(n)])]
    ppermute x19, starting transfers between devices: 39.1 us -> 41.5 us  [from_ahead(): return lax.ppermute(value, axis, [((i + k) % n, i) for i in range(n)])]
    ppermute x19, waiting for transfers between devices: 20.1 us -> 21.8 us  [from_ahead(): return lax.ppermute(value, axis, [((i + k) % n, i) for i in range(n)])]
    ppermute x22 -> x23, starting transfers between devices: 34.4 us -> 33 us  [to_ahead(): return lax.ppermute(value, axis, [(i, (i + k) % n) for i in range(n)])]
  transfers between devices with their start and end apart: 41 -> 42, of which waited for: 21 -> 22; matrix products, arithmetic and copies ran while one was open for 2% -> 2% of each run, Pallas kernels for 10% -> 10%
where the time goes in v9:
time: 156 us; the launch traced here: 154 us
  starting transfers between devices  74.5 us (48%)
  waiting for transfers between devices  47.4 us (30%)
  Pallas kernels  24.7 us (16%)
  other arithmetic  4.17 us (3%)
  local copies, waits for them, and re-layouts  1.64 us (1%)
    ppermute x19, starting transfers between devices, from_ahead(): return lax.ppermute(value, axis, [((i + k) % n, i) for i in range(n)])  41.5 us
    ppermute x23, starting transfers between devices, to_ahead(): return lax.ppermute(value, axis, [(i, (i + k) % n) for i in range(n)])  33 us
    ppermute x23, waiting for transfers between devices, to_ahead(): return lax.ppermute(value, axis, [(i, (i + k) % n) for i in range(n)])  25.6 us
    pallas_call x9, Pallas kernels, call(): pl.pallas_call(body, out_shape=outs, in_specs=[pl.BlockSpec(memory_space=...  24.7 us
    ppermute x19, waiting for transfers between devices, from_ahead(): return lax.ppermute(value, axis, [((i + k) % n, i) for i in range(n)])  21.8 us
  transfers between devices with their start and end apart: 42, of which 22 were waited for; matrix products, arithmetic and copies ran while one was open for 2% of the time, Pallas kernels for 10%

profile of v9, /device:TPU:6, one launch (start us, length us, event | category | flops | bytes accessed | tf_op | source)
XLA Modules:
  0.0 154.0 jit_solution(3853624796029333576)
XLA Ops:
  0.6 7.3 %collective-permute-start = (bf16[48,1024]{1,0:T(8,128)(2,1)}, bf16[48,1024]{1,0:T(8,128)(2,1)S(1)}, u32[]{:S(2)}, u32[]{:S(2)}) collective-permute-start(bf16[48,1024]{1,0:T(8,128)(2,1)} %param.6), channel_id=1, source_target_pairs={{32,0},{40,8},{48,16},{56,24},{0,32},{8,40},{16,48},{24,56},{33,1}... | collective-permute-start | bytes 294920 | tf_op jit(solution)/shard_map/ppermute | solution.py:23
  7.9 3.1 %collective-permute-done = bf16[48,1024]{1,0:T(8,128)(2,1)S(1)} collective-permute-done((bf16[48,1024]{1,0:T(8,128)(2,1)}, bf16[48,1024]{1,0:T(8,128)(2,1)S(1)}, u32[]{:S(2)}, u32[]{:S(2)}) %collective-permute-start) | collective-permute-done | bytes 98336 | tf_op jit(solution)/shard_map/ppermute | solution.py:23
  11.9 2.6 %collective-permute-start.6 = (bf16[2,48,512]{2,1,0:T(8,128)(2,1)S(1)}, bf16[2,48,512]{2,1,0:T(8,128)(2,1)S(1)}, u32[]{:S(2)}, u32[]{:S(2)}) collective-permute-start(bf16[2,48,512]{2,1,0:T(8,128)(2,1)S(1)} %get-tuple-element.47), channel_id=1, source_target_pairs={{56,0},{0,8},{8,16},{16,24},{24,32},{32,40},{40,48},{48,56},{57,1}... | collective-permute-start | bytes 294920 | tf_op jit(solution)/shard_map/ppermute | solution.py:23
  14.4 4.2 %collective-permute-start.5 = (bf16[2,48,512]{2,1,0:T(8,128)(2,1)S(1)}, bf16[2,48,512]{2,1,0:T(8,128)(2,1)S(1)}, u32[]{:S(2)}, u32[]{:S(2)}) collective-permute-start(bf16[2,48,512]{2,1,0:T(8,128)(2,1)S(1)} %get-tuple-element.47), channel_id=1, source_target_pairs={{16,0},{24,8},{32,16},{40,24},{48,32},{56,40},{0,48},{8,56},{17,1}... | collective-permute-start | bytes 294920 | tf_op jit(solution)/shard_map/ppermute | solution.py:23
  18.6 1.9 %collective-permute-start.4 = (bf16[2,48,512]{2,1,0:T(8,128)(2,1)S(1)}, bf16[2,48,512]{2,1,0:T(8,128)(2,1)S(1)}, u32[]{:S(2)}, u32[]{:S(2)}) collective-permute-start(bf16[2,48,512]{2,1,0:T(8,128)(2,1)S(1)} %get-tuple-element.47), channel_id=1, source_target_pairs={{8,0},{16,8},{24,16},{32,24},{40,32},{48,40},{56,48},{0,56},{9,1},... | collective-permute-start | bytes 294920 | tf_op jit(solution)/shard_map/ppermute | solution.py:23
  22.1 2.9 %collective-permute-start.2 = (bf16[2,48,512]{2,1,0:T(8,128)(2,1)S(1)}, bf16[2,48,512]{2,1,0:T(8,128)(2,1)S(1)}, u32[]{:S(2)}, u32[]{:S(2)}) collective-permute-start(bf16[2,48,512]{2,1,0:T(8,128)(2,1)S(1)} %get-tuple-element.43), channel_id=1, source_target_pairs={{128,0},{192,64},{0,128},{64,192},{129,1},{193,65},{1,129},{65,193... | collective-permute-start | bytes 294920 | tf_op jit(solution)/shard_map/ppermute | solution.py:23
  29.9 2.4 %collective-permute-start.10 = (bf16[4,2,48,512]{3,2,1,0:T(8,128)(2,1)S(1)}, bf16[4,2,48,512]{3,2,1,0:T(8,128)(2,1)S(1)}, u32[]{:S(2)}, u32[]{:S(2)}) collective-permute-start(bf16[4,2,48,512]{3,2,1,0:T(8,128)(2,1)S(1)} %pad_maximum_fusion.3.refs_4_), channel_id=1, source_target_pairs={{64,0},{128,64},{192,128},{0,192},{65,1},{129,65},{193,129},{1,193... | collective-permute-start | bytes 1179656 | tf_op jit(solution)/shard_map/ppermute | solution.py:23
  34.5 4.8 %collective-permute-done.10.refs_5_ = bf16[4,2,48,512]{3,2,1,0:T(8,128)(2,1)S(1)} collective-permute-done((bf16[4,2,48,512]{3,2,1,0:T(8,128)(2,1)S(1)}, bf16[4,2,48,512]{3,2,1,0:T(8,128)(2,1)S(1)}, u32[]{:S(2)}, u32[]{:S(2)}) %collective-permute-start.10) | collective-permute-done | bytes 393248 | tf_op jit(solution)/shard_map/ppermute | solution.py:23
  39.3 2.3 %collective-permute-start.11 = (bf16[4,2,48,512]{3,2,1,0:T(8,128)(2,1)S(1)}, bf16[4,2,48,512]{3,2,1,0:T(8,128)(2,1)S(1)}, u32[]{:S(2)}, u32[]{:S(2)}) collective-permute-start(bf16[4,2,48,512]{3,2,1,0:T(8,128)(2,1)S(1)} %collective-permute-done.10.refs_5_), channel_id=1, source_target_pairs={{64,0},{128,64},{192,128},{0,192},{65,1},{129,65},{193,129},{1,193... | collective-permute-start | bytes 1179656 | tf_op jit(solution)/shard_map/ppermute | solution.py:23
  41.6 2.3 %collective-permute-start.8 = (bf16[4,2,48,512]{3,2,1,0:T(8,128)(2,1)S(1)}, bf16[4,2,48,512]{3,2,1,0:T(8,128)(2,1)S(1)}, u32[]{:S(2)}, u32[]{:S(2)}) collective-permute-start(bf16[4,2,48,512]{3,2,1,0:T(8,128)(2,1)S(1)} %collective-permute-done.7.refs_1_), channel_id=1, source_target_pairs={{8,0},{16,8},{24,16},{32,24},{40,32},{48,40},{56,48},{0,56},{9,1},... | collective-permute-start | bytes 1179656 | tf_op jit(solution)/shard_map/ppermute | solution.py:23
  46.9 1.9 %shard_map.85 = (bf16[1024,1024]{1,0:T(8,128)(2,1)S(1)}, bf16[1024,1024]{1,0:T(8,128)(2,1)S(1)}) custom-call(s32[32]{0:T(128)S(1)} %get-tuple-element.92.rows, s32[32]{0:T(128)S(1)} %get-tuple-element.91.cols, s32[1]{0:T(128)} %bitcast.59.count, bf16[1024,1024]{1,0:T(8,128)(2,1)S(1)} %copy-done), custom_call_target="tpu_custom_call" | custom-call | bytes 6291456 | tf_op jit(solution)/shard_map/pallas_call | solution.py:33
  49.4 5.4 %shard_map.86 = (f32[4,192,1024]{2,1,0:T(8,128)S(1)}, bf16[4,192,512]{2,1,0:T(8,128)(2,1)S(1)}, bf16[4,192,512]{2,1,0:T(8,128)(2,1)S(1)}, bf16[4,8,48,1024]{3,2,1,0:T(8,128)(2,1)S(1)}) custom-call(s32[4]{0:T(128)S(1)} %pad_add_fusion.pos, bf16[4,2,48,512]{3,2,1,0:T(8,128)(2,1)S(1)} %pad_maximum_fusion.2.refs_0_, ...), custom_call_target="tpu_custom_call" | custom-call | flops 3221225472 | bytes 13107200 | tf_op jit(solution)/shard_map/pallas_call | solution.py:33
  58.7 2.0 %collective-permute-start.15 = (bf16[192,512]{1,0:T(8,128)(2,1)S(1)}, bf16[192,512]{1,0:T(8,128)(2,1)S(1)}, u32[]{:S(2)}, u32[]{:S(2)}) collective-permute-start(bf16[192,512]{1,0:T(8,128)(2,1)S(1)} %get-tuple-element.56), channel_id=1, source_target_pairs={{0,4},{2,6},{4,0},{6,2},{1,5},{3,7},{5,1},{7,3},{8,12},{10,14},{12... | collective-permute-start | bytes 589832 | tf_op jit(solution)/shard_map/ppermute | solution.py:28
  61.1 3.3 %collective-permute-start.18 = (bf16[192,512]{1,0:T(8,128)(2,1)S(1)}, bf16[192,512]{1,0:T(8,128)(2,1)S(1)}, u32[]{:S(2)}, u32[]{:S(2)}) collective-permute-start(bf16[192,512]{1,0:T(8,128)(2,1)S(1)} %get-tuple-element.61), channel_id=1, source_target_pairs={{0,2},{2,4},{4,6},{6,0},{1,3},{3,5},{5,7},{7,1},{8,10},{10,12},{12... | collective-permute-start | bytes 589832 | tf_op jit(solution)/shard_map/ppermute | solution.py:28
  65.4 5.2 %collective-permute-start.20 = (bf16[192,512]{1,0:T(8,128)(2,1)S(1)}, bf16[192,512]{1,0:T(8,128)(2,1)S(1)}, u32[]{:S(2)}, u32[]{:S(2)}) collective-permute-start(bf16[192,512]{1,0:T(8,128)(2,1)S(1)} %get-tuple-element.63), channel_id=1, source_target_pairs={{0,6},{2,0},{4,2},{6,4},{1,7},{3,1},{5,3},{7,5},{8,14},{10,8},{12,... | collective-permute-start | bytes 589832 | tf_op jit(solution)/shard_map/ppermute | solution.py:28
  73.2 2.0 %collective-permute-start.26 = (bf16[192,512]{1,0:T(8,128)(2,1)S(1)}, bf16[192,512]{1,0:T(8,128)(2,1)S(1)}, u32[]{:S(2)}, u32[]{:S(2)}) collective-permute-start(bf16[192,512]{1,0:T(8,128)(2,1)S(1)} %get-tuple-element.67), channel_id=1, source_target_pairs={{4,0},{6,2},{0,4},{2,6},{5,1},{7,3},{1,5},{3,7},{12,8},{14,10},{8,... | collective-permute-start | bytes 589832 | tf_op jit(solution)/shard_map/ppermute | solution.py:23
  75.1 2.8 %collective-permute-start.25 = (bf16[192,512]{1,0:T(8,128)(2,1)S(1)}, bf16[192,512]{1,0:T(8,128)(2,1)S(1)}, u32[]{:S(2)}, u32[]{:S(2)}) collective-permute-start(bf16[192,512]{1,0:T(8,128)(2,1)S(1)} %get-tuple-element.67), channel_id=1, source_target_pairs={{2,0},{4,2},{6,4},{0,6},{3,1},{5,3},{7,5},{1,7},{10,8},{12,10},{14... | collective-permute-start | bytes 589832 | tf_op jit(solution)/shard_map/ppermute | solution.py:23
  77.9 2.8 %collective-permute-done.20.r3 = bf16[192,512]{1,0:T(8,128)(2,1)S(1)} collective-permute-done((bf16[192,512]{1,0:T(8,128)(2,1)S(1)}, bf16[192,512]{1,0:T(8,128)(2,1)S(1)}, u32[]{:S(2)}, u32[]{:S(2)}) %collective-permute-start.20) | collective-permute-done | bytes 196640 | tf_op jit(solution)/shard_map/ppermute | solution.py:28
  81.7 2.0 %collective-permute-start.22 = (bf16[192,512]{1,0:T(8,128)(2,1)S(1)}, bf16[192,512]{1,0:T(8,128)(2,1)S(1)}, u32[]{:S(2)}, u32[]{:S(2)}) collective-permute-start(bf16[192,512]{1,0:T(8,128)(2,1)S(1)} %get-tuple-element.65), channel_id=1, source_target_pairs={{4,0},{6,2},{0,4},{2,6},{5,1},{7,3},{1,5},{3,7},{12,8},{14,10},{8,... | collective-permute-start | bytes 589832 | tf_op jit(solution)/shard_map/ppermute | solution.py:23
  83.6 2.7 %collective-permute-start.21 = (bf16[192,512]{1,0:T(8,128)(2,1)S(1)}, bf16[192,512]{1,0:T(8,128)(2,1)S(1)}, u32[]{:S(2)}, u32[]{:S(2)}) collective-permute-start(bf16[192,512]{1,0:T(8,128)(2,1)S(1)} %get-tuple-element.65), channel_id=1, source_target_pairs={{2,0},{4,2},{6,4},{0,6},{3,1},{5,3},{7,5},{1,7},{10,8},{12,10},{14... | collective-permute-start | bytes 589832 | tf_op jit(solution)/shard_map/ppermute | solution.py:23
  86.3 2.8 %collective-permute-done.25 = bf16[192,512]{1,0:T(8,128)(2,1)S(1)} collective-permute-done((bf16[192,512]{1,0:T(8,128)(2,1)S(1)}, bf16[192,512]{1,0:T(8,128)(2,1)S(1)}, u32[]{:S(2)}, u32[]{:S(2)}) %collective-permute-start.25) | collective-permute-done | bytes 196640 | tf_op jit(solution)/shard_map/ppermute | solution.py:23
  90.8 2.6 %collective-permute-done.22 = bf16[192,512]{1,0:T(8,128)(2,1)S(1)} collective-permute-done((bf16[192,512]{1,0:T(8,128)(2,1)S(1)}, bf16[192,512]{1,0:T(8,128)(2,1)S(1)}, u32[]{:S(2)}, u32[]{:S(2)}) %collective-permute-start.22) | collective-permute-done | bytes 196640 | tf_op jit(solution)/shard_map/ppermute | solution.py:23
  93.4 2.9 %collective-permute-done.21 = bf16[192,512]{1,0:T(8,128)(2,1)S(1)} collective-permute-done((bf16[192,512]{1,0:T(8,128)(2,1)S(1)}, bf16[192,512]{1,0:T(8,128)(2,1)S(1)}, u32[]{:S(2)}, u32[]{:S(2)}) %collective-permute-start.21) | collective-permute-done | bytes 196640 | tf_op jit(solution)/shard_map/ppermute | solution.py:23
  96.6 3.0 %shard_map.91 = (f32[4,8,48,1024]{3,2,1,0:T(8,128)S(1)}, bf16[4,2,192,512]{3,2,1,0:T(8,128)(2,1)S(1)}) custom-call(s32[4]{0:T(128)S(1)} %pad_add_fusion.pos, bf16[4,192,512]{2,1,0:T(8,128)(2,1)S(1)} %pad_maximum_fusion.1.refs_0_, bf16[4,192,512]{2,1,0:T(8,128)(2,1)S(1)} %collective-permute-done.28.refs_1_, bf16[1024,1024]{1,0:T(8,128)(2,1)S(1)} %get-tuple-element.66.refs_2_), custom_call_target="tpu_custom_call" | custom-call | flops 1610612736 | bytes 11534336 | tf_op jit(solution)/shard_map/pallas_call | solution.py:33
  99.6 4.4 %shard_map.92 = (f32[4,2,48,512]{3,2,1,0:T(8,128)S(1)}, f32[4,2,48,512]{3,2,1,0:T(8,128)S(1)}, bf16[4,2,48,512]{3,2,1,0:T(8,128)(2,1)S(1)}, bf16[4,2,48,512]{3,2...) custom-call(s32[4]{0:T(128)S(1)} %pad_add_fusion.pos, ...), custom_call_target="tpu_custom_call" | custom-call | flops 1610612736 | bytes 19398656 | tf_op jit(solution)/shard_map/pallas_call | solution.py:33
  105.4 3.5 %collective-permute-start.29 = (bf16[4,2,48,512]{3,2,1,0:T(8,128)(2,1)S(1)}, bf16[4,2,48,512]{3,2,1,0:T(8,128)(2,1)S(1)}, u32[]{:S(2)}, u32[]{:S(2)}) collective-permute-start(bf16[4,2,48,512]{3,2,1,0:T(8,128)(2,1)S(1)} %get-tuple-element.71), channel_id=1, source_target_pairs={{0,56},{8,0},{16,8},{24,16},{32,24},{40,32},{48,40},{56,48},{1,57}... | collective-permute-start | bytes 1179656 | tf_op jit(solution)/shard_map/ppermute | solution.py:28
  110.6 6.2 %collective-permute-done.30 = bf16[4,2,48,512]{3,2,1,0:T(8,128)(2,1)S(1)} collective-permute-done((bf16[4,2,48,512]{3,2,1,0:T(8,128)(2,1)S(1)}, bf16[4,2,48,512]{3,2,1,0:T(8,128)(2,1)S(1)}, u32[]{:S(2)}, u32[]{:S(2)}) %collective-permute-start.30) | collective-permute-done | bytes 393248 | tf_op jit(solution)/shard_map/ppermute | solution.py:28
  118.8 8.6 %shard_map.93 = bf16[1024,1024]{1,0:T(8,128)(2,1)} custom-call(s32[32]{0:T(128)S(1)} %get-tuple-element.92.rows, s32[32]{0:T(128)S(1)} %get-tuple-element.91.cols, s32[1]{0:T(128)} %bitcast.60.count, bf16[4,8,48,1024]{3,2,1,0:T(8,128)(2,1)S(1)} %get-tuple-element.78.toks, bf16[4,2,192,1024]{3,2,1,0:T(8,128)(2,1)S(1)} %get-tuple-element.79.grads), custom_call_target="tpu_custom_call" | custom-call | flops 3221225472 | bytes 8388608 | tf_op jit(solution)/shard_map/pallas_call | solution.py:33
  134.2 2.6 %collective-permute-start.40 = (bf16[2,48,512]{2,1,0:T(8,128)(2,1)S(1)}, bf16[2,48,512]{2,1,0:T(8,128)(2,1)S(1)}, u32[]{:S(2)}, u32[]{:S(2)}) collective-permute-start(bf16[2,48,512]{2,1,0:T(8,128)(2,1)S(1)} %get-tuple-element.84), channel_id=1, source_target_pairs={{0,56},{8,0},{16,8},{24,16},{32,24},{40,32},{48,40},{56,48},{1,57}... | collective-permute-start | bytes 294920 | tf_op jit(solution)/shard_map/ppermute | solution.py:28
  139.4 5.2 %collective-permute-done.39 = bf16[2,48,512]{2,1,0:T(8,128)(2,1)S(1)} collective-permute-done((bf16[2,48,512]{2,1,0:T(8,128)(2,1)S(1)}, bf16[2,48,512]{2,1,0:T(8,128)(2,1)S(1)}, u32[]{:S(2)}, u32[]{:S(2)}) %collective-permute-start.39) | collective-permute-done | bytes 98336 | tf_op jit(solution)/shard_map/ppermute | solution.py:28
  144.7 4.2 %collective-permute-start.41 = (bf16[48,1024]{1,0:T(8,128)(2,1)S(1)}, bf16[48,1024]{1,0:T(8,128)(2,1)S(1)}, u32[]{:S(2)}, u32[]{:S(2)}) collective-permute-start(bf16[48,1024]{1,0:T(8,128)(2,1)S(1)} %fusion.10), channel_id=1, source_target_pairs={{0,32},{8,40},{16,48},{24,56},{32,0},{40,8},{48,16},{56,24},{1,33}... | collective-permute-start | bytes 294920 | tf_op jit(solution)/shard_map/ppermute | solution.py:28
  149.7 3.6 %collective-permute-done.41 = bf16[48,1024]{1,0:T(8,128)(2,1)S(1)} collective-permute-done((bf16[48,1024]{1,0:T(8,128)(2,1)S(1)}, bf16[48,1024]{1,0:T(8,128)(2,1)S(1)}, u32[]{:S(2)}, u32[]{:S(2)}) %collective-permute-start.41) | collective-permute-done | bytes 98336 | tf_op jit(solution)/shard_map/ppermute | solution.py:28
  (85 shorter events, 38.9 us)
Async XLA Ops:
  0.6 10.4 %collective-permute-start = (bf16[48,1024]{1,0:T(8,128)(2,1)}, bf16[48,1024]{1,0:T(8,128)(2,1)S(1)}, u32[]{:S(2)}, u32[]{:S(2)}) collective-permute-start(bf16[48,1024]{1,0:T(8,128)(2,1)} %param.6), channel_id=1, source_target_pairs={{32,0},{40,8},{48,16},{56,24},{0,32},{8,40},{16,48},{24,56},{33,1}... | collective-permute-start | bytes 294920 | tf_op jit(solution)/shard_map/ppermute | solution.py:23
  11.9 13.2 %collective-permute-start.6 = (bf16[2,48,512]{2,1,0:T(8,128)(2,1)S(1)}, bf16[2,48,512]{2,1,0:T(8,128)(2,1)S(1)}, u32[]{:S(2)}, u32[]{:S(2)}) collective-permute-start(bf16[2,48,512]{2,1,0:T(8,128)(2,1)S(1)} %get-tuple-element.47), channel_id=1, source_target_pairs={{56,0},{0,8},{8,16},{16,24},{24,32},{32,40},{40,48},{48,56},{57,1}... | collective-permute-start | bytes 294920 | tf_op jit(solution)/shard_map/ppermute | solution.py:23
  14.4 12.0 %collective-permute-start.5 = (bf16[2,48,512]{2,1,0:T(8,128)(2,1)S(1)}, bf16[2,48,512]{2,1,0:T(8,128)(2,1)S(1)}, u32[]{:S(2)}, u32[]{:S(2)}) collective-permute-start(bf16[2,48,512]{2,1,0:T(8,128)(2,1)S(1)} %get-tuple-element.47), channel_id=1, source_target_pairs={{16,0},{24,8},{32,16},{40,24},{48,32},{56,40},{0,48},{8,56},{17,1}... | collective-permute-start | bytes 294920 | tf_op jit(solution)/shard_map/ppermute | solution.py:23
  18.6 7.8 %collective-permute-start.4 = (bf16[2,48,512]{2,1,0:T(8,128)(2,1)S(1)}, bf16[2,48,512]{2,1,0:T(8,128)(2,1)S(1)}, u32[]{:S(2)}, u32[]{:S(2)}) collective-permute-start(bf16[2,48,512]{2,1,0:T(8,128)(2,1)S(1)} %get-tuple-element.47), channel_id=1, source_target_pairs={{8,0},{16,8},{24,16},{32,24},{40,32},{48,40},{56,48},{0,56},{9,1},... | collective-permute-start | bytes 294920 | tf_op jit(solution)/shard_map/ppermute | solution.py:23
  29.9 9.4 %collective-permute-start.10 = (bf16[4,2,48,512]{3,2,1,0:T(8,128)(2,1)S(1)}, bf16[4,2,48,512]{3,2,1,0:T(8,128)(2,1)S(1)}, u32[]{:S(2)}, u32[]{:S(2)}) collective-permute-start(bf16[4,2,48,512]{3,2,1,0:T(8,128)(2,1)S(1)} %pad_maximum_fusion.3.refs_4_), channel_id=1, source_target_pairs={{64,0},{128,64},{192,128},{0,192},{65,1},{129,65},{193,129},{1,193... | collective-permute-start | bytes 1179656 | tf_op jit(solution)/shard_map/ppermute | solution.py:23
  32.4 9.2 %collective-permute-start.7 = (bf16[4,2,48,512]{3,2,1,0:T(8,128)(2,1)S(1)}, bf16[4,2,48,512]{3,2,1,0:T(8,128)(2,1)S(1)}, u32[]{:S(2)}, u32[]{:S(2)}) collective-permute-start(bf16[4,2,48,512]{3,2,1,0:T(8,128)(2,1)S(1)} %pad_maximum_fusion.2.refs_0_), channel_id=1, source_target_pairs={{8,0},{16,8},{24,16},{32,24},{40,32},{48,40},{56,48},{0,56},{9,1},... | collective-permute-start | bytes 1179656 | tf_op jit(solution)/shard_map/ppermute | solution.py:23
  33.7 15.1 %collective-permute-start.12 = (bf16[4,2,48,512]{3,2,1,0:T(8,128)(2,1)S(1)}, bf16[4,2,48,512]{3,2,1,0:T(8,128)(2,1)S(1)}, u32[]{:S(2)}, u32[]{:S(2)}) collective-permute-start(bf16[4,2,48,512]{3,2,1,0:T(8,128)(2,1)S(1)} %pad_maximum_fusion.3.refs_4_), channel_id=1, source_target_pairs={{192,0},{0,64},{64,128},{128,192},{193,1},{1,65},{65,129},{129,193... | collective-permute-start | bytes 1179656 | tf_op jit(solution)/shard_map/ppermute | solution.py:23
  34.2 14.7 %collective-permute-start.9 = (bf16[4,2,48,512]{3,2,1,0:T(8,128)(2,1)S(1)}, bf16[4,2,48,512]{3,2,1,0:T(8,128)(2,1)S(1)}, u32[]{:S(2)}, u32[]{:S(2)}) collective-permute-start(bf16[4,2,48,512]{3,2,1,0:T(8,128)(2,1)S(1)} %pad_maximum_fusion.2.refs_0_), channel_id=1, source_target_pairs={{56,0},{0,8},{8,16},{16,24},{24,32},{32,40},{40,48},{48,56},{57,1}... | collective-permute-start | bytes 1179656 | tf_op jit(solution)/shard_map/ppermute | solution.py:23
  39.3 9.6 %collective-permute-start.11 = (bf16[4,2,48,512]{3,2,1,0:T(8,128)(2,1)S(1)}, bf16[4,2,48,512]{3,2,1,0:T(8,128)(2,1)S(1)}, u32[]{:S(2)}, u32[]{:S(2)}) collective-permute-start(bf16[4,2,48,512]{3,2,1,0:T(8,128)(2,1)S(1)} %collective-permute-done.10.refs_5_), channel_id=1, source_target_pairs={{64,0},{128,64},{192,128},{0,192},{65,1},{129,65},{193,129},{1,193... | collective-permute-start | bytes 1179656 | tf_op jit(solution)/shard_map/ppermute | solution.py:23
  41.6 7.8 %collective-permute-start.8 = (bf16[4,2,48,512]{3,2,1,0:T(8,128)(2,1)S(1)}, bf16[4,2,48,512]{3,2,1,0:T(8,128)(2,1)S(1)}, u32[]{:S(2)}, u32[]{:S(2)}) collective-permute-start(bf16[4,2,48,512]{3,2,1,0:T(8,128)(2,1)S(1)} %collective-permute-done.7.refs_1_), channel_id=1, source_target_pairs={{8,0},{16,8},{24,16},{32,24},{40,32},{48,40},{56,48},{0,56},{9,1},... | collective-permute-start | bytes 1179656 | tf_op jit(solution)/shard_map/ppermute | solution.py:23
  57.6 7.8 %collective-permute-start.14 = (bf16[192,512]{1,0:T(8,128)(2,1)S(1)}, bf16[192,512]{1,0:T(8,128)(2,1)S(1)}, u32[]{:S(2)}, u32[]{:S(2)}) collective-permute-start(bf16[192,512]{1,0:T(8,128)(2,1)S(1)} %get-tuple-element.55), channel_id=1, source_target_pairs={{0,2},{2,4},{4,6},{6,0},{1,3},{3,5},{5,7},{7,1},{8,10},{10,12},{12... | collective-permute-start | bytes 589832 | tf_op jit(solution)/shard_map/ppermute | solution.py:28
  58.7 11.9 %collective-permute-start.15 = (bf16[192,512]{1,0:T(8,128)(2,1)S(1)}, bf16[192,512]{1,0:T(8,128)(2,1)S(1)}, u32[]{:S(2)}, u32[]{:S(2)}) collective-permute-start(bf16[192,512]{1,0:T(8,128)(2,1)S(1)} %get-tuple-element.56), channel_id=1, source_target_pairs={{0,4},{2,6},{4,0},{6,2},{1,5},{3,7},{5,1},{7,3},{8,12},{10,14},{12... | collective-permute-start | bytes 589832 | tf_op jit(solution)/shard_map/ppermute | solution.py:28
  60.7 11.6 %collective-permute-start.16 = (bf16[192,512]{1,0:T(8,128)(2,1)S(1)}, bf16[192,512]{1,0:T(8,128)(2,1)S(1)}, u32[]{:S(2)}, u32[]{:S(2)}) collective-permute-start(bf16[192,512]{1,0:T(8,128)(2,1)S(1)} %get-tuple-element.57), channel_id=1, source_target_pairs={{0,6},{2,0},{4,2},{6,4},{1,7},{3,1},{5,3},{7,5},{8,14},{10,8},{12,... | collective-permute-start | bytes 589832 | tf_op jit(solution)/shard_map/ppermute | solution.py:28
  61.1 14.1 %collective-permute-start.18 = (bf16[192,512]{1,0:T(8,128)(2,1)S(1)}, bf16[192,512]{1,0:T(8,128)(2,1)S(1)}, u32[]{:S(2)}, u32[]{:S(2)}) collective-permute-start(bf16[192,512]{1,0:T(8,128)(2,1)S(1)} %get-tuple-element.61), channel_id=1, source_target_pairs={{0,2},{2,4},{4,6},{6,0},{1,3},{3,5},{5,7},{7,1},{8,10},{10,12},{12... | collective-permute-start | bytes 589832 | tf_op jit(solution)/shard_map/ppermute | solution.py:28
  64.4 13.5 %collective-permute-start.19 = (bf16[192,512]{1,0:T(8,128)(2,1)S(1)}, bf16[192,512]{1,0:T(8,128)(2,1)S(1)}, u32[]{:S(2)}, u32[]{:S(2)}) collective-permute-start(bf16[192,512]{1,0:T(8,128)(2,1)S(1)} %get-tuple-element.62), channel_id=1, source_target_pairs={{0,4},{2,6},{4,0},{6,2},{1,5},{3,7},{5,1},{7,3},{8,12},{10,14},{12... | collective-permute-start | bytes 589832 | tf_op jit(solution)/shard_map/ppermute | solution.py:28
  65.4 15.3 %collective-permute-start.20 = (bf16[192,512]{1,0:T(8,128)(2,1)S(1)}, bf16[192,512]{1,0:T(8,128)(2,1)S(1)}, u32[]{:S(2)}, u32[]{:S(2)}) collective-permute-start(bf16[192,512]{1,0:T(8,128)(2,1)S(1)} %get-tuple-element.63), channel_id=1, source_target_pairs={{0,6},{2,0},{4,2},{6,4},{1,7},{3,1},{5,3},{7,5},{8,14},{10,8},{12,... | collective-permute-start | bytes 589832 | tf_op jit(solution)/shard_map/ppermute | solution.py:28
  72.6 11.0 %collective-permute-start.27 = (bf16[192,512]{1,0:T(8,128)(2,1)S(1)}, bf16[192,512]{1,0:T(8,128)(2,1)S(1)}, u32[]{:S(2)}, u32[]{:S(2)}) collective-permute-start(bf16[192,512]{1,0:T(8,128)(2,1)S(1)} %get-tuple-element.67), channel_id=1, source_target_pairs={{6,0},{0,2},{2,4},{4,6},{7,1},{1,3},{3,5},{5,7},{14,8},{8,10},{10,... | collective-permute-start | bytes 589832 | tf_op jit(solution)/shard_map/ppermute | solution.py:23
  73.2 13.1 %collective-permute-start.26 = (bf16[192,512]{1,0:T(8,128)(2,1)S(1)}, bf16[192,512]{1,0:T(8,128)(2,1)S(1)}, u32[]{:S(2)}, u32[]{:S(2)}) collective-permute-start(bf16[192,512]{1,0:T(8,128)(2,1)S(1)} %get-tuple-element.67), channel_id=1, source_target_pairs={{4,0},{6,2},{0,4},{2,6},{5,1},{7,3},{1,5},{3,7},{12,8},{14,10},{8,... | collective-permute-start | bytes 589832 | tf_op jit(solution)/shard_map/ppermute | solution.py:23
  75.1 14.0 %collective-permute-start.25 = (bf16[192,512]{1,0:T(8,128)(2,1)S(1)}, bf16[192,512]{1,0:T(8,128)(2,1)S(1)}, u32[]{:S(2)}, u32[]{:S(2)}) collective-permute-start(bf16[192,512]{1,0:T(8,128)(2,1)S(1)} %get-tuple-element.67), channel_id=1, source_target_pairs={{2,0},{4,2},{6,4},{0,6},{3,1},{5,3},{7,5},{1,7},{10,8},{12,10},{14... | collective-permute-start | bytes 589832 | tf_op jit(solution)/shard_map/ppermute | solution.py:23
  81.1 9.8 %collective-permute-start.23 = (bf16[192,512]{1,0:T(8,128)(2,1)S(1)}, bf16[192,512]{1,0:T(8,128)(2,1)S(1)}, u32[]{:S(2)}, u32[]{:S(2)}) collective-permute-start(bf16[192,512]{1,0:T(8,128)(2,1)S(1)} %get-tuple-element.65), channel_id=1, source_target_pairs={{6,0},{0,2},{2,4},{4,6},{7,1},{1,3},{3,5},{5,7},{14,8},{8,10},{10,... | collective-permute-start | bytes 589832 | tf_op jit(solution)/shard_map/ppermute | solution.py:23
  81.7 11.8 %collective-permute-start.22 = (bf16[192,512]{1,0:T(8,128)(2,1)S(1)}, bf16[192,512]{1,0:T(8,128)(2,1)S(1)}, u32[]{:S(2)}, u32[]{:S(2)}) collective-permute-start(bf16[192,512]{1,0:T(8,128)(2,1)S(1)} %get-tuple-element.65), channel_id=1, source_target_pairs={{4,0},{6,2},{0,4},{2,6},{5,1},{7,3},{1,5},{3,7},{12,8},{14,10},{8,... | collective-permute-start | bytes 589832 | tf_op jit(solution)/shard_map/ppermute | solution.py:23
  83.6 12.7 %collective-permute-start.21 = (bf16[192,512]{1,0:T(8,128)(2,1)S(1)}, bf16[192,512]{1,0:T(8,128)(2,1)S(1)}, u32[]{:S(2)}, u32[]{:S(2)}) collective-permute-start(bf16[192,512]{1,0:T(8,128)(2,1)S(1)} %get-tuple-element.65), channel_id=1, source_target_pairs={{2,0},{4,2},{6,4},{0,6},{3,1},{5,3},{7,5},{1,7},{10,8},{12,10},{14... | collective-permute-start | bytes 589832 | tf_op jit(solution)/shard_map/ppermute | solution.py:23
  89.2 7.3 %collective-permute-start.28 = (bf16[4,192,512]{2,1,0:T(8,128)(2,1)S(1)}, bf16[4,192,512]{2,1,0:T(8,128)(2,1)S(1)}, u32[]{:S(2)}, u32[]{:S(2)}) collective-permute-start(bf16[4,192,512]{2,1,0:T(8,128)(2,1)S(1)} %pad_maximum_fusion.1.refs_0_), channel_id=1, source_target_pairs={{0,1},{1,0},{2,3},{3,2},{4,5},{5,4},{6,7},{7,6},{8,9},{9,8},{10,11... | collective-permute-start | bytes 2359304 | tf_op jit(solution)/shard_map/ppermute | solution.py:28
  104.0 12.8 %collective-permute-start.30 = (bf16[4,2,48,512]{3,2,1,0:T(8,128)(2,1)S(1)}, bf16[4,2,48,512]{3,2,1,0:T(8,128)(2,1)S(1)}, u32[]{:S(2)}, u32[]{:S(2)}) collective-permute-start(bf16[4,2,48,512]{3,2,1,0:T(8,128)(2,1)S(1)} %get-tuple-element.73), channel_id=1, source_target_pairs={{0,8},{8,16},{16,24},{24,32},{32,40},{40,48},{48,56},{56,0},{1,9},... | collective-permute-start | bytes 1179656 | tf_op jit(solution)/shard_map/ppermute | solution.py:28
  105.1 12.4 %collective-permute-start.33 = (bf16[4,2,48,512]{3,2,1,0:T(8,128)(2,1)S(1)}, bf16[4,2,48,512]{3,2,1,0:T(8,128)(2,1)S(1)}, u32[]{:S(2)}, u32[]{:S(2)}) collective-permute-start(bf16[4,2,48,512]{3,2,1,0:T(8,128)(2,1)S(1)} %get-tuple-element.77), channel_id=1, source_target_pairs={{0,64},{64,128},{128,192},{192,0},{1,65},{65,129},{129,193},{193,1... | collective-permute-start | bytes 1179656 | tf_op jit(solution)/shard_map/ppermute | solution.py:28
  105.4 22.1 %collective-permute-start.29 = (bf16[4,2,48,512]{3,2,1,0:T(8,128)(2,1)S(1)}, bf16[4,2,48,512]{3,2,1,0:T(8,128)(2,1)S(1)}, u32[]{:S(2)}, u32[]{:S(2)}) collective-permute-start(bf16[4,2,48,512]{3,2,1,0:T(8,128)(2,1)S(1)} %get-tuple-element.71), channel_id=1, source_target_pairs={{0,56},{8,0},{16,8},{24,16},{32,24},{40,32},{48,40},{56,48},{1,57}... | collective-permute-start | bytes 1179656 | tf_op jit(solution)/shard_map/ppermute | solution.py:28
  108.9 20.3 %collective-permute-start.32 = (bf16[4,2,48,512]{3,2,1,0:T(8,128)(2,1)S(1)}, bf16[4,2,48,512]{3,2,1,0:T(8,128)(2,1)S(1)}, u32[]{:S(2)}, u32[]{:S(2)}) collective-permute-start(bf16[4,2,48,512]{3,2,1,0:T(8,128)(2,1)S(1)} %get-tuple-element.75), channel_id=1, source_target_pairs={{0,192},{64,0},{128,64},{192,128},{1,193},{65,1},{129,65},{193,129... | collective-permute-start | bytes 1179656 | tf_op jit(solution)/shard_map/ppermute | solution.py:28
  117.0 12.0 %collective-permute-start.31 = (bf16[4,2,48,512]{3,2,1,0:T(8,128)(2,1)S(1)}, bf16[4,2,48,512]{3,2,1,0:T(8,128)(2,1)S(1)}, u32[]{:S(2)}, u32[]{:S(2)}) collective-permute-start(bf16[4,2,48,512]{3,2,1,0:T(8,128)(2,1)S(1)} %add_convert_fusion.1), channel_id=1, source_target_pairs={{0,8},{8,16},{16,24},{24,32},{32,40},{40,48},{48,56},{56,0},{1,9},... | collective-permute-start | bytes 1179656 | tf_op jit(solution)/shard_map/ppermute | solution.py:28
  117.7 11.7 %collective-permute-start.34 = (bf16[4,2,48,512]{3,2,1,0:T(8,128)(2,1)S(1)}, bf16[4,2,48,512]{3,2,1,0:T(8,128)(2,1)S(1)}, u32[]{:S(2)}, u32[]{:S(2)}) collective-permute-start(bf16[4,2,48,512]{3,2,1,0:T(8,128)(2,1)S(1)} %add_convert_fusion), channel_id=1, source_target_pairs={{0,64},{64,128},{128,192},{192,0},{1,65},{65,129},{129,193},{193,1... | collective-permute-start | bytes 1179656 | tf_op jit(solution)/shard_map/ppermute | solution.py:28
  129.7 7.2 %collective-permute-start.35 = (bf16[2,48,512]{2,1,0:T(8,128)(2,1)S(1)}, bf16[2,48,512]{2,1,0:T(8,128)(2,1)S(1)}, u32[]{:S(2)}, u32[]{:S(2)}) collective-permute-start(bf16[2,48,512]{2,1,0:T(8,128)(2,1)S(1)} %get-tuple-element.86), channel_id=1, source_target_pairs={{0,64},{64,128},{128,192},{192,0},{1,65},{65,129},{129,193},{193,1... | collective-permute-start | bytes 294920 | tf_op jit(solution)/shard_map/ppermute | solution.py:28
  136.8 7.8 %collective-permute-start.39 = (bf16[2,48,512]{2,1,0:T(8,128)(2,1)S(1)}, bf16[2,48,512]{2,1,0:T(8,128)(2,1)S(1)}, u32[]{:S(2)}, u32[]{:S(2)}) collective-permute-start(bf16[2,48,512]{2,1,0:T(8,128)(2,1)S(1)} %get-tuple-element.85), channel_id=1, source_target_pairs={{0,16},{8,24},{16,32},{24,40},{32,48},{40,56},{48,0},{56,8},{1,17}... | collective-permute-start | bytes 294920 | tf_op jit(solution)/shard_map/ppermute | solution.py:28
  144.7 8.6 %collective-permute-start.41 = (bf16[48,1024]{1,0:T(8,128)(2,1)S(1)}, bf16[48,1024]{1,0:T(8,128)(2,1)S(1)}, u32[]{:S(2)}, u32[]{:S(2)}) collective-permute-start(bf16[48,1024]{1,0:T(8,128)(2,1)S(1)} %fusion.10), channel_id=1, source_target_pairs={{0,32},{8,40},{16,48},{24,56},{32,0},{40,8},{48,16},{56,24},{1,33}... | collective-permute-start | bytes 294920 | tf_op jit(solution)/shard_map/ppermute | solution.py:28
  (12 other events, 69.4 us)

commit v10 on v9

--- a/solution.py
+++ b/solution.py
@@ -153,21 +153,22 @@
                 b3[k][i, hi] = piece.astype(b3[k].dtype)
 
 
-def add_body(cols, keep, recv, *out):
-    for d in range(4):
+def add_body(cols, way, keep, recv, *out):
+    for k in range(4):
+        d = k * way % 4
 
         @pl.loop(0, keep.shape[1] // 16)
-        def _(i, d=d):
+        def _(i, d=d, k=k):
             at = pl.ds(pl.multiple_of(i * 16, 16), 16)
             total = keep[d, at, cols] + recv[d, at].astype(F32)
-            out[d][at] = total.astype(out[d].dtype)
-
-
-def act_body(cols, own, r1, r2, r3, cot, hidden, grad_pre):
+            out[k][at] = total.astype(out[k].dtype)
+
+
+def act_body(cols, own, r1, r2, cot, hidden, grad_pre):
     @pl.loop(0, own.shape[0] // 16)
     def _(i):
         at = pl.ds(pl.multiple_of(i * 16, 16), 16)
-        pre_act = own[at] + r1[at].astype(F32) + r2[at].astype(F32) + r3[at].astype(F32)
+        pre_act = own[at] + r1[at].astype(F32) + r2[at].astype(F32)
         gate = jax.nn.sigmoid(pre_act)
         hidden[at] = (pre_act * gate).astype(BF16)
         slope = gate * (1.0 + pre_act * (1.0 - gate))
@@ -216,20 +217,25 @@
     return ring_gather(jnp.stack(a2), "z"), ring_gather(jnp.stack(b2), "y")
 
 
-def partial_sums(keep, recv, cols):
+def partial_sums(keep, recv, cols, way):
     shape = (keep.shape[1], cols.stop - cols.start)
-    body = functools.partial(add_body, cols)
-    return call(body, [(shape, F32)] + [(shape, BF16)] * 3, [], [keep, recv])
-
-
-def activation(own, sends, cot, cols):
-    recvs = [to_ahead(s, "x", d + 1) for d, s in enumerate(sends)]
+    body = functools.partial(add_body, cols, way)
+    outs = [(shape, d) for d in (F32, F32, BF16, BF16)]
+    return call(body, outs, [], [keep, recv])
+
+
+def activation(own, near, far, other, cot, cols, way):
+    behind = to_ahead(other, "x", -way)
+    through = to_ahead(far, "x", way)
+    near = to_ahead((near + through.astype(F32)).astype(BF16), "x", way)
     body = functools.partial(act_body, cols)
-    return call(body, [(own.shape, BF16)] * 2, [], [own] + recvs + [cot])
-
-
-def gather_grads(grad_pre):
-    mine = jnp.stack([grad_pre] + [from_ahead(grad_pre, "x", d) for d in range(1, 4)])
+    return call(body, [(own.shape, BF16)] * 2, [], [own, near, behind, cot])
+
+
+def gather_grads(grad_pre, way):
+    near, other = from_ahead(grad_pre, "x", way), from_ahead(grad_pre, "x", -way)
+    far = from_ahead(near, "x", way)
+    mine = jnp.stack([grad_pre] + ([near, far, other] if way == 1 else [other, far, near]))
     return [mine, to_ahead(mine, "core", 1)]
 
 
@@ -265,13 +271,13 @@
         [VM((2, rows, width), F32)],
     )
     cols1, cols2 = slice(0, cut), slice(cut, width)
-    own1, *sends1 = partial_sums(keep, to_ahead(send1, "core", 1), cols1)
-    own2, *sends2 = partial_sums(keep, to_ahead(send2, "core", 1), cols2)
-    hidden1, grad1 = activation(own1, sends1, cot, cols1)
-    hidden2, grad2 = activation(own2, sends2, cot, cols2)
+    sums1 = partial_sums(keep, to_ahead(send1, "core", 1), cols1, 1)
+    sums2 = partial_sums(keep, to_ahead(send2, "core", 1), cols2, -1)
+    hidden1, grad1 = activation(*sums1, cot, cols1, 1)
+    hidden2, grad2 = activation(*sums2, cot, cols2, -1)
     hidden = jnp.concatenate([hidden1, hidden2], axis=1)
-    parts1 = gather_grads(grad1)
-    parts2 = gather_grads(grad2)
+    parts1 = gather_grads(grad1, -1)
+    parts2 = gather_grads(grad2, 1)
     g_shape = ((4, 2, rows, cut), BF16)
     sems = pltpu.SemaphoreType.DMA((2,))
     sums = (4, 8, rows // 4, depth)

time: 156 us -> 153 us (0.981)
  starting transfers between devices: 74.5 us -> 66.4 us
  waiting for transfers between devices: 47.4 us -> 52.1 us
    ppermute x19, starting transfers between devices: 41.5 us -> 37.5 us  [from_ahead(): return lax.ppermute(value, axis, [((i + k) % n, i) for i in range(n)])]
    ppermute x23, starting transfers between devices: 33 us -> 28.9 us  [to_ahead(): return lax.ppermute(value, axis, [(i, (i + k) % n) for i in range(n)])]
    ppermute x23, waiting for transfers between devices: 25.6 us -> 28.9 us  [to_ahead(): return lax.ppermute(value, axis, [(i, (i + k) % n) for i in range(n)])]
  transfers between devices with their start and end apart: 42 -> 42, of which waited for: 22 -> 23; matrix products, arithmetic and copies ran while one was open for 2% -> 2% of each run, Pallas kernels for 10% -> 10%
where the time goes in v10:
time: 153 us; the launch traced here: 151 us
  starting transfers between devices  66.4 us (43%)
  waiting for transfers between devices  52.1 us (34%)
  Pallas kernels  24.7 us (16%)
  other arithmetic  4.26 us (3%)
  local copies, waits for them, and re-layouts  1.64 us (1%)
  between operations  1.57 us (1%)
    ppermute x19, starting transfers between devices, from_ahead(): return lax.ppermute(value, axis, [((i + k) % n, i) for i in range(n)])  37.5 us
    ppermute x23, starting transfers between devices, to_ahead(): return lax.ppermute(value, axis, [(i, (i + k) % n) for i in range(n)])  28.9 us
    ppermute x23, waiting for transfers between devices, to_ahead(): return lax.ppermute(value, axis, [(i, (i + k) % n) for i in range(n)])  28.9 us
    pallas_call x9, Pallas kernels, call(): pl.pallas_call(body, out_shape=outs, in_specs=[pl.BlockSpec(memory_space=...  24.7 us
    ppermute x19, waiting for transfers between devices, from_ahead(): return lax.ppermute(value, axis, [((i + k) % n, i) for i in range(n)])  23.2 us
  transfers between devices with their start and end apart: 42, of which 23 were waited for; matrix products, arithmetic and copies ran while one was open for 2% of the time, Pallas kernels for 10%

profile of v10, /device:TPU:6, one launch (start us, length us, event | category | flops | bytes accessed | tf_op | source)
XLA Modules:
  0.0 150.6 jit_solution(12728373564453123905)
XLA Ops:
  0.6 7.3 %collective-permute-start = (bf16[48,1024]{1,0:T(8,128)(2,1)}, bf16[48,1024]{1,0:T(8,128)(2,1)S(1)}, u32[]{:S(2)}, u32[]{:S(2)}) collective-permute-start(bf16[48,1024]{1,0:T(8,128)(2,1)} %param.6), channel_id=1, source_target_pairs={{32,0},{40,8},{48,16},{56,24},{0,32},{8,40},{16,48},{24,56},{33,1}... | collective-permute-start | bytes 294920 | tf_op jit(solution)/shard_map/ppermute | solution.py:23
  7.9 3.1 %collective-permute-done = bf16[48,1024]{1,0:T(8,128)(2,1)S(1)} collective-permute-done((bf16[48,1024]{1,0:T(8,128)(2,1)}, bf16[48,1024]{1,0:T(8,128)(2,1)S(1)}, u32[]{:S(2)}, u32[]{:S(2)}) %collective-permute-start) | collective-permute-done | bytes 98336 | tf_op jit(solution)/shard_map/ppermute | solution.py:23
  11.9 2.6 %collective-permute-start.6 = (bf16[2,48,512]{2,1,0:T(8,128)(2,1)S(1)}, bf16[2,48,512]{2,1,0:T(8,128)(2,1)S(1)}, u32[]{:S(2)}, u32[]{:S(2)}) collective-permute-start(bf16[2,48,512]{2,1,0:T(8,128)(2,1)S(1)} %get-tuple-element.47), channel_id=1, source_target_pairs={{56,0},{0,8},{8,16},{16,24},{24,32},{32,40},{40,48},{48,56},{57,1}... | collective-permute-start | bytes 294920 | tf_op jit(solution)/shard_map/ppermute | solution.py:23
  14.4 4.2 %collective-permute-start.5 = (bf16[2,48,512]{2,1,0:T(8,128)(2,1)S(1)}, bf16[2,48,512]{2,1,0:T(8,128)(2,1)S(1)}, u32[]{:S(2)}, u32[]{:S(2)}) collective-permute-start(bf16[2,48,512]{2,1,0:T(8,128)(2,1)S(1)} %get-tuple-element.47), channel_id=1, source_target_pairs={{16,0},{24,8},{32,16},{40,24},{48,32},{56,40},{0,48},{8,56},{17,1}... | collective-permute-start | bytes 294920 | tf_op jit(solution)/shard_map/ppermute | solution.py:23
  18.6 1.9 %collective-permute-start.4 = (bf16[2,48,512]{2,1,0:T(8,128)(2,1)S(1)}, bf16[2,48,512]{2,1,0:T(8,128)(2,1)S(1)}, u32[]{:S(2)}, u32[]{:S(2)}) collective-permute-start(bf16[2,48,512]{2,1,0:T(8,128)(2,1)S(1)} %get-tuple-element.47), channel_id=1, source_target_pairs={{8,0},{16,8},{24,16},{32,24},{40,32},{48,40},{56,48},{0,56},{9,1},... | collective-permute-start | bytes 294920 | tf_op jit(solution)/shard_map/ppermute | solution.py:23
  22.1 2.9 %collective-permute-start.2 = (bf16[2,48,512]{2,1,0:T(8,128)(2,1)S(1)}, bf16[2,48,512]{2,1,0:T(8,128)(2,1)S(1)}, u32[]{:S(2)}, u32[]{:S(2)}) collective-permute-start(bf16[2,48,512]{2,1,0:T(8,128)(2,1)S(1)} %get-tuple-element.43), channel_id=1, source_target_pairs={{128,0},{192,64},{0,128},{64,192},{129,1},{193,65},{1,129},{65,193... | collective-permute-start | bytes 294920 | tf_op jit(solution)/shard_map/ppermute | solution.py:23
  29.9 2.4 %collective-permute-start.10 = (bf16[4,2,48,512]{3,2,1,0:T(8,128)(2,1)S(1)}, bf16[4,2,48,512]{3,2,1,0:T(8,128)(2,1)S(1)}, u32[]{:S(2)}, u32[]{:S(2)}) collective-permute-start(bf16[4,2,48,512]{3,2,1,0:T(8,128)(2,1)S(1)} %pad_maximum_fusion.3.refs_4_), channel_id=1, source_target_pairs={{64,0},{128,64},{192,128},{0,192},{65,1},{129,65},{193,129},{1,193... | collective-permute-start | bytes 1179656 | tf_op jit(solution)/shard_map/ppermute | solution.py:23
  34.5 4.8 %collective-permute-done.10.refs_5_ = bf16[4,2,48,512]{3,2,1,0:T(8,128)(2,1)S(1)} collective-permute-done((bf16[4,2,48,512]{3,2,1,0:T(8,128)(2,1)S(1)}, bf16[4,2,48,512]{3,2,1,0:T(8,128)(2,1)S(1)}, u32[]{:S(2)}, u32[]{:S(2)}) %collective-permute-start.10) | collective-permute-done | bytes 393248 | tf_op jit(solution)/shard_map/ppermute | solution.py:23
  39.3 2.3 %collective-permute-start.11 = (bf16[4,2,48,512]{3,2,1,0:T(8,128)(2,1)S(1)}, bf16[4,2,48,512]{3,2,1,0:T(8,128)(2,1)S(1)}, u32[]{:S(2)}, u32[]{:S(2)}) collective-permute-start(bf16[4,2,48,512]{3,2,1,0:T(8,128)(2,1)S(1)} %collective-permute-done.10.refs_5_), channel_id=1, source_target_pairs={{64,0},{128,64},{192,128},{0,192},{65,1},{129,65},{193,129},{1,193... | collective-permute-start | bytes 1179656 | tf_op jit(solution)/shard_map/ppermute | solution.py:23
  41.6 2.3 %collective-permute-start.8 = (bf16[4,2,48,512]{3,2,1,0:T(8,128)(2,1)S(1)}, bf16[4,2,48,512]{3,2,1,0:T(8,128)(2,1)S(1)}, u32[]{:S(2)}, u32[]{:S(2)}) collective-permute-start(bf16[4,2,48,512]{3,2,1,0:T(8,128)(2,1)S(1)} %collective-permute-done.7.refs_1_), channel_id=1, source_target_pairs={{8,0},{16,8},{24,16},{32,24},{40,32},{48,40},{56,48},{0,56},{9,1},... | collective-permute-start | bytes 1179656 | tf_op jit(solution)/shard_map/ppermute | solution.py:23
  46.9 1.9 %shard_map.85 = (bf16[1024,1024]{1,0:T(8,128)(2,1)S(1)}, bf16[1024,1024]{1,0:T(8,128)(2,1)S(1)}) custom-call(s32[32]{0:T(128)S(1)} %get-tuple-element.92.rows, s32[32]{0:T(128)S(1)} %get-tuple-element.91.cols, s32[1]{0:T(128)} %bitcast.59.count, bf16[1024,1024]{1,0:T(8,128)(2,1)S(1)} %copy-done), custom_call_target="tpu_custom_call" | custom-call | bytes 6291456 | tf_op jit(solution)/shard_map/pallas_call | solution.py:33
  49.4 5.4 %shard_map.86 = (f32[4,192,1024]{2,1,0:T(8,128)S(1)}, bf16[4,192,512]{2,1,0:T(8,128)(2,1)S(1)}, bf16[4,192,512]{2,1,0:T(8,128)(2,1)S(1)}, bf16[4,8,48,1024]{3,2,1,0:T(8,128)(2,1)S(1)}) custom-call(s32[4]{0:T(128)S(1)} %pad_add_fusion.pos, bf16[4,2,48,512]{3,2,1,0:T(8,128)(2,1)S(1)} %pad_maximum_fusion.2.refs_0_, ...), custom_call_target="tpu_custom_call" | custom-call | flops 3221225472 | bytes 13107200 | tf_op jit(solution)/shard_map/pallas_call | solution.py:33
  61.0 2.4 %collective-permute-start.20 = (bf16[192,512]{1,0:T(8,128)(2,1)S(1)}, bf16[192,512]{1,0:T(8,128)(2,1)S(1)}, u32[]{:S(2)}, u32[]{:S(2)}) collective-permute-start(bf16[192,512]{1,0:T(8,128)(2,1)S(1)} %get-tuple-element.63), channel_id=1, source_target_pairs={{0,2},{2,4},{4,6},{6,0},{1,3},{3,5},{5,7},{7,1},{8,10},{10,12},{12... | collective-permute-start | bytes 589832 | tf_op jit(solution)/shard_map/ppermute | solution.py:28
  63.4 2.0 %collective-permute-done.14 = bf16[192,512]{1,0:T(8,128)(2,1)S(1)} collective-permute-done((bf16[192,512]{1,0:T(8,128)(2,1)S(1)}, bf16[192,512]{1,0:T(8,128)(2,1)S(1)}, u32[]{:S(2)}, u32[]{:S(2)}) %collective-permute-start.14) | collective-permute-done | bytes 196640 | tf_op jit(solution)/shard_map/ppermute | solution.py:28
  67.2 3.5 %collective-permute-done.18 = bf16[192,512]{1,0:T(8,128)(2,1)S(1)} collective-permute-done((bf16[192,512]{1,0:T(8,128)(2,1)S(1)}, bf16[192,512]{1,0:T(8,128)(2,1)S(1)}, u32[]{:S(2)}, u32[]{:S(2)}) %collective-permute-start.18) | collective-permute-done | bytes 196640 | tf_op jit(solution)/shard_map/ppermute | solution.py:28
  70.9 2.1 %collective-permute-done.15.r1 = bf16[192,512]{1,0:T(8,128)(2,1)S(1)} collective-permute-done((bf16[192,512]{1,0:T(8,128)(2,1)S(1)}, bf16[192,512]{1,0:T(8,128)(2,1)S(1)}, u32[]{:S(2)}, u32[]{:S(2)}) %collective-permute-start.15) | collective-permute-done | bytes 196640 | tf_op jit(solution)/shard_map/ppermute | solution.py:28
  73.3 2.3 %collective-permute-start.26 = (bf16[192,512]{1,0:T(8,128)(2,1)S(1)}, bf16[192,512]{1,0:T(8,128)(2,1)S(1)}, u32[]{:S(2)}, u32[]{:S(2)}) collective-permute-start(bf16[192,512]{1,0:T(8,128)(2,1)S(1)} %get-tuple-element.67), channel_id=1, source_target_pairs={{6,0},{0,2},{2,4},{4,6},{7,1},{1,3},{3,5},{5,7},{14,8},{8,10},{10,... | collective-permute-start | bytes 589832 | tf_op jit(solution)/shard_map/ppermute | solution.py:23
  75.6 2.3 %collective-permute-done.19.r1 = bf16[192,512]{1,0:T(8,128)(2,1)S(1)} collective-permute-done((bf16[192,512]{1,0:T(8,128)(2,1)S(1)}, bf16[192,512]{1,0:T(8,128)(2,1)S(1)}, u32[]{:S(2)}, u32[]{:S(2)}) %collective-permute-start.19) | collective-permute-done | bytes 196640 | tf_op jit(solution)/shard_map/ppermute | solution.py:28
  79.5 3.2 %collective-permute-start.27 = (bf16[192,512]{1,0:T(8,128)(2,1)S(1)}, bf16[192,512]{1,0:T(8,128)(2,1)S(1)}, u32[]{:S(2)}, u32[]{:S(2)}) collective-permute-start(bf16[192,512]{1,0:T(8,128)(2,1)S(1)} %collective-permute-done.26), channel_id=1, source_target_pairs={{6,0},{0,2},{2,4},{4,6},{7,1},{1,3},{3,5},{5,7},{14,8},{8,10},{10,... | collective-permute-start | bytes 589832 | tf_op jit(solution)/shard_map/ppermute | solution.py:23
  83.5 3.4 %collective-permute-done.21 = bf16[192,512]{1,0:T(8,128)(2,1)S(1)} collective-permute-done((bf16[192,512]{1,0:T(8,128)(2,1)S(1)}, bf16[192,512]{1,0:T(8,128)(2,1)S(1)}, u32[]{:S(2)}, u32[]{:S(2)}) %collective-permute-start.21) | collective-permute-done | bytes 196640 | tf_op jit(solution)/shard_map/ppermute | solution.py:23
  87.0 3.7 %collective-permute-done.25 = bf16[192,512]{1,0:T(8,128)(2,1)S(1)} collective-permute-done((bf16[192,512]{1,0:T(8,128)(2,1)S(1)}, bf16[192,512]{1,0:T(8,128)(2,1)S(1)}, u32[]{:S(2)}, u32[]{:S(2)}) %collective-permute-start.25) | collective-permute-done | bytes 196640 | tf_op jit(solution)/shard_map/ppermute | solution.py:23
  90.9 3.0 %collective-permute-done.22 = bf16[192,512]{1,0:T(8,128)(2,1)S(1)} collective-permute-done((bf16[192,512]{1,0:T(8,128)(2,1)S(1)}, bf16[192,512]{1,0:T(8,128)(2,1)S(1)}, u32[]{:S(2)}, u32[]{:S(2)}) %collective-permute-start.22) | collective-permute-done | bytes 196640 | tf_op jit(solution)/shard_map/ppermute | solution.py:23
  94.1 3.0 %shard_map.91 = (f32[4,8,48,1024]{3,2,1,0:T(8,128)S(1)}, bf16[4,2,192,512]{3,2,1,0:T(8,128)(2,1)S(1)}) custom-call(s32[4]{0:T(128)S(1)} %pad_add_fusion.pos, bf16[4,192,512]{2,1,0:T(8,128)(2,1)S(1)} %pad_maximum_fusion.1.refs_0_, bf16[4,192,512]{2,1,0:T(8,128)(2,1)S(1)} %collective-permute-done.28.refs_1_, bf16[1024,1024]{1,0:T(8,128)(2,1)S(1)} %get-tuple-element.66.refs_2_), custom_call_target="tpu_custom_call" | custom-call | flops 1610612736 | bytes 11534336 | tf_op jit(solution)/shard_map/pallas_call | solution.py:33
  97.1 4.4 %shard_map.92 = (f32[4,2,48,512]{3,2,1,0:T(8,128)S(1)}, f32[4,2,48,512]{3,2,1,0:T(8,128)S(1)}, bf16[4,2,48,512]{3,2,1,0:T(8,128)(2,1)S(1)}, bf16[4,2,48,512]{3,2...) custom-call(s32[4]{0:T(128)S(1)} %pad_add_fusion.pos, ...), custom_call_target="tpu_custom_call" | custom-call | flops 1610612736 | bytes 19398656 | tf_op jit(solution)/shard_map/pallas_call | solution.py:33
  103.0 3.4 %collective-permute-start.29 = (bf16[4,2,48,512]{3,2,1,0:T(8,128)(2,1)S(1)}, bf16[4,2,48,512]{3,2,1,0:T(8,128)(2,1)S(1)}, u32[]{:S(2)}, u32[]{:S(2)}) collective-permute-start(bf16[4,2,48,512]{3,2,1,0:T(8,128)(2,1)S(1)} %get-tuple-element.71), channel_id=1, source_target_pairs={{0,56},{8,0},{16,8},{24,16},{32,24},{40,32},{48,40},{56,48},{1,57}... | collective-permute-start | bytes 1179656 | tf_op jit(solution)/shard_map/ppermute | solution.py:28
  106.4 1.9 %collective-permute-start.32 = (bf16[4,2,48,512]{3,2,1,0:T(8,128)(2,1)S(1)}, bf16[4,2,48,512]{3,2,1,0:T(8,128)(2,1)S(1)}, u32[]{:S(2)}, u32[]{:S(2)}) collective-permute-start(bf16[4,2,48,512]{3,2,1,0:T(8,128)(2,1)S(1)} %get-tuple-element.75), channel_id=1, source_target_pairs={{0,192},{64,0},{128,64},{192,128},{1,193},{65,1},{129,65},{193,129... | collective-permute-start | bytes 1179656 | tf_op jit(solution)/shard_map/ppermute | solution.py:28
  108.3 6.4 %collective-permute-done.30 = bf16[4,2,48,512]{3,2,1,0:T(8,128)(2,1)S(1)} collective-permute-done((bf16[4,2,48,512]{3,2,1,0:T(8,128)(2,1)S(1)}, bf16[4,2,48,512]{3,2,1,0:T(8,128)(2,1)S(1)}, u32[]{:S(2)}, u32[]{:S(2)}) %collective-permute-start.30) | collective-permute-done | bytes 393248 | tf_op jit(solution)/shard_map/ppermute | solution.py:28
  116.6 8.6 %shard_map.93 = bf16[1024,1024]{1,0:T(8,128)(2,1)} custom-call(s32[32]{0:T(128)S(1)} %get-tuple-element.92.rows, s32[32]{0:T(128)S(1)} %get-tuple-element.91.cols, s32[1]{0:T(128)} %bitcast.60.count, bf16[4,8,48,1024]{3,2,1,0:T(8,128)(2,1)S(1)} %get-tuple-element.78.toks, bf16[4,2,192,1024]{3,2,1,0:T(8,128)(2,1)S(1)} %get-tuple-element.79.grads), custom_call_target="tpu_custom_call" | custom-call | flops 3221225472 | bytes 8388608 | tf_op jit(solution)/shard_map/pallas_call | solution.py:33
  131.9 2.6 %collective-permute-start.40 = (bf16[2,48,512]{2,1,0:T(8,128)(2,1)S(1)}, bf16[2,48,512]{2,1,0:T(8,128)(2,1)S(1)}, u32[]{:S(2)}, u32[]{:S(2)}) collective-permute-start(bf16[2,48,512]{2,1,0:T(8,128)(2,1)S(1)} %get-tuple-element.84), channel_id=1, source_target_pairs={{0,56},{8,0},{16,8},{24,16},{32,24},{40,32},{48,40},{56,48},{1,57}... | collective-permute-start | bytes 294920 | tf_op jit(solution)/shard_map/ppermute | solution.py:28
  137.1 4.1 %collective-permute-done.39 = bf16[2,48,512]{2,1,0:T(8,128)(2,1)S(1)} collective-permute-done((bf16[2,48,512]{2,1,0:T(8,128)(2,1)S(1)}, bf16[2,48,512]{2,1,0:T(8,128)(2,1)S(1)}, u32[]{:S(2)}, u32[]{:S(2)}) %collective-permute-start.39) | collective-permute-done | bytes 98336 | tf_op jit(solution)/shard_map/ppermute | solution.py:28
  141.3 5.1 %collective-permute-start.41 = (bf16[48,1024]{1,0:T(8,128)(2,1)S(1)}, bf16[48,1024]{1,0:T(8,128)(2,1)S(1)}, u32[]{:S(2)}, u32[]{:S(2)}) collective-permute-start(bf16[48,1024]{1,0:T(8,128)(2,1)S(1)} %fusion.10), channel_id=1, source_target_pairs={{0,32},{8,40},{16,48},{24,56},{32,0},{40,8},{48,16},{56,24},{1,33}... | collective-permute-start | bytes 294920 | tf_op jit(solution)/shard_map/ppermute | solution.py:28
  147.2 2.7 %collective-permute-done.41 = bf16[48,1024]{1,0:T(8,128)(2,1)S(1)} collective-permute-done((bf16[48,1024]{1,0:T(8,128)(2,1)S(1)}, bf16[48,1024]{1,0:T(8,128)(2,1)S(1)}, u32[]{:S(2)}, u32[]{:S(2)}) %collective-permute-start.41) | collective-permute-done | bytes 98336 | tf_op jit(solution)/shard_map/ppermute | solution.py:28
  (87 shorter events, 37.7 us)
Async XLA Ops:
  0.6 10.4 %collective-permute-start = (bf16[48,1024]{1,0:T(8,128)(2,1)}, bf16[48,1024]{1,0:T(8,128)(2,1)S(1)}, u32[]{:S(2)}, u32[]{:S(2)}) collective-permute-start(bf16[48,1024]{1,0:T(8,128)(2,1)} %param.6), channel_id=1, source_target_pairs={{32,0},{40,8},{48,16},{56,24},{0,32},{8,40},{16,48},{24,56},{33,1}... | collective-permute-start | bytes 294920 | tf_op jit(solution)/shard_map/ppermute | solution.py:23
  11.9 13.2 %collective-permute-start.6 = (bf16[2,48,512]{2,1,0:T(8,128)(2,1)S(1)}, bf16[2,48,512]{2,1,0:T(8,128)(2,1)S(1)}, u32[]{:S(2)}, u32[]{:S(2)}) collective-permute-start(bf16[2,48,512]{2,1,0:T(8,128)(2,1)S(1)} %get-tuple-element.47), channel_id=1, source_target_pairs={{56,0},{0,8},{8,16},{16,24},{24,32},{32,40},{40,48},{48,56},{57,1}... | collective-permute-start | bytes 294920 | tf_op jit(solution)/shard_map/ppermute | solution.py:23
  14.4 12.0 %collective-permute-start.5 = (bf16[2,48,512]{2,1,0:T(8,128)(2,1)S(1)}, bf16[2,48,512]{2,1,0:T(8,128)(2,1)S(1)}, u32[]{:S(2)}, u32[]{:S(2)}) collective-permute-start(bf16[2,48,512]{2,1,0:T(8,128)(2,1)S(1)} %get-tuple-element.47), channel_id=1, source_target_pairs={{16,0},{24,8},{32,16},{40,24},{48,32},{56,40},{0,48},{8,56},{17,1}... | collective-permute-start | bytes 294920 | tf_op jit(solution)/shard_map/ppermute | solution.py:23
  18.6 7.8 %collective-permute-start.4 = (bf16[2,48,512]{2,1,0:T(8,128)(2,1)S(1)}, bf16[2,48,512]{2,1,0:T(8,128)(2,1)S(1)}, u32[]{:S(2)}, u32[]{:S(2)}) collective-permute-start(bf16[2,48,512]{2,1,0:T(8,128)(2,1)S(1)} %get-tuple-element.47), channel_id=1, source_target_pairs={{8,0},{16,8},{24,16},{32,24},{40,32},{48,40},{56,48},{0,56},{9,1},... | collective-permute-start | bytes 294920 | tf_op jit(solution)/shard_map/ppermute | solution.py:23
  22.1 6.5 %collective-permute-start.2 = (bf16[2,48,512]{2,1,0:T(8,128)(2,1)S(1)}, bf16[2,48,512]{2,1,0:T(8,128)(2,1)S(1)}, u32[]{:S(2)}, u32[]{:S(2)}) collective-permute-start(bf16[2,48,512]{2,1,0:T(8,128)(2,1)S(1)} %get-tuple-element.43), channel_id=1, source_target_pairs={{128,0},{192,64},{0,128},{64,192},{129,1},{193,65},{1,129},{65,193... | collective-permute-start | bytes 294920 | tf_op jit(solution)/shard_map/ppermute | solution.py:23
  29.9 9.4 %collective-permute-start.10 = (bf16[4,2,48,512]{3,2,1,0:T(8,128)(2,1)S(1)}, bf16[4,2,48,512]{3,2,1,0:T(8,128)(2,1)S(1)}, u32[]{:S(2)}, u32[]{:S(2)}) collective-permute-start(bf16[4,2,48,512]{3,2,1,0:T(8,128)(2,1)S(1)} %pad_maximum_fusion.3.refs_4_), channel_id=1, source_target_pairs={{64,0},{128,64},{192,128},{0,192},{65,1},{129,65},{193,129},{1,193... | collective-permute-start | bytes 1179656 | tf_op jit(solution)/shard_map/ppermute | solution.py:23
  32.4 9.2 %collective-permute-start.7 = (bf16[4,2,48,512]{3,2,1,0:T(8,128)(2,1)S(1)}, bf16[4,2,48,512]{3,2,1,0:T(8,128)(2,1)S(1)}, u32[]{:S(2)}, u32[]{:S(2)}) collective-permute-start(bf16[4,2,48,512]{3,2,1,0:T(8,128)(2,1)S(1)} %pad_maximum_fusion.2.refs_0_), channel_id=1, source_target_pairs={{8,0},{16,8},{24,16},{32,24},{40,32},{48,40},{56,48},{0,56},{9,1},... | collective-permute-start | bytes 1179656 | tf_op jit(solution)/shard_map/ppermute | solution.py:23
  33.7 15.1 %collective-permute-start.12 = (bf16[4,2,48,512]{3,2,1,0:T(8,128)(2,1)S(1)}, bf16[4,2,48,512]{3,2,1,0:T(8,128)(2,1)S(1)}, u32[]{:S(2)}, u32[]{:S(2)}) collective-permute-start(bf16[4,2,48,512]{3,2,1,0:T(8,128)(2,1)S(1)} %pad_maximum_fusion.3.refs_4_), channel_id=1, source_target_pairs={{192,0},{0,64},{64,128},{128,192},{193,1},{1,65},{65,129},{129,193... | collective-permute-start | bytes 1179656 | tf_op jit(solution)/shard_map/ppermute | solution.py:23
  34.2 14.7 %collective-permute-start.9 = (bf16[4,2,48,512]{3,2,1,0:T(8,128)(2,1)S(1)}, bf16[4,2,48,512]{3,2,1,0:T(8,128)(2,1)S(1)}, u32[]{:S(2)}, u32[]{:S(2)}) collective-permute-start(bf16[4,2,48,512]{3,2,1,0:T(8,128)(2,1)S(1)} %pad_maximum_fusion.2.refs_0_), channel_id=1, source_target_pairs={{56,0},{0,8},{8,16},{16,24},{24,32},{32,40},{40,48},{48,56},{57,1}... | collective-permute-start | bytes 1179656 | tf_op jit(solution)/shard_map/ppermute | solution.py:23
  39.3 9.6 %collective-permute-start.11 = (bf16[4,2,48,512]{3,2,1,0:T(8,128)(2,1)S(1)}, bf16[4,2,48,512]{3,2,1,0:T(8,128)(2,1)S(1)}, u32[]{:S(2)}, u32[]{:S(2)}) collective-permute-start(bf16[4,2,48,512]{3,2,1,0:T(8,128)(2,1)S(1)} %collective-permute-done.10.refs_5_), channel_id=1, source_target_pairs={{64,0},{128,64},{192,128},{0,192},{65,1},{129,65},{193,129},{1,193... | collective-permute-start | bytes 1179656 | tf_op jit(solution)/shard_map/ppermute | solution.py:23
  41.6 7.8 %collective-permute-start.8 = (bf16[4,2,48,512]{3,2,1,0:T(8,128)(2,1)S(1)}, bf16[4,2,48,512]{3,2,1,0:T(8,128)(2,1)S(1)}, u32[]{:S(2)}, u32[]{:S(2)}) collective-permute-start(bf16[4,2,48,512]{3,2,1,0:T(8,128)(2,1)S(1)} %collective-permute-done.7.refs_1_), channel_id=1, source_target_pairs={{8,0},{16,8},{24,16},{32,24},{40,32},{48,40},{56,48},{0,56},{9,1},... | collective-permute-start | bytes 1179656 | tf_op jit(solution)/shard_map/ppermute | solution.py:23
  57.6 7.8 %collective-permute-start.14 = (bf16[192,512]{1,0:T(8,128)(2,1)S(1)}, bf16[192,512]{1,0:T(8,128)(2,1)S(1)}, u32[]{:S(2)}, u32[]{:S(2)}) collective-permute-start(bf16[192,512]{1,0:T(8,128)(2,1)S(1)} %get-tuple-element.56), channel_id=1, source_target_pairs={{0,2},{2,4},{4,6},{6,0},{1,3},{3,5},{5,7},{7,1},{8,10},{10,12},{12... | collective-permute-start | bytes 589832 | tf_op jit(solution)/shard_map/ppermute | solution.py:28
  58.7 12.2 %collective-permute-start.16 = (bf16[192,512]{1,0:T(8,128)(2,1)S(1)}, bf16[192,512]{1,0:T(8,128)(2,1)S(1)}, u32[]{:S(2)}, u32[]{:S(2)}) collective-permute-start(bf16[192,512]{1,0:T(8,128)(2,1)S(1)} %get-tuple-element.57), channel_id=1, source_target_pairs={{0,6},{2,0},{4,2},{6,4},{1,7},{3,1},{5,3},{7,5},{8,14},{10,8},{12,... | collective-permute-start | bytes 589832 | tf_op jit(solution)/shard_map/ppermute | solution.py:28
  60.1 10.7 %collective-permute-start.18 = (bf16[192,512]{1,0:T(8,128)(2,1)S(1)}, bf16[192,512]{1,0:T(8,128)(2,1)S(1)}, u32[]{:S(2)}, u32[]{:S(2)}) collective-permute-start(bf16[192,512]{1,0:T(8,128)(2,1)S(1)} %get-tuple-element.62), channel_id=1, source_target_pairs={{0,6},{2,0},{4,2},{6,4},{1,7},{3,1},{5,3},{7,5},{8,14},{10,8},{12,... | collective-permute-start | bytes 589832 | tf_op jit(solution)/shard_map/ppermute | solution.py:28
  61.0 14.7 %collective-permute-start.20 = (bf16[192,512]{1,0:T(8,128)(2,1)S(1)}, bf16[192,512]{1,0:T(8,128)(2,1)S(1)}, u32[]{:S(2)}, u32[]{:S(2)}) collective-permute-start(bf16[192,512]{1,0:T(8,128)(2,1)S(1)} %get-tuple-element.63), channel_id=1, source_target_pairs={{0,2},{2,4},{4,6},{6,0},{1,3},{3,5},{5,7},{7,1},{8,10},{10,12},{12... | collective-permute-start | bytes 589832 | tf_op jit(solution)/shard_map/ppermute | solution.py:28
  65.4 7.6 %collective-permute-start.15 = (bf16[192,512]{1,0:T(8,128)(2,1)S(1)}, bf16[192,512]{1,0:T(8,128)(2,1)S(1)}, u32[]{:S(2)}, u32[]{:S(2)}) collective-permute-start(bf16[192,512]{1,0:T(8,128)(2,1)S(1)} %add_convert_fusion.3), channel_id=1, source_target_pairs={{0,2},{2,4},{4,6},{6,0},{1,3},{3,5},{5,7},{7,1},{8,10},{10,12},{12... | collective-permute-start | bytes 589832 | tf_op jit(solution)/shard_map/ppermute | solution.py:28
  70.8 7.1 %collective-permute-start.19 = (bf16[192,512]{1,0:T(8,128)(2,1)S(1)}, bf16[192,512]{1,0:T(8,128)(2,1)S(1)}, u32[]{:S(2)}, u32[]{:S(2)}) collective-permute-start(bf16[192,512]{1,0:T(8,128)(2,1)S(1)} %add_convert_fusion.2), channel_id=1, source_target_pairs={{0,6},{2,0},{4,2},{6,4},{1,7},{3,1},{5,3},{7,5},{8,14},{10,8},{12,... | collective-permute-start | bytes 589832 | tf_op jit(solution)/shard_map/ppermute | solution.py:28
  78.2 8.8 %collective-permute-start.21 = (bf16[192,512]{1,0:T(8,128)(2,1)S(1)}, bf16[192,512]{1,0:T(8,128)(2,1)S(1)}, u32[]{:S(2)}, u32[]{:S(2)}) collective-permute-start(bf16[192,512]{1,0:T(8,128)(2,1)S(1)} %get-tuple-element.65), channel_id=1, source_target_pairs={{2,0},{4,2},{6,4},{0,6},{3,1},{5,3},{7,5},{1,7},{10,8},{12,10},{14... | collective-permute-start | bytes 589832 | tf_op jit(solution)/shard_map/ppermute | solution.py:23
  78.3 12.4 %collective-permute-start.25 = (bf16[192,512]{1,0:T(8,128)(2,1)S(1)}, bf16[192,512]{1,0:T(8,128)(2,1)S(1)}, u32[]{:S(2)}, u32[]{:S(2)}) collective-permute-start(bf16[192,512]{1,0:T(8,128)(2,1)S(1)} %get-tuple-element.67), channel_id=1, source_target_pairs={{2,0},{4,2},{6,4},{0,6},{3,1},{5,3},{7,5},{1,7},{10,8},{12,10},{14... | collective-permute-start | bytes 589832 | tf_op jit(solution)/shard_map/ppermute | solution.py:23
  79.5 11.2 %collective-permute-start.27 = (bf16[192,512]{1,0:T(8,128)(2,1)S(1)}, bf16[192,512]{1,0:T(8,128)(2,1)S(1)}, u32[]{:S(2)}, u32[]{:S(2)}) collective-permute-start(bf16[192,512]{1,0:T(8,128)(2,1)S(1)} %collective-permute-done.26), channel_id=1, source_target_pairs={{6,0},{0,2},{2,4},{4,6},{7,1},{1,3},{3,5},{5,7},{14,8},{8,10},{10,... | collective-permute-start | bytes 589832 | tf_op jit(solution)/shard_map/ppermute | solution.py:23
  82.7 8.2 %collective-permute-start.23 = (bf16[192,512]{1,0:T(8,128)(2,1)S(1)}, bf16[192,512]{1,0:T(8,128)(2,1)S(1)}, u32[]{:S(2)}, u32[]{:S(2)}) collective-permute-start(bf16[192,512]{1,0:T(8,128)(2,1)S(1)} %get-tuple-element.65), channel_id=1, source_target_pairs={{6,0},{0,2},{2,4},{4,6},{7,1},{1,3},{3,5},{5,7},{14,8},{8,10},{10,... | collective-permute-start | bytes 589832 | tf_op jit(solution)/shard_map/ppermute | solution.py:23
  87.0 6.9 %collective-permute-start.22 = (bf16[192,512]{1,0:T(8,128)(2,1)S(1)}, bf16[192,512]{1,0:T(8,128)(2,1)S(1)}, u32[]{:S(2)}, u32[]{:S(2)}) collective-permute-start(bf16[192,512]{1,0:T(8,128)(2,1)S(1)} %collective-permute-done.21), channel_id=1, source_target_pairs={{2,0},{4,2},{6,4},{0,6},{3,1},{5,3},{7,5},{1,7},{10,8},{12,10},{14... | collective-permute-start | bytes 589832 | tf_op jit(solution)/shard_map/ppermute | solution.py:23
  101.5 13.2 %collective-permute-start.30 = (bf16[4,2,48,512]{3,2,1,0:T(8,128)(2,1)S(1)}, bf16[4,2,48,512]{3,2,1,0:T(8,128)(2,1)S(1)}, u32[]{:S(2)}, u32[]{:S(2)}) collective-permute-start(bf16[4,2,48,512]{3,2,1,0:T(8,128)(2,1)S(1)} %get-tuple-element.73), channel_id=1, source_target_pairs={{0,8},{8,16},{16,24},{24,32},{32,40},{40,48},{48,56},{56,0},{1,9},... | collective-permute-start | bytes 1179656 | tf_op jit(solution)/shard_map/ppermute | solution.py:28
  103.0 12.4 %collective-permute-start.33 = (bf16[4,2,48,512]{3,2,1,0:T(8,128)(2,1)S(1)}, bf16[4,2,48,512]{3,2,1,0:T(8,128)(2,1)S(1)}, u32[]{:S(2)}, u32[]{:S(2)}) collective-permute-start(bf16[4,2,48,512]{3,2,1,0:T(8,128)(2,1)S(1)} %get-tuple-element.77), channel_id=1, source_target_pairs={{0,64},{64,128},{128,192},{192,0},{1,65},{65,129},{129,193},{193,1... | collective-permute-start | bytes 1179656 | tf_op jit(solution)/shard_map/ppermute | solution.py:28
  103.0 22.2 %collective-permute-start.29 = (bf16[4,2,48,512]{3,2,1,0:T(8,128)(2,1)S(1)}, bf16[4,2,48,512]{3,2,1,0:T(8,128)(2,1)S(1)}, u32[]{:S(2)}, u32[]{:S(2)}) collective-permute-start(bf16[4,2,48,512]{3,2,1,0:T(8,128)(2,1)S(1)} %get-tuple-element.71), channel_id=1, source_target_pairs={{0,56},{8,0},{16,8},{24,16},{32,24},{40,32},{48,40},{56,48},{1,57}... | collective-permute-start | bytes 1179656 | tf_op jit(solution)/shard_map/ppermute | solution.py:28
  106.4 20.8 %collective-permute-start.32 = (bf16[4,2,48,512]{3,2,1,0:T(8,128)(2,1)S(1)}, bf16[4,2,48,512]{3,2,1,0:T(8,128)(2,1)S(1)}, u32[]{:S(2)}, u32[]{:S(2)}) collective-permute-start(bf16[4,2,48,512]{3,2,1,0:T(8,128)(2,1)S(1)} %get-tuple-element.75), channel_id=1, source_target_pairs={{0,192},{64,0},{128,64},{192,128},{1,193},{65,1},{129,65},{193,129... | collective-permute-start | bytes 1179656 | tf_op jit(solution)/shard_map/ppermute | solution.py:28
  114.9 12.1 %collective-permute-start.31 = (bf16[4,2,48,512]{3,2,1,0:T(8,128)(2,1)S(1)}, bf16[4,2,48,512]{3,2,1,0:T(8,128)(2,1)S(1)}, u32[]{:S(2)}, u32[]{:S(2)}) collective-permute-start(bf16[4,2,48,512]{3,2,1,0:T(8,128)(2,1)S(1)} %add_convert_fusion.1), channel_id=1, source_target_pairs={{0,8},{8,16},{16,24},{24,32},{32,40},{40,48},{48,56},{56,0},{1,9},... | collective-permute-start | bytes 1179656 | tf_op jit(solution)/shard_map/ppermute | solution.py:28
  115.6 11.7 %collective-permute-start.34 = (bf16[4,2,48,512]{3,2,1,0:T(8,128)(2,1)S(1)}, bf16[4,2,48,512]{3,2,1,0:T(8,128)(2,1)S(1)}, u32[]{:S(2)}, u32[]{:S(2)}) collective-permute-start(bf16[4,2,48,512]{3,2,1,0:T(8,128)(2,1)S(1)} %add_convert_fusion), channel_id=1, source_target_pairs={{0,64},{64,128},{128,192},{192,0},{1,65},{65,129},{129,193},{193,1... | collective-permute-start | bytes 1179656 | tf_op jit(solution)/shard_map/ppermute | solution.py:28
  127.5 7.0 %collective-permute-start.35 = (bf16[2,48,512]{2,1,0:T(8,128)(2,1)S(1)}, bf16[2,48,512]{2,1,0:T(8,128)(2,1)S(1)}, u32[]{:S(2)}, u32[]{:S(2)}) collective-permute-start(bf16[2,48,512]{2,1,0:T(8,128)(2,1)S(1)} %get-tuple-element.86), channel_id=1, source_target_pairs={{0,64},{64,128},{128,192},{192,0},{1,65},{65,129},{129,193},{193,1... | collective-permute-start | bytes 294920 | tf_op jit(solution)/shard_map/ppermute | solution.py:28
  129.0 6.6 %collective-permute-start.37 = (bf16[2,48,512]{2,1,0:T(8,128)(2,1)S(1)}, bf16[2,48,512]{2,1,0:T(8,128)(2,1)S(1)}, u32[]{:S(2)}, u32[]{:S(2)}) collective-permute-start(bf16[2,48,512]{2,1,0:T(8,128)(2,1)S(1)} %get-tuple-element.87), channel_id=1, source_target_pairs={{0,192},{64,0},{128,64},{192,128},{1,193},{65,1},{129,65},{193,129... | collective-permute-start | bytes 294920 | tf_op jit(solution)/shard_map/ppermute | solution.py:28
  134.5 6.7 %collective-permute-start.39 = (bf16[2,48,512]{2,1,0:T(8,128)(2,1)S(1)}, bf16[2,48,512]{2,1,0:T(8,128)(2,1)S(1)}, u32[]{:S(2)}, u32[]{:S(2)}) collective-permute-start(bf16[2,48,512]{2,1,0:T(8,128)(2,1)S(1)} %get-tuple-element.85), channel_id=1, source_target_pairs={{0,16},{8,24},{16,32},{24,40},{32,48},{40,56},{48,0},{56,8},{1,17}... | collective-permute-start | bytes 294920 | tf_op jit(solution)/shard_map/ppermute | solution.py:28
  141.3 8.6 %collective-permute-start.41 = (bf16[48,1024]{1,0:T(8,128)(2,1)S(1)}, bf16[48,1024]{1,0:T(8,128)(2,1)S(1)}, u32[]{:S(2)}, u32[]{:S(2)}) collective-permute-start(bf16[48,1024]{1,0:T(8,128)(2,1)S(1)} %fusion.10), channel_id=1, source_target_pairs={{0,32},{8,40},{16,48},{24,56},{32,0},{40,8},{48,16},{56,24},{1,33}... | collective-permute-start | bytes 294920 | tf_op jit(solution)/shard_map/ppermute | solution.py:28
  (12 other events, 64.2 us)

commit v11 on v10

--- a/solution.py
+++ b/solution.py
@@ -26,6 +26,19 @@
 def to_ahead(value, axis, k):
     n = SIZES[axis]
     return lax.ppermute(value, axis, [(i, (i + k) % n) for i in range(n)])
+
+
+def ring_pairs(axis, k):
+    n = SIZES[axis]
+    return [(i * 2 + c, (i + (k if c == 0 else -k)) % n * 2 + c) for i in range(n) for c in range(2)]
+
+
+def ring_from(value, axis, k):
+    return lax.ppermute(value, (axis, "core"), [(b, a) for a, b in ring_pairs(axis, k)])
+
+
+def ring_to(value, axis, k):
+    return lax.ppermute(value, (axis, "core"), ring_pairs(axis, k))
 
 
 def call(body, outs, smem, vmem, flops=0, scratch=(), limit=24):
@@ -73,6 +86,7 @@
     keep, send1, send2, toks, acc = refs[9:]
     core = pos[3]
     cut = a3[0].shape[-1]
+    way = 1 - 2 * core
     back = pos[0] - pos[2] + 4
     for j in range(4):
         d = (j + back) % 4
@@ -80,9 +94,10 @@
 
             @pl.loop(0, 2)
             def _(hi, i=i, j=j, d=d):
-                at = zpos(pos, STEPS[i], hi)
-                toks[d, at, :, :cut] = a3[i][j, hi]
-                toks[d, at, :, cut:] = b3[j][i, hi]
+                low = zpos(pos, way * STEPS[i], hi)
+                high = zpos(pos, STEPS[i], hi)
+                toks[d, low, :, :cut] = a3[i][j, hi]
+                toks[(j * way + back + 4) % 4, high, :, cut:] = b3[j][i, hi]
 
     @pl.loop(0, 4)
     def _(d):
@@ -128,6 +143,7 @@
     kept = pltpu.make_async_copy(first, grads.at[:, :, :, pl.ds(0, cut)], first_sem)
     kept.start()
     collect(pos, mine, other, lambda side: grads.at[:, side, :, pl.ds(cut, cut)], sems)
+    way = 1 - 2 * pos[3]
     back = pos[0] - pos[2] + 4
 
     @pl.loop(0, 4)
@@ -144,12 +160,13 @@
 
             @pl.loop(0, 4)
             def _(j, k=k, hi=hi):
-                piece = acc[j, zpos(pos, STEPS[k], hi), :, :cut]
+                piece = acc[j, zpos(pos, way * STEPS[k], hi), :, :cut]
                 a3[k][j, hi] = piece.astype(a3[k].dtype)
 
             @pl.loop(0, 4)
             def _(i, k=k, hi=hi):
-                piece = acc[k, zpos(pos, jnp.where(i == 3, -1, i), hi), :, cut:]
+                j = (k * way + 4) % 4
+                piece = acc[j, zpos(pos, jnp.where(i == 3, -1, i), hi), :, cut:]
                 b3[k][i, hi] = piece.astype(b3[k].dtype)
 
 
@@ -203,9 +220,9 @@
 
 
 def ring_gather(piece, axis):
-    ahead = from_ahead(piece, axis, 1)
-    behind = from_ahead(piece, axis, -1)
-    return [piece, ahead, from_ahead(ahead, axis, 1), behind]
+    ahead = ring_from(piece, axis, 1)
+    behind = ring_from(piece, axis, -1)
+    return [piece, ahead, ring_from(ahead, axis, 1), behind]
 
 
 def gather_tokens(tokens):
@@ -247,9 +264,9 @@
 
 
 def ring_reduce(own, ahead, far, behind, axis):
-    through = to_ahead(far, axis, 1).astype(F32)
-    total = own + to_ahead(behind, axis, -1).astype(F32)
-    return total + to_ahead((ahead + through).astype(BF16), axis, 1).astype(F32)
+    through = ring_to(far, axis, 1).astype(F32)
+    total = own + ring_to(behind, axis, -1).astype(F32)
+    return total + ring_to((ahead + through).astype(BF16), axis, 1).astype(F32)
 
 
 def middle(a3, b3, wm, flipped, pos, cot):

time: 153 us -> 152 us (level); the launches traced: 151 us -> 151 us
  waiting for transfers between devices: 52.1 us -> 56.4 us
  starting transfers between devices: 66.4 us -> 63 us
    ppermute x0 -> x12, starting transfers between devices: none -> 17.2 us  [the longest x6 10.2 us: ring_from(): lax.ppermute(value, (axis, 'core'), [(b, a) for a, b in ring_pairs(axis,...]
    ppermute x0 -> x12, waiting for transfers between devices: none -> 11.5 us  [the longest x6 6.34 us: ring_from(): lax.ppermute(value, (axis, 'core'), [(b, a) for a, b in ring_pairs(axis,...]
    ppermute x23 -> x17, starting transfers between devices: 28.9 us -> 18.5 us  [to_ahead(): return lax.ppermute(value, axis, [(i, (i + k) % n) for i in range(n)])]
    ppermute x19 -> x13, starting transfers between devices: 37.5 us -> 27.3 us  [from_ahead(): return lax.ppermute(value, axis, [((i + k) % n, i) for i in range(n)])]
    ppermute x19 -> x13, waiting for transfers between devices: 23.2 us -> 18.3 us  [from_ahead(): return lax.ppermute(value, axis, [((i + k) % n, i) for i in range(n)])]
    ppermute x23 -> x17, waiting for transfers between devices: 28.9 us -> 26.6 us  [to_ahead(): return lax.ppermute(value, axis, [(i, (i + k) % n) for i in range(n)])]
  transfers between devices with their start and end apart: 42 -> 42, of which waited for: 23 -> 22; matrix products, arithmetic and copies ran while one was open for 2% -> 2% of each run, Pallas kernels for 10% -> 10%
where the time goes in v11:
time: 152 us; the launch traced here: 151 us
  starting transfers between devices  63 us (41%)
  waiting for transfers between devices  56.4 us (37%)
  Pallas kernels  24.6 us (16%)
  other arithmetic  4.27 us (3%)
  local copies, waits for them, and re-layouts  1.64 us (1%)
  between operations  1.57 us (1%)
    ppermute x13, starting transfers between devices, from_ahead(): return lax.ppermute(value, axis, [((i + k) % n, i) for i in range(n)])  27.3 us
    ppermute x17, waiting for transfers between devices, to_ahead(): return lax.ppermute(value, axis, [(i, (i + k) % n) for i in range(n)])  26.6 us
    pallas_call x9, Pallas kernels, call(): pl.pallas_call(body, out_shape=outs, in_specs=[pl.BlockSpec(memory_space=...  24.6 us
    ppermute x17, starting transfers between devices, to_ahead(): return lax.ppermute(value, axis, [(i, (i + k) % n) for i in range(n)])  18.5 us
    ppermute x13, waiting for transfers between devices, from_ahead(): return lax.ppermute(value, axis, [((i + k) % n, i) for i in range(n)])  18.3 us
    ppermute x6, starting transfers between devices, ring_from(): lax.ppermute(value, (axis, 'core'), [(b, a) for a, b in ring_pairs(axis,...  10.2 us
    ppermute x6, starting transfers between devices, ring_to(): return lax.ppermute(value, (axis, 'core'), ring_pairs(axis, k))  6.94 us
    ppermute x6, waiting for transfers between devices, ring_from(): lax.ppermute(value, (axis, 'core'), [(b, a) for a, b in ring_pairs(axis,...  6.34 us
  transfers between devices with their start and end apart: 42, of which 22 were waited for; matrix products, arithmetic and copies ran while one was open for 2% of the time, Pallas kernels for 10%

profile of v11, /device:TPU:6, one launch (start us, length us, event | category | flops | bytes accessed | tf_op | source)
XLA Modules:
  0.0 151.4 jit_solution(3079550559692921987)
XLA Ops:
  0.6 7.3 %collective-permute-start = (bf16[48,1024]{1,0:T(8,128)(2,1)}, bf16[48,1024]{1,0:T(8,128)(2,1)S(1)}, u32[]{:S(2)}, u32[]{:S(2)}) collective-permute-start(bf16[48,1024]{1,0:T(8,128)(2,1)} %param.6), channel_id=1, source_target_pairs={{32,0},{40,8},{48,16},{56,24},{0,32},{8,40},{16,48},{24,56},{33,1}... | collective-permute-start | bytes 294920 | tf_op jit(solution)/shard_map/ppermute | solution.py:23
  7.9 3.1 %collective-permute-done = bf16[48,1024]{1,0:T(8,128)(2,1)S(1)} collective-permute-done((bf16[48,1024]{1,0:T(8,128)(2,1)}, bf16[48,1024]{1,0:T(8,128)(2,1)S(1)}, u32[]{:S(2)}, u32[]{:S(2)}) %collective-permute-start) | collective-permute-done | bytes 98336 | tf_op jit(solution)/shard_map/ppermute | solution.py:23
  11.9 2.6 %collective-permute-start.6 = (bf16[2,48,512]{2,1,0:T(8,128)(2,1)S(1)}, bf16[2,48,512]{2,1,0:T(8,128)(2,1)S(1)}, u32[]{:S(2)}, u32[]{:S(2)}) collective-permute-start(bf16[2,48,512]{2,1,0:T(8,128)(2,1)S(1)} %get-tuple-element.47), channel_id=1, source_target_pairs={{56,0},{0,8},{8,16},{16,24},{24,32},{32,40},{40,48},{48,56},{57,1}... | collective-permute-start | bytes 294920 | tf_op jit(solution)/shard_map/ppermute | solution.py:23
  14.4 4.2 %collective-permute-start.5 = (bf16[2,48,512]{2,1,0:T(8,128)(2,1)S(1)}, bf16[2,48,512]{2,1,0:T(8,128)(2,1)S(1)}, u32[]{:S(2)}, u32[]{:S(2)}) collective-permute-start(bf16[2,48,512]{2,1,0:T(8,128)(2,1)S(1)} %get-tuple-element.47), channel_id=1, source_target_pairs={{16,0},{24,8},{32,16},{40,24},{48,32},{56,40},{0,48},{8,56},{17,1}... | collective-permute-start | bytes 294920 | tf_op jit(solution)/shard_map/ppermute | solution.py:23
  18.6 1.9 %collective-permute-start.4 = (bf16[2,48,512]{2,1,0:T(8,128)(2,1)S(1)}, bf16[2,48,512]{2,1,0:T(8,128)(2,1)S(1)}, u32[]{:S(2)}, u32[]{:S(2)}) collective-permute-start(bf16[2,48,512]{2,1,0:T(8,128)(2,1)S(1)} %get-tuple-element.47), channel_id=1, source_target_pairs={{8,0},{16,8},{24,16},{32,24},{40,32},{48,40},{56,48},{0,56},{9,1},... | collective-permute-start | bytes 294920 | tf_op jit(solution)/shard_map/ppermute | solution.py:23
  22.1 2.9 %collective-permute-start.2 = (bf16[2,48,512]{2,1,0:T(8,128)(2,1)S(1)}, bf16[2,48,512]{2,1,0:T(8,128)(2,1)S(1)}, u32[]{:S(2)}, u32[]{:S(2)}) collective-permute-start(bf16[2,48,512]{2,1,0:T(8,128)(2,1)S(1)} %get-tuple-element.43), channel_id=1, source_target_pairs={{128,0},{192,64},{0,128},{64,192},{129,1},{193,65},{1,129},{65,193... | collective-permute-start | bytes 294920 | tf_op jit(solution)/shard_map/ppermute | solution.py:23
  29.7 2.6 %collective-permute-start.10 = (bf16[4,2,48,512]{3,2,1,0:T(8,128)(2,1)S(1)}, bf16[4,2,48,512]{3,2,1,0:T(8,128)(2,1)S(1)}, u32[]{:S(2)}, u32[]{:S(2)}) collective-permute-start(bf16[4,2,48,512]{3,2,1,0:T(8,128)(2,1)S(1)} %pad_maximum_fusion.3.refs_4_), channel_id=1, source_target_pairs={{64,0},{193,1},{128,64},{1,65},{192,128},{65,129},{0,192},{129,193... | collective-permute-start | bytes 1179656 | tf_op jit(solution)/shard_map/ppermute | solution.py:37
  34.5 5.1 %collective-permute-done.10.refs_5_ = bf16[4,2,48,512]{3,2,1,0:T(8,128)(2,1)S(1)} collective-permute-done((bf16[4,2,48,512]{3,2,1,0:T(8,128)(2,1)S(1)}, bf16[4,2,48,512]{3,2,1,0:T(8,128)(2,1)S(1)}, u32[]{:S(2)}, u32[]{:S(2)}) %collective-permute-start.10) | collective-permute-done | bytes 393248 | tf_op jit(solution)/shard_map/ppermute | solution.py:37
  39.7 3.7 %collective-permute-start.11 = (bf16[4,2,48,512]{3,2,1,0:T(8,128)(2,1)S(1)}, bf16[4,2,48,512]{3,2,1,0:T(8,128)(2,1)S(1)}, u32[]{:S(2)}, u32[]{:S(2)}) collective-permute-start(bf16[4,2,48,512]{3,2,1,0:T(8,128)(2,1)S(1)} %collective-permute-done.10.refs_5_), channel_id=1, source_target_pairs={{64,0},{193,1},{128,64},{1,65},{192,128},{65,129},{0,192},{129,193... | collective-permute-start | bytes 1179656 | tf_op jit(solution)/shard_map/ppermute | solution.py:37
  43.3 1.8 %collective-permute-start.8 = (bf16[4,2,48,512]{3,2,1,0:T(8,128)(2,1)S(1)}, bf16[4,2,48,512]{3,2,1,0:T(8,128)(2,1)S(1)}, u32[]{:S(2)}, u32[]{:S(2)}) collective-permute-start(bf16[4,2,48,512]{3,2,1,0:T(8,128)(2,1)S(1)} %collective-permute-done.7.refs_1_), channel_id=1, source_target_pairs={{8,0},{57,1},{16,8},{1,9},{24,16},{9,17},{32,24},{17,25},{40,32},{... | collective-permute-start | bytes 1179656 | tf_op jit(solution)/shard_map/ppermute | solution.py:37
  51.1 5.4 %shard_map.86 = (f32[4,192,1024]{2,1,0:T(8,128)S(1)}, bf16[4,192,512]{2,1,0:T(8,128)(2,1)S(1)}, bf16[4,192,512]{2,1,0:T(8,128)(2,1)S(1)}, bf16[4,8,48,1024]{3,2,1,0:T(8,128)(2,1)S(1)}) custom-call(s32[4]{0:T(128)S(1)} %pad_add_fusion.pos, bf16[4,2,48,512]{3,2,1,0:T(8,128)(2,1)S(1)} %pad_maximum_fusion.2.refs_0_, ...), custom_call_target="tpu_custom_call" | custom-call | flops 3221225472 | bytes 13107200 | tf_op jit(solution)/shard_map/pallas_call | solution.py:46
  57.1 1.8 %collective-permute-done.13.recv = bf16[4,192,512]{2,1,0:T(8,128)(2,1)S(1)} collective-permute-done((bf16[4,192,512]{2,1,0:T(8,128)(2,1)S(1)}, bf16[4,192,512]{2,1,0:T(8,128)(2,1)S(1)}, u32[]{:S(2)}, u32[]{:S(2)}) %collective-permute-start.13) | collective-permute-done | bytes 786464 | tf_op jit(solution)/shard_map/ppermute | solution.py:28
  62.7 2.4 %collective-permute-start.20 = (bf16[192,512]{1,0:T(8,128)(2,1)S(1)}, bf16[192,512]{1,0:T(8,128)(2,1)S(1)}, u32[]{:S(2)}, u32[]{:S(2)}) collective-permute-start(bf16[192,512]{1,0:T(8,128)(2,1)S(1)} %get-tuple-element.63), channel_id=1, source_target_pairs={{0,2},{2,4},{4,6},{6,0},{1,3},{3,5},{5,7},{7,1},{8,10},{10,12},{12... | collective-permute-start | bytes 589832 | tf_op jit(solution)/shard_map/ppermute | solution.py:28
  65.1 2.0 %collective-permute-done.14 = bf16[192,512]{1,0:T(8,128)(2,1)S(1)} collective-permute-done((bf16[192,512]{1,0:T(8,128)(2,1)S(1)}, bf16[192,512]{1,0:T(8,128)(2,1)S(1)}, u32[]{:S(2)}, u32[]{:S(2)}) %collective-permute-start.14) | collective-permute-done | bytes 196640 | tf_op jit(solution)/shard_map/ppermute | solution.py:28
  68.1 3.8 %collective-permute-done.18 = bf16[192,512]{1,0:T(8,128)(2,1)S(1)} collective-permute-done((bf16[192,512]{1,0:T(8,128)(2,1)S(1)}, bf16[192,512]{1,0:T(8,128)(2,1)S(1)}, u32[]{:S(2)}, u32[]{:S(2)}) %collective-permute-start.18) | collective-permute-done | bytes 196640 | tf_op jit(solution)/shard_map/ppermute | solution.py:28
  72.4 2.3 %collective-permute-done.15.r1 = bf16[192,512]{1,0:T(8,128)(2,1)S(1)} collective-permute-done((bf16[192,512]{1,0:T(8,128)(2,1)S(1)}, bf16[192,512]{1,0:T(8,128)(2,1)S(1)}, u32[]{:S(2)}, u32[]{:S(2)}) %collective-permute-start.15) | collective-permute-done | bytes 196640 | tf_op jit(solution)/shard_map/ppermute | solution.py:28
  75.0 2.0 %collective-permute-start.26 = (bf16[192,512]{1,0:T(8,128)(2,1)S(1)}, bf16[192,512]{1,0:T(8,128)(2,1)S(1)}, u32[]{:S(2)}, u32[]{:S(2)}) collective-permute-start(bf16[192,512]{1,0:T(8,128)(2,1)S(1)} %get-tuple-element.67), channel_id=1, source_target_pairs={{6,0},{0,2},{2,4},{4,6},{7,1},{1,3},{3,5},{5,7},{14,8},{8,10},{10,... | collective-permute-start | bytes 589832 | tf_op jit(solution)/shard_map/ppermute | solution.py:23
  77.0 2.0 %collective-permute-done.19.r1 = bf16[192,512]{1,0:T(8,128)(2,1)S(1)} collective-permute-done((bf16[192,512]{1,0:T(8,128)(2,1)S(1)}, bf16[192,512]{1,0:T(8,128)(2,1)S(1)}, u32[]{:S(2)}, u32[]{:S(2)}) %collective-permute-start.19) | collective-permute-done | bytes 196640 | tf_op jit(solution)/shard_map/ppermute | solution.py:28
  79.5 1.8 %collective-permute-done.26 = bf16[192,512]{1,0:T(8,128)(2,1)S(1)} collective-permute-done((bf16[192,512]{1,0:T(8,128)(2,1)S(1)}, bf16[192,512]{1,0:T(8,128)(2,1)S(1)}, u32[]{:S(2)}, u32[]{:S(2)}) %collective-permute-start.26) | collective-permute-done | bytes 196640 | tf_op jit(solution)/shard_map/ppermute | solution.py:23
  81.2 2.7 %collective-permute-start.27 = (bf16[192,512]{1,0:T(8,128)(2,1)S(1)}, bf16[192,512]{1,0:T(8,128)(2,1)S(1)}, u32[]{:S(2)}, u32[]{:S(2)}) collective-permute-start(bf16[192,512]{1,0:T(8,128)(2,1)S(1)} %collective-permute-done.26), channel_id=1, source_target_pairs={{6,0},{0,2},{2,4},{4,6},{7,1},{1,3},{3,5},{5,7},{14,8},{8,10},{10,... | collective-permute-start | bytes 589832 | tf_op jit(solution)/shard_map/ppermute | solution.py:23
  84.6 3.4 %collective-permute-done.21 = bf16[192,512]{1,0:T(8,128)(2,1)S(1)} collective-permute-done((bf16[192,512]{1,0:T(8,128)(2,1)S(1)}, bf16[192,512]{1,0:T(8,128)(2,1)S(1)}, u32[]{:S(2)}, u32[]{:S(2)}) %collective-permute-start.21) | collective-permute-done | bytes 196640 | tf_op jit(solution)/shard_map/ppermute | solution.py:23
  88.1 3.7 %collective-permute-done.25 = bf16[192,512]{1,0:T(8,128)(2,1)S(1)} collective-permute-done((bf16[192,512]{1,0:T(8,128)(2,1)S(1)}, bf16[192,512]{1,0:T(8,128)(2,1)S(1)}, u32[]{:S(2)}, u32[]{:S(2)}) %collective-permute-start.25) | collective-permute-done | bytes 196640 | tf_op jit(solution)/shard_map/ppermute | solution.py:23
  92.0 3.0 %collective-permute-done.22 = bf16[192,512]{1,0:T(8,128)(2,1)S(1)} collective-permute-done((bf16[192,512]{1,0:T(8,128)(2,1)S(1)}, bf16[192,512]{1,0:T(8,128)(2,1)S(1)}, u32[]{:S(2)}, u32[]{:S(2)}) %collective-permute-start.22) | collective-permute-done | bytes 196640 | tf_op jit(solution)/shard_map/ppermute | solution.py:23
  95.2 3.0 %shard_map.91 = (f32[4,8,48,1024]{3,2,1,0:T(8,128)S(1)}, bf16[4,2,192,512]{3,2,1,0:T(8,128)(2,1)S(1)}) custom-call(s32[4]{0:T(128)S(1)} %pad_add_fusion.pos, bf16[4,192,512]{2,1,0:T(8,128)(2,1)S(1)} %pad_maximum_fusion.1.refs_0_, bf16[4,192,512]{2,1,0:T(8,128)(2,1)S(1)} %collective-permute-done.28.refs_1_, bf16[1024,1024]{1,0:T(8,128)(2,1)S(1)} %get-tuple-element.66.refs_2_), custom_call_target="tpu_custom_call" | custom-call | flops 1610612736 | bytes 11534336 | tf_op jit(solution)/shard_map/pallas_call | solution.py:46
  98.2 4.5 %shard_map.92 = (f32[4,2,48,512]{3,2,1,0:T(8,128)S(1)}, f32[4,2,48,512]{3,2,1,0:T(8,128)S(1)}, bf16[4,2,48,512]{3,2,1,0:T(8,128)(2,1)S(1)}, bf16[4,2,48,512]{3,2...) custom-call(s32[4]{0:T(128)S(1)} %pad_add_fusion.pos, ...), custom_call_target="tpu_custom_call" | custom-call | flops 1610612736 | bytes 19398656 | tf_op jit(solution)/shard_map/pallas_call | solution.py:46
  103.5 2.7 %collective-permute-start.29 = (bf16[4,2,48,512]{3,2,1,0:T(8,128)(2,1)S(1)}, bf16[4,2,48,512]{3,2,1,0:T(8,128)(2,1)S(1)}, u32[]{:S(2)}, u32[]{:S(2)}) collective-permute-start(bf16[4,2,48,512]{3,2,1,0:T(8,128)(2,1)S(1)} %get-tuple-element.71), channel_id=1, source_target_pairs={{0,56},{1,9},{8,0},{9,17},{16,8},{17,25},{24,16},{25,33},{32,24},{... | collective-permute-start | bytes 1179656 | tf_op jit(solution)/shard_map/ppermute | solution.py:41
  106.2 3.2 %collective-permute-start.32 = (bf16[4,2,48,512]{3,2,1,0:T(8,128)(2,1)S(1)}, bf16[4,2,48,512]{3,2,1,0:T(8,128)(2,1)S(1)}, u32[]{:S(2)}, u32[]{:S(2)}) collective-permute-start(bf16[4,2,48,512]{3,2,1,0:T(8,128)(2,1)S(1)} %get-tuple-element.75), channel_id=1, source_target_pairs={{0,192},{1,65},{64,0},{65,129},{128,64},{129,193},{192,128},{193,1... | collective-permute-start | bytes 1179656 | tf_op jit(solution)/shard_map/ppermute | solution.py:41
  109.4 3.8 %collective-permute-done.30 = bf16[4,2,48,512]{3,2,1,0:T(8,128)(2,1)S(1)} collective-permute-done((bf16[4,2,48,512]{3,2,1,0:T(8,128)(2,1)S(1)}, bf16[4,2,48,512]{3,2,1,0:T(8,128)(2,1)S(1)}, u32[]{:S(2)}, u32[]{:S(2)}) %collective-permute-start.30) | collective-permute-done | bytes 393248 | tf_op jit(solution)/shard_map/ppermute | solution.py:41
  114.4 8.6 %shard_map.93 = bf16[1024,1024]{1,0:T(8,128)(2,1)} custom-call(s32[32]{0:T(128)S(1)} %get-tuple-element.92.rows, s32[32]{0:T(128)S(1)} %get-tuple-element.91.cols, s32[1]{0:T(128)} %bitcast.60.count, bf16[4,8,48,1024]{3,2,1,0:T(8,128)(2,1)S(1)} %get-tuple-element.78.toks, bf16[4,2,192,1024]{3,2,1,0:T(8,128)(2,1)S(1)} %get-tuple-element.79.grads), custom_call_target="tpu_custom_call" | custom-call | flops 3221225472 | bytes 8388608 | tf_op jit(solution)/shard_map/pallas_call | solution.py:46
  129.8 2.4 %collective-permute-start.40 = (bf16[2,48,512]{2,1,0:T(8,128)(2,1)S(1)}, bf16[2,48,512]{2,1,0:T(8,128)(2,1)S(1)}, u32[]{:S(2)}, u32[]{:S(2)}) collective-permute-start(bf16[2,48,512]{2,1,0:T(8,128)(2,1)S(1)} %get-tuple-element.84), channel_id=1, source_target_pairs={{0,56},{8,0},{16,8},{24,16},{32,24},{40,32},{48,40},{56,48},{1,57}... | collective-permute-start | bytes 294920 | tf_op jit(solution)/shard_map/ppermute | solution.py:28
  135.8 6.0 %collective-permute-done.39 = bf16[2,48,512]{2,1,0:T(8,128)(2,1)S(1)} collective-permute-done((bf16[2,48,512]{2,1,0:T(8,128)(2,1)S(1)}, bf16[2,48,512]{2,1,0:T(8,128)(2,1)S(1)}, u32[]{:S(2)}, u32[]{:S(2)}) %collective-permute-start.39) | collective-permute-done | bytes 98336 | tf_op jit(solution)/shard_map/ppermute | solution.py:28
  143.8 6.9 %collective-permute-done.41 = bf16[48,1024]{1,0:T(8,128)(2,1)S(1)} collective-permute-done((bf16[48,1024]{1,0:T(8,128)(2,1)S(1)}, bf16[48,1024]{1,0:T(8,128)(2,1)S(1)}, u32[]{:S(2)}, u32[]{:S(2)}) %collective-permute-start.41) | collective-permute-done | bytes 98336 | tf_op jit(solution)/shard_map/ppermute | solution.py:28
  (87 shorter events, 37.2 us)
Async XLA Ops:
  0.6 10.4 %collective-permute-start = (bf16[48,1024]{1,0:T(8,128)(2,1)}, bf16[48,1024]{1,0:T(8,128)(2,1)S(1)}, u32[]{:S(2)}, u32[]{:S(2)}) collective-permute-start(bf16[48,1024]{1,0:T(8,128)(2,1)} %param.6), channel_id=1, source_target_pairs={{32,0},{40,8},{48,16},{56,24},{0,32},{8,40},{16,48},{24,56},{33,1}... | collective-permute-start | bytes 294920 | tf_op jit(solution)/shard_map/ppermute | solution.py:23
  11.9 13.2 %collective-permute-start.6 = (bf16[2,48,512]{2,1,0:T(8,128)(2,1)S(1)}, bf16[2,48,512]{2,1,0:T(8,128)(2,1)S(1)}, u32[]{:S(2)}, u32[]{:S(2)}) collective-permute-start(bf16[2,48,512]{2,1,0:T(8,128)(2,1)S(1)} %get-tuple-element.47), channel_id=1, source_target_pairs={{56,0},{0,8},{8,16},{16,24},{24,32},{32,40},{40,48},{48,56},{57,1}... | collective-permute-start | bytes 294920 | tf_op jit(solution)/shard_map/ppermute | solution.py:23
  14.4 12.0 %collective-permute-start.5 = (bf16[2,48,512]{2,1,0:T(8,128)(2,1)S(1)}, bf16[2,48,512]{2,1,0:T(8,128)(2,1)S(1)}, u32[]{:S(2)}, u32[]{:S(2)}) collective-permute-start(bf16[2,48,512]{2,1,0:T(8,128)(2,1)S(1)} %get-tuple-element.47), channel_id=1, source_target_pairs={{16,0},{24,8},{32,16},{40,24},{48,32},{56,40},{0,48},{8,56},{17,1}... | collective-permute-start | bytes 294920 | tf_op jit(solution)/shard_map/ppermute | solution.py:23
  18.6 7.8 %collective-permute-start.4 = (bf16[2,48,512]{2,1,0:T(8,128)(2,1)S(1)}, bf16[2,48,512]{2,1,0:T(8,128)(2,1)S(1)}, u32[]{:S(2)}, u32[]{:S(2)}) collective-permute-start(bf16[2,48,512]{2,1,0:T(8,128)(2,1)S(1)} %get-tuple-element.47), channel_id=1, source_target_pairs={{8,0},{16,8},{24,16},{32,24},{40,32},{48,40},{56,48},{0,56},{9,1},... | collective-permute-start | bytes 294920 | tf_op jit(solution)/shard_map/ppermute | solution.py:23
  22.1 6.5 %collective-permute-start.2 = (bf16[2,48,512]{2,1,0:T(8,128)(2,1)S(1)}, bf16[2,48,512]{2,1,0:T(8,128)(2,1)S(1)}, u32[]{:S(2)}, u32[]{:S(2)}) collective-permute-start(bf16[2,48,512]{2,1,0:T(8,128)(2,1)S(1)} %get-tuple-element.43), channel_id=1, source_target_pairs={{128,0},{192,64},{0,128},{64,192},{129,1},{193,65},{1,129},{65,193... | collective-permute-start | bytes 294920 | tf_op jit(solution)/shard_map/ppermute | solution.py:23
  29.7 9.9 %collective-permute-start.10 = (bf16[4,2,48,512]{3,2,1,0:T(8,128)(2,1)S(1)}, bf16[4,2,48,512]{3,2,1,0:T(8,128)(2,1)S(1)}, u32[]{:S(2)}, u32[]{:S(2)}) collective-permute-start(bf16[4,2,48,512]{3,2,1,0:T(8,128)(2,1)S(1)} %pad_maximum_fusion.3.refs_4_), channel_id=1, source_target_pairs={{64,0},{193,1},{128,64},{1,65},{192,128},{65,129},{0,192},{129,193... | collective-permute-start | bytes 1179656 | tf_op jit(solution)/shard_map/ppermute | solution.py:37
  32.4 10.9 %collective-permute-start.7 = (bf16[4,2,48,512]{3,2,1,0:T(8,128)(2,1)S(1)}, bf16[4,2,48,512]{3,2,1,0:T(8,128)(2,1)S(1)}, u32[]{:S(2)}, u32[]{:S(2)}) collective-permute-start(bf16[4,2,48,512]{3,2,1,0:T(8,128)(2,1)S(1)} %pad_maximum_fusion.2.refs_0_), channel_id=1, source_target_pairs={{8,0},{57,1},{16,8},{1,9},{24,16},{9,17},{32,24},{17,25},{40,32},{... | collective-permute-start | bytes 1179656 | tf_op jit(solution)/shard_map/ppermute | solution.py:37
  33.7 16.2 %collective-permute-start.12 = (bf16[4,2,48,512]{3,2,1,0:T(8,128)(2,1)S(1)}, bf16[4,2,48,512]{3,2,1,0:T(8,128)(2,1)S(1)}, u32[]{:S(2)}, u32[]{:S(2)}) collective-permute-start(bf16[4,2,48,512]{3,2,1,0:T(8,128)(2,1)S(1)} %pad_maximum_fusion.3.refs_4_), channel_id=1, source_target_pairs={{192,0},{65,1},{0,64},{129,65},{64,128},{193,129},{128,192},{1,193... | collective-permute-start | bytes 1179656 | tf_op jit(solution)/shard_map/ppermute | solution.py:37
  33.7 16.2 %collective-permute-start.9 = (bf16[4,2,48,512]{3,2,1,0:T(8,128)(2,1)S(1)}, bf16[4,2,48,512]{3,2,1,0:T(8,128)(2,1)S(1)}, u32[]{:S(2)}, u32[]{:S(2)}) collective-permute-start(bf16[4,2,48,512]{3,2,1,0:T(8,128)(2,1)S(1)} %pad_maximum_fusion.2.refs_0_), channel_id=1, source_target_pairs={{56,0},{9,1},{0,8},{17,9},{8,16},{25,17},{16,24},{33,25},{24,32},{... | collective-permute-start | bytes 1179656 | tf_op jit(solution)/shard_map/ppermute | solution.py:37
  39.7 10.3 %collective-permute-start.11 = (bf16[4,2,48,512]{3,2,1,0:T(8,128)(2,1)S(1)}, bf16[4,2,48,512]{3,2,1,0:T(8,128)(2,1)S(1)}, u32[]{:S(2)}, u32[]{:S(2)}) collective-permute-start(bf16[4,2,48,512]{3,2,1,0:T(8,128)(2,1)S(1)} %collective-permute-done.10.refs_5_), channel_id=1, source_target_pairs={{64,0},{193,1},{128,64},{1,65},{192,128},{65,129},{0,192},{129,193... | collective-permute-start | bytes 1179656 | tf_op jit(solution)/shard_map/ppermute | solution.py:37
  43.3 7.8 %collective-permute-start.8 = (bf16[4,2,48,512]{3,2,1,0:T(8,128)(2,1)S(1)}, bf16[4,2,48,512]{3,2,1,0:T(8,128)(2,1)S(1)}, u32[]{:S(2)}, u32[]{:S(2)}) collective-permute-start(bf16[4,2,48,512]{3,2,1,0:T(8,128)(2,1)S(1)} %collective-permute-done.7.refs_1_), channel_id=1, source_target_pairs={{8,0},{57,1},{16,8},{1,9},{24,16},{9,17},{32,24},{17,25},{40,32},{... | collective-permute-start | bytes 1179656 | tf_op jit(solution)/shard_map/ppermute | solution.py:37
  59.3 7.8 %collective-permute-start.14 = (bf16[192,512]{1,0:T(8,128)(2,1)S(1)}, bf16[192,512]{1,0:T(8,128)(2,1)S(1)}, u32[]{:S(2)}, u32[]{:S(2)}) collective-permute-start(bf16[192,512]{1,0:T(8,128)(2,1)S(1)} %get-tuple-element.56), channel_id=1, source_target_pairs={{0,2},{2,4},{4,6},{6,0},{1,3},{3,5},{5,7},{7,1},{8,10},{10,12},{12... | collective-permute-start | bytes 589832 | tf_op jit(solution)/shard_map/ppermute | solution.py:28
  59.8 12.6 %collective-permute-start.16 = (bf16[192,512]{1,0:T(8,128)(2,1)S(1)}, bf16[192,512]{1,0:T(8,128)(2,1)S(1)}, u32[]{:S(2)}, u32[]{:S(2)}) collective-permute-start(bf16[192,512]{1,0:T(8,128)(2,1)S(1)} %get-tuple-element.57), channel_id=1, source_target_pairs={{0,6},{2,0},{4,2},{6,4},{1,7},{3,1},{5,3},{7,5},{8,14},{10,8},{12,... | collective-permute-start | bytes 589832 | tf_op jit(solution)/shard_map/ppermute | solution.py:28
  61.8 10.1 %collective-permute-start.18 = (bf16[192,512]{1,0:T(8,128)(2,1)S(1)}, bf16[192,512]{1,0:T(8,128)(2,1)S(1)}, u32[]{:S(2)}, u32[]{:S(2)}) collective-permute-start(bf16[192,512]{1,0:T(8,128)(2,1)S(1)} %get-tuple-element.62), channel_id=1, source_target_pairs={{0,6},{2,0},{4,2},{6,4},{1,7},{3,1},{5,3},{7,5},{8,14},{10,8},{12,... | collective-permute-start | bytes 589832 | tf_op jit(solution)/shard_map/ppermute | solution.py:28
  62.7 14.3 %collective-permute-start.20 = (bf16[192,512]{1,0:T(8,128)(2,1)S(1)}, bf16[192,512]{1,0:T(8,128)(2,1)S(1)}, u32[]{:S(2)}, u32[]{:S(2)}) collective-permute-start(bf16[192,512]{1,0:T(8,128)(2,1)S(1)} %get-tuple-element.63), channel_id=1, source_target_pairs={{0,2},{2,4},{4,6},{6,0},{1,3},{3,5},{5,7},{7,1},{8,10},{10,12},{12... | collective-permute-start | bytes 589832 | tf_op jit(solution)/shard_map/ppermute | solution.py:28
  67.2 7.6 %collective-permute-start.15 = (bf16[192,512]{1,0:T(8,128)(2,1)S(1)}, bf16[192,512]{1,0:T(8,128)(2,1)S(1)}, u32[]{:S(2)}, u32[]{:S(2)}) collective-permute-start(bf16[192,512]{1,0:T(8,128)(2,1)S(1)} %add_convert_fusion.3), channel_id=1, source_target_pairs={{0,2},{2,4},{4,6},{6,0},{1,3},{3,5},{5,7},{7,1},{8,10},{10,12},{12... | collective-permute-start | bytes 589832 | tf_op jit(solution)/shard_map/ppermute | solution.py:28
  71.9 7.1 %collective-permute-start.19 = (bf16[192,512]{1,0:T(8,128)(2,1)S(1)}, bf16[192,512]{1,0:T(8,128)(2,1)S(1)}, u32[]{:S(2)}, u32[]{:S(2)}) collective-permute-start(bf16[192,512]{1,0:T(8,128)(2,1)S(1)} %add_convert_fusion.2), channel_id=1, source_target_pairs={{0,6},{2,0},{4,2},{6,4},{1,7},{3,1},{5,3},{7,5},{8,14},{10,8},{12,... | collective-permute-start | bytes 589832 | tf_op jit(solution)/shard_map/ppermute | solution.py:28
  79.3 8.8 %collective-permute-start.21 = (bf16[192,512]{1,0:T(8,128)(2,1)S(1)}, bf16[192,512]{1,0:T(8,128)(2,1)S(1)}, u32[]{:S(2)}, u32[]{:S(2)}) collective-permute-start(bf16[192,512]{1,0:T(8,128)(2,1)S(1)} %get-tuple-element.65), channel_id=1, source_target_pairs={{2,0},{4,2},{6,4},{0,6},{3,1},{5,3},{7,5},{1,7},{10,8},{12,10},{14... | collective-permute-start | bytes 589832 | tf_op jit(solution)/shard_map/ppermute | solution.py:23
  79.4 12.4 %collective-permute-start.25 = (bf16[192,512]{1,0:T(8,128)(2,1)S(1)}, bf16[192,512]{1,0:T(8,128)(2,1)S(1)}, u32[]{:S(2)}, u32[]{:S(2)}) collective-permute-start(bf16[192,512]{1,0:T(8,128)(2,1)S(1)} %get-tuple-element.67), channel_id=1, source_target_pairs={{2,0},{4,2},{6,4},{0,6},{3,1},{5,3},{7,5},{1,7},{10,8},{12,10},{14... | collective-permute-start | bytes 589832 | tf_op jit(solution)/shard_map/ppermute | solution.py:23
  81.2 10.5 %collective-permute-start.27 = (bf16[192,512]{1,0:T(8,128)(2,1)S(1)}, bf16[192,512]{1,0:T(8,128)(2,1)S(1)}, u32[]{:S(2)}, u32[]{:S(2)}) collective-permute-start(bf16[192,512]{1,0:T(8,128)(2,1)S(1)} %collective-permute-done.26), channel_id=1, source_target_pairs={{6,0},{0,2},{2,4},{4,6},{7,1},{1,3},{3,5},{5,7},{14,8},{8,10},{10,... | collective-permute-start | bytes 589832 | tf_op jit(solution)/shard_map/ppermute | solution.py:23
  83.9 8.0 %collective-permute-start.23 = (bf16[192,512]{1,0:T(8,128)(2,1)S(1)}, bf16[192,512]{1,0:T(8,128)(2,1)S(1)}, u32[]{:S(2)}, u32[]{:S(2)}) collective-permute-start(bf16[192,512]{1,0:T(8,128)(2,1)S(1)} %get-tuple-element.65), channel_id=1, source_target_pairs={{6,0},{0,2},{2,4},{4,6},{7,1},{1,3},{3,5},{5,7},{14,8},{8,10},{10,... | collective-permute-start | bytes 589832 | tf_op jit(solution)/shard_map/ppermute | solution.py:23
  88.1 6.9 %collective-permute-start.22 = (bf16[192,512]{1,0:T(8,128)(2,1)S(1)}, bf16[192,512]{1,0:T(8,128)(2,1)S(1)}, u32[]{:S(2)}, u32[]{:S(2)}) collective-permute-start(bf16[192,512]{1,0:T(8,128)(2,1)S(1)} %collective-permute-done.21), channel_id=1, source_target_pairs={{2,0},{4,2},{6,4},{0,6},{3,1},{5,3},{7,5},{1,7},{10,8},{12,10},{14... | collective-permute-start | bytes 589832 | tf_op jit(solution)/shard_map/ppermute | solution.py:23
  102.7 10.5 %collective-permute-start.30 = (bf16[4,2,48,512]{3,2,1,0:T(8,128)(2,1)S(1)}, bf16[4,2,48,512]{3,2,1,0:T(8,128)(2,1)S(1)}, u32[]{:S(2)}, u32[]{:S(2)}) collective-permute-start(bf16[4,2,48,512]{3,2,1,0:T(8,128)(2,1)S(1)} %get-tuple-element.73), channel_id=1, source_target_pairs={{0,8},{1,57},{8,16},{9,1},{16,24},{17,9},{24,32},{25,17},{32,40},{... | collective-permute-start | bytes 1179656 | tf_op jit(solution)/shard_map/ppermute | solution.py:41
  103.5 10.7 %collective-permute-start.33 = (bf16[4,2,48,512]{3,2,1,0:T(8,128)(2,1)S(1)}, bf16[4,2,48,512]{3,2,1,0:T(8,128)(2,1)S(1)}, u32[]{:S(2)}, u32[]{:S(2)}) collective-permute-start(bf16[4,2,48,512]{3,2,1,0:T(8,128)(2,1)S(1)} %get-tuple-element.77), channel_id=1, source_target_pairs={{0,64},{1,193},{64,128},{65,1},{128,192},{129,65},{192,0},{193,129... | collective-permute-start | bytes 1179656 | tf_op jit(solution)/shard_map/ppermute | solution.py:41
  103.5 19.6 %collective-permute-start.29 = (bf16[4,2,48,512]{3,2,1,0:T(8,128)(2,1)S(1)}, bf16[4,2,48,512]{3,2,1,0:T(8,128)(2,1)S(1)}, u32[]{:S(2)}, u32[]{:S(2)}) collective-permute-start(bf16[4,2,48,512]{3,2,1,0:T(8,128)(2,1)S(1)} %get-tuple-element.71), channel_id=1, source_target_pairs={{0,56},{1,9},{8,0},{9,17},{16,8},{17,25},{24,16},{25,33},{32,24},{... | collective-permute-start | bytes 1179656 | tf_op jit(solution)/shard_map/ppermute | solution.py:41
  106.2 17.6 %collective-permute-start.32 = (bf16[4,2,48,512]{3,2,1,0:T(8,128)(2,1)S(1)}, bf16[4,2,48,512]{3,2,1,0:T(8,128)(2,1)S(1)}, u32[]{:S(2)}, u32[]{:S(2)}) collective-permute-start(bf16[4,2,48,512]{3,2,1,0:T(8,128)(2,1)S(1)} %get-tuple-element.75), channel_id=1, source_target_pairs={{0,192},{1,65},{64,0},{65,129},{128,64},{129,193},{192,128},{193,1... | collective-permute-start | bytes 1179656 | tf_op jit(solution)/shard_map/ppermute | solution.py:41
  113.3 10.3 %collective-permute-start.31 = (bf16[4,2,48,512]{3,2,1,0:T(8,128)(2,1)S(1)}, bf16[4,2,48,512]{3,2,1,0:T(8,128)(2,1)S(1)}, u32[]{:S(2)}, u32[]{:S(2)}) collective-permute-start(bf16[4,2,48,512]{3,2,1,0:T(8,128)(2,1)S(1)} %add_convert_fusion.1), channel_id=1, source_target_pairs={{0,8},{1,57},{8,16},{9,1},{16,24},{17,9},{24,32},{25,17},{32,40},{... | collective-permute-start | bytes 1179656 | tf_op jit(solution)/shard_map/ppermute | solution.py:41
  114.3 9.5 %collective-permute-start.34 = (bf16[4,2,48,512]{3,2,1,0:T(8,128)(2,1)S(1)}, bf16[4,2,48,512]{3,2,1,0:T(8,128)(2,1)S(1)}, u32[]{:S(2)}, u32[]{:S(2)}) collective-permute-start(bf16[4,2,48,512]{3,2,1,0:T(8,128)(2,1)S(1)} %add_convert_fusion), channel_id=1, source_target_pairs={{0,64},{1,193},{64,128},{65,1},{128,192},{129,65},{192,0},{193,129... | collective-permute-start | bytes 1179656 | tf_op jit(solution)/shard_map/ppermute | solution.py:41
  124.1 8.1 %collective-permute-start.35 = (bf16[2,48,512]{2,1,0:T(8,128)(2,1)S(1)}, bf16[2,48,512]{2,1,0:T(8,128)(2,1)S(1)}, u32[]{:S(2)}, u32[]{:S(2)}) collective-permute-start(bf16[2,48,512]{2,1,0:T(8,128)(2,1)S(1)} %get-tuple-element.86), channel_id=1, source_target_pairs={{0,64},{64,128},{128,192},{192,0},{1,65},{65,129},{129,193},{193,1... | collective-permute-start | bytes 294920 | tf_op jit(solution)/shard_map/ppermute | solution.py:28
  125.7 8.3 %collective-permute-start.37 = (bf16[2,48,512]{2,1,0:T(8,128)(2,1)S(1)}, bf16[2,48,512]{2,1,0:T(8,128)(2,1)S(1)}, u32[]{:S(2)}, u32[]{:S(2)}) collective-permute-start(bf16[2,48,512]{2,1,0:T(8,128)(2,1)S(1)} %get-tuple-element.87), channel_id=1, source_target_pairs={{0,192},{64,0},{128,64},{192,128},{1,193},{65,1},{129,65},{193,129... | collective-permute-start | bytes 294920 | tf_op jit(solution)/shard_map/ppermute | solution.py:28
  132.2 9.6 %collective-permute-start.39 = (bf16[2,48,512]{2,1,0:T(8,128)(2,1)S(1)}, bf16[2,48,512]{2,1,0:T(8,128)(2,1)S(1)}, u32[]{:S(2)}, u32[]{:S(2)}) collective-permute-start(bf16[2,48,512]{2,1,0:T(8,128)(2,1)S(1)} %get-tuple-element.85), channel_id=1, source_target_pairs={{0,16},{8,24},{16,32},{24,40},{32,48},{40,56},{48,0},{56,8},{1,17}... | collective-permute-start | bytes 294920 | tf_op jit(solution)/shard_map/ppermute | solution.py:28
  141.9 8.9 %collective-permute-start.41 = (bf16[48,1024]{1,0:T(8,128)(2,1)S(1)}, bf16[48,1024]{1,0:T(8,128)(2,1)S(1)}, u32[]{:S(2)}, u32[]{:S(2)}) collective-permute-start(bf16[48,1024]{1,0:T(8,128)(2,1)S(1)} %fusion.10), channel_id=1, source_target_pairs={{0,32},{8,40},{16,48},{24,56},{32,0},{40,8},{48,16},{56,24},{1,33}... | collective-permute-start | bytes 294920 | tf_op jit(solution)/shard_map/ppermute | solution.py:28
  (12 other events, 66.1 us)

commit v12 on v11

--- a/solution.py
+++ b/solution.py
@@ -317,7 +317,7 @@
 def reduce_inputs(sends, weight_grad):
     a2 = ring_reduce(*sends[:4], "z")
     b2 = ring_reduce(*sends[4:], "y")
-    a2, b2, weight_grad = lax.optimization_barrier((a2, b2, weight_grad))
+    a2, b2 = lax.optimization_barrier((a2, b2))
     a1 = reduce_four(a2[0], a2[1:], "y")
     b1 = reduce_four(b2[0], b2[1:], "z")
     both = jnp.concatenate([a1, b1], axis=-1)

time: 152 us -> 155 us (1.020)
  waiting for transfers between devices: 56.4 us -> 61.5 us
  starting transfers between devices: 63 us -> 60.1 us
    ppermute x6, waiting for transfers between devices: 5.14 us -> 17.7 us  [ring_to(): return lax.ppermute(value, (axis, 'core'), ring_pairs(axis, k))]
    ppermute x17, waiting for transfers between devices: 26.6 us -> 20.5 us  [to_ahead(): return lax.ppermute(value, axis, [(i, (i + k) % n) for i in range(n)])]
    ppermute x17, starting transfers between devices: 18.5 us -> 16.5 us  [to_ahead(): return lax.ppermute(value, axis, [(i, (i + k) % n) for i in range(n)])]
where the time goes in v12:
time: 155 us
  waiting for transfers between devices  61.5 us (40%)
  starting transfers between devices  60.1 us (39%)
  Pallas kernels  26 us (17%)
  other arithmetic  4.29 us (3%)
  local copies, waits for them, and re-layouts  1.64 us (1%)
  between operations  1.57 us (1%)
    ppermute x13, starting transfers between devices, from_ahead(): return lax.ppermute(value, axis, [((i + k) % n, i) for i in range(n)])  27.5 us
    pallas_call x9, Pallas kernels, call(): pl.pallas_call(body, out_shape=outs, in_specs=[pl.BlockSpec(memory_space=...  26 us
    ppermute x17, waiting for transfers between devices, to_ahead(): return lax.ppermute(value, axis, [(i, (i + k) % n) for i in range(n)])  20.5 us
    ppermute x13, waiting for transfers between devices, from_ahead(): return lax.ppermute(value, axis, [((i + k) % n, i) for i in range(n)])  18.1 us
    ppermute x6, waiting for transfers between devices, ring_to(): return lax.ppermute(value, (axis, 'core'), ring_pairs(axis, k))  17.7 us
    ppermute x17, starting transfers between devices, to_ahead(): return lax.ppermute(value, axis, [(i, (i + k) % n) for i in range(n)])  16.5 us
    ppermute x6, starting transfers between devices, ring_from(): lax.ppermute(value, (axis, 'core'), [(b, a) for a, b in ring_pairs(axis,...  10.2 us
    ppermute x6, starting transfers between devices, ring_to(): return lax.ppermute(value, (axis, 'core'), ring_pairs(axis, k))  5.8 us
  transfers between devices with their start and end apart: 42, of which 22 were waited for; matrix products, arithmetic and copies ran while one was open for 2% of the time, Pallas kernels for 10%

profile of v12, /device:TPU:6, one launch (start us, length us, event | category | flops | bytes accessed | tf_op | source)
XLA Modules:
  0.0 155.1 jit_solution(8408332624135166663)
XLA Ops:
  0.6 7.3 %collective-permute-start = (bf16[48,1024]{1,0:T(8,128)(2,1)}, bf16[48,1024]{1,0:T(8,128)(2,1)S(1)}, u32[]{:S(2)}, u32[]{:S(2)}) collective-permute-start(bf16[48,1024]{1,0:T(8,128)(2,1)} %param.6), channel_id=1, source_target_pairs={{32,0},{40,8},{48,16},{56,24},{0,32},{8,40},{16,48},{24,56},{33,1}... | collective-permute-start | bytes 294920 | tf_op jit(solution)/shard_map/ppermute | solution.py:23
  7.9 3.1 %collective-permute-done = bf16[48,1024]{1,0:T(8,128)(2,1)S(1)} collective-permute-done((bf16[48,1024]{1,0:T(8,128)(2,1)}, bf16[48,1024]{1,0:T(8,128)(2,1)S(1)}, u32[]{:S(2)}, u32[]{:S(2)}) %collective-permute-start) | collective-permute-done | bytes 98336 | tf_op jit(solution)/shard_map/ppermute | solution.py:23
  11.9 2.6 %collective-permute-start.6 = (bf16[2,48,512]{2,1,0:T(8,128)(2,1)S(1)}, bf16[2,48,512]{2,1,0:T(8,128)(2,1)S(1)}, u32[]{:S(2)}, u32[]{:S(2)}) collective-permute-start(bf16[2,48,512]{2,1,0:T(8,128)(2,1)S(1)} %get-tuple-element.46), channel_id=1, source_target_pairs={{56,0},{0,8},{8,16},{16,24},{24,32},{32,40},{40,48},{48,56},{57,1}... | collective-permute-start | bytes 294920 | tf_op jit(solution)/shard_map/ppermute | solution.py:23
  14.4 4.2 %collective-permute-start.5 = (bf16[2,48,512]{2,1,0:T(8,128)(2,1)S(1)}, bf16[2,48,512]{2,1,0:T(8,128)(2,1)S(1)}, u32[]{:S(2)}, u32[]{:S(2)}) collective-permute-start(bf16[2,48,512]{2,1,0:T(8,128)(2,1)S(1)} %get-tuple-element.46), channel_id=1, source_target_pairs={{16,0},{24,8},{32,16},{40,24},{48,32},{56,40},{0,48},{8,56},{17,1}... | collective-permute-start | bytes 294920 | tf_op jit(solution)/shard_map/ppermute | solution.py:23
  18.6 1.9 %collective-permute-start.4 = (bf16[2,48,512]{2,1,0:T(8,128)(2,1)S(1)}, bf16[2,48,512]{2,1,0:T(8,128)(2,1)S(1)}, u32[]{:S(2)}, u32[]{:S(2)}) collective-permute-start(bf16[2,48,512]{2,1,0:T(8,128)(2,1)S(1)} %get-tuple-element.46), channel_id=1, source_target_pairs={{8,0},{16,8},{24,16},{32,24},{40,32},{48,40},{56,48},{0,56},{9,1},... | collective-permute-start | bytes 294920 | tf_op jit(solution)/shard_map/ppermute | solution.py:23
  22.1 2.9 %collective-permute-start.2 = (bf16[2,48,512]{2,1,0:T(8,128)(2,1)S(1)}, bf16[2,48,512]{2,1,0:T(8,128)(2,1)S(1)}, u32[]{:S(2)}, u32[]{:S(2)}) collective-permute-start(bf16[2,48,512]{2,1,0:T(8,128)(2,1)S(1)} %get-tuple-element.42), channel_id=1, source_target_pairs={{128,0},{192,64},{0,128},{64,192},{129,1},{193,65},{1,129},{65,193... | collective-permute-start | bytes 294920 | tf_op jit(solution)/shard_map/ppermute | solution.py:23
  29.7 2.6 %collective-permute-start.10 = (bf16[4,2,48,512]{3,2,1,0:T(8,128)(2,1)S(1)}, bf16[4,2,48,512]{3,2,1,0:T(8,128)(2,1)S(1)}, u32[]{:S(2)}, u32[]{:S(2)}) collective-permute-start(bf16[4,2,48,512]{3,2,1,0:T(8,128)(2,1)S(1)} %pad_maximum_fusion.3.refs_4_), channel_id=1, source_target_pairs={{64,0},{193,1},{128,64},{1,65},{192,128},{65,129},{0,192},{129,193... | collective-permute-start | bytes 1179656 | tf_op jit(solution)/shard_map/ppermute | solution.py:37
  34.5 5.1 %collective-permute-done.10.refs_5_ = bf16[4,2,48,512]{3,2,1,0:T(8,128)(2,1)S(1)} collective-permute-done((bf16[4,2,48,512]{3,2,1,0:T(8,128)(2,1)S(1)}, bf16[4,2,48,512]{3,2,1,0:T(8,128)(2,1)S(1)}, u32[]{:S(2)}, u32[]{:S(2)}) %collective-permute-start.10) | collective-permute-done | bytes 393248 | tf_op jit(solution)/shard_map/ppermute | solution.py:37
  39.7 3.7 %collective-permute-start.11 = (bf16[4,2,48,512]{3,2,1,0:T(8,128)(2,1)S(1)}, bf16[4,2,48,512]{3,2,1,0:T(8,128)(2,1)S(1)}, u32[]{:S(2)}, u32[]{:S(2)}) collective-permute-start(bf16[4,2,48,512]{3,2,1,0:T(8,128)(2,1)S(1)} %collective-permute-done.10.refs_5_), channel_id=1, source_target_pairs={{64,0},{193,1},{128,64},{1,65},{192,128},{65,129},{0,192},{129,193... | collective-permute-start | bytes 1179656 | tf_op jit(solution)/shard_map/ppermute | solution.py:37
  48.1 2.9 %shard_map.85 = (bf16[1024,1024]{1,0:T(8,128)(2,1)S(1)}, bf16[1024,1024]{1,0:T(8,128)(2,1)S(1)}) custom-call(s32[32]{0:T(128)S(1)} %get-tuple-element.90.rows, s32[32]{0:T(128)S(1)} %get-tuple-element.89.cols, s32[1]{0:T(128)} %bitcast.59.count, bf16[1024,1024]{1,0:T(8,128)(2,1)S(1)} %copy-done), custom_call_target="tpu_custom_call" | custom-call | bytes 6291456 | tf_op jit(solution)/shard_map/pallas_call | solution.py:46
  51.1 5.4 %shard_map.86 = (f32[4,192,1024]{2,1,0:T(8,128)S(1)}, bf16[4,192,512]{2,1,0:T(8,128)(2,1)S(1)}, bf16[4,192,512]{2,1,0:T(8,128)(2,1)S(1)}, bf16[4,8,48,1024]{3,2,1,0:T(8,128)(2,1)S(1)}) custom-call(s32[4]{0:T(128)S(1)} %pad_add_fusion.pos, bf16[4,2,48,512]{3,2,1,0:T(8,128)(2,1)S(1)} %pad_maximum_fusion.2.refs_0_, ...), custom_call_target="tpu_custom_call" | custom-call | flops 3221225472 | bytes 13107200 | tf_op jit(solution)/shard_map/pallas_call | solution.py:46
  62.7 2.4 %collective-permute-start.20 = (bf16[192,512]{1,0:T(8,128)(2,1)S(1)}, bf16[192,512]{1,0:T(8,128)(2,1)S(1)}, u32[]{:S(2)}, u32[]{:S(2)}) collective-permute-start(bf16[192,512]{1,0:T(8,128)(2,1)S(1)} %get-tuple-element.62), channel_id=1, source_target_pairs={{0,2},{2,4},{4,6},{6,0},{1,3},{3,5},{5,7},{7,1},{8,10},{10,12},{12... | collective-permute-start | bytes 589832 | tf_op jit(solution)/shard_map/ppermute | solution.py:28
  65.1 2.0 %collective-permute-done.14 = bf16[192,512]{1,0:T(8,128)(2,1)S(1)} collective-permute-done((bf16[192,512]{1,0:T(8,128)(2,1)S(1)}, bf16[192,512]{1,0:T(8,128)(2,1)S(1)}, u32[]{:S(2)}, u32[]{:S(2)}) %collective-permute-start.14) | collective-permute-done | bytes 196640 | tf_op jit(solution)/shard_map/ppermute | solution.py:28
  68.2 3.8 %collective-permute-done.18 = bf16[192,512]{1,0:T(8,128)(2,1)S(1)} collective-permute-done((bf16[192,512]{1,0:T(8,128)(2,1)S(1)}, bf16[192,512]{1,0:T(8,128)(2,1)S(1)}, u32[]{:S(2)}, u32[]{:S(2)}) %collective-permute-start.18) | collective-permute-done | bytes 196640 | tf_op jit(solution)/shard_map/ppermute | solution.py:28
  72.4 2.3 %collective-permute-done.15.r1 = bf16[192,512]{1,0:T(8,128)(2,1)S(1)} collective-permute-done((bf16[192,512]{1,0:T(8,128)(2,1)S(1)}, bf16[192,512]{1,0:T(8,128)(2,1)S(1)}, u32[]{:S(2)}, u32[]{:S(2)}) %collective-permute-start.15) | collective-permute-done | bytes 196640 | tf_op jit(solution)/shard_map/ppermute | solution.py:28
  75.0 2.0 %collective-permute-start.26 = (bf16[192,512]{1,0:T(8,128)(2,1)S(1)}, bf16[192,512]{1,0:T(8,128)(2,1)S(1)}, u32[]{:S(2)}, u32[]{:S(2)}) collective-permute-start(bf16[192,512]{1,0:T(8,128)(2,1)S(1)} %get-tuple-element.66), channel_id=1, source_target_pairs={{6,0},{0,2},{2,4},{4,6},{7,1},{1,3},{3,5},{5,7},{14,8},{8,10},{10,... | collective-permute-start | bytes 589832 | tf_op jit(solution)/shard_map/ppermute | solution.py:23
  77.0 2.2 %collective-permute-done.19.r1 = bf16[192,512]{1,0:T(8,128)(2,1)S(1)} collective-permute-done((bf16[192,512]{1,0:T(8,128)(2,1)S(1)}, bf16[192,512]{1,0:T(8,128)(2,1)S(1)}, u32[]{:S(2)}, u32[]{:S(2)}) %collective-permute-start.19) | collective-permute-done | bytes 196640 | tf_op jit(solution)/shard_map/ppermute | solution.py:28
  81.2 2.9 %collective-permute-start.27 = (bf16[192,512]{1,0:T(8,128)(2,1)S(1)}, bf16[192,512]{1,0:T(8,128)(2,1)S(1)}, u32[]{:S(2)}, u32[]{:S(2)}) collective-permute-start(bf16[192,512]{1,0:T(8,128)(2,1)S(1)} %collective-permute-done.26), channel_id=1, source_target_pairs={{6,0},{0,2},{2,4},{4,6},{7,1},{1,3},{3,5},{5,7},{14,8},{8,10},{10,... | collective-permute-start | bytes 589832 | tf_op jit(solution)/shard_map/ppermute | solution.py:23
  84.8 3.4 %collective-permute-done.21 = bf16[192,512]{1,0:T(8,128)(2,1)S(1)} collective-permute-done((bf16[192,512]{1,0:T(8,128)(2,1)S(1)}, bf16[192,512]{1,0:T(8,128)(2,1)S(1)}, u32[]{:S(2)}, u32[]{:S(2)}) %collective-permute-start.21) | collective-permute-done | bytes 196640 | tf_op jit(solution)/shard_map/ppermute | solution.py:23
  88.3 3.7 %collective-permute-done.25 = bf16[192,512]{1,0:T(8,128)(2,1)S(1)} collective-permute-done((bf16[192,512]{1,0:T(8,128)(2,1)S(1)}, bf16[192,512]{1,0:T(8,128)(2,1)S(1)}, u32[]{:S(2)}, u32[]{:S(2)}) %collective-permute-start.25) | collective-permute-done | bytes 196640 | tf_op jit(solution)/shard_map/ppermute | solution.py:23
  92.2 3.0 %collective-permute-done.22 = bf16[192,512]{1,0:T(8,128)(2,1)S(1)} collective-permute-done((bf16[192,512]{1,0:T(8,128)(2,1)S(1)}, bf16[192,512]{1,0:T(8,128)(2,1)S(1)}, u32[]{:S(2)}, u32[]{:S(2)}) %collective-permute-start.22) | collective-permute-done | bytes 196640 | tf_op jit(solution)/shard_map/ppermute | solution.py:23
  95.3 3.0 %shard_map.91 = (f32[4,8,48,1024]{3,2,1,0:T(8,128)S(1)}, bf16[4,2,192,512]{3,2,1,0:T(8,128)(2,1)S(1)}) custom-call(s32[4]{0:T(128)S(1)} %pad_add_fusion.pos, bf16[4,192,512]{2,1,0:T(8,128)(2,1)S(1)} %pad_maximum_fusion.1.refs_0_, bf16[4,192,512]{2,1,0:T(8,128)(2,1)S(1)} %collective-permute-done.28.refs_1_, bf16[1024,1024]{1,0:T(8,128)(2,1)S(1)} %get-tuple-element.65.refs_2_), custom_call_target="tpu_custom_call" | custom-call | flops 1610612736 | bytes 11534336 | tf_op jit(solution)/shard_map/pallas_call | solution.py:46
  98.4 4.5 %shard_map.92 = (f32[4,2,48,512]{3,2,1,0:T(8,128)S(1)}, f32[4,2,48,512]{3,2,1,0:T(8,128)S(1)}, bf16[4,2,48,512]{3,2,1,0:T(8,128)(2,1)S(1)}, bf16[4,2,48,512]{3,2...) custom-call(s32[4]{0:T(128)S(1)} %pad_add_fusion.pos, ...), custom_call_target="tpu_custom_call" | custom-call | flops 1610612736 | bytes 19398656 | tf_op jit(solution)/shard_map/pallas_call | solution.py:46
  103.5 2.9 %collective-permute-start.29 = (bf16[4,2,48,512]{3,2,1,0:T(8,128)(2,1)S(1)}, bf16[4,2,48,512]{3,2,1,0:T(8,128)(2,1)S(1)}, u32[]{:S(2)}, u32[]{:S(2)}) collective-permute-start(bf16[4,2,48,512]{3,2,1,0:T(8,128)(2,1)S(1)} %get-tuple-element.70), channel_id=1, source_target_pairs={{0,56},{1,9},{8,0},{9,17},{16,8},{17,25},{24,16},{25,33},{32,24},{... | collective-permute-start | bytes 1179656 | tf_op jit(solution)/shard_map/ppermute | solution.py:41
  106.4 7.2 %collective-permute-done.30 = bf16[4,2,48,512]{3,2,1,0:T(8,128)(2,1)S(1)} collective-permute-done((bf16[4,2,48,512]{3,2,1,0:T(8,128)(2,1)S(1)}, bf16[4,2,48,512]{3,2,1,0:T(8,128)(2,1)S(1)}, u32[]{:S(2)}, u32[]{:S(2)}) %collective-permute-start.30) | collective-permute-done | bytes 393248 | tf_op jit(solution)/shard_map/ppermute | solution.py:41
  116.9 6.8 %collective-permute-done.31 = bf16[4,2,48,512]{3,2,1,0:T(8,128)(2,1)S(1)} collective-permute-done((bf16[4,2,48,512]{3,2,1,0:T(8,128)(2,1)S(1)}, bf16[4,2,48,512]{3,2,1,0:T(8,128)(2,1)S(1)}, u32[]{:S(2)}, u32[]{:S(2)}) %collective-permute-start.31) | collective-permute-done | bytes 393248 | tf_op jit(solution)/shard_map/ppermute | solution.py:41
  123.9 3.8 %collective-permute-done.34 = bf16[4,2,48,512]{3,2,1,0:T(8,128)(2,1)S(1)} collective-permute-done((bf16[4,2,48,512]{3,2,1,0:T(8,128)(2,1)S(1)}, bf16[4,2,48,512]{3,2,1,0:T(8,128)(2,1)S(1)}, u32[]{:S(2)}, u32[]{:S(2)}) %collective-permute-start.34) | collective-permute-done | bytes 393248 | tf_op jit(solution)/shard_map/ppermute | solution.py:41
  128.0 3.2 %collective-permute-start.37 = (bf16[2,48,512]{2,1,0:T(8,128)(2,1)S(1)}, bf16[2,48,512]{2,1,0:T(8,128)(2,1)S(1)}, u32[]{:S(2)}, u32[]{:S(2)}) collective-permute-start(bf16[2,48,512]{2,1,0:T(8,128)(2,1)S(1)} %get-tuple-element.85), channel_id=1, source_target_pairs={{0,192},{64,0},{128,64},{192,128},{1,193},{65,1},{129,65},{193,129... | collective-permute-start | bytes 294920 | tf_op jit(solution)/shard_map/ppermute | solution.py:28
  132.2 2.5 %collective-permute-start.40 = (bf16[2,48,512]{2,1,0:T(8,128)(2,1)S(1)}, bf16[2,48,512]{2,1,0:T(8,128)(2,1)S(1)}, u32[]{:S(2)}, u32[]{:S(2)}) collective-permute-start(bf16[2,48,512]{2,1,0:T(8,128)(2,1)S(1)} %get-tuple-element.82), channel_id=1, source_target_pairs={{0,56},{8,0},{16,8},{24,16},{32,24},{40,32},{48,40},{56,48},{1,57}... | collective-permute-start | bytes 294920 | tf_op jit(solution)/shard_map/ppermute | solution.py:28
  138.2 4.9 %collective-permute-done.39 = bf16[2,48,512]{2,1,0:T(8,128)(2,1)S(1)} collective-permute-done((bf16[2,48,512]{2,1,0:T(8,128)(2,1)S(1)}, bf16[2,48,512]{2,1,0:T(8,128)(2,1)S(1)}, u32[]{:S(2)}, u32[]{:S(2)}) %collective-permute-start.39) | collective-permute-done | bytes 98336 | tf_op jit(solution)/shard_map/ppermute | solution.py:28
  143.2 2.3 %collective-permute-start.41 = (bf16[48,1024]{1,0:T(8,128)(2,1)S(1)}, bf16[48,1024]{1,0:T(8,128)(2,1)S(1)}, u32[]{:S(2)}, u32[]{:S(2)}) collective-permute-start(bf16[48,1024]{1,0:T(8,128)(2,1)S(1)} %fusion.10), channel_id=1, source_target_pairs={{0,32},{8,40},{16,48},{24,56},{32,0},{40,8},{48,16},{56,24},{1,33}... | collective-permute-start | bytes 294920 | tf_op jit(solution)/shard_map/ppermute | solution.py:28
  145.5 8.9 %shard_map.93 = bf16[1024,1024]{1,0:T(8,128)(2,1)} custom-call(s32[32]{0:T(128)S(1)} %get-tuple-element.90.rows, s32[32]{0:T(128)S(1)} %get-tuple-element.89.cols, s32[1]{0:T(128)} %bitcast.60.count, bf16[4,8,48,1024]{3,2,1,0:T(8,128)(2,1)S(1)} %get-tuple-element.79.toks, bf16[4,2,192,1024]{3,2,1,0:T(8,128)(2,1)S(1)} %get-tuple-element.80.grads), custom_call_target="tpu_custom_call" | custom-call | flops 3221225472 | bytes 8388608 | tf_op jit(solution)/shard_map/pallas_call | solution.py:46
  (87 shorter events, 34.2 us)
Async XLA Ops:
  0.6 10.4 %collective-permute-start = (bf16[48,1024]{1,0:T(8,128)(2,1)}, bf16[48,1024]{1,0:T(8,128)(2,1)S(1)}, u32[]{:S(2)}, u32[]{:S(2)}) collective-permute-start(bf16[48,1024]{1,0:T(8,128)(2,1)} %param.6), channel_id=1, source_target_pairs={{32,0},{40,8},{48,16},{56,24},{0,32},{8,40},{16,48},{24,56},{33,1}... | collective-permute-start | bytes 294920 | tf_op jit(solution)/shard_map/ppermute | solution.py:23
  11.9 13.2 %collective-permute-start.6 = (bf16[2,48,512]{2,1,0:T(8,128)(2,1)S(1)}, bf16[2,48,512]{2,1,0:T(8,128)(2,1)S(1)}, u32[]{:S(2)}, u32[]{:S(2)}) collective-permute-start(bf16[2,48,512]{2,1,0:T(8,128)(2,1)S(1)} %get-tuple-element.46), channel_id=1, source_target_pairs={{56,0},{0,8},{8,16},{16,24},{24,32},{32,40},{40,48},{48,56},{57,1}... | collective-permute-start | bytes 294920 | tf_op jit(solution)/shard_map/ppermute | solution.py:23
  14.4 12.0 %collective-permute-start.5 = (bf16[2,48,512]{2,1,0:T(8,128)(2,1)S(1)}, bf16[2,48,512]{2,1,0:T(8,128)(2,1)S(1)}, u32[]{:S(2)}, u32[]{:S(2)}) collective-permute-start(bf16[2,48,512]{2,1,0:T(8,128)(2,1)S(1)} %get-tuple-element.46), channel_id=1, source_target_pairs={{16,0},{24,8},{32,16},{40,24},{48,32},{56,40},{0,48},{8,56},{17,1}... | collective-permute-start | bytes 294920 | tf_op jit(solution)/shard_map/ppermute | solution.py:23
  18.6 7.8 %collective-permute-start.4 = (bf16[2,48,512]{2,1,0:T(8,128)(2,1)S(1)}, bf16[2,48,512]{2,1,0:T(8,128)(2,1)S(1)}, u32[]{:S(2)}, u32[]{:S(2)}) collective-permute-start(bf16[2,48,512]{2,1,0:T(8,128)(2,1)S(1)} %get-tuple-element.46), channel_id=1, source_target_pairs={{8,0},{16,8},{24,16},{32,24},{40,32},{48,40},{56,48},{0,56},{9,1},... | collective-permute-start | bytes 294920 | tf_op jit(solution)/shard_map/ppermute | solution.py:23
  29.7 9.9 %collective-permute-start.10 = (bf16[4,2,48,512]{3,2,1,0:T(8,128)(2,1)S(1)}, bf16[4,2,48,512]{3,2,1,0:T(8,128)(2,1)S(1)}, u32[]{:S(2)}, u32[]{:S(2)}) collective-permute-start(bf16[4,2,48,512]{3,2,1,0:T(8,128)(2,1)S(1)} %pad_maximum_fusion.3.refs_4_), channel_id=1, source_target_pairs={{64,0},{193,1},{128,64},{1,65},{192,128},{65,129},{0,192},{129,193... | collective-permute-start | bytes 1179656 | tf_op jit(solution)/shard_map/ppermute | solution.py:37
  32.4 10.9 %collective-permute-start.7 = (bf16[4,2,48,512]{3,2,1,0:T(8,128)(2,1)S(1)}, bf16[4,2,48,512]{3,2,1,0:T(8,128)(2,1)S(1)}, u32[]{:S(2)}, u32[]{:S(2)}) collective-permute-start(bf16[4,2,48,512]{3,2,1,0:T(8,128)(2,1)S(1)} %pad_maximum_fusion.2.refs_0_), channel_id=1, source_target_pairs={{8,0},{57,1},{16,8},{1,9},{24,16},{9,17},{32,24},{17,25},{40,32},{... | collective-permute-start | bytes 1179656 | tf_op jit(solution)/shard_map/ppermute | solution.py:37
  33.7 17.4 %collective-permute-start.12 = (bf16[4,2,48,512]{3,2,1,0:T(8,128)(2,1)S(1)}, bf16[4,2,48,512]{3,2,1,0:T(8,128)(2,1)S(1)}, u32[]{:S(2)}, u32[]{:S(2)}) collective-permute-start(bf16[4,2,48,512]{3,2,1,0:T(8,128)(2,1)S(1)} %pad_maximum_fusion.3.refs_4_), channel_id=1, source_target_pairs={{192,0},{65,1},{0,64},{129,65},{64,128},{193,129},{128,192},{1,193... | collective-permute-start | bytes 1179656 | tf_op jit(solution)/shard_map/ppermute | solution.py:37
  33.7 17.4 %collective-permute-start.9 = (bf16[4,2,48,512]{3,2,1,0:T(8,128)(2,1)S(1)}, bf16[4,2,48,512]{3,2,1,0:T(8,128)(2,1)S(1)}, u32[]{:S(2)}, u32[]{:S(2)}) collective-permute-start(bf16[4,2,48,512]{3,2,1,0:T(8,128)(2,1)S(1)} %pad_maximum_fusion.2.refs_0_), channel_id=1, source_target_pairs={{56,0},{9,1},{0,8},{17,9},{8,16},{25,17},{16,24},{33,25},{24,32},{... | collective-permute-start | bytes 1179656 | tf_op jit(solution)/shard_map/ppermute | solution.py:37
  39.7 11.4 %collective-permute-start.11 = (bf16[4,2,48,512]{3,2,1,0:T(8,128)(2,1)S(1)}, bf16[4,2,48,512]{3,2,1,0:T(8,128)(2,1)S(1)}, u32[]{:S(2)}, u32[]{:S(2)}) collective-permute-start(bf16[4,2,48,512]{3,2,1,0:T(8,128)(2,1)S(1)} %collective-permute-done.10.refs_5_), channel_id=1, source_target_pairs={{64,0},{193,1},{128,64},{1,65},{192,128},{65,129},{0,192},{129,193... | collective-permute-start | bytes 1179656 | tf_op jit(solution)/shard_map/ppermute | solution.py:37
  43.3 7.8 %collective-permute-start.8 = (bf16[4,2,48,512]{3,2,1,0:T(8,128)(2,1)S(1)}, bf16[4,2,48,512]{3,2,1,0:T(8,128)(2,1)S(1)}, u32[]{:S(2)}, u32[]{:S(2)}) collective-permute-start(bf16[4,2,48,512]{3,2,1,0:T(8,128)(2,1)S(1)} %collective-permute-done.7.refs_1_), channel_id=1, source_target_pairs={{8,0},{57,1},{16,8},{1,9},{24,16},{9,17},{32,24},{17,25},{40,32},{... | collective-permute-start | bytes 1179656 | tf_op jit(solution)/shard_map/ppermute | solution.py:37
  59.3 7.8 %collective-permute-start.14 = (bf16[192,512]{1,0:T(8,128)(2,1)S(1)}, bf16[192,512]{1,0:T(8,128)(2,1)S(1)}, u32[]{:S(2)}, u32[]{:S(2)}) collective-permute-start(bf16[192,512]{1,0:T(8,128)(2,1)S(1)} %get-tuple-element.55), channel_id=1, source_target_pairs={{0,2},{2,4},{4,6},{6,0},{1,3},{3,5},{5,7},{7,1},{8,10},{10,12},{12... | collective-permute-start | bytes 589832 | tf_op jit(solution)/shard_map/ppermute | solution.py:28
  60.0 12.4 %collective-permute-start.16 = (bf16[192,512]{1,0:T(8,128)(2,1)S(1)}, bf16[192,512]{1,0:T(8,128)(2,1)S(1)}, u32[]{:S(2)}, u32[]{:S(2)}) collective-permute-start(bf16[192,512]{1,0:T(8,128)(2,1)S(1)} %get-tuple-element.56), channel_id=1, source_target_pairs={{0,6},{2,0},{4,2},{6,4},{1,7},{3,1},{5,3},{7,5},{8,14},{10,8},{12,... | collective-permute-start | bytes 589832 | tf_op jit(solution)/shard_map/ppermute | solution.py:28
  61.8 10.3 %collective-permute-start.18 = (bf16[192,512]{1,0:T(8,128)(2,1)S(1)}, bf16[192,512]{1,0:T(8,128)(2,1)S(1)}, u32[]{:S(2)}, u32[]{:S(2)}) collective-permute-start(bf16[192,512]{1,0:T(8,128)(2,1)S(1)} %get-tuple-element.61), channel_id=1, source_target_pairs={{0,6},{2,0},{4,2},{6,4},{1,7},{3,1},{5,3},{7,5},{8,14},{10,8},{12,... | collective-permute-start | bytes 589832 | tf_op jit(solution)/shard_map/ppermute | solution.py:28
  62.7 14.3 %collective-permute-start.20 = (bf16[192,512]{1,0:T(8,128)(2,1)S(1)}, bf16[192,512]{1,0:T(8,128)(2,1)S(1)}, u32[]{:S(2)}, u32[]{:S(2)}) collective-permute-start(bf16[192,512]{1,0:T(8,128)(2,1)S(1)} %get-tuple-element.62), channel_id=1, source_target_pairs={{0,2},{2,4},{4,6},{6,0},{1,3},{3,5},{5,7},{7,1},{8,10},{10,12},{12... | collective-permute-start | bytes 589832 | tf_op jit(solution)/shard_map/ppermute | solution.py:28
  67.2 7.6 %collective-permute-start.15 = (bf16[192,512]{1,0:T(8,128)(2,1)S(1)}, bf16[192,512]{1,0:T(8,128)(2,1)S(1)}, u32[]{:S(2)}, u32[]{:S(2)}) collective-permute-start(bf16[192,512]{1,0:T(8,128)(2,1)S(1)} %add_convert_fusion.3), channel_id=1, source_target_pairs={{0,2},{2,4},{4,6},{6,0},{1,3},{3,5},{5,7},{7,1},{8,10},{10,12},{12... | collective-permute-start | bytes 589832 | tf_op jit(solution)/shard_map/ppermute | solution.py:28
  72.1 7.1 %collective-permute-start.19 = (bf16[192,512]{1,0:T(8,128)(2,1)S(1)}, bf16[192,512]{1,0:T(8,128)(2,1)S(1)}, u32[]{:S(2)}, u32[]{:S(2)}) collective-permute-start(bf16[192,512]{1,0:T(8,128)(2,1)S(1)} %add_convert_fusion.2), channel_id=1, source_target_pairs={{0,6},{2,0},{4,2},{6,4},{1,7},{3,1},{5,3},{7,5},{8,14},{10,8},{12,... | collective-permute-start | bytes 589832 | tf_op jit(solution)/shard_map/ppermute | solution.py:28
  79.5 8.8 %collective-permute-start.21 = (bf16[192,512]{1,0:T(8,128)(2,1)S(1)}, bf16[192,512]{1,0:T(8,128)(2,1)S(1)}, u32[]{:S(2)}, u32[]{:S(2)}) collective-permute-start(bf16[192,512]{1,0:T(8,128)(2,1)S(1)} %get-tuple-element.64), channel_id=1, source_target_pairs={{2,0},{4,2},{6,4},{0,6},{3,1},{5,3},{7,5},{1,7},{10,8},{12,10},{14... | collective-permute-start | bytes 589832 | tf_op jit(solution)/shard_map/ppermute | solution.py:23
  79.6 12.4 %collective-permute-start.25 = (bf16[192,512]{1,0:T(8,128)(2,1)S(1)}, bf16[192,512]{1,0:T(8,128)(2,1)S(1)}, u32[]{:S(2)}, u32[]{:S(2)}) collective-permute-start(bf16[192,512]{1,0:T(8,128)(2,1)S(1)} %get-tuple-element.66), channel_id=1, source_target_pairs={{2,0},{4,2},{6,4},{0,6},{3,1},{5,3},{7,5},{1,7},{10,8},{12,10},{14... | collective-permute-start | bytes 589832 | tf_op jit(solution)/shard_map/ppermute | solution.py:23
  81.2 10.7 %collective-permute-start.27 = (bf16[192,512]{1,0:T(8,128)(2,1)S(1)}, bf16[192,512]{1,0:T(8,128)(2,1)S(1)}, u32[]{:S(2)}, u32[]{:S(2)}) collective-permute-start(bf16[192,512]{1,0:T(8,128)(2,1)S(1)} %collective-permute-done.26), channel_id=1, source_target_pairs={{6,0},{0,2},{2,4},{4,6},{7,1},{1,3},{3,5},{5,7},{14,8},{8,10},{10,... | collective-permute-start | bytes 589832 | tf_op jit(solution)/shard_map/ppermute | solution.py:23
  84.1 8.0 %collective-permute-start.23 = (bf16[192,512]{1,0:T(8,128)(2,1)S(1)}, bf16[192,512]{1,0:T(8,128)(2,1)S(1)}, u32[]{:S(2)}, u32[]{:S(2)}) collective-permute-start(bf16[192,512]{1,0:T(8,128)(2,1)S(1)} %get-tuple-element.64), channel_id=1, source_target_pairs={{6,0},{0,2},{2,4},{4,6},{7,1},{1,3},{3,5},{5,7},{14,8},{8,10},{10,... | collective-permute-start | bytes 589832 | tf_op jit(solution)/shard_map/ppermute | solution.py:23
  88.2 6.9 %collective-permute-start.22 = (bf16[192,512]{1,0:T(8,128)(2,1)S(1)}, bf16[192,512]{1,0:T(8,128)(2,1)S(1)}, u32[]{:S(2)}, u32[]{:S(2)}) collective-permute-start(bf16[192,512]{1,0:T(8,128)(2,1)S(1)} %collective-permute-done.21), channel_id=1, source_target_pairs={{2,0},{4,2},{6,4},{0,6},{3,1},{5,3},{7,5},{1,7},{10,8},{12,10},{14... | collective-permute-start | bytes 589832 | tf_op jit(solution)/shard_map/ppermute | solution.py:23
  102.8 10.7 %collective-permute-start.30 = (bf16[4,2,48,512]{3,2,1,0:T(8,128)(2,1)S(1)}, bf16[4,2,48,512]{3,2,1,0:T(8,128)(2,1)S(1)}, u32[]{:S(2)}, u32[]{:S(2)}) collective-permute-start(bf16[4,2,48,512]{3,2,1,0:T(8,128)(2,1)S(1)} %get-tuple-element.72), channel_id=1, source_target_pairs={{0,8},{1,57},{8,16},{9,1},{16,24},{17,9},{24,32},{25,17},{32,40},{... | collective-permute-start | bytes 1179656 | tf_op jit(solution)/shard_map/ppermute | solution.py:41
  103.5 12.0 %collective-permute-start.33 = (bf16[4,2,48,512]{3,2,1,0:T(8,128)(2,1)S(1)}, bf16[4,2,48,512]{3,2,1,0:T(8,128)(2,1)S(1)}, u32[]{:S(2)}, u32[]{:S(2)}) collective-permute-start(bf16[4,2,48,512]{3,2,1,0:T(8,128)(2,1)S(1)} %get-tuple-element.76), channel_id=1, source_target_pairs={{0,64},{1,193},{64,128},{65,1},{128,192},{129,65},{192,0},{193,129... | collective-permute-start | bytes 1179656 | tf_op jit(solution)/shard_map/ppermute | solution.py:41
  103.5 13.4 %collective-permute-start.29 = (bf16[4,2,48,512]{3,2,1,0:T(8,128)(2,1)S(1)}, bf16[4,2,48,512]{3,2,1,0:T(8,128)(2,1)S(1)}, u32[]{:S(2)}, u32[]{:S(2)}) collective-permute-start(bf16[4,2,48,512]{3,2,1,0:T(8,128)(2,1)S(1)} %get-tuple-element.70), channel_id=1, source_target_pairs={{0,56},{1,9},{8,0},{9,17},{16,8},{17,25},{24,16},{25,33},{32,24},{... | collective-permute-start | bytes 1179656 | tf_op jit(solution)/shard_map/ppermute | solution.py:41
  113.7 10.0 %collective-permute-start.31 = (bf16[4,2,48,512]{3,2,1,0:T(8,128)(2,1)S(1)}, bf16[4,2,48,512]{3,2,1,0:T(8,128)(2,1)S(1)}, u32[]{:S(2)}, u32[]{:S(2)}) collective-permute-start(bf16[4,2,48,512]{3,2,1,0:T(8,128)(2,1)S(1)} %add_convert_fusion.1), channel_id=1, source_target_pairs={{0,8},{1,57},{8,16},{9,1},{16,24},{17,9},{24,32},{25,17},{32,40},{... | collective-permute-start | bytes 1179656 | tf_op jit(solution)/shard_map/ppermute | solution.py:41
  113.8 10.1 %collective-permute-start.32 = (bf16[4,2,48,512]{3,2,1,0:T(8,128)(2,1)S(1)}, bf16[4,2,48,512]{3,2,1,0:T(8,128)(2,1)S(1)}, u32[]{:S(2)}, u32[]{:S(2)}) collective-permute-start(bf16[4,2,48,512]{3,2,1,0:T(8,128)(2,1)S(1)} %get-tuple-element.74), channel_id=1, source_target_pairs={{0,192},{1,65},{64,0},{65,129},{128,64},{129,193},{192,128},{193,1... | collective-permute-start | bytes 1179656 | tf_op jit(solution)/shard_map/ppermute | solution.py:41
  115.6 12.0 %collective-permute-start.34 = (bf16[4,2,48,512]{3,2,1,0:T(8,128)(2,1)S(1)}, bf16[4,2,48,512]{3,2,1,0:T(8,128)(2,1)S(1)}, u32[]{:S(2)}, u32[]{:S(2)}) collective-permute-start(bf16[4,2,48,512]{3,2,1,0:T(8,128)(2,1)S(1)} %add_convert_fusion), channel_id=1, source_target_pairs={{0,64},{1,193},{64,128},{65,1},{128,192},{129,65},{192,0},{193,129... | collective-permute-start | bytes 1179656 | tf_op jit(solution)/shard_map/ppermute | solution.py:41
  127.9 6.9 %collective-permute-start.35 = (bf16[2,48,512]{2,1,0:T(8,128)(2,1)S(1)}, bf16[2,48,512]{2,1,0:T(8,128)(2,1)S(1)}, u32[]{:S(2)}, u32[]{:S(2)}) collective-permute-start(bf16[2,48,512]{2,1,0:T(8,128)(2,1)S(1)} %get-tuple-element.84), channel_id=1, source_target_pairs={{0,64},{64,128},{128,192},{192,0},{1,65},{65,129},{129,193},{193,1... | collective-permute-start | bytes 294920 | tf_op jit(solution)/shard_map/ppermute | solution.py:28
  128.0 8.3 %collective-permute-start.37 = (bf16[2,48,512]{2,1,0:T(8,128)(2,1)S(1)}, bf16[2,48,512]{2,1,0:T(8,128)(2,1)S(1)}, u32[]{:S(2)}, u32[]{:S(2)}) collective-permute-start(bf16[2,48,512]{2,1,0:T(8,128)(2,1)S(1)} %get-tuple-element.85), channel_id=1, source_target_pairs={{0,192},{64,0},{128,64},{192,128},{1,193},{65,1},{129,65},{193,129... | collective-permute-start | bytes 294920 | tf_op jit(solution)/shard_map/ppermute | solution.py:28
  131.3 6.9 %collective-permute-start.38 = (bf16[2,48,512]{2,1,0:T(8,128)(2,1)S(1)}, bf16[2,48,512]{2,1,0:T(8,128)(2,1)S(1)}, u32[]{:S(2)}, u32[]{:S(2)}) collective-permute-start(bf16[2,48,512]{2,1,0:T(8,128)(2,1)S(1)} %get-tuple-element.81), channel_id=1, source_target_pairs={{0,8},{8,16},{16,24},{24,32},{32,40},{40,48},{48,56},{56,0},{1,9},... | collective-permute-start | bytes 294920 | tf_op jit(solution)/shard_map/ppermute | solution.py:28
  134.8 8.3 %collective-permute-start.39 = (bf16[2,48,512]{2,1,0:T(8,128)(2,1)S(1)}, bf16[2,48,512]{2,1,0:T(8,128)(2,1)S(1)}, u32[]{:S(2)}, u32[]{:S(2)}) collective-permute-start(bf16[2,48,512]{2,1,0:T(8,128)(2,1)S(1)} %get-tuple-element.83), channel_id=1, source_target_pairs={{0,16},{8,24},{16,32},{24,40},{32,48},{40,56},{48,0},{56,8},{1,17}... | collective-permute-start | bytes 294920 | tf_op jit(solution)/shard_map/ppermute | solution.py:28
  143.2 11.2 %collective-permute-start.41 = (bf16[48,1024]{1,0:T(8,128)(2,1)S(1)}, bf16[48,1024]{1,0:T(8,128)(2,1)S(1)}, u32[]{:S(2)}, u32[]{:S(2)}) collective-permute-start(bf16[48,1024]{1,0:T(8,128)(2,1)S(1)} %fusion.10), channel_id=1, source_target_pairs={{0,32},{8,40},{16,48},{24,56},{32,0},{40,8},{48,16},{56,24},{1,33}... | collective-permute-start | bytes 294920 | tf_op jit(solution)/shard_map/ppermute | solution.py:28
  (12 other events, 66.5 us)
